TPU v7x, 32 devices: a whole 2x2x4 slice. The times are simulated.
32 devices in a mesh: dp: 8 (over z, y), tensor: 4 (over x, core).
Axes of the slice: x: 2, y: 2, z: 4, core: 2. Of those that a mesh axis runs over, the one named last changes fastest.
Arguments:
- inputs: bfloat16 [8, 4096, 768], P('dp', 'tensor'), may hold values from -6 to 6
- w_qkv: bfloat16 [3, 768, 768], P(None, None, 'tensor'), may hold values from -0.21875 to 0.21875
- qv_bias: float32 [2, 768], P(None, 'tensor'), may hold values from -3 to 3
- w_proj: bfloat16 [768, 768], P('tensor'), may hold values from -0.875 to 0.875
- proj_bias: float32 [768], replicated, may hold values from -3 to 3
- w_fc1: bfloat16 [768, 3072], P(None, 'tensor'), may hold values from -0.21875 to 0.21875
- fc1_bias: float32 [3072], P('tensor'), may hold values from -3 to 3
- w_fc2: bfloat16 [3072, 768], P('tensor'), may hold values from -0.109375 to 0.109375
- fc2_bias: float32 [768], replicated, may hold values from -3 to 3
- norm1_gain: float32 [768], replicated, may hold values from 0.25 to 1.75
- norm1_shift: float32 [768], replicated, may hold values from -2 to 2
- norm2_gain: float32 [768], replicated, may hold values from 0.25 to 1.75
- norm2_shift: float32 [768], replicated, may hold values from -2 to 2
- rel_h: bfloat16 [27, 64], replicated, may hold values from -0.59765625 to 0.59765625
- rel_w: bfloat16 [27, 64], replicated, may hold values from -0.59765625 to 0.59765625
- cotangent: bfloat16 [8, 4096, 768], P('dp', 'tensor'), may hold values from -9 to 9
Outputs:
- output: bfloat16 [8, 4096, 768], P('dp', 'tensor')
- input_grad: bfloat16 [8, 4096, 768], P('dp', 'tensor')
- grad_qkv: float32 [3, 768, 768], P(None, None, 'tensor')
- grad_qv_bias: float32 [2, 768], P(None, 'tensor')
- grad_proj: float32 [768, 768], P('tensor')
- grad_proj_bias: float32 [768], replicated
- grad_fc1: float32 [768, 3072], P(None, 'tensor')
- grad_fc1_bias: float32 [3072], P('tensor')
- grad_fc2: float32 [3072, 768], P('tensor')
- grad_fc2_bias: float32 [768], replicated
- grad_norms: float32 [4, 768], replicated
- grad_rel: float32 [2, 27, 64], replicated
- clipped_qk: bfloat16 [2, 768, 768], P(None, None, 'tensor')
- head_max: float32 [12], P('tensor')
All inputs are finite; a program needn't handle non-finite values.
Results may differ from a plain program's by a relative error of at most 0.019.
Values may be sent and summed in bfloat16 or wider, within the bound.
A program may use at most 384 MiB of HBM per device.

v0:
```python
import jax
import jax.numpy as jnp
from jax import lax
from jax.sharding import PartitionSpec as P

HD = 64
GRID = 64
WIN = 14


eps_norm = 1e-06
clip_limit = 3.0
precise = lax.Precision.HIGHEST


def norm_rows(values, gain, shift):
    centre = values - jnp.mean(values, axis=-1, keepdims=True)
    spread = jnp.mean(centre * centre, axis=-1, keepdims=True)
    inverse = lax.rsqrt(spread + eps_norm)
    normal = centre * inverse
    return (normal * gain + shift, normal, inverse)


def norm_back(grad_norm, normal, inverse, gain):
    scaled = grad_norm * gain
    first_mean = jnp.mean(scaled, axis=-1, keepdims=True)
    second_mean = jnp.mean(scaled * normal, axis=-1, keepdims=True)
    grad_input = inverse * (scaled - first_mean - normal * second_mean)
    return (grad_input, jnp.sum(grad_norm * normal, axis=(0, 1)), jnp.sum(grad_norm, axis=(0, 1)))


def gelu_exact(values):
    return jax.nn.gelu(values, approximate=False)


def shards(
    inputs,
    w_qkv,
    qv_bias,
    w_proj,
    proj_bias,
    w_fc1,
    fc1_bias,
    w_fc2,
    fc2_bias,
    norm1_gain,
    norm1_shift,
    norm2_gain,
    norm2_shift,
    rel_h,
    rel_w,
    cotangent,
):
    single = jnp.float32
    narrow = jnp.bfloat16
    batch = inputs.shape[0]
    local = w_qkv.shape[2]
    groups = local // HD
    tiles = (GRID + WIN - 1) // WIN
    padg = tiles * WIN
    span = WIN * WIN
    count = batch * tiles * tiles
    inside = jnp.arange(padg) < GRID
    inside = inside[:, None] & inside[None, :]

    def to_windows(field):
        width = field.shape[-1]
        grid = field.reshape(batch, GRID, GRID, width)
        padded = jnp.pad(grid, ((0, 0), (0, padg - GRID), (0, padg - GRID), (0, 0)))
        padded = padded.reshape(batch, tiles, WIN, tiles, WIN, width).transpose(0, 1, 3, 2, 4, 5)
        return padded.reshape(count, span, width)

    def from_windows(field):
        width = field.shape[-1]
        grid = field.reshape(batch, tiles, tiles, WIN, WIN, width).transpose(0, 1, 3, 2, 4, 5)
        grid = grid.reshape(batch, padg, padg, width)[:, :GRID, :GRID]
        return grid.reshape(batch, GRID * GRID, width)

    offsets = jnp.arange(WIN)[:, None] - jnp.arange(WIN)[None, :] + (WIN - 1)
    one_hot = (offsets[:, :, None] == jnp.arange(2 * WIN - 1)[None, None, :]).astype(narrow)
    rows_table = jnp.einsum("xar,rc->xac", one_hot, rel_h, preferred_element_type=single).astype(
        narrow
    )
    cols_table = jnp.einsum("ybr,rc->ybc", one_hot, rel_w, preferred_element_type=single).astype(
        narrow
    )

    def scores_of(q_win, k_win):
        logits = jnp.einsum("nlgc,nmgc->nglm", q_win, k_win, preferred_element_type=single) * 0.125
        q_grid = q_win.reshape(count, WIN, WIN, groups, HD)
        rel_rows = jnp.einsum("nxygc,xac->ngxya", q_grid, rows_table, preferred_element_type=single)
        rel_cols = jnp.einsum("nxygc,ybc->ngxyb", q_grid, cols_table, preferred_element_type=single)
        scores = (
            logits.reshape(count, groups, WIN, WIN, WIN, WIN)
            + rel_rows[..., :, None]
            + rel_cols[..., None, :]
        )
        return (logits, scores.reshape(count, groups, span, span))

    source = inputs.astype(single)
    first, normal1, inverse1 = norm_rows(source, norm1_gain, norm1_shift)
    first_full = lax.all_gather(first.astype(narrow), "tensor", axis=1, tiled=True)
    first_win = to_windows(first_full)
    projected = jnp.einsum("nld,jdc->jnlc", first_win, w_qkv, preferred_element_type=single)
    q_win = (projected[0] + qv_bias[0]).astype(narrow).reshape(count, span, groups, HD)
    k_win = projected[1].astype(narrow).reshape(count, span, groups, HD)
    v_win = (projected[2] + qv_bias[1]).astype(narrow).reshape(count, span, groups, HD)
    logits, scores = scores_of(q_win, k_win)
    row_valid = (
        inside.reshape(tiles, WIN, tiles, WIN).transpose(0, 2, 1, 3).reshape(tiles * tiles, span)
    )
    row_valid = jnp.tile(row_valid, (batch, 1))
    local_max = jnp.max(jnp.where(row_valid[:, None, :, None], logits, -1e30), axis=(0, 2, 3))
    head_max = lax.pmax(local_max, "dp")
    top = jnp.max(scores, axis=-1, keepdims=True)
    log_total = top + jnp.log(jnp.sum(jnp.exp(scores - top), axis=-1, keepdims=True))
    probs = jnp.exp(scores - log_total).astype(narrow)
    mixed = jnp.einsum("nglm,nmgc->nlgc", probs, v_win, preferred_element_type=single).astype(
        narrow
    )
    mixed = mixed.reshape(count, span, local)
    attn_win = jnp.einsum("nlc,cd->nld", mixed, w_proj, preferred_element_type=single)
    attn_terms = from_windows(attn_win)
    attn = (
        lax.psum_scatter(
            attn_terms.astype(jnp.bfloat16), "tensor", scatter_dimension=1, tiled=True
        ).astype(jnp.float32)
        + proj_bias
    )
    middle = source + attn
    second, normal2, inverse2 = norm_rows(middle, norm2_gain, norm2_shift)
    second_low = second.astype(narrow)
    grad_out = cotangent.astype(single)
    grad_fc2_bias = jnp.sum(grad_out, axis=(0, 1))
    second_full = lax.all_gather(second_low, "tensor", axis=1, tiled=True)
    hidden_pre = (
        jnp.einsum("btd,df->btf", second_full, w_fc1, preferred_element_type=single) + fc1_bias
    )
    activated, gelu_back = jax.vjp(gelu_exact, hidden_pre)
    hidden = activated.astype(narrow)
    mlp_terms = jnp.einsum("btf,fd->btd", hidden, w_fc2, preferred_element_type=single)
    branch = (
        lax.psum_scatter(
            mlp_terms.astype(jnp.bfloat16), "tensor", scatter_dimension=1, tiled=True
        ).astype(jnp.float32)
        + fc2_bias
    )
    output = (middle + branch).astype(narrow)
    out_full = lax.all_gather(cotangent, "tensor", axis=1, tiled=True)
    grad_fc2 = jnp.einsum("btf,btd->fd", hidden, out_full, preferred_element_type=single)
    grad_hidden = jnp.einsum("btd,fd->btf", out_full, w_fc2, preferred_element_type=single)
    grad_pre = gelu_back(grad_hidden)[0].astype(narrow)
    grad_fc1_bias = jnp.sum(grad_pre, axis=(0, 1), dtype=single)
    grad_fc1 = jnp.einsum("btd,btf->df", second_full, grad_pre, preferred_element_type=single)
    second_terms = jnp.einsum("btf,df->btd", grad_pre, w_fc1, preferred_element_type=single)
    grad_second = lax.psum_scatter(
        second_terms.astype(jnp.bfloat16), "tensor", scatter_dimension=1, tiled=True
    ).astype(jnp.float32)
    grad_middle, gain2_grad, shift2_grad = norm_back(grad_second, normal2, inverse2, norm2_gain)
    grad_middle = grad_middle + grad_out
    grad_attn = grad_middle.astype(narrow)
    grad_proj_bias = jnp.sum(grad_attn, axis=(0, 1), dtype=single)
    attn_full = lax.all_gather(grad_attn, "tensor", axis=1, tiled=True)
    attn_grad_win = to_windows(attn_full)
    grad_proj = jnp.einsum("nlc,nld->cd", mixed, attn_grad_win, preferred_element_type=single)
    grad_mixed = jnp.einsum(
        "nld,cd->nlc", attn_grad_win, w_proj, preferred_element_type=single
    ).astype(narrow)
    grad_mixed = grad_mixed.reshape(count, span, groups, HD)
    _, scores = scores_of(q_win, k_win)
    probs_full = jnp.exp(scores - log_total)
    probs_low = probs_full.astype(narrow)
    grad_probs = jnp.einsum("nlgc,nmgc->nglm", grad_mixed, v_win, preferred_element_type=single)
    grad_value = jnp.einsum(
        "nglm,nlgc->nmgc", probs_low, grad_mixed, preferred_element_type=single
    ).astype(narrow)
    row_dot = jnp.sum(probs_full * grad_probs, axis=-1, keepdims=True)
    grad_scores = (probs_full * (grad_probs - row_dot)).astype(narrow)
    query_main = (
        jnp.einsum("nglm,nmgc->nlgc", grad_scores, k_win, preferred_element_type=single) * 0.125
    )
    grad_key = (
        jnp.einsum("nglm,nlgc->nmgc", grad_scores, q_win, preferred_element_type=single) * 0.125
    ).astype(narrow)
    grad_grid = grad_scores.reshape(count, groups, WIN, WIN, WIN, WIN)
    grad_rows = jnp.sum(grad_grid, axis=5, dtype=single)
    grad_cols = jnp.sum(grad_grid, axis=4, dtype=single)
    query_grid = q_win.reshape(count, WIN, WIN, groups, HD).astype(single)
    query_rel = jnp.einsum(
        "ngxya,xac->nxygc", grad_rows, rows_table.astype(single), precision=precise
    )
    query_rel = query_rel + jnp.einsum(
        "ngxyb,ybc->nxygc", grad_cols, cols_table.astype(single), precision=precise
    )
    grad_query = (query_main + query_rel.reshape(count, span, groups, HD)).astype(narrow)
    rows_full = jnp.einsum("ngxya,nxygc->xac", grad_rows, query_grid, precision=precise)
    cols_full = jnp.einsum("ngxyb,nxygc->ybc", grad_cols, query_grid, precision=precise)
    hot_single = one_hot.astype(single)
    grad_rel = jnp.stack(
        [
            jnp.einsum("xar,xac->rc", hot_single, rows_full, precision=precise),
            jnp.einsum("ybr,ybc->rc", hot_single, cols_full, precision=precise),
        ]
    )
    grad_qv_bias = jnp.stack(
        [
            jnp.sum(grad_query, axis=(0, 1), dtype=single).reshape(local),
            jnp.sum(grad_value, axis=(0, 1), dtype=single).reshape(local),
        ]
    )
    stacked = jnp.stack(
        [
            grad_query.reshape(count, span, local),
            grad_key.reshape(count, span, local),
            grad_value.reshape(count, span, local),
        ]
    )
    grad_qkv = jnp.einsum("nld,jnlc->jdc", first_win, stacked, preferred_element_type=single)
    first_win_terms = jnp.einsum("jnlc,jdc->nld", stacked, w_qkv, preferred_element_type=single)
    first_terms = from_windows(first_win_terms)
    grad_first = lax.psum_scatter(
        first_terms.astype(jnp.bfloat16), "tensor", scatter_dimension=1, tiled=True
    ).astype(jnp.float32)
    grad_source, gain1_grad, shift1_grad = norm_back(grad_first, normal1, inverse1, norm1_gain)
    input_grad = (grad_middle + grad_source).astype(narrow)
    grad_norms = jnp.stack([gain1_grad, shift1_grad, gain2_grad, shift2_grad])
    grad_norms, grad_proj_bias, grad_fc2_bias, grad_rel = lax.psum(
        (grad_norms, grad_proj_bias, grad_fc2_bias, grad_rel), ("dp", "tensor")
    )
    grad_qkv, grad_qv_bias, grad_proj, grad_fc1, grad_fc1_bias, grad_fc2 = lax.psum(
        (grad_qkv, grad_qv_bias, grad_proj, grad_fc1, grad_fc1_bias, grad_fc2), "dp"
    )
    factor = jnp.sqrt(clip_limit / jnp.maximum(head_max, clip_limit))
    columns = jnp.repeat(factor, HD)
    clipped_qk = (w_qkv[:2].astype(single) * columns).astype(narrow)
    return (
        output,
        input_grad,
        grad_qkv,
        grad_qv_bias,
        grad_proj,
        grad_proj_bias,
        grad_fc1,
        grad_fc1_bias,
        grad_fc2,
        grad_fc2_bias,
        grad_norms,
        grad_rel,
        clipped_qk,
        head_max,
    )


def solution(mesh):
    return jax.shard_map(
        shards,
        mesh=mesh,
        in_specs=(
            P("dp", "tensor", None),
            P(None, None, "tensor"),
            P(None, "tensor"),
            P("tensor", None),
            P(),
            P(None, "tensor"),
            P("tensor"),
            P("tensor", None),
            P(),
            P(),
            P(),
            P(),
            P(),
            P(),
            P(),
            P("dp", "tensor", None),
        ),
        out_specs=(
            P("dp", "tensor", None),
            P("dp", "tensor", None),
            P(None, None, "tensor"),
            P(None, "tensor"),
            P("tensor", None),
            P(),
            P(None, "tensor"),
            P("tensor"),
            P("tensor", None),
            P(),
            P(),
            P(),
            P(None, None, "tensor"),
            P("tensor"),
        ),
        check_vma=False,
    )
```

profile of v0, /device:TPU:0, one launch (start us, length us, event | category | flops | bytes accessed | tf_op | source)
XLA Modules:
  0.0 1579.4 jit_solution(3225467008868292127)
XLA Ops:
  17.5 46.6 %all-gather.5.cloned.1.call-done = bf16[1,4096,768]{2,1,0:T(8,128)(2,1)} async-done(((bf16[1,1024,768]{2,1,0:T(8,128)(2,1)}), bf16[1,4096,768]{2,1,0:T(8,128)(2,1)}) %all-gather.5.cloned.1.call-update) | async-done | bytes 6291472 | tf_op jit(solution)/shard_map/all_gather | solution.py:102
  70.6 11.5 reshape.380
  89.8 11.4 reshape.395
  154.9 34.3 %add.203 = f32[25,3,14,14,14,14]{0,5,4,3,2,1:T(8,128)} broadcast(f32[25,3,14,14,14]{0,4,3,2,1:T(8,128)} %copy.114), dimensions={0,1,2,3,4} | broadcast | bytes 12348000 | tf_op jit(solution)/shard_map/add | solution.py:94
  189.2 64.5 %add.204 = f32[25,3,196,196]{0,3,2,1:T(8,128)} reshape(f32[25,3,14,14,14,14]{0,5,4,3,2,1:T(8,128)} %add.203) | data formatting | bytes 23049600 | tf_op jit(solution)/shard_map/add | solution.py:94
  253.8 38.9 %copy.115 = f32[25,3,196,196]{2,3,1,0:T(8,128)} copy(f32[25,3,196,196]{0,3,2,1:T(8,128)} %add.204) | data formatting | bytes 23049600 | tf_op jit(solution)/shard_map/add | solution.py:94
  292.7 24.2 %add.206 = f32[25,3,14,14,14,14]{0,5,4,3,2,1:T(8,128)} broadcast(f32[25,3,14,14,14]{0,4,3,2,1:T(8,128)} %copy.118), dimensions={0,1,2,3,5} | broadcast | bytes 12348000 | tf_op jit(solution)/shard_map/add | solution.py:94
  316.9 64.5 %add.207 = f32[25,3,196,196]{0,3,2,1:T(8,128)} reshape(f32[25,3,14,14,14,14]{0,5,4,3,2,1:T(8,128)} %add.206) | data formatting | bytes 23049600 | tf_op jit(solution)/shard_map/add | solution.py:94
  381.4 39.0 %copy.119 = f32[25,3,196,196]{2,3,1,0:T(8,128)} copy(f32[25,3,196,196]{0,3,2,1:T(8,128)} %add.207) | data formatting | bytes 23049600 | tf_op jit(solution)/shard_map/add | solution.py:94
  420.4 19.6 %fusion.98 = (f32[25,3,196]{2,1,0:T(4,128)S(1)}, f32[25,3,196,196]{2,3,1,0:T(8,128)}, f32[3]{0:T(128)}) fusion(f32[25,3,196,196]{2,3,1,0:T(8,128)} %copy.119, f32[25,3,196,196]{2,3,1,0:T(8,128)} %copy.115, pred[25,196]{1,0:T(8,128)(4,1)S(1)} %copy-done.39, bf16[25,196,3,64]{1,3,2,0:T(8,128)(2,1)} %bitcast.163, f32[25,196,3,64]{1,3,2,0:T(8,128)} %bitcast.154, ...), kind=kOutput, calls=%fused_computation.161 | convolution fusion | flops 387947744 | bytes 40283680 | tf_op jit(solution)/shard_map/nlgc,nmgc->nglm/dot_general | solution.py:89
  449.4 11.1 convolution_convert_fusion.4
  494.0 11.5 reshape.383
  512.3 58.1 %reduce-scatter.5.cloned.1.call-done = bf16[1,1024,768]{2,1,0:T(8,128)(2,1)} async-done(((bf16[1,4096,768]{2,1,0:T(8,128)(2,1)}), bf16[1,1024,768]{2,1,0:T(8,128)(2,1)}) %reduce-scatter.5.cloned.1.call-update) | async-done | bytes 1572880 | tf_op jit(solution)/shard_map/reduce_scatter | solution.py:125
  577.5 45.9 %all-gather.7.cloned.1.call-done = bf16[1,4096,768]{2,1,0:T(8,128)(2,1)} async-done(((bf16[1,1024,768]{2,1,0:T(8,128)(2,1)}), bf16[1,4096,768]{2,1,0:T(8,128)(2,1)}) %all-gather.7.cloned.1.call-update) | async-done | bytes 6291472 | tf_op jit(solution)/shard_map/all_gather | solution.py:135
  633.6 37.7 %all-gather.9.cloned.1.call-done = bf16[1,4096,768]{2,1,0:T(8,128)(2,1)} async-done(((bf16[1,1024,768]{2,1,0:T(8,128)(2,1)}), bf16[1,4096,768]{2,1,0:T(8,128)(2,1)}) %all-gather.9.cloned.1.call-update) | async-done | bytes 6291472 | tf_op jit(solution)/shard_map/all_gather | solution.py:149
  671.3 36.9 %convert_reduce_fusion = (f32[768]{0:T(1024)}, bf16[4096,768]{1,0:T(8,128)(2,1)S(1)}, f32[4096,768]{1,0:T(8,128)}) fusion(f32[4096,768]{1,0:T(8,128)} %fusion.17, f32[768]{0:T(1024)S(1)} %copy-done.48, bf16[768,768]{1,0:T(8,128)(2,1)S(1)} %copy-done, bf16[1,4096,768]{2,1,0:T(8,128)(2,1)} %all-gather.9.cloned.1.call-done), kind=kOutput, calls=%fused_computation.9 | convolution fusion | flops 5067766784 | bytes 38934528 | tf_op jit(solution)/shard_map/btd,fd->btf/dot_general | solution.py:151
  717.9 11.2 multiply_convert_fusion.1
  738.8 37.6 %reduce-scatter.9.cloned.1.call-done = bf16[1,1024,768]{2,1,0:T(8,128)(2,1)} async-done(((bf16[1,4096,768]{2,1,0:T(8,128)(2,1)}), bf16[1,1024,768]{2,1,0:T(8,128)(2,1)}) %reduce-scatter.9.cloned.1.call-update) | async-done | bytes 1572880 | tf_op jit(solution)/shard_map/reduce_scatter | solution.py:156
  780.4 56.8 %reduce-scatter.7.cloned.1.call-done = bf16[1,1024,768]{2,1,0:T(8,128)(2,1)} async-done(((bf16[1,4096,768]{2,1,0:T(8,128)(2,1)}), bf16[1,1024,768]{2,1,0:T(8,128)(2,1)}) %reduce-scatter.7.cloned.1.call-update) | async-done | bytes 1572880 | tf_op jit(solution)/shard_map/reduce_scatter | solution.py:143
  843.6 46.5 %all-gather.11.cloned.1.call-done = bf16[1,4096,768]{2,1,0:T(8,128)(2,1)} async-done(((bf16[1,1024,768]{2,1,0:T(8,128)(2,1)}), bf16[1,4096,768]{2,1,0:T(8,128)(2,1)}) %all-gather.11.cloned.1.call-update) | async-done | bytes 6291472 | tf_op jit(solution)/shard_map/all_gather | solution.py:163
  896.7 11.7 reshape.387
  916.1 11.4 reshape.388
  943.2 13.2 multiply_reduce_fusion
  976.9 30.4 %copy.125 = f32[25,3,196,196]{0,3,2,1:T(8,128)} copy(bf16[25,3,196,196]{2,3,1,0:T(8,128)(2,1)} %copy-done.4) | data formatting | bytes 17287200 | tf_op jit(solution)/shard_map/convert_element_type | solution.py:186
  1007.3 64.5 %reshape.394 = f32[25,3,14,14,14,14]{0,5,4,3,2,1:T(8,128)} reshape(f32[25,3,196,196]{0,3,2,1:T(8,128)} %copy.125) | data formatting | bytes 23049600 | tf_op jit(solution)/shard_map/convert_element_type | solution.py:186
  1071.8 94.8 %fusion.96 = (f32[25,3,14,14,14]{0,4,3,2,1:T(8,128)}, f32[25,3,14,14,14]{0,4,3,2,1:T(8,128)}) fusion(f32[25,3,14,14,14,14]{0,5,4,3,2,1:T(8,128)} %reshape.394), kind=kLoop, calls=%fused_computation.160 | loop fusion | flops 5350800 | bytes 13171200 | tf_op jit(solution)/shard_map/reduce_sum | solution.py:186
  1227.3 11.4 reshape.391
  1246.0 11.5 reshape.392
  1296.3 21.6 %pmax.7 = f32[3]{0:T(128)S(1)} all-reduce(f32[3]{0:T(128)S(1)} %copy-done.53), channel_id=1, replica_groups=mesh['dp'=8,'tensor'=4] {'dp'}, use_global_device_ids=true, to_apply=%region_37.38 | all-reduce | flops 3 | bytes 24 | tf_op jit(solution)/shard_map/pmax | solution.py:114
  1319.3 18.3 %all-reduce.3 = (f32[2,192]{1,0:T(2,128)}, f32[768]{0:T(1024)}) all-reduce(f32[2,192]{1,0:T(2,128)S(1)} %pad_maximum_fusion.7, f32[768]{0:T(1024)S(1)} %copy-done.49), channel_id=1, replica_groups=mesh['dp'=8,'tensor'=4] {'dp'}, use_global_device_ids=true, to_apply=%region_20.21 | all-reduce | flops 1152 | bytes 9216 | tf_op jit(solution)/shard_map/psum | solution.py:230
  1360.6 43.6 %all-reduce.2 = (f32[768]{0:T(1024)}, f32[768]{0:T(1024)}, f32[4,768]{1,0:T(4,128)}, f32[2,27,64]{2,1,0:T(8,128)S(1)}) all-reduce(f32[768]{0:T(1024)S(1)} %copy-done.44, f32[768]{0:T(1024)S(1)} %copy-done.45, f32[4,768]{1,0:T(4,128)S(1)} %pad_maximum_fusion.6, ...), channel_id=1, replica_groups=mesh['dp'=8,'tensor'=4] {'dp','tensor'}, use_global_device_ids=true, to_apply=%region_23.24 | all-reduce | flops 8064 | bytes 64512 | tf_op jit(solution)/shard_map/psum | solution.py:227
  1408.6 156.0 %all-reduce.7.cloned.1.call-done = (f32[3,768,192]{1,2,0:T(8,128)}, f32[192,768]{1,0:T(8,128)}, f32[768,768]{1,0:T(8,128)}, f32[768,768]{1,0:T(8,128)}) async-done(((f32[3,768,192]{1,2,0:T(8,128)}, f32[192,768]{1,0:T(8,128)}, f32[768,768]{1,0:T(8,128)}, f32[768,768]{1,0:T(8,128)}), (f32[3,768,192]{1,2,0:T(8,128)}, f32[192,768]{1,0:T(8,128)}, f32[768,768]{1,0:T(8,128)}, ...) | async-done | bytes 7077904 | tf_op jit(solution)/shard_map/psum | solution.py:230
  (235 shorter events, 368.1 us)
Async XLA Ops:
  7.2 664.1 %copy-start = (bf16[768,768]{1,0:T(8,128)(2,1)S(1)}, bf16[768,768]{1,0:T(8,128)(2,1)}, u32[]{:S(2)}) copy-start(bf16[768,768]{1,0:T(8,128)(2,1)} %param.23) | copy-start | bytes 3538948
  7.2 56.9 %all-gather.5.cloned.1.call-start = ((), (), s32[]{:S(2)}) async-start(), calls=%async_computation.4 | async-start | bytes 7864320 | tf_op jit(solution)/shard_map/all_gather | solution.py:102
  14.9 555.4 %reduce-scatter.5.cloned.1.call-start = ((), (), s32[]{:S(2)}) async-start(), calls=%async_computation.5 | async-start | bytes 7864320 | tf_op jit(solution)/shard_map/reduce_scatter | solution.py:125
  15.7 116.1 %copy-start.36 = (f32[3,64]{1,0:T(4,128)}, f32[3,64]{1,0:T(4,128)S(1)}, u32[]{:S(2)}) copy-start(f32[3,64]{1,0:T(4,128)S(1)} %add.196) | copy-start | bytes 2308
  17.3 128.5 %copy-start.19 = (bf16[14,14,64,1,1]{2,1,4,3,0:T(8,128)(2,1)}, bf16[14,14,64,1,1]{2,1,4,3,0:T(8,128)(2,1)S(1)}, u32[]{:S(2)}) copy-start(bf16[14,14,64,1,1]{2,1,4,3,0:T(8,128)(2,1)S(1)} %fusion.76) | copy-start | bytes 75268
  17.5 119.3 %copy-start.25 = (bf16[14,14,64]{2,1,0:T(8,128)(2,1)}, bf16[14,14,64]{2,1,0:T(8,128)(2,1)S(1)}, u32[]{:S(2)}) copy-start(bf16[14,14,64]{2,1,0:T(8,128)(2,1)S(1)} %convolution_convert_fusion.5) | copy-start | bytes 75268
  381.4 39.0 %copy-start.37 = (f32[3,64]{1,0:T(4,128)S(1)}, f32[3,64]{1,0:T(4,128)}, u32[]{:S(2)}) copy-start(f32[3,64]{1,0:T(4,128)} %copy-done.36) | copy-start | bytes 2308
  381.4 39.0 %copy-start.39 = (pred[25,196]{1,0:T(8,128)(4,1)S(1)}, pred[25,196]{1,0:T(8,128)(4,1)}, u32[]{:S(2)}) copy-start(pred[25,196]{1,0:T(8,128)(4,1)} %and.22) | copy-start | bytes 14704
  511.8 58.6 %copy-start.1 = (bf16[1,1024,768]{2,1,0:T(8,128)(2,1)S(1)}, bf16[1,1024,768]{2,1,0:T(8,128)(2,1)}, u32[]{:S(2)}) copy-start(bf16[1,1024,768]{2,1,0:T(8,128)(2,1)} %param.16) | copy-start | bytes 4718596
  511.8 58.6 %copy-start.31 = (f32[768]{0:T(1024)S(1)}, f32[768]{0:T(1024)}, u32[]{:S(2)}) copy-start(f32[768]{0:T(1024)} %param.20) | copy-start | bytes 9220
  511.8 62.9 %copy-start.35 = (f32[768]{0:T(1024)S(1)}, f32[768]{0:T(1024)}, u32[]{:S(2)}) copy-start(f32[768]{0:T(1024)} %param.27) | copy-start | bytes 9220
  511.8 62.9 %copy-start.50 = (f32[768]{0:T(1024)S(1)}, f32[768]{0:T(1024)}, u32[]{:S(2)}) copy-start(f32[768]{0:T(1024)} %param.28) | copy-start | bytes 9220
  511.8 111.5 %all-gather.7.cloned.1.call-start = ((), (), s32[]{:S(2)}) async-start(), calls=%async_computation.6 | async-start | bytes 7864320 | tf_op jit(solution)/shard_map/all_gather | solution.py:135
  576.8 94.5 %all-gather.9.cloned.1.call-start = ((), (), s32[]{:S(2)}) async-start(), calls=%async_computation.8 | async-start | bytes 7864320 | tf_op jit(solution)/shard_map/all_gather | solution.py:149
  577.4 93.9 %copy-start.48 = (f32[768]{0:T(1024)S(1)}, f32[768]{0:T(1024)}, u32[]{:S(2)}) copy-start(f32[768]{0:T(1024)} %param.22) | copy-start | bytes 9220
  577.4 198.9 %reduce-scatter.9.cloned.1.call-start = ((), (), s32[]{:S(2)}) async-start(), calls=%async_computation.9 | async-start | bytes 7864320 | tf_op jit(solution)/shard_map/reduce_scatter | solution.py:156
  671.3 39.5 %copy-start.54 = (bf16[768,768]{1,0:T(8,128)(2,1)S(1)}, bf16[768,768]{1,0:T(8,128)(2,1)}, u32[]{:S(2)}) copy-start(bf16[768,768]{1,0:T(8,128)(2,1)} %param.21) | copy-start | bytes 3538948
  717.8 119.3 %reduce-scatter.7.cloned.1.call-start = ((), (), s32[]{:S(2)}) async-start(), calls=%async_computation.7 | async-start | bytes 7864320 | tf_op jit(solution)/shard_map/reduce_scatter | solution.py:143
  738.7 98.4 %copy-start.51 = (f32[768]{0:T(1024)S(1)}, f32[768]{0:T(1024)}, u32[]{:S(2)}) copy-start(f32[768]{0:T(1024)} %param.24) | copy-start | bytes 9220
  738.7 151.4 %all-gather.11.cloned.1.call-start = ((), (), s32[]{:S(2)}) async-start(), calls=%async_computation.10 | async-start | bytes 7864320 | tf_op jit(solution)/shard_map/all_gather | solution.py:163
  843.6 513.7 %reduce-scatter.11.cloned.1.call-start = ((), (), s32[]{:S(2)}) async-start(), calls=%async_computation.11 | async-start | bytes 7864320 | tf_op jit(solution)/shard_map/reduce_scatter | solution.py:221
  956.4 14.1 copy-start.38
  1071.8 94.8 %copy-start.26 = (bf16[14,14,64]{2,1,0:T(8,128)(2,1)S(1)}, bf16[14,14,64]{2,1,0:T(8,128)(2,1)}, u32[]{:S(2)}) copy-start(bf16[14,14,64]{2,1,0:T(8,128)(2,1)} %copy-done.25) | copy-start | bytes 75268
  1263.7 301.0 %all-reduce.7.cloned.1.call-start = ((), (), s32[]{:S(2)}) async-start(), calls=%async_computation.12 | async-start | bytes 14155776 | tf_op jit(solution)/shard_map/psum | solution.py:230
  1263.8 21.2 %slice-start.2 = ((s8[7680000]{0:T(1024)(128)(4,1)}), s8[4194304]{0:T(1024)(128)(4,1)S(1)}, s32[]{:S(2)}) async-start(s8[7680000]{0:T(1024)(128)(4,1)} %bitcast.171), calls=%async_computation.15 | async-start | bytes 8388608
  1263.8 23.9 %slice-start = ((s8[7680000]{0:T(1024)(128)(4,1)}), s8[4194304]{0:T(1024)(128)(4,1)S(1)}, s32[]{:S(2)}) async-start(s8[7680000]{0:T(1024)(128)(4,1)} %bitcast.169), calls=%async_computation.13 | async-start | bytes 8388608
  1295.7 23.4 %copy-start.43 = (f32[768]{0:T(1024)S(1)}, f32[768]{0:T(1024)}, u32[]{:S(2)}) copy-start(f32[768]{0:T(1024)} %get-tuple-element.72) | copy-start | bytes 9220
  1295.7 23.4 %copy-start.42 = (f32[768]{0:T(1024)S(1)}, f32[768]{0:T(1024)}, u32[]{:S(2)}) copy-start(f32[768]{0:T(1024)} %get-tuple-element.79) | copy-start | bytes 9220
  1295.7 23.4 %copy-start.46 = (f32[3,64]{1,0:T(4,128)S(1)}, f32[3,64]{1,0:T(4,128)}, u32[]{:S(2)}) copy-start(f32[3,64]{1,0:T(4,128)} %get-tuple-element.107) | copy-start | bytes 2308
  1295.7 23.6 %copy-start.49 = (f32[768]{0:T(1024)S(1)}, f32[768]{0:T(1024)}, u32[]{:S(2)}) copy-start(f32[768]{0:T(1024)} %get-tuple-element.95) | copy-start | bytes 9220
  1317.9 29.1 %copy-start.56 = (f32[3]{0:T(128)}, f32[3]{0:T(128)S(1)}, u32[]{:S(2)}) copy-start(f32[3]{0:T(128)S(1)} %pmax.7) | copy-start | bytes 40
  1319.1 27.9 %copy-start.28 = (s32[14,14]{0,1:T(8,128)S(1)}, s32[14,14]{0,1:T(8,128)}, u32[]{:S(2)}) copy-start(s32[14,14]{0,1:T(8,128)} %copy-done.27) | copy-start | bytes 2356
  (39 other events, 292.6 us)
Sparse Core Ops, SparseCore 0:
  15.0 49.0 all-gather.4
  512.0 58.3 reduce-scatter.4
  576.9 46.3 all-gather.6
  624.8 46.3 all-gather.8
  718.0 58.3 reduce-scatter.8
  778.7 58.3 reduce-scatter.6
  843.7 46.3 all-gather.10
  1263.8 58.3 reduce-scatter.10
  1327.8 236.8 all-reduce.6
where the time goes:
time: 1600 us; the launch traced here: 1580 us
  local copies, waits for them, and re-layouts  590 us (37%)
  waiting for transfers between devices  486 us (30%)
  matrix products  241 us (15%)
  other arithmetic  163 us (10%)
  blocking collectives  83.5 us (5%)
    add x6, local copies, waits for them, and re-layouts, scores_of(): logits.reshape(count, groups, WIN, WIN, WIN, WIN) + rel_rows[..., :, None]  266 us
    psum x1, waiting for transfers between devices, shards(): lax.psum((grad_qkv, grad_qv_bias, grad_proj, grad_fc1, grad_fc1_bias, gra...  156 us
    convert_element_type x2, local copies, waits for them, and re-layouts, shards(): grad_rows = jnp.sum(grad_grid, axis=5, dtype=single)  94.9 us
    reduce_sum x1, other arithmetic, shards(): grad_rows = jnp.sum(grad_grid, axis=5, dtype=single)  94.8 us
    reduce_scatter x1, waiting for transfers between devices, shards(): lax.psum_scatter(attn_terms.astype(jnp.bfloat16), 'tensor', scatter_dimen...  58.1 us
    reduce_scatter x1, waiting for transfers between devices, shards(): lax.psum_scatter(mlp_terms.astype(jnp.bfloat16), 'tensor', scatter_dimens...  56.8 us
    all_gather x1, waiting for transfers between devices, shards(): lax.all_gather(first.astype(narrow), 'tensor', axis=1, tiled=True)  46.6 us
    all_gather x1, waiting for transfers between devices, shards(): attn_full = lax.all_gather(grad_attn, 'tensor', axis=1, tiled=True)  46.5 us
  transfers between devices with their start and end apart: 9, of which 8 were waited for; matrix products, arithmetic and copies ran while one was open for 6% of the time, Pallas kernels for 0%

commit v1 on v0

v1 whole, which is shorter than its diff:
```python
import functools

import jax
import jax.numpy as jnp
import numpy as np
from jax import lax
from jax.experimental import pallas as pl
from jax.experimental.pallas import tpu as pltpu
from jax.sharding import PartitionSpec as P

HD = 64
GRID = 64
WIN = 14
TILES = 5
SPAN = WIN * WIN
ROWS = 208
SLOTS = 7
SLAB = 6 * ROWS
LEFT = 6
RIGHT = 12
LANES = 128
EPS = 1e-6
CLIP = 3.0
VMEM = 60 * 1024 * 1024

single = jnp.float32
narrow = jnp.bfloat16

OWNED = (
    ((0, 0), (0, 1), (0, 2), (0, 3), (0, 4), (1, 0)),
    ((1, 1), (1, 2), (1, 3), (1, 4), (2, 0), (2, 1)),
    ((2, 2), (2, 3), (2, 4), (3, 0), (3, 1), (3, 2)),
    ((3, 3), (3, 4), (4, 0), (4, 1), (4, 2), (4, 3), (4, 4)),
)
FIELDS = 6


def owner_table(rows_held):
    table = np.zeros((len(OWNED), SLOTS, FIELDS), np.int32)
    for device, windows in enumerate(OWNED):
        offset = 0
        for slot, (i, j) in enumerate(windows):
            high = min(WIN, GRID - i * WIN)
            wide = min(WIN, GRID - j * WIN)
            first = i * WIN - device * rows_held + LEFT
            table[device, slot] = (first, j * WIN, high, wide, offset, 1)
            offset += ROWS if high == WIN else -(-high * WIN // 16) * 16
    return table.reshape(len(OWNED), SLOTS * FIELDS)


def lane_tables():
    row = np.arange(ROWS)
    x, y = row // WIN, row % WIN
    lane = np.arange(LANES) % 64
    part = lane // 32
    at = lane % 32
    amount = np.where(part[None, :] == 0, 13 - x[:, None], 13 - y[:, None])
    amount = np.where((row < SPAN)[:, None], amount, 0)
    bits = np.stack([(amount >> b) & 1 for b in range(4)]).astype(np.float32)
    lanes = np.zeros((8, LANES), np.float32)
    lanes[0] = at < WIN
    lanes[1] = (at >= 16) & (at < 16 + WIN)
    lanes[2] = lane == 31
    sides = np.zeros((16, LANES), np.float32)
    sides[0] = np.arange(LANES) < 64
    sides[1] = np.arange(LANES) >= 64
    place = np.where(part[None, :] == 0, x[:, None], y[:, None])
    hot = ((at % 16)[None, :] == place) & ((at % 16) < WIN)[None, :] & (row < SPAN)[:, None]
    keys = hot.astype(np.float32)
    keys[SPAN:, lane == 31] = -1e30
    return (
        jnp.asarray(bits),
        jnp.asarray(lanes),
        jnp.asarray(sides, narrow),
        jnp.asarray(keys, narrow),
    )


def dot(a, b):
    return jnp.dot(a, b, preferred_element_type=single)


def dot_nt(a, b):
    return lax.dot_general(a, b, (((1,), (1,)), ((), ())), preferred_element_type=single)


def dot_tn(a, b):
    return lax.dot_general(a, b, (((0,), (0,)), ((), ())), preferred_element_type=single)


def norm_parts(values):
    centre = values - jnp.mean(values, axis=-1, keepdims=True)
    inverse = lax.rsqrt(jnp.mean(centre * centre, axis=-1, keepdims=True) + EPS)
    return centre * inverse, inverse


def norm_back(grad, normal, inverse, gain):
    scaled = grad * gain
    first = jnp.mean(scaled, axis=-1, keepdims=True)
    second = jnp.mean(scaled * normal, axis=-1, keepdims=True)
    return inverse * (scaled - first - normal * second)


def slot_fields(tab):
    base = pl.program_id(0) * FIELDS
    return tuple(tab[base + i] for i in range(FIELDS))


def positions(axis, first_col, high, wide):
    shape = (ROWS, 1) if axis == 0 else (1, ROWS)
    row = lax.broadcasted_iota(jnp.int32, shape, axis)
    x = lax.shift_right_logical(row * 4682, 16)
    y = row - x * WIN
    valid = (x < high) & (y < wide)
    return jnp.where(valid, x * GRID + first_col + y, -1), valid


def gather_window(source, target):
    token = lax.broadcasted_iota(jnp.int32, (ROWS, WIN * GRID), 1)
    choose = jnp.where(token == target, 1.0, 0.0).astype(narrow)
    return dot(choose, source)


def shift_left(values, bits):
    for b in range(4):
        values = jnp.where(bits[b] > 0.5, pltpu.roll(values, LANES - (1 << b), 1), values)
    return values


def shift_right(values, bits):
    for b in range(4):
        values = jnp.where(bits[b] > 0.5, pltpu.roll(values, 1 << b, 1), values)
    return values


def forward_kernel(
    first, tab, ext, gain, shift, known, w, bias, wproj, wrel, bits, lanes, sides, keys, *outs
):
    if first:
        slab, n1_out, qkv, mixed, attn, peak = outs
    else:
        slab, qkv, mixed, attn, peak = outs
    row0, col0, high, wide, offset, live = slot_fields(tab)
    half = w.shape[2]

    @pl.when(pl.program_id(0) == 0)
    def _():
        slab[...] = jnp.zeros_like(slab)
        attn[...] = jnp.zeros_like(attn)
        peak[...] = jnp.zeros_like(peak)

    @pl.when(live == 1)
    def _():
        target, valid = positions(0, col0, high, wide)
        source = ext[pl.ds(pl.multiple_of(row0 * GRID, GRID), WIN * GRID), :]
        window = gather_window(source, target)
        place = pl.ds(pl.multiple_of(offset, 16), ROWS)
        slab[place, :] = window.astype(narrow)
        if first:
            normal, _ = norm_parts(window)
            n1 = jnp.where(valid, normal * gain[...] + shift[...], 0.0).astype(narrow)
            n1_out[0] = n1
        else:
            n1 = known[0]
        query = jnp.where(valid, dot(n1, w[0]) + bias[0:1], 0.0).astype(narrow)
        key8 = dot(n1, w[1]).astype(narrow) * jnp.asarray(0.125, narrow)
        value = (dot(n1, w[2]) + bias[1:2]).astype(narrow)
        qkv[0, 0] = query
        qkv[0, 1] = key8
        qkv[0, 2] = value
        low_lane = lax.broadcasted_iota(jnp.int32, (ROWS, LANES), 1) < 64
        for pair in range(half // LANES):
            cut = slice(pair * LANES, (pair + 1) * LANES)
            q, k8, v = query[:, cut], key8[:, cut], value[:, cut]
            rel = shift_left(dot(q, wrel[...]), bits)
            rest = rel - rel.astype(narrow).astype(single)
            rel = rel * lanes[0:1] + pltpu.roll(rest, 16, 1) * lanes[1:2] + lanes[2:3]
            rel = rel.astype(narrow)
            qkv[0, 3, :, cut] = rel
            pieces = []
            for head in range(2):
                mine, other = sides[head : head + 1], sides[1 - head : 2 - head]
                only = q * mine
                logits = dot_nt(only, k8)
                at = 2 * pair + head
                peak[at : at + 1, :] = jnp.maximum(
                    peak[at : at + 1, :], jnp.max(logits, axis=0, keepdims=True)
                )
                scores = dot_nt(only + rel * other, k8 * mine + keys[...] * other)
                top = jnp.max(scores, axis=1, keepdims=True)
                probs = jnp.exp(scores - top)
                total = jnp.sum(probs, axis=1, keepdims=True)
                pieces.append(dot(probs.astype(narrow), v) * (1.0 / total))
            mixed[0, :, cut] = jnp.where(low_lane, pieces[0], pieces[1]).astype(narrow)
        terms = dot(mixed[0], wproj[...])
        attn[place, :] = jnp.where(valid, terms, 0.0)


def whole(shape):
    zeros = (0,) * len(shape)
    return pl.BlockSpec(shape, lambda *_: zeros, pipeline_mode=pl.Buffered(1))


def held(shape):
    zeros = (0,) * len(shape)
    return pl.BlockSpec(shape, lambda *_: zeros)


def by_slot(shape):
    rest = (0,) * len(shape)
    return pl.BlockSpec((1,) + tuple(shape), lambda s, *_: (s,) + rest)


def forward_half(tab, ext, norm, known, w, bias, wproj, wrel, tables):
    first = known is None
    width = ext.shape[1]
    half = w.shape[2]
    bits, lanes, sides, keys = tables
    if first:
        known = jnp.zeros((SLOTS, 16, LANES), narrow)
    known_spec = by_slot(known.shape[1:])
    outs = [
        (jax.ShapeDtypeStruct((SLAB, width), narrow), held((SLAB, width))),
        (jax.ShapeDtypeStruct((SLOTS, ROWS, width), narrow), by_slot((ROWS, width))),
        (jax.ShapeDtypeStruct((SLOTS, 4, ROWS, half), narrow), by_slot((4, ROWS, half))),
        (jax.ShapeDtypeStruct((SLOTS, ROWS, half), narrow), by_slot((ROWS, half))),
        (jax.ShapeDtypeStruct((SLAB, width), single), held((SLAB, width))),
        (jax.ShapeDtypeStruct((8, ROWS), single), held((8, ROWS))),
    ]
    if not first:
        del outs[1]
    gain, shift = norm
    operands = (ext, gain, shift, known, w, bias, wproj, wrel, bits, lanes, sides, keys)
    in_specs = [whole(a.shape) for a in operands]
    in_specs[3] = known_spec
    return pl.pallas_call(
        functools.partial(forward_kernel, first),
        out_shape=[o[0] for o in outs],
        grid_spec=pltpu.PrefetchScalarGridSpec(
            num_scalar_prefetch=1,
            grid=(SLOTS,),
            in_specs=in_specs,
            out_specs=[o[1] for o in outs],
        ),
        compiler_params=pltpu.CompilerParams(vmem_limit_bytes=VMEM),
        cost_estimate=pl.CostEstimate(
            flops=13_000_000_000, bytes_accessed=30_000_000, transcendentals=4_000_000
        ),
        name="attention_forward",
    )(tab, *operands)


BLOCK = 256
CHUNK = 416


def gelu_parts(z):
    size = jnp.abs(z)
    bell = jnp.exp(-0.5 * z * z)
    t = 1.0 / (1.0 + 0.2316418882663604 * size)
    poly = 0.5 * 1.061405429 * t + (0.5 * -1.453152027)
    poly = poly * t + 0.5 * 1.421413741
    poly = poly * t + 0.5 * -0.284496736
    poly = poly * t + 0.5 * 0.254829592
    tail = poly * t * bell
    phi_total = jnp.where(z >= 0, 1.0 - tail, tail)
    return z * phi_total, phi_total + z * bell * 0.3989422804014327


def mlp_kernel(first, *refs):
    if first:
        (xs, attn1, attn2, gs, pbias, gain, shift, w1a, w1b, b1a, b1b, w2a, w2b) = refs[:13]
        (x1, n2, n2t, gt, branch, dn2, gw1a, gw1b, gw2a, gw2b, w1, w2, b1, hs, zs, gb) = refs[13:]
    else:
        (x1, n2, n2t, gs, gt, branch0, dn20, fbias, gain, w1a, w1b, b1a, b1b, w2a, w2b) = refs[:15]
        (out, dx1, da, sums, gw1a, gw1b, gw2a, gw2b, branch, dn2, w1, w2, b1, hs, zs, gb) = refs[15:]
    step = pl.program_id(0)
    count = pl.num_programs(0) // 2
    rows, width = gs.shape

    @pl.when(step == 0)
    def _():
        if first:

            @pl.loop(0, SLAB // ROWS)
            def _(c):
                sl = pl.ds(pl.multiple_of(c * ROWS, 16), ROWS)
                middle = xs[sl, :].astype(single) + (attn1[sl, :] + attn2[sl, :] + pbias[...])
                x1[sl, :] = middle
                normal, _ = norm_parts(middle)
                n2[sl, :] = (normal * gain[...] + shift[...]).astype(narrow)
                branch[sl, :] = jnp.zeros((ROWS, width), single)
                dn2[sl, :] = jnp.zeros((ROWS, width), single)

            for j in range(width // LANES):
                cut = slice(j * LANES, (j + 1) * LANES)
                n2t[cut, :] = n2[:, cut].T
                gt[cut, :] = gs[:, cut].T
        else:

            @pl.loop(0, SLAB // ROWS)
            def _(c):
                sl = pl.ds(pl.multiple_of(c * ROWS, 16), ROWS)
                branch[sl, :] = branch0[sl, :]
                dn2[sl, :] = dn20[sl, :]

    @pl.when(step < count)
    def _():
        w1[...] = w1a[...]
        w2[...] = w2a[...]
        b1[...] = b1a[...]

    @pl.when(step >= count)
    def _():
        w1[...] = w1b[...]
        w2[...] = w2b[...]
        b1[...] = b1b[...]

    gb[...] = jnp.zeros_like(gb)

    @pl.loop(0, SLAB // CHUNK)
    def _(c):
        sl = pl.ds(pl.multiple_of(c * CHUNK, 16), CHUNK)
        z = dot(n2[sl, :], w1[...]) + b1[0:1]
        dh = dot_nt(gs[sl, :], w2[...])
        act, slope = gelu_parts(z)
        h = act.astype(narrow)
        dz = (dh * slope).astype(narrow)
        hs[sl, :] = h
        zs[sl, :] = dz
        gb[0:1, :] += jnp.sum(dz.astype(single), axis=0, keepdims=True)
        branch[sl, :] += dot(h, w2[...])
        dn2[sl, :] += dot_nt(dz, w1[...])

    def store(gw1, gw2):
        @pl.loop(0, width // 256)
        def _(r):
            sl = pl.ds(pl.multiple_of(r * 256, 256), 256)
            gw1[sl, :] = dot(n2t[sl, :], zs[...]).astype(narrow)
            gw2[sl, :] = dot(gt[sl, :], hs[...]).astype(narrow)

        pad = gw1.shape[0] - width
        gw1[width:, :] = jnp.broadcast_to(gb[0:1, :], (pad, BLOCK)).astype(narrow)

    @pl.when(step < count)
    def _():
        store(gw1a, gw2a)

    @pl.when(step >= count)
    def _():
        store(gw1b, gw2b)

    if not first:

        @pl.when(step == 2 * count - 1)
        def _():
            sums[...] = jnp.zeros_like(sums)

            @pl.loop(0, SLAB // ROWS)
            def _(c):
                sl = pl.ds(pl.multiple_of(c * ROWS, 16), ROWS)
                middle = x1[sl, :]
                normal, inverse = norm_parts(middle)
                out[sl, :] = (middle + (branch[sl, :] + fbias[...])).astype(narrow)
                grad = dn2[sl, :]
                cot = gs[sl, :].astype(single)
                total = cot + norm_back(grad, normal, inverse, gain[...])
                dx1[sl, :] = total
                low = total.astype(narrow)
                da[sl, :] = low
                sums[0:1, :] += jnp.sum(grad * normal, axis=0, keepdims=True)
                sums[1:2, :] += jnp.sum(grad, axis=0, keepdims=True)
                sums[2:3, :] += jnp.sum(low.astype(single), axis=0, keepdims=True)
                sums[3:4, :] += jnp.sum(cot, axis=0, keepdims=True)


PADROWS = 16


def mlp_half(first, residents, w1a, w1b, b1a, b1b, w2a, w2b):
    width, local = w1a.shape
    count = local // BLOCK

    def early(shape, dim):
        def index(i):
            at = jnp.minimum(i, count - 1)
            return (0, at) if dim == 1 else (at, 0)

        return pl.BlockSpec(shape, index)

    def late(shape, dim):
        def index(i):
            at = jnp.maximum(i - count, 0)
            return (0, at) if dim == 1 else (at, 0)

        return pl.BlockSpec(shape, index)

    in_specs = [whole(a.shape) for a in residents] + [
        early((width, BLOCK), 1),
        late((width, BLOCK), 1),
        early((1, BLOCK), 1),
        late((1, BLOCK), 1),
        early((BLOCK, width), 0),
        late((BLOCK, width), 0),
    ]
    slab = (SLAB, width)
    flipped = (width, SLAB)
    shape = jax.ShapeDtypeStruct
    if first:
        outs = [
            (shape(slab, single), whole(slab)),
            (shape(slab, narrow), whole(slab)),
            (shape(flipped, narrow), whole(flipped)),
            (shape(flipped, narrow), whole(flipped)),
            (shape(slab, single), whole(slab)),
            (shape(slab, single), whole(slab)),
        ]
        scratch = []
    else:
        outs = [
            (shape(slab, narrow), whole(slab)),
            (shape(slab, single), whole(slab)),
            (shape(slab, narrow), whole(slab)),
            (shape((8, width), single), whole((8, width))),
        ]
        scratch = [pltpu.VMEM(slab, single), pltpu.VMEM(slab, single)]
    tall = width + PADROWS
    outs += [
        (shape((tall, local), narrow), early((tall, BLOCK), 1)),
        (shape((tall, local), narrow), late((tall, BLOCK), 1)),
        (shape((width, local), narrow), early((width, BLOCK), 1)),
        (shape((width, local), narrow), late((width, BLOCK), 1)),
    ]
    scratch += [
        pltpu.VMEM((width, BLOCK), narrow),
        pltpu.VMEM((BLOCK, width), narrow),
        pltpu.VMEM((1, BLOCK), single),
        pltpu.VMEM((SLAB, BLOCK), narrow),
        pltpu.VMEM((SLAB, BLOCK), narrow),
        pltpu.VMEM((8, BLOCK), single),
    ]
    return pl.pallas_call(
        functools.partial(mlp_kernel, first),
        out_shape=[o[0] for o in outs],
        grid=(2 * count,),
        in_specs=in_specs,
        out_specs=[o[1] for o in outs],
        scratch_shapes=scratch,
        compiler_params=pltpu.CompilerParams(vmem_limit_bytes=VMEM),
        cost_estimate=pl.CostEstimate(
            flops=18_000_000_000, bytes_accessed=40_000_000, transcendentals=4_000_000
        ),
        name="mlp",
    )(*residents, w1a, w1b, b1a[None], b1b[None], w2a, w2b)


def backward_kernel(first, *refs):
    if first:
        (tab, da, n1, qkv, mixed, w, wproj, wrel, bits, lanes, sides, keys) = refs[:12]
        (dn1, gw, gproj, grel, gw_acc, gproj_acc, bias_acc, dqkv) = refs[12:]
    else:
        (tab, da, n1, qkv, mixed, w, wproj, wrel, bits, lanes, sides, keys) = refs[:12]
        (prior, xs, dx1, gain) = refs[12:16]
        (back, sums, gw, gproj, grel, gw_acc, gproj_acc, bias_acc, dqkv) = refs[16:]
    _, col0, high, wide, offset, live = slot_fields(tab)
    half = w.shape[2]
    width = w.shape[1]

    @pl.when(pl.program_id(0) == 0)
    def _():
        gw_acc[...] = jnp.zeros_like(gw_acc)
        gproj_acc[...] = jnp.zeros_like(gproj_acc)
        bias_acc[...] = jnp.zeros_like(bias_acc)
        grel[...] = jnp.zeros_like(grel)
        if not first:
            back[...] = jnp.zeros_like(back)
            sums[...] = jnp.zeros_like(sums)

    @pl.when(live == 1)
    def _():
        _, valid = positions(0, col0, high, wide)
        place = pl.ds(pl.multiple_of(offset, 16), ROWS)
        da_win = jnp.where(valid, da[place, :].astype(single), 0.0).astype(narrow)
        gproj_acc[...] += dot_tn(mixed[0], da_win)
        dmix = dot_nt(da_win, wproj[...]).astype(narrow)
        low_lane = lax.broadcasted_iota(jnp.int32, (ROWS, LANES), 1) < 64
        for pair in range(half // LANES):
            cut = slice(pair * LANES, (pair + 1) * LANES)
            q, k8, v, rel = (qkv[0, j, :, cut] for j in range(4))
            do = dmix[:, cut]
            dqs, dks, dvs = [], [], []
            for head in range(2):
                mine, other = sides[head : head + 1], sides[1 - head : 2 - head]
                full_key = k8 * mine + keys[...] * other
                scores = dot_nt(full_key, q * mine + rel * other)
                top = jnp.max(scores, axis=0, keepdims=True)
                probs = jnp.exp(scores - top)
                probs = probs * (1.0 / jnp.sum(probs, axis=0, keepdims=True))
                dprobs = dot_nt(v, do * mine)
                mean = jnp.sum(probs * dprobs, axis=0, keepdims=True)
                dscores = (probs * (dprobs - mean)).astype(narrow)
                dvs.append(dot(probs.astype(narrow), do))
                dks.append(dot(dscores, q))
                dqs.append(dot_tn(dscores, full_key))
            dv = jnp.where(low_lane, dvs[0], dvs[1])
            dk = jnp.where(low_lane, dks[0], dks[1]) * 0.125
            dq = jnp.where(low_lane, dqs[0], dqs[1])
            drel = jnp.where(low_lane, dqs[1], dqs[0]) * lanes[0:1]
            drel = shift_right(drel, bits).astype(narrow)
            dq = dq + dot_nt(drel, wrel[...])
            grel[...] += dot_tn(drel, q)
            dqkv[0, :, cut] = dq.astype(narrow)
            dqkv[1, :, cut] = dk.astype(narrow)
            dqkv[2, :, cut] = dv.astype(narrow)
        n1t = n1[0].T
        total = None
        for j in range(3):
            part = dqkv[j]
            gw_acc[j] += dot(n1t, part)
            bias_acc[j : j + 1, :] += jnp.sum(part.astype(single), axis=0, keepdims=True)
            back_part = dot_nt(part, w[j])
            total = back_part if total is None else total + back_part
        if first:
            dn1[0] = total
        else:
            grad = jnp.where(valid, total + prior[0], 0.0)
            normal, inverse = norm_parts(xs[place, :].astype(single))
            sums[0:1, :] += jnp.sum(grad * normal, axis=0, keepdims=True)
            sums[1:2, :] += jnp.sum(grad, axis=0, keepdims=True)
            result = dx1[place, :] + norm_back(grad, normal, inverse, gain[...])
            back[place, :] = jnp.where(valid, result, 0.0).astype(narrow)

    @pl.when(pl.program_id(0) == SLOTS - 1)
    def _():
        gproj[...] = gproj_acc[...].astype(narrow)
        pad = gw.shape[1] - width
        for j in range(3):
            gw[j, :width, :] = gw_acc[j].astype(narrow)
            gw[j, width:, :] = jnp.broadcast_to(bias_acc[j : j + 1, :], (pad, half)).astype(narrow)


def backward_half(tab, da, n1, qkv, mixed, w, wproj, wrel, tables, final):
    first = final is None
    width = da.shape[1]
    half = w.shape[2]
    shape = jax.ShapeDtypeStruct
    operands = [da, n1, qkv, mixed, w, wproj, wrel, *tables]
    in_specs = [whole(a.shape) for a in operands]
    for at in (1, 2, 3):
        in_specs[at] = by_slot(operands[at].shape[1:])
    tall = width + PADROWS
    if first:
        outs = [(shape((SLOTS, ROWS, width), single), by_slot((ROWS, width)))]
    else:
        prior, xs, dx1, gain = final
        operands += [prior, xs, dx1, gain]
        in_specs += [by_slot((ROWS, width)), whole(xs.shape), whole(dx1.shape), whole(gain.shape)]
        outs = [
            (shape((SLAB, width), narrow), whole((SLAB, width))),
            (shape((8, width), single), whole((8, width))),
        ]
    outs += [
        (shape((3, tall, half), narrow), whole((3, tall, half))),
        (shape((half, width), narrow), whole((half, width))),
        (shape((LANES, LANES), single), whole((LANES, LANES))),
    ]
    return pl.pallas_call(
        functools.partial(backward_kernel, first),
        out_shape=[o[0] for o in outs],
        grid_spec=pltpu.PrefetchScalarGridSpec(
            num_scalar_prefetch=1,
            grid=(SLOTS,),
            in_specs=in_specs,
            out_specs=[o[1] for o in outs],
            scratch_shapes=[
                pltpu.VMEM((3, width, half), single),
                pltpu.VMEM((half, width), single),
                pltpu.VMEM((8, half), single),
                pltpu.VMEM((3, ROWS, half), narrow),
            ],
        ),
        compiler_params=pltpu.CompilerParams(vmem_limit_bytes=VMEM),
        cost_estimate=pl.CostEstimate(
            flops=26_000_000_000, bytes_accessed=40_000_000, transcendentals=4_000_000
        ),
        name="attention_backward",
    )(tab, *operands)


def place_kernel(tab, slab, ext):
    row0, col0, high, wide, offset, live = slot_fields(tab)

    @pl.when(pl.program_id(0) == 0)
    def _():
        ext[...] = jnp.zeros_like(ext)

    @pl.when(live == 1)
    def _():
        target, _ = positions(1, col0, high, wide)
        token = lax.broadcasted_iota(jnp.int32, (WIN * GRID, ROWS), 0)
        choose = jnp.where(token == target, 1.0, 0.0).astype(narrow)
        window = slab[pl.ds(pl.multiple_of(offset, 16), ROWS), :]
        where_to = pl.ds(pl.multiple_of(row0 * GRID, GRID), WIN * GRID)
        ext[where_to, :] += dot(choose, window).astype(narrow)


def place_windows(tab, slab, tokens):
    width = slab.shape[1]
    return pl.pallas_call(
        place_kernel,
        out_shape=jax.ShapeDtypeStruct((tokens, width), narrow),
        grid_spec=pltpu.PrefetchScalarGridSpec(
            num_scalar_prefetch=1,
            grid=(SLOTS,),
            in_specs=[whole(slab.shape)],
            out_specs=whole((tokens, width)),
        ),
        compiler_params=pltpu.CompilerParams(vmem_limit_bytes=VMEM),
        cost_estimate=pl.CostEstimate(
            flops=2_000_000_000, bytes_accessed=6_000_000, transcendentals=0
        ),
        name="place_windows",
    )(tab, slab)


CORE_SWAP = ((0, 1), (1, 0), (2, 3), (3, 2))
CHIP_SWAP = ((0, 2), (2, 0), (1, 3), (3, 1))
UP = ((0, 1), (1, 2), (2, 3))
DOWN = ((1, 0), (2, 1), (3, 2))


def swap(value, pairs):
    return jax.tree.map(lambda a: lax.ppermute(a, "tensor", pairs), value)


def add_low(a, b):
    return jax.tree.map(lambda u, v: (u.astype(single) + v.astype(single)).astype(narrow), a, b)


def spread(tokens, rows):
    grid = tokens.reshape(rows, GRID, tokens.shape[-1])
    above = lax.ppermute(grid[rows - LEFT :], "tensor", UP)
    below = lax.ppermute(grid[:RIGHT], "tensor", DOWN)
    whole_grid = jnp.concatenate([above, grid, below], axis=0)
    return whole_grid.reshape(-1, tokens.shape[-1])


def collect(ext, rows):
    width = ext.shape[-1]
    grid = ext.reshape(rows + LEFT + RIGHT, GRID, width)
    from_below = lax.ppermute(grid[:LEFT], "tensor", DOWN)
    from_above = lax.ppermute(grid[LEFT + rows :], "tensor", UP)
    mine = grid[LEFT : LEFT + rows]
    mine = mine + jnp.pad(from_below, ((rows - LEFT, 0), (0, 0), (0, 0)))
    mine = mine + jnp.pad(from_above, ((0, rows - RIGHT), (0, 0), (0, 0)))
    return mine.reshape(1, rows * GRID, width)


def shards(
    inputs,
    w_qkv,
    qv_bias,
    w_proj,
    proj_bias,
    w_fc1,
    fc1_bias,
    w_fc2,
    fc2_bias,
    norm1_gain,
    norm1_shift,
    norm2_gain,
    norm2_shift,
    rel_h,
    rel_w,
    cotangent,
):
    width = inputs.shape[2]
    rows = inputs.shape[1] // GRID
    local = w_qkv.shape[2]
    heads = local // HD
    place = lax.axis_index("tensor")
    tab = jnp.asarray(owner_table(rows))[place]
    tables = lane_tables()

    block = jnp.zeros((2, 32, HD), narrow)
    block = block.at[0, : 2 * WIN - 1].set(rel_h[::-1]).at[1, : 2 * WIN - 1].set(rel_w[::-1])
    block = block.reshape(HD, HD).T
    wrel = jnp.zeros((LANES, LANES), narrow).at[:HD, HD:].set(block).at[HD:, :HD].set(block)

    x_ext = spread(inputs[0], rows)
    g_ext = spread(cotangent[0], rows)

    mine = (w_qkv, qv_bias, w_proj, w_fc1, fc1_bias, w_fc2)
    beside = swap(mine, CORE_SWAP)
    across = swap(mine, CHIP_SWAP)
    corner = swap(across, CORE_SWAP)

    def joined(a, b):
        return (
            jnp.concatenate([a[0], b[0]], axis=2),
            jnp.concatenate([a[1], b[1]], axis=1),
            jnp.concatenate([a[2], b[2]], axis=0),
        )

    near_w, near_bias, near_proj = joined(mine, beside)
    far_w, far_bias, far_proj = joined(across, corner)
    norm1 = (norm1_gain[None], norm1_shift[None])

    xs, n1, near_qkv, near_mixed, near_attn, near_peak = forward_half(
        tab, x_ext, norm1, None, near_w, near_bias, near_proj, wrel, tables
    )
    gs, far_qkv, far_mixed, far_attn, far_peak = forward_half(
        tab, g_ext, norm1, n1, far_w, far_bias, far_proj, wrel, tables
    )

    x1, n2, n2t, gt, branch, dn2, *near_fc = mlp_half(
        True,
        (xs, near_attn, far_attn, gs, proj_bias[None], norm2_gain[None], norm2_shift[None]),
        mine[3],
        beside[3],
        mine[4],
        beside[4],
        mine[5],
        beside[5],
    )
    out, dx1, da, sums2, *far_fc = mlp_half(
        False,
        (x1, n2, n2t, gs, gt, branch, dn2, fc2_bias[None], norm2_gain[None]),
        across[3],
        corner[3],
        across[4],
        corner[4],
        across[5],
        corner[5],
    )

    dn1, far_gw, far_gproj, far_rel = backward_half(
        tab, da, n1, far_qkv, far_mixed, far_w, far_proj, wrel, tables, None
    )
    back, sums1, near_gw, near_gproj, near_rel = backward_half(
        tab,
        da,
        n1,
        near_qkv,
        near_mixed,
        near_w,
        near_proj,
        wrel,
        tables,
        (dn1, xs, dx1, norm1_gain[None]),
    )

    output = collect(place_windows(tab, out, x_ext.shape[0]), rows)
    input_grad = collect(place_windows(tab, back, x_ext.shape[0]), rows)

    def both(fc, gw, gproj):
        keep = (fc[0], fc[2], gw[:, :, :local], gproj[:local])
        send = (fc[1], fc[3], gw[:, :, local:], gproj[local:])
        return add_low(keep, swap(send, CORE_SWAP))

    far_total = both(far_fc, far_gw, far_gproj)
    near_total = both(near_fc, near_gw, near_gproj)
    totals = add_low(near_total, swap(far_total, CHIP_SWAP))
    totals = lax.psum(totals, "dp")
    gw1, gw2, gw, gproj = jax.tree.map(lambda a: a.astype(single), totals)

    blocks = near_rel + far_rel
    blocks = blocks[HD:, :HD] + blocks[:HD, HD:]
    grad_rel = jnp.stack([blocks[: 2 * WIN - 1][::-1], blocks[32 : 32 + 2 * WIN - 1][::-1]])
    sums, grad_rel = lax.psum((jnp.concatenate([sums1[:2], sums2[:4]]), grad_rel), ("dp", "tensor"))

    def peaks(peak):
        top = jnp.max(peak, axis=1)[: 2 * heads]
        return jnp.maximum(top[:heads], lax.ppermute(top[heads:], "tensor", CORE_SWAP))

    head_max = jnp.maximum(
        peaks(near_peak), lax.ppermute(peaks(far_peak), "tensor", CHIP_SWAP)
    )
    head_max = lax.pmax(head_max, "dp")
    factor = jnp.sqrt(CLIP / jnp.maximum(head_max, CLIP))
    clipped_qk = (w_qkv[:2].astype(single) * jnp.repeat(factor, HD)).astype(narrow)

    return (
        output,
        input_grad,
        gw[:, :width],
        jnp.stack([gw[0, width], gw[2, width]]),
        gproj,
        sums[4],
        gw1[:width],
        gw1[width],
        gw2.T,
        sums[5],
        sums[:4],
        grad_rel,
        clipped_qk,
        head_max,
    )


def solution(mesh):
    return jax.shard_map(
        shards,
        mesh=mesh,
        in_specs=(
            P("dp", "tensor", None),
            P(None, None, "tensor"),
            P(None, "tensor"),
            P("tensor", None),
            P(),
            P(None, "tensor"),
            P("tensor"),
            P("tensor", None),
            P(),
            P(),
            P(),
            P(),
            P(),
            P(),
            P(),
            P("dp", "tensor", None),
        ),
        out_specs=(
            P("dp", "tensor", None),
            P("dp", "tensor", None),
            P(None, None, "tensor"),
            P(None, "tensor"),
            P("tensor", None),
            P(),
            P(None, "tensor"),
            P("tensor"),
            P("tensor", None),
            P(),
            P(),
            P(),
            P(None, None, "tensor"),
            P("tensor"),
        ),
        check_vma=False,
    )
```

time: 1600 us -> 688 us (0.43)
  local copies, waits for them, and re-layouts: 590 us -> 67.5 us
  waiting for transfers between devices: 486 us -> 137 us
  Pallas kernels: 0 us -> 256 us
  matrix products: 241 us -> 0 us
  other arithmetic: 163 us -> 45.4 us
  starting transfers between devices: 0.77 us -> 98.4 us
  blocking collectives: 83.5 us -> 64.2 us
    add x9 -> x0, local copies, waits for them, and re-layouts: 274 us -> none  [the longest x6 266 us: scores_of(): logits.reshape(count, groups, WIN, WIN, WIN, WIN) + rel_rows[..., :, None]]
    pallas_call x0 -> x8, Pallas kernels: none -> 256 us  [the longest x2 95.2 us: mlp_half(): pl.pallas_call(functools.partial(mlp_kernel, first), out_shape=[o[0] for...]
    dot_general x28 -> x0, matrix products: 241 us -> none  [the longest x1 36.9 us: shards(): jnp.einsum('btd,fd->btf', out_full, w_fc2, preferred_element_type=single)]
    all_gather x4 -> x0, waiting for transfers between devices: 177 us -> none  [the longest x1 46.6 us: shards(): lax.all_gather(first.astype(narrow), 'tensor', axis=1, tiled=True)]
    reduce_scatter x4 -> x0, waiting for transfers between devices: 152 us -> none  [the longest x1 58.1 us: shards(): lax.psum_scatter(attn_terms.astype(jnp.bfloat16), 'tensor', scatter_dimen...]
    reduce_sum x9 -> x0, other arithmetic: 126 us -> none  [the longest x1 94.8 us: shards(): grad_rows = jnp.sum(grad_grid, axis=5, dtype=single)]
    psum x1, waiting for transfers between devices: 156 us -> 35.2 us  [shards(): totals = lax.psum(totals, 'dp')]
    reshape x10 -> x1, local copies, waits for them, and re-layouts: 105 us -> 0.09 us  [shards(): block = block.reshape(HD, HD).T]
  transfers between devices with their start and end apart: 9 -> 42, of which waited for: 8 -> 13; matrix products, arithmetic and copies ran while one was open for 6% -> 14% of each run, Pallas kernels for 0% -> 37%
where the time goes in v1:
time: 688 us; the launch traced here: 683 us
  Pallas kernels  256 us (37%)
  waiting for transfers between devices  137 us (20%)
  starting transfers between devices  98.4 us (14%)
  local copies, waits for them, and re-layouts  67.5 us (10%)
  blocking collectives  64.2 us (9%)
  other arithmetic  45.4 us (7%)
  between operations  14.8 us (2%)
    ppermute x30, waiting for transfers between devices, swap(): return jax.tree.map(lambda a: lax.ppermute(a, 'tensor', pairs), value)  99.1 us
    pallas_call x2, Pallas kernels, mlp_half(): pl.pallas_call(functools.partial(mlp_kernel, first), out_shape=[o[0] for...  95.2 us
    pallas_call x2, Pallas kernels, backward_half(): pl.pallas_call(functools.partial(backward_kernel, first), out_shape=[o[0]...  80.9 us
    ppermute x30, starting transfers between devices, swap(): return jax.tree.map(lambda a: lax.ppermute(a, 'tensor', pairs), value)  78.6 us
    pallas_call x2, Pallas kernels, forward_half(): pl.pallas_call(functools.partial(forward_kernel, first), out_shape=[o[0]...  64.8 us
    psum x1, blocking collectives, shards(): lax.psum((jnp.concatenate([sums1[:2], sums2[:4]]), grad_rel), ('dp', 'ten...  41.6 us
    psum x1, waiting for transfers between devices, shards(): totals = lax.psum(totals, 'dp')  35.2 us
    pmax x1, blocking collectives, shards(): head_max = lax.pmax(head_max, 'dp')  22.6 us
  transfers between devices with their start and end apart: 42, of which 13 were waited for; matrix products, arithmetic and copies ran while one was open for 14% of the time, Pallas kernels for 37%

profile of v1, /device:TPU:0, one launch (start us, length us, event | category | flops | bytes accessed | tf_op | source)
XLA Modules:
  0.0 682.9 jit_solution(4834283900641078632)
XLA Ops:
  12.2 2.9 collective-permute-start
  16.7 3.8 collective-permute-done.9
  20.5 3.5 collective-permute-start.10
  49.5 3.4 collective-permute-start.16
  59.7 4.0 collective-permute-done.7
  74.4 3.5 pad_maximum_fusion.2.w.refs_5_
  77.9 11.0 %collective-permute-start.13 = (bf16[768,768]{1,0:T(8,128)(2,1)}, bf16[768,768]{1,0:T(8,128)(2,1)}, u32[]{:S(2)}, u32[]{:S(2)}) collective-permute-start(bf16[768,768]{1,0:T(8,128)(2,1)} %refs_7_.1), channel_id=1, source_target_pairs={{0,1},{1,0},{2,3},{3,2},{4,5},{5,4},{6,7},{7,6},{8,9},{9,8},{10,11... | collective-permute-start | bytes 3538952 | tf_op jit(solution)/shard_map/ppermute | solution.py:633
  88.8 3.1 pad_maximum_fusion
  91.9 27.9 %collective-permute-start.15 = (bf16[768,768]{1,0:T(8,128)(2,1)}, bf16[768,768]{1,0:T(8,128)(2,1)}, u32[]{:S(2)}, u32[]{:S(2)}) collective-permute-start(bf16[768,768]{1,0:T(8,128)(2,1)} %refs_11_.3), channel_id=1, source_target_pairs={{0,1},{1,0},{2,3},{3,2},{4,5},{5,4},{6,7},{7,6},{8,9},{9,8},{10,11... | collective-permute-start | bytes 3538952 | tf_op jit(solution)/shard_map/ppermute | solution.py:633
  119.8 6.9 %collective-permute-done.16.refs_9_ = bf16[768,768]{1,0:T(8,128)(2,1)} collective-permute-done((bf16[768,768]{1,0:T(8,128)(2,1)}, bf16[768,768]{1,0:T(8,128)(2,1)}, u32[]{:S(2)}, u32[]{:S(2)}) %collective-permute-start.16) | collective-permute-done | bytes 1179680 | tf_op jit(solution)/shard_map/ppermute | solution.py:633
  126.7 12.6 %collective-permute-done.20.refs_13_ = bf16[768,768]{1,0:T(8,128)(2,1)} collective-permute-done((bf16[768,768]{1,0:T(8,128)(2,1)}, bf16[768,768]{1,0:T(8,128)(2,1)}, u32[]{:S(2)}, u32[]{:S(2)}) %collective-permute-start.20) | collective-permute-done | bytes 1179680 | tf_op jit(solution)/shard_map/ppermute | solution.py:633
  139.4 3.1 pad_maximum_fusion.1
  143.0 33.5 %attention_forward.2 = (bf16[1248,768]{1,0:T(8,128)(2,1)}, bf16[7,208,768]{2,1,0:T(8,128)(2,1)}, bf16[7,4,208,384]{3,2,1,0:T(8,128)(2,1)}, bf16[7,208,384]{2,1,0...) custom-call(s32[42]{0:T(128)} %dynamic-slice_bitcast_fusion.tab.refs_0_, bf16[2176,768]{1,0:T(8,128)(2,1)} %bitcast.37, ...), custom_call_target="tpu_custom_call" | custom-call | flops 12999999488 | bytes 30000000 | tf_op jit(solution)/shard_map/attention_forward/pallas_call | solution.py:236
  180.1 31.3 %attention_forward.3 = (bf16[1248,768]{1,0:T(8,128)(2,1)}, bf16[7,4,208,384]{3,2,1,0:T(8,128)(2,1)}, bf16[7,208,384]{2,1,0:T(8,128)(2,1)}, f32[1248,768]{1,0:T(8,128)}, f32[8,208]{1,0:T(8,128)}) custom-call(s32[42]{0:T(128)} %dynamic-slice_bitcast_fusion.tab.refs_0_, bf16[2176,768]{1,0:T(8,128)(2,1)} %bitcast.38, f32[1,768]{1,0:T(1,128)} %broadcast_in_dim.42.gain.refs_15_, ...), custom_call_target="tpu_custom_call" | custom-call | flops 12999999488 | bytes 30000000 | tf_op jit(solution)/shard_map/attention_forward/pallas_call | solution.py:236
  211.4 48.0 %mlp.2 = (f32[1248,768]{1,0:T(8,128)}, bf16[1248,768]{1,0:T(8,128)(2,1)}, bf16[768,1248]{1,0:T(8,128)(2,1)}, bf16[768,1248]{1,0:T(8,128)(2,1)}, f32[1248,768]{1,...) custom-call(bf16[1248,768]{1,0:T(8,128)(2,1)} %get-tuple-element.100, ...), custom_call_target="tpu_custom_call" | custom-call | flops 17999998976 | bytes 40000000 | tf_op jit(solution)/shard_map/mlp/pallas_call | solution.py:442
  260.0 47.2 %mlp.3 = (bf16[1248,768]{1,0:T(8,128)(2,1)}, f32[1248,768]{1,0:T(8,128)}, bf16[1248,768]{1,0:T(8,128)(2,1)}, f32[8,768]{1,0:T(8,128)}, bf16[784,768]{1,0:T(8,128...) custom-call(f32[1248,768]{1,0:T(8,128)} %get-tuple-element.105.refs_0_, ...), custom_call_target="tpu_custom_call" | custom-call | flops 17999998976 | bytes 40000000 | tf_op jit(solution)/shard_map/mlp/pallas_call | solution.py:442
  307.3 38.4 %attention_backward.2 = (f32[7,208,768]{2,1,0:T(8,128)}, bf16[3,784,384]{2,1,0:T(8,128)(2,1)}, bf16[384,768]{1,0:T(8,128)(2,1)}, f32[128,128]{1,0:T(8,128)}) custom-call(s32[42]{0:T(128)} %dynamic-slice_bitcast_fusion.tab.refs_0_, bf16[1248,768]{1,0:T(8,128)(2,1)} %get-tuple-element.112.refs_1_, bf16[7,208,768]{2,1,0:T(8,128)(2,1)} %get-tuple-element.102.known.refs_2_, ...), custom_call_target="tpu_custom_call" | custom-call | flops 25999998976 | bytes 40000000 | tf_op jit(solution)/shard_map/attention_backward/pallas_call | solution.py:567
  351.6 42.5 %attention_backward.3 = (bf16[1248,768]{1,0:T(8,128)(2,1)}, f32[8,768]{1,0:T(8,128)}, bf16[3,784,384]{2,1,0:T(8,128)(2,1)}, bf16[384,768]{1,0:T(8,128)(2,1)}, f32[128,128]{1,0:T(8,128)}) custom-call(s32[42]{0:T(128)} %dynamic-slice_bitcast_fusion.tab.refs_0_, bf16[1248,768]{1,0:T(8,128)(2,1)} %get-tuple-element.112.refs_1_, ...), custom_call_target="tpu_custom_call" | custom-call | flops 25999998976 | bytes 40000000 | tf_op jit(solution)/shard_map/attention_backward/pallas_call | solution.py:567
  406.6 18.0 %collective-permute-start.28 = (bf16[3,784,192]{1,2,0:T(8,128)(2,1)S(1)}, bf16[3,784,192]{1,2,0:T(8,128)(2,1)}, u32[]{:S(2)}, u32[]{:S(2)}) collective-permute-start(bf16[3,784,192]{1,2,0:T(8,128)(2,1)S(1)} %copy-done.12), channel_id=1, source_target_pairs={{0,2},{2,0},{1,3},{3,1},{4,6},{6,4},{5,7},{7,5},{8,10},{10,8},{9,1... | collective-permute-start | bytes 2709512 | tf_op jit(solution)/shard_map/ppermute | solution.py:633
  430.4 49.2 %collective-permute-done.31 = bf16[192,768]{1,0:T(8,128)(2,1)S(1)} collective-permute-done((bf16[192,768]{1,0:T(8,128)(2,1)S(1)}, bf16[192,768]{1,0:T(8,128)(2,1)S(1)}, u32[]{:S(2)}, u32[]{:S(2)}) %collective-permute-start.31) | collective-permute-done | bytes 294944 | tf_op jit(solution)/shard_map/ppermute | solution.py:633
  485.0 2.9 add_convert_fusion.3
  487.8 3.1 fusion
  491.0 17.8 %collective-permute-done.34 = bf16[784,768]{1,0:T(8,128)(2,1)} collective-permute-done((bf16[784,768]{1,0:T(8,128)(2,1)}, bf16[784,768]{1,0:T(8,128)(2,1)}, u32[]{:S(2)}, u32[]{:S(2)}) %collective-permute-start.34) | collective-permute-done | bytes 1204256 | tf_op jit(solution)/shard_map/ppermute | solution.py:633
  508.8 3.2 add_convert_fusion
  518.0 22.6 %pmax.7 = f32[3]{0:T(128)S(1)} all-reduce(f32[3]{0:T(128)S(1)} %maximum_maximum_fusion), channel_id=1, replica_groups=mesh['dp'=8,'tensor'=4] {'dp'}, use_global_device_ids=true, to_apply=%region_9.10 | all-reduce | flops 3 | bytes 24 | tf_op jit(solution)/shard_map/pmax | solution.py:779
  540.7 7.5 %place_windows.3 = bf16[2176,768]{1,0:T(8,128)(2,1)} custom-call(s32[42]{0:T(128)} %dynamic-slice_bitcast_fusion.tab.refs_0_, bf16[1248,768]{1,0:T(8,128)(2,1)} %get-tuple-element.119.slab), custom_call_target="tpu_custom_call" | custom-call | flops 2000000000 | bytes 6000000 | tf_op jit(solution)/shard_map/place_windows/pallas_call | solution.py:609
  552.9 7.5 %place_windows.2 = bf16[2176,768]{1,0:T(8,128)(2,1)} custom-call(s32[42]{0:T(128)} %dynamic-slice_bitcast_fusion.tab.refs_0_, bf16[1248,768]{1,0:T(8,128)(2,1)} %get-tuple-element.111.slab), custom_call_target="tpu_custom_call" | custom-call | flops 2000000000 | bytes 6000000 | tf_op jit(solution)/shard_map/place_windows/pallas_call | solution.py:609
  562.9 4.6 collective-permute-start.23
  578.6 41.6 %all-reduce.5 = (f32[6,768]{1,0:T(8,128)S(1)}, f32[2,27,64]{2,1,0:T(8,128)S(1)}) all-reduce(f32[6,768]{1,0:T(8,128)S(1)} %pad_maximum_fusion.5, f32[2,27,64]{2,1,0:T(8,128)S(1)} %pad_maximum_fusion.4), channel_id=1, replica_groups=mesh['dp'=8,'tensor'=4] {'dp','tensor'}, use_global_device_ids=true, to_apply=%region_3.0 | all-reduce | flops 8064 | bytes 64512 | tf_op jit(solution)/shard_map/psum | solution.py:770
  622.1 3.3 pad_add_fusion
  625.5 2.8 pad_add_fusion.1
  628.2 35.2 %all-reduce.9.cloned.1.call-done = (bf16[768,768]{0,1:T(8,128)(2,1)}, bf16[3,784,192]{2,1,0:T(8,128)(2,1)}, bf16[192,768]{1,0:T(8,128)(2,1)}, bf16[784,768]{1,0:T(8,128)(2,1)}) async-done(((bf16[768,768]{0,1:T(8,128)(2,1)}, bf16[3,784,192]{2,1,0:T(8,128)(2,1)}, bf16[192,768]{1,0:T(8,128)(2,1)}, bf16[784,768]{1,0:T(8,128)(2,1)}), (bf16[768,768]{0,1:T(8,128)(2,1)}, bf16[3,784,192]{2,1,0:T(8,128)(2,1)}, ...) | async-done | bytes 3581968 | tf_op jit(solution)/shard_map/psum | solution.py:764
  (232 shorter events, 122.5 us)
Async XLA Ops:
  7.2 656.2 %all-reduce.9.cloned.1.call-start = ((), (), s32[]{:S(2)}) async-start(), calls=%async_computation | async-start | bytes 7766016 | tf_op jit(solution)/shard_map/psum | solution.py:764
  7.2 45.7 %collective-permute-start.2 = (bf16[3,768,192]{1,2,0:T(8,128)(2,1)}, bf16[3,768,192]{1,2,0:T(8,128)(2,1)}, u32[]{:S(2)}, u32[]{:S(2)}) collective-permute-start(bf16[3,768,192]{1,2,0:T(8,128)(2,1)} %param.30), channel_id=1, source_target_pairs={{0,1},{1,0},{2,3},{3,2},{4,5},{5,4},{6,7},{7,6},{8,9},{9,8},{10,11... | collective-permute-start | bytes 2654216 | tf_op jit(solution)/shard_map/ppermute | solution.py:633
  7.8 35.1 %collective-permute-start.11 = (bf16[192,768]{1,0:T(8,128)(2,1)}, bf16[192,768]{1,0:T(8,128)(2,1)}, u32[]{:S(2)}, u32[]{:S(2)}) collective-permute-start(bf16[192,768]{1,0:T(8,128)(2,1)} %param.32), channel_id=1, source_target_pairs={{0,2},{2,0},{1,3},{3,1},{4,6},{6,4},{5,7},{7,5},{8,10},{10,8},{9,1... | collective-permute-start | bytes 884744 | tf_op jit(solution)/shard_map/ppermute | solution.py:633
  12.2 35.9 %collective-permute-start = (bf16[6,64,768]{2,1,0:T(8,128)(2,1)}, bf16[6,64,768]{2,1,0:T(8,128)(2,1)}, u32[]{:S(2)}, u32[]{:S(2)}) collective-permute-start(bf16[6,64,768]{2,1,0:T(8,128)(2,1)} %bitcast.1), channel_id=1, source_target_pairs={{0,1},{1,2},{2,3},{4,5},{5,6},{6,7},{8,9},{9,10},{10,11},{12,13},{... | collective-permute-start | bytes 1769480 | tf_op jit(solution)/shard_map/ppermute | solution.py:642
  15.1 28.6 %collective-permute-start.4 = (bf16[192,768]{1,0:T(8,128)(2,1)}, bf16[192,768]{1,0:T(8,128)(2,1)}, u32[]{:S(2)}, u32[]{:S(2)}) collective-permute-start(bf16[192,768]{1,0:T(8,128)(2,1)} %param.32), channel_id=1, source_target_pairs={{0,1},{1,0},{2,3},{3,2},{4,5},{5,4},{6,7},{7,6},{8,9},{9,8},{10,11... | collective-permute-start | bytes 884744 | tf_op jit(solution)/shard_map/ppermute | solution.py:633
  40.9 22.8 %collective-permute-start.7 = (bf16[3,768,192]{1,2,0:T(8,128)(2,1)}, bf16[3,768,192]{1,2,0:T(8,128)(2,1)}, u32[]{:S(2)}, u32[]{:S(2)}) collective-permute-start(bf16[3,768,192]{1,2,0:T(8,128)(2,1)} %param.30), channel_id=1, source_target_pairs={{0,2},{2,0},{1,3},{3,1},{4,6},{6,4},{5,7},{7,5},{8,10},{10,8},{9,1... | collective-permute-start | bytes 2654216 | tf_op jit(solution)/shard_map/ppermute | solution.py:633
  43.7 34.2 %collective-permute-start.1 = (bf16[12,64,768]{2,1,0:T(8,128)(2,1)}, bf16[12,64,768]{2,1,0:T(8,128)(2,1)}, u32[]{:S(2)}, u32[]{:S(2)}) collective-permute-start(bf16[12,64,768]{2,1,0:T(8,128)(2,1)} %bitcast.42), channel_id=1, source_target_pairs={{1,0},{2,1},{3,2},{5,4},{6,5},{7,6},{9,8},{10,9},{11,10},{13,12},{... | collective-permute-start | bytes 3538952 | tf_op jit(solution)/shard_map/ppermute | solution.py:643
  48.2 71.6 %collective-permute-start.6 = (bf16[12,64,768]{2,1,0:T(8,128)(2,1)}, bf16[12,64,768]{2,1,0:T(8,128)(2,1)}, u32[]{:S(2)}, u32[]{:S(2)}) collective-permute-start(bf16[12,64,768]{2,1,0:T(8,128)(2,1)} %bitcast.41), channel_id=1, source_target_pairs={{1,0},{2,1},{3,2},{5,4},{6,5},{7,6},{9,8},{10,9},{11,10},{13,12},{... | collective-permute-start | bytes 3538952 | tf_op jit(solution)/shard_map/ppermute | solution.py:643
  49.5 77.2 %collective-permute-start.16 = (bf16[768,768]{1,0:T(8,128)(2,1)}, bf16[768,768]{1,0:T(8,128)(2,1)}, u32[]{:S(2)}, u32[]{:S(2)}) collective-permute-start(bf16[768,768]{1,0:T(8,128)(2,1)} %refs_7_.1), channel_id=1, source_target_pairs={{0,2},{2,0},{1,3},{3,1},{4,6},{6,4},{5,7},{7,5},{8,10},{10,8},{9,1... | collective-permute-start | bytes 3538952 | tf_op jit(solution)/shard_map/ppermute | solution.py:633
  52.9 86.4 %collective-permute-start.20 = (bf16[768,768]{1,0:T(8,128)(2,1)}, bf16[768,768]{1,0:T(8,128)(2,1)}, u32[]{:S(2)}, u32[]{:S(2)}) collective-permute-start(bf16[768,768]{1,0:T(8,128)(2,1)} %refs_11_.3), channel_id=1, source_target_pairs={{0,2},{2,0},{1,3},{3,1},{4,6},{6,4},{5,7},{7,5},{8,10},{10,8},{9,1... | collective-permute-start | bytes 3538952 | tf_op jit(solution)/shard_map/ppermute | solution.py:633
  63.7 28.2 %collective-permute-start.5 = (bf16[6,64,768]{2,1,0:T(8,128)(2,1)}, bf16[6,64,768]{2,1,0:T(8,128)(2,1)}, u32[]{:S(2)}, u32[]{:S(2)}) collective-permute-start(bf16[6,64,768]{2,1,0:T(8,128)(2,1)} %bitcast.43), channel_id=1, source_target_pairs={{0,1},{1,2},{2,3},{4,5},{5,6},{6,7},{8,9},{9,10},{10,11},{12,13},{... | collective-permute-start | bytes 1769480 | tf_op jit(solution)/shard_map/ppermute | solution.py:642
  77.9 133.5 %collective-permute-start.13 = (bf16[768,768]{1,0:T(8,128)(2,1)}, bf16[768,768]{1,0:T(8,128)(2,1)}, u32[]{:S(2)}, u32[]{:S(2)}) collective-permute-start(bf16[768,768]{1,0:T(8,128)(2,1)} %refs_7_.1), channel_id=1, source_target_pairs={{0,1},{1,0},{2,3},{3,2},{4,5},{5,4},{6,7},{7,6},{8,9},{9,8},{10,11... | collective-permute-start | bytes 3538952 | tf_op jit(solution)/shard_map/ppermute | solution.py:633
  91.9 119.5 %collective-permute-start.15 = (bf16[768,768]{1,0:T(8,128)(2,1)}, bf16[768,768]{1,0:T(8,128)(2,1)}, u32[]{:S(2)}, u32[]{:S(2)}) collective-permute-start(bf16[768,768]{1,0:T(8,128)(2,1)} %refs_11_.3), channel_id=1, source_target_pairs={{0,1},{1,0},{2,3},{3,2},{4,5},{5,4},{6,7},{7,6},{8,9},{9,8},{10,11... | collective-permute-start | bytes 3538952 | tf_op jit(solution)/shard_map/ppermute | solution.py:633
  119.8 56.8 %collective-permute-start.8 = (bf16[3,768,192]{1,2,0:T(8,128)(2,1)}, bf16[3,768,192]{1,2,0:T(8,128)(2,1)}, u32[]{:S(2)}, u32[]{:S(2)}) collective-permute-start(bf16[3,768,192]{1,2,0:T(8,128)(2,1)} %collective-permute-done.7), channel_id=1, source_target_pairs={{0,1},{1,0},{2,3},{3,2},{4,5},{5,4},{6,7},{7,6},{8,9},{9,8},{10,11... | collective-permute-start | bytes 2654216 | tf_op jit(solution)/shard_map/ppermute | solution.py:633
  126.7 133.3 %collective-permute-start.17 = (bf16[768,768]{1,0:T(8,128)(2,1)}, bf16[768,768]{1,0:T(8,128)(2,1)}, u32[]{:S(2)}, u32[]{:S(2)}) collective-permute-start(bf16[768,768]{1,0:T(8,128)(2,1)} %collective-permute-done.16.refs_9_), channel_id=1, source_target_pairs={{0,1},{1,0},{2,3},{3,2},{4,5},{5,4},{6,7},{7,6},{8,9},{9,8},{10,11... | collective-permute-start | bytes 3538952 | tf_op jit(solution)/shard_map/ppermute | solution.py:633
  139.4 120.6 %collective-permute-start.21 = (bf16[768,768]{1,0:T(8,128)(2,1)}, bf16[768,768]{1,0:T(8,128)(2,1)}, u32[]{:S(2)}, u32[]{:S(2)}) collective-permute-start(bf16[768,768]{1,0:T(8,128)(2,1)} %collective-permute-done.20.refs_13_), channel_id=1, source_target_pairs={{0,1},{1,0},{2,3},{3,2},{4,5},{5,4},{6,7},{7,6},{8,9},{9,8},{10,11... | collective-permute-start | bytes 3538952 | tf_op jit(solution)/shard_map/ppermute | solution.py:633
  259.4 228.4 %collective-permute-start.35 = (bf16[768,768]{1,0:T(8,128)(2,1)}, bf16[768,768]{1,0:T(8,128)(2,1)}, u32[]{:S(2)}, u32[]{:S(2)}) collective-permute-start(bf16[768,768]{1,0:T(8,128)(2,1)} %get-tuple-element.131), channel_id=1, source_target_pairs={{0,1},{1,0},{2,3},{3,2},{4,5},{5,4},{6,7},{7,6},{8,9},{9,8},{10,11... | collective-permute-start | bytes 3538952 | tf_op jit(solution)/shard_map/ppermute | solution.py:633
  307.2 118.5 %collective-permute-start.33 = (bf16[784,768]{1,0:T(8,128)(2,1)}, bf16[784,768]{1,0:T(8,128)(2,1)}, u32[]{:S(2)}, u32[]{:S(2)}) collective-permute-start(bf16[784,768]{1,0:T(8,128)(2,1)} %get-tuple-element.129), channel_id=1, source_target_pairs={{0,1},{1,0},{2,3},{3,2},{4,5},{5,4},{6,7},{7,6},{8,9},{9,8},{10,11... | collective-permute-start | bytes 3612680 | tf_op jit(solution)/shard_map/ppermute | solution.py:633
  347.4 59.2 %collective-permute-start.30 = (bf16[192,768]{1,0:T(8,128)(2,1)}, bf16[192,768]{1,0:T(8,128)(2,1)}, u32[]{:S(2)}, u32[]{:S(2)}) collective-permute-start(bf16[192,768]{1,0:T(8,128)(2,1)} %slice.277), channel_id=1, source_target_pairs={{0,1},{1,0},{2,3},{3,2},{4,5},{5,4},{6,7},{7,6},{8,9},{9,8},{10,11... | collective-permute-start | bytes 884744 | tf_op jit(solution)/shard_map/ppermute | solution.py:633
  351.0 48.2 %collective-permute-start.27 = (bf16[3,784,192]{1,2,0:T(8,128)(2,1)S(1)}, bf16[3,784,192]{1,2,0:T(8,128)(2,1)S(1)}, u32[]{:S(2)}, u32[]{:S(2)}) collective-permute-start(bf16[3,784,192]{1,2,0:T(8,128)(2,1)S(1)} %copy.70), channel_id=1, source_target_pairs={{0,1},{1,0},{2,3},{3,2},{4,5},{5,4},{6,7},{7,6},{8,9},{9,8},{10,11... | collective-permute-start | bytes 2709512 | tf_op jit(solution)/shard_map/ppermute | solution.py:633
  351.1 52.2 %collective-permute-start.36 = (bf16[768,768]{1,0:T(8,128)(2,1)}, bf16[768,768]{1,0:T(8,128)(2,1)}, u32[]{:S(2)}, u32[]{:S(2)}) collective-permute-start(bf16[768,768]{1,0:T(8,128)(2,1)} %get-tuple-element.133), channel_id=1, source_target_pairs={{0,1},{1,0},{2,3},{3,2},{4,5},{5,4},{6,7},{7,6},{8,9},{9,8},{10,11... | collective-permute-start | bytes 3538952 | tf_op jit(solution)/shard_map/ppermute | solution.py:633
  399.2 80.3 %collective-permute-start.26 = (bf16[3,784,192]{1,2,0:T(8,128)(2,1)}, bf16[3,784,192]{1,2,0:T(8,128)(2,1)S(1)}, u32[]{:S(2)}, u32[]{:S(2)}) collective-permute-start(bf16[3,784,192]{1,2,0:T(8,128)(2,1)} %copy.68), channel_id=1, source_target_pairs={{0,1},{1,0},{2,3},{3,2},{4,5},{5,4},{6,7},{7,6},{8,9},{9,8},{10,11... | collective-permute-start | bytes 2709512 | tf_op jit(solution)/shard_map/ppermute | solution.py:633
  403.4 21.2 %collective-permute-start.29 = (bf16[192,768]{1,0:T(8,128)(2,1)}, bf16[192,768]{1,0:T(8,128)(2,1)S(1)}, u32[]{:S(2)}, u32[]{:S(2)}) collective-permute-start(bf16[192,768]{1,0:T(8,128)(2,1)} %slice.275), channel_id=1, source_target_pairs={{0,1},{1,0},{2,3},{3,2},{4,5},{5,4},{6,7},{7,6},{8,9},{9,8},{10,11... | collective-permute-start | bytes 884744 | tf_op jit(solution)/shard_map/ppermute | solution.py:633
  406.6 76.5 %collective-permute-start.28 = (bf16[3,784,192]{1,2,0:T(8,128)(2,1)S(1)}, bf16[3,784,192]{1,2,0:T(8,128)(2,1)}, u32[]{:S(2)}, u32[]{:S(2)}) collective-permute-start(bf16[3,784,192]{1,2,0:T(8,128)(2,1)S(1)} %copy-done.12), channel_id=1, source_target_pairs={{0,2},{2,0},{1,3},{3,1},{4,6},{6,4},{5,7},{7,5},{8,10},{10,8},{9,1... | collective-permute-start | bytes 2709512 | tf_op jit(solution)/shard_map/ppermute | solution.py:633
  424.5 63.3 %collective-permute-start.37 = (bf16[768,768]{1,0:T(8,128)(2,1)}, bf16[768,768]{1,0:T(8,128)(2,1)}, u32[]{:S(2)}, u32[]{:S(2)}) collective-permute-start(bf16[768,768]{1,0:T(8,128)(2,1)} %add_convert_fusion.7), channel_id=1, source_target_pairs={{0,2},{2,0},{1,3},{3,1},{4,6},{6,4},{5,7},{7,5},{8,10},{10,8},{9,1... | collective-permute-start | bytes 3538952 | tf_op jit(solution)/shard_map/ppermute | solution.py:633
  425.6 53.9 %collective-permute-start.31 = (bf16[192,768]{1,0:T(8,128)(2,1)S(1)}, bf16[192,768]{1,0:T(8,128)(2,1)S(1)}, u32[]{:S(2)}, u32[]{:S(2)}) collective-permute-start(bf16[192,768]{1,0:T(8,128)(2,1)S(1)} %add_convert_fusion.10), channel_id=1, source_target_pairs={{0,2},{2,0},{1,3},{3,1},{4,6},{6,4},{5,7},{7,5},{8,10},{10,8},{9,1... | collective-permute-start | bytes 884744 | tf_op jit(solution)/shard_map/ppermute | solution.py:633
  479.6 11.4 %collective-permute-start.32 = (bf16[784,768]{1,0:T(8,128)(2,1)}, bf16[784,768]{1,0:T(8,128)(2,1)}, u32[]{:S(2)}, u32[]{:S(2)}) collective-permute-start(bf16[784,768]{1,0:T(8,128)(2,1)} %get-tuple-element.127), channel_id=1, source_target_pairs={{0,1},{1,0},{2,3},{3,2},{4,5},{5,4},{6,7},{7,6},{8,9},{9,8},{10,11... | collective-permute-start | bytes 3612680 | tf_op jit(solution)/shard_map/ppermute | solution.py:633
  479.6 29.3 %collective-permute-start.34 = (bf16[784,768]{1,0:T(8,128)(2,1)}, bf16[784,768]{1,0:T(8,128)(2,1)}, u32[]{:S(2)}, u32[]{:S(2)}) collective-permute-start(bf16[784,768]{1,0:T(8,128)(2,1)} %add_convert_fusion.1), channel_id=1, source_target_pairs={{0,2},{2,0},{1,3},{3,1},{4,6},{6,4},{5,7},{7,5},{8,10},{10,8},{9,1... | collective-permute-start | bytes 3612680 | tf_op jit(solution)/shard_map/ppermute | solution.py:633
  550.6 71.5 %collective-permute-start.25 = (bf16[12,64,768]{2,1,0:T(8,128)(2,1)}, bf16[12,64,768]{2,1,0:T(8,128)(2,1)}, u32[]{:S(2)}, u32[]{:S(2)}) collective-permute-start(bf16[12,64,768]{2,1,0:T(8,128)(2,1)} %bitcast.21), channel_id=1, source_target_pairs={{0,1},{1,2},{2,3},{4,5},{5,6},{6,7},{8,9},{9,10},{10,11},{12,13},{... | collective-permute-start | bytes 3538952 | tf_op jit(solution)/shard_map/ppermute | solution.py:652
  562.9 62.5 %collective-permute-start.23 = (bf16[12,64,768]{2,1,0:T(8,128)(2,1)}, bf16[12,64,768]{2,1,0:T(8,128)(2,1)}, u32[]{:S(2)}, u32[]{:S(2)}) collective-permute-start(bf16[12,64,768]{2,1,0:T(8,128)(2,1)} %bitcast.17), channel_id=1, source_target_pairs={{0,1},{1,2},{2,3},{4,5},{5,6},{6,7},{8,9},{9,10},{10,11},{12,13},{... | collective-permute-start | bytes 3538952 | tf_op jit(solution)/shard_map/ppermute | solution.py:652
  571.6 50.5 %collective-permute-start.24 = (bf16[6,64,768]{2,1,0:T(8,128)(2,1)}, bf16[6,64,768]{2,1,0:T(8,128)(2,1)}, u32[]{:S(2)}, u32[]{:S(2)}) collective-permute-start(bf16[6,64,768]{2,1,0:T(8,128)(2,1)} %bitcast.20), channel_id=1, source_target_pairs={{1,0},{2,1},{3,2},{5,4},{6,5},{7,6},{9,8},{10,9},{11,10},{13,12},{... | collective-permute-start | bytes 1769480 | tf_op jit(solution)/shard_map/ppermute | solution.py:651
  574.6 50.8 %collective-permute-start.22 = (bf16[6,64,768]{2,1,0:T(8,128)(2,1)}, bf16[6,64,768]{2,1,0:T(8,128)(2,1)}, u32[]{:S(2)}, u32[]{:S(2)}) collective-permute-start(bf16[6,64,768]{2,1,0:T(8,128)(2,1)} %bitcast.16), channel_id=1, source_target_pairs={{1,0},{2,1},{3,2},{5,4},{6,5},{7,6},{9,8},{10,9},{11,10},{13,12},{... | collective-permute-start | bytes 1769480 | tf_op jit(solution)/shard_map/ppermute | solution.py:651
  (45 other events, 375.2 us)
Sparse Core Ops, SparseCore 0:
  512.2 151.1 all-reduce.8

commit v2 on v1

v2 whole, which is shorter than its diff:
```python
import functools

import jax
import jax.numpy as jnp
import numpy as np
from jax import lax
from jax.experimental import pallas as pl
from jax.experimental.pallas import tpu as pltpu
from jax.sharding import PartitionSpec as P

HD = 64
GRID = 64
WIN = 14
TILES = 5
SPAN = WIN * WIN
ROWS = 208
SLOTS = 7
SLAB = 6 * ROWS
SPLIT = 4
SHORT = 112
LEFT = 6
RIGHT = 12
LANES = 128
EPS = 1e-6
CLIP = 3.0
VMEM = 60 * 1024 * 1024

single = jnp.float32
narrow = jnp.bfloat16

def lane_tables():
    row = np.arange(ROWS)
    x, y = row // WIN, row % WIN
    lane = np.arange(LANES) % 64
    part = lane // 32
    at = lane % 32
    amount = np.where(part[None, :] == 0, 13 - x[:, None], 13 - y[:, None])
    amount = np.where((row < SPAN)[:, None], amount, 0)
    bits = np.stack([(amount >> b) & 1 for b in range(4)]).astype(np.float32)
    lanes = np.zeros((8, LANES), np.float32)
    lanes[0] = at < WIN
    lanes[1] = (at >= 16) & (at < 16 + WIN)
    lanes[2] = lane == 31
    sides = np.zeros((16, LANES), np.float32)
    sides[0] = np.arange(LANES) < 64
    sides[1] = np.arange(LANES) >= 64
    place = np.where(part[None, :] == 0, x[:, None], y[:, None])
    hot = ((at % 16)[None, :] == place) & ((at % 16) < WIN)[None, :] & (row < SPAN)[:, None]
    keys = hot.astype(np.float32)
    keys[SPAN:, lane == 31] = -1e30
    return (
        jnp.asarray(bits),
        jnp.asarray(lanes),
        jnp.asarray(sides, narrow),
        jnp.asarray(keys, narrow),
    )


def dot(a, b):
    return jnp.dot(a, b, preferred_element_type=single)


def dot_nt(a, b):
    return lax.dot_general(a, b, (((1,), (1,)), ((), ())), preferred_element_type=single)


def dot_tn(a, b):
    return lax.dot_general(a, b, (((0,), (0,)), ((), ())), preferred_element_type=single)


def norm_parts(values):
    centre = values - jnp.mean(values, axis=-1, keepdims=True)
    inverse = lax.rsqrt(jnp.mean(centre * centre, axis=-1, keepdims=True) + EPS)
    return centre * inverse, inverse


def norm_back(grad, normal, inverse, gain):
    scaled = grad * gain
    first = jnp.mean(scaled, axis=-1, keepdims=True)
    second = jnp.mean(scaled * normal, axis=-1, keepdims=True)
    return inverse * (scaled - first - normal * second)


def slot_fields(rows_held):
    device, slot = lax.axis_index("tensor"), pl.program_id(0)
    return window_fields(rows_held, device, slot)


def window_fields(rows_held, device, slot):
    window = device * (SLOTS - 1) + slot
    i, j = window // TILES, window % TILES
    last = device // (SPLIT - 1)
    live = slot < SLOTS - 1 + last
    row0 = i * WIN - device * rows_held + LEFT
    high = jnp.minimum(WIN, GRID - i * WIN)
    wide = jnp.minimum(WIN, GRID - j * WIN)
    tall = jnp.where(last == 1, SLOTS - TILES, SLOTS)
    offset = ROWS * jnp.minimum(slot, tall) + SHORT * jnp.maximum(slot - tall, 0)
    return row0, j * WIN, high, wide, offset, live


def positions(axis, first_col, high, wide):
    shape = (ROWS, 1) if axis == 0 else (1, ROWS)
    row = lax.broadcasted_iota(jnp.int32, shape, axis)
    x = lax.shift_right_logical(row * 4682, 16)
    y = row - x * WIN
    valid = (x < high) & (y < wide)
    return jnp.where(valid, x * GRID + first_col + y, -1), valid


def gather_window(source, target):
    token = lax.broadcasted_iota(jnp.int32, (ROWS, WIN * GRID), 1)
    choose = jnp.where(token == target, 1.0, 0.0).astype(narrow)
    return dot(choose, source)


def shift_left(values, bits):
    for b in range(4):
        values = jnp.where(bits[b] > 0.5, pltpu.roll(values, LANES - (1 << b), 1), values)
    return values


def shift_right(values, bits):
    for b in range(4):
        values = jnp.where(bits[b] > 0.5, pltpu.roll(values, 1 << b, 1), values)
    return values


def partners(device):
    beside = device + 1 - 2 * (device % 2)
    across = (device + 2) % SPLIT
    corner = (beside + 2) % SPLIT
    return beside, across, corner


def greet(places):
    barrier = pltpu.get_barrier_semaphore()
    for place in places:
        pl.semaphore_signal(barrier, inc=1, device_id=place, device_id_type=pl.DeviceIdType.MESH)
    pl.semaphore_wait(barrier, len(places))


class Sender:
    def __init__(self, sends, recvs, locals_):
        self.sends, self.recvs, self.locals = sends, recvs, locals_

    def remote(self, at, source, target, place):
        return pltpu.make_async_remote_copy(
            src_ref=source,
            dst_ref=target,
            send_sem=self.sends.at[at],
            recv_sem=self.recvs.at[at],
            device_id=place,
            device_id_type=pl.DeviceIdType.MESH,
        )

    def local(self, at, source, target):
        return pltpu.make_async_copy(source, target, self.locals.at[at])


def attend(n1, valid, weights, qbias, vbias, wrel, bits, lanes, sides, keys, qkv, mixed, peak):
    half = weights.shape[1]
    query = jnp.where(valid, dot_nt(n1, weights[0]) + qbias, 0.0).astype(narrow)
    key8 = dot_nt(n1, weights[1]).astype(narrow) * jnp.asarray(0.125, narrow)
    value = (dot_nt(n1, weights[2]) + vbias).astype(narrow)
    qkv[0, 0] = query
    qkv[0, 1] = key8
    qkv[0, 2] = value
    low_lane = lax.broadcasted_iota(jnp.int32, (ROWS, LANES), 1) < 64
    for pair in range(half // LANES):
        cut = slice(pair * LANES, (pair + 1) * LANES)
        q, k8, v = query[:, cut], key8[:, cut], value[:, cut]
        rel = shift_left(dot(q, wrel[...]), bits)
        rest = rel - rel.astype(narrow).astype(single)
        rel = rel * lanes[0:1] + pltpu.roll(rest, 16, 1) * lanes[1:2] + lanes[2:3]
        rel = rel.astype(narrow)
        qkv[0, 3, :, cut] = rel
        pieces = []
        for head in range(2):
            mine, other = sides[head : head + 1], sides[1 - head : 2 - head]
            only = q * mine
            logits = dot_nt(only, k8)
            at = 2 * pair + head
            peak[at : at + 1, :] = jnp.maximum(
                peak[at : at + 1, :], jnp.max(logits, axis=0, keepdims=True)
            )
            scores = dot_nt(only + rel * other, k8 * mine + keys[...] * other)
            top = jnp.max(scores, axis=1, keepdims=True)
            probs = jnp.exp(scores - top)
            total = jnp.sum(probs, axis=1, keepdims=True)
            pieces.append(dot(probs.astype(narrow), v) * (1.0 / total))
        mixed[0, :, cut] = jnp.where(low_lane, pieces[0], pieces[1]).astype(narrow)
    return dot(mixed[0], weights[3])


def halo_copies(send, base, grid, ext, device, rows):
    top, bottom = LEFT * GRID, RIGHT * GRID
    held_rows = rows * GRID
    down = send.remote(
        base,
        grid.at[pl.ds(held_rows - top, top), :],
        ext.at[pl.ds(0, top), :],
        {"tensor": (device + 1) % SPLIT},
    )
    up = send.remote(
        base + 1,
        grid.at[pl.ds(0, bottom), :],
        ext.at[pl.ds(top + held_rows, bottom), :],
        {"tensor": (device + SPLIT - 1) % SPLIT},
    )
    return down, up


def when_all(*conditions):
    def run(action):
        flag = conditions[0]
        for more in conditions[1:]:
            flag = jnp.logical_and(flag, more)
        pl.when(flag)(action)

    return run


def near_kernel(
    x, pack, fc1, fc2, small, gain, shift, wrel, bits, lanes, sides, keys,
    slab, n1_out, qkv, mixed, attn, peak, weights_out, across_out, beside1, beside2, small_out,
    ext, weights, smalls, sends, recvs, locals_,
):
    step = pl.program_id(0)
    device = lax.axis_index("tensor")
    tokens, width = x.shape
    rows = tokens // GRID
    part = pack.shape[0] // 4
    beside, across, corner = partners(device)
    send = Sender(sends, recvs, locals_)
    down, up = halo_copies(send, 0, x, ext, device, rows)
    packs = [
        send.remote(
            2 + j,
            pack.at[pl.ds(j * part, part), :],
            weights.at[j, pl.ds(part, part), :],
            {"tensor": beside},
        )
        for j in range(4)
    ]
    notes = [
        send.remote(6 + k, small, smalls.at[k + 1], {"tensor": place})
        for k, place in enumerate((beside, across, corner))
    ]
    far = send.remote(9, pack, across_out, {"tensor": across})
    fcs = [
        send.remote(10, fc1, beside1, {"tensor": beside}),
        send.remote(11, fc2, beside2, {"tensor": beside}),
    ]
    mine = [
        send.local(j, pack.at[pl.ds(j * part, part), :], weights.at[j, pl.ds(0, part), :])
        for j in range(4)
    ]
    mine.append(send.local(4, x, ext.at[pl.ds(LEFT * GRID, tokens), :]))
    mine.append(send.local(5, small, smalls.at[0]))
    kept = [send.local(6, weights, weights_out), send.local(7, smalls, small_out)]
    row0, col0, high, wide, offset, live = slot_fields(rows)

    @pl.when(step == 0)
    def _():
        slab[...] = jnp.zeros_like(slab)
        attn[...] = jnp.zeros_like(attn)
        peak[...] = jnp.zeros_like(peak)
        ext[pl.ds(0, LEFT * GRID), :] = jnp.zeros((LEFT * GRID, width), narrow)
        ext[pl.ds(LEFT * GRID + tokens, RIGHT * GRID), :] = jnp.zeros((RIGHT * GRID, width), narrow)
        greet([{"tensor": place} for place in (beside, across, corner)])
        pl.when(device < SPLIT - 1)(down.start)
        pl.when(device > 0)(up.start)
        for copy in packs + notes + mine:
            copy.start()
        far.start()
        for copy in fcs:
            copy.start()
        for copy in mine:
            copy.wait()
        for copy in packs + notes:
            copy.wait()
        for copy in kept:
            copy.start()
        pl.when(device > 0)(down.wait_recv)

    when_all(step == 3, device < SPLIT - 1)(up.wait_recv)

    @pl.when(live)
    def _():
        target, valid = positions(0, col0, high, wide)
        source = ext[pl.ds(pl.multiple_of(row0 * GRID, GRID), WIN * GRID), :]
        window = gather_window(source, target)
        place = pl.ds(pl.multiple_of(offset, 16), ROWS)
        slab[place, :] = window.astype(narrow)
        normal, _ = norm_parts(window)
        n1 = jnp.where(valid, normal * gain[...] + shift[...], 0.0).astype(narrow)
        n1_out[0] = n1
        half = 2 * part
        qbias = smalls[0, 1:2, :half] + smalls[1, 2:3, :half]
        vbias = smalls[0, 3:4, :half] + smalls[1, 4:5, :half]
        terms = attend(
            n1, valid, weights, qbias, vbias, wrel, bits, lanes, sides, keys, qkv, mixed, peak
        )
        attn[place, :] = jnp.where(valid, terms, 0.0)

    @pl.when(step == SLOTS - 1)
    def _():
        pl.when(device < SPLIT - 1)(down.wait_send)
        pl.when(device > 0)(up.wait_send)
        for copy in kept + fcs:
            copy.wait()
        far.wait()


def far_kernel(
    g, pack, fc1, fc2, smalls, n1_in, wrel, bits, lanes, sides, keys,
    slab, qkv, mixed, attn, peak, weights_out, across1, across2,
    ext, weights, sends, recvs, locals_,
):
    step = pl.program_id(0)
    device, image = lax.axis_index("tensor"), lax.axis_index("dp")
    tokens, width = g.shape
    rows = tokens // GRID
    part = pack.shape[0] // 4
    beside, across, _ = partners(device)
    side = image % 2
    mate = image + 1 - 2 * side
    send = Sender(sends, recvs, locals_)
    down, up = halo_copies(send, 0, g, ext, device, rows)
    packs = [
        send.remote(
            2 + j,
            pack.at[pl.ds(j * part, part), :],
            weights.at[j, pl.ds(part, part), :],
            {"tensor": beside},
        )
        for j in range(4)
    ]
    firsts, seconds = [], []
    for k, (source, target) in enumerate(((fc1, across1), (fc2, across2))):
        quarter = source.shape[0] // 4
        for piece in range(2):
            cut = pl.ds(pl.multiple_of((side * 2 + piece) * quarter, 16), quarter)
            at = 6 + 2 * (2 * k + piece)
            firsts.append(send.remote(at, source.at[cut, :], target.at[cut, :], {"tensor": across}))
            seconds.append(
                send.remote(at + 1, target.at[cut, :], target.at[cut, :], {"dp": mate})
            )
    mine = [
        send.local(j, pack.at[pl.ds(j * part, part), :], weights.at[j, pl.ds(0, part), :])
        for j in range(4)
    ]
    whole_grid = send.local(4, g, ext.at[pl.ds(LEFT * GRID, tokens), :])
    kept = send.local(5, weights, weights_out)

    @pl.when(step == 0)
    def _():
        slab[...] = jnp.zeros_like(slab)
        attn[...] = jnp.zeros_like(attn)
        peak[...] = jnp.zeros_like(peak)
        ext[pl.ds(0, LEFT * GRID), :] = jnp.zeros((LEFT * GRID, width), narrow)
        ext[pl.ds(LEFT * GRID + tokens, RIGHT * GRID), :] = jnp.zeros((RIGHT * GRID, width), narrow)
        greet(
            [
                {"tensor": beside},
                {"tensor": across},
                {"tensor": (beside + 2) % SPLIT},
                {"dp": mate},
            ]
        )
        for copy in packs + mine + firsts:
            copy.start()
        pl.when(device < SPLIT - 1)(down.start)
        pl.when(device > 0)(up.start)
        whole_grid.start()
        for copy in packs + mine:
            copy.wait()
        kept.start()

    for piece, at in enumerate((2, 3, 5, 6)):

        @pl.when(step == at)
        def _():
            firsts[piece].wait_recv()
            seconds[piece].start()

    _, col0, high, wide, offset, live = slot_fields(rows)

    @pl.when(live)
    def _():
        _, valid = positions(0, col0, high, wide)
        place = pl.ds(pl.multiple_of(offset, 16), ROWS)
        half = 2 * part
        qbias = smalls[2, 1:2, :half] + smalls[3, 2:3, :half]
        vbias = smalls[2, 3:4, :half] + smalls[3, 4:5, :half]
        terms = attend(
            n1_in[0], valid, weights, qbias, vbias, wrel, bits, lanes, sides, keys, qkv, mixed, peak
        )
        attn[place, :] = jnp.where(valid, terms, 0.0)

    @pl.when(step == SLOTS - 1)
    def _():
        whole_grid.wait()
        pl.when(device < SPLIT - 1)(down.wait_send)
        pl.when(device > 0)(down.wait_recv)
        pl.when(device > 0)(up.wait_send)
        pl.when(device < SPLIT - 1)(up.wait_recv)

        @pl.loop(0, SLOTS)
        def _(slot):
            row0, col0, high, wide, offset, live = window_fields(rows, device, slot)

            @pl.when(live)
            def _():
                target, _ = positions(0, col0, high, wide)
                source = ext[pl.ds(pl.multiple_of(row0 * GRID, GRID), WIN * GRID), :]
                slab[pl.ds(pl.multiple_of(offset, 16), ROWS), :] = gather_window(
                    source, target
                ).astype(narrow)

        kept.wait()
        for copy in firsts:
            copy.wait_send()
        for copy in seconds:
            copy.wait()


def whole(shape):
    zeros = (0,) * len(shape)
    return pl.BlockSpec(shape, lambda *_: zeros, pipeline_mode=pl.Buffered(1))


def by_slot(shape):
    rest = (0,) * len(shape)
    return pl.BlockSpec((1,) + tuple(shape), lambda s, *_: (s,) + rest)


ANY = pl.BlockSpec(memory_space=pl.ANY)


def of(shape, dtype=narrow):
    return jax.ShapeDtypeStruct(shape, dtype)


FORWARD_COST = pl.CostEstimate(
    flops=13_000_000_000, bytes_accessed=30_000_000, transcendentals=4_000_000
)


def near_forward(x, pack, fc1, fc2, small, norm, wrel, tables):
    tokens, width = x.shape
    half = pack.shape[0] // 2
    slab = (SLAB, width)
    outs = [
        (of(slab), whole(slab)),
        (of((SLOTS, ROWS, width)), by_slot((ROWS, width))),
        (of((SLOTS, 4, ROWS, half)), by_slot((4, ROWS, half))),
        (of((SLOTS, ROWS, half)), by_slot((ROWS, half))),
        (of(slab, single), whole(slab)),
        (of((8, ROWS), single), whole((8, ROWS))),
        (of((4, half, width)), ANY),
        (of(pack.shape), ANY),
        (of(fc1.shape), ANY),
        (of(fc2.shape), ANY),
        (of((SPLIT,) + small.shape, single), ANY),
    ]
    operands = (x, pack, fc1, fc2, small, *norm, wrel, *tables)
    return pl.pallas_call(
        near_kernel,
        out_shape=[o[0] for o in outs],
        grid=(SLOTS,),
        in_specs=[ANY] * 5 + [whole(a.shape) for a in operands[5:]],
        out_specs=[o[1] for o in outs],
        scratch_shapes=[
            pltpu.VMEM((tokens + (LEFT + RIGHT) * GRID, width), narrow),
            pltpu.VMEM((4, half, width), narrow),
            pltpu.VMEM((SPLIT,) + small.shape, single),
            pltpu.SemaphoreType.DMA((12,)),
            pltpu.SemaphoreType.DMA((12,)),
            pltpu.SemaphoreType.DMA((8,)),
        ],
        compiler_params=pltpu.CompilerParams(
            vmem_limit_bytes=VMEM, collective_id=0, has_side_effects=True
        ),
        cost_estimate=FORWARD_COST,
        name="near_forward",
    )(*operands)


def far_forward(g, pack, fc1, fc2, smalls, n1, wrel, tables):
    tokens, width = g.shape
    half = pack.shape[0] // 2
    slab = (SLAB, width)
    outs = [
        (of(slab), whole(slab)),
        (of((SLOTS, 4, ROWS, half)), by_slot((4, ROWS, half))),
        (of((SLOTS, ROWS, half)), by_slot((ROWS, half))),
        (of(slab, single), whole(slab)),
        (of((8, ROWS), single), whole((8, ROWS))),
        (of((4, half, width)), ANY),
        (of(fc1.shape), ANY),
        (of(fc2.shape), ANY),
    ]
    operands = (g, pack, fc1, fc2, smalls, n1, wrel, *tables)
    in_specs = [ANY] * 4 + [whole(a.shape) for a in operands[4:]]
    in_specs[5] = by_slot((ROWS, width))
    return pl.pallas_call(
        far_kernel,
        out_shape=[o[0] for o in outs],
        grid=(SLOTS,),
        in_specs=in_specs,
        out_specs=[o[1] for o in outs],
        scratch_shapes=[
            pltpu.VMEM((tokens + (LEFT + RIGHT) * GRID, width), narrow),
            pltpu.VMEM((4, half, width), narrow),
            pltpu.SemaphoreType.DMA((14,)),
            pltpu.SemaphoreType.DMA((14,)),
            pltpu.SemaphoreType.DMA((6,)),
        ],
        compiler_params=pltpu.CompilerParams(
            vmem_limit_bytes=VMEM, collective_id=1, has_side_effects=True
        ),
        cost_estimate=FORWARD_COST,
        name="far_forward",
    )(*operands)


BLOCK = 256
CHUNK = 416


def gelu_parts(z):
    size = jnp.abs(z)
    bell = jnp.exp(-0.5 * z * z)
    t = 1.0 / (1.0 + 0.2316418882663604 * size)
    poly = 0.5 * 1.061405429 * t + (0.5 * -1.453152027)
    poly = poly * t + 0.5 * 1.421413741
    poly = poly * t + 0.5 * -0.284496736
    poly = poly * t + 0.5 * 0.254829592
    tail = poly * t * bell
    phi_total = jnp.where(z >= 0, 1.0 - tail, tail)
    return z * phi_total, phi_total + z * bell * 0.3989422804014327


def mlp_kernel(first, *refs):
    if first:
        (xs, attn1, attn2, gs, pbias, gain, shift, smalls, src1, src2, w1a, w2a) = refs[:12]
        (x1, n2, n2t, gt, branch, dn2, gw1a, gw1b, gw2a, gw2b, gb) = refs[12:23]
        (corner1, corner2, sends, recvs, w1, w2, b1, hs, zs) = refs[23:]
        kinds = (2, 3)
    else:
        (x1, n2, n2t, gs, gt, branch0, dn20, fbias, gain, smalls, w1a, w1b, w2a, w2b) = refs[:14]
        (out, dx1, da, sums, gw1a, gw1b, gw2a, gw2b, gb) = refs[14:23]
        (branch, dn2, w1, w2, b1, hs, zs) = refs[23:]
        kinds = (0, 1)
    step = pl.program_id(0)
    count = pl.num_programs(0) // 2
    rows, width = gs.shape
    if first:
        beside, _, _ = partners(lax.axis_index("tensor"))
        send = Sender(sends, recvs, None)
        corners = [
            send.remote(0, src1, corner1, {"tensor": beside}),
            send.remote(1, src2, corner2, {"tensor": beside}),
        ]

    @pl.when(step == 0)
    def _():
        gb[...] = jnp.zeros_like(gb)
        if first:
            greet([{"tensor": beside}])
            for copy in corners:
                copy.start()

            @pl.loop(0, SLAB // ROWS)
            def _(c):
                sl = pl.ds(pl.multiple_of(c * ROWS, 16), ROWS)
                middle = xs[sl, :].astype(single) + (attn1[sl, :] + attn2[sl, :] + pbias[...])
                x1[sl, :] = middle
                normal, _ = norm_parts(middle)
                n2[sl, :] = (normal * gain[...] + shift[...]).astype(narrow)
                branch[sl, :] = jnp.zeros((ROWS, width), single)
                dn2[sl, :] = jnp.zeros((ROWS, width), single)

            for j in range(width // LANES):
                cut = slice(j * LANES, (j + 1) * LANES)
                n2t[cut, :] = n2[:, cut].T
                gt[cut, :] = gs[:, cut].T
        else:

            @pl.loop(0, SLAB // ROWS)
            def _(c):
                sl = pl.ds(pl.multiple_of(c * ROWS, 16), ROWS)
                branch[sl, :] = branch0[sl, :]
                dn2[sl, :] = dn20[sl, :]

    if first:

        @pl.when(step == count)
        def _():
            for copy in corners:
                copy.wait()

    @pl.when(step < count)
    def _():
        w1[...] = w1a[...]
        w2[...] = w2a[...]
        b1[...] = smalls[kinds[0], 0:1, pl.ds(pl.multiple_of(step * BLOCK, BLOCK), BLOCK)]

    @pl.when(step >= count)
    def _():
        cut = pl.ds(pl.multiple_of((step - count) * BLOCK, BLOCK), BLOCK)
        if first:
            w1[...] = corner1[:, cut]
            w2[...] = corner2[cut, :]
        else:
            w1[...] = w1b[...]
            w2[...] = w2b[...]
        b1[...] = smalls[kinds[1], 0:1, cut]

    bias_row = step // count
    bias_cut = pl.ds(pl.multiple_of((step % count) * BLOCK, BLOCK), BLOCK)

    @pl.loop(0, SLAB // CHUNK)
    def _(c):
        sl = pl.ds(pl.multiple_of(c * CHUNK, 16), CHUNK)
        z = dot(n2[sl, :], w1[...]) + b1[0:1]
        dh = dot_nt(gs[sl, :], w2[...])
        act, slope = gelu_parts(z)
        h = act.astype(narrow)
        dz = (dh * slope).astype(narrow)
        hs[sl, :] = h
        zs[sl, :] = dz
        gb[bias_row, 0:1, bias_cut] += jnp.sum(dz.astype(single), axis=0, keepdims=True)
        branch[sl, :] += dot(h, w2[...])
        dn2[sl, :] += dot_nt(dz, w1[...])

    def store(gw1, gw2):
        @pl.loop(0, width // 256)
        def _(r):
            sl = pl.ds(pl.multiple_of(r * 256, 256), 256)
            gw1[sl, :] = dot(n2t[sl, :], zs[...]).astype(narrow)
            gw2[sl, :] = dot(gt[sl, :], hs[...]).astype(narrow)

    @pl.when(step < count)
    def _():
        store(gw1a, gw2a)

    @pl.when(step >= count)
    def _():
        store(gw1b, gw2b)

    if not first:

        @pl.when(step == 2 * count - 1)
        def _():
            sums[...] = jnp.zeros_like(sums)

            @pl.loop(0, SLAB // ROWS)
            def _(c):
                sl = pl.ds(pl.multiple_of(c * ROWS, 16), ROWS)
                middle = x1[sl, :]
                normal, inverse = norm_parts(middle)
                out[sl, :] = (middle + (branch[sl, :] + fbias[...])).astype(narrow)
                grad = dn2[sl, :]
                cot = gs[sl, :].astype(single)
                total = cot + norm_back(grad, normal, inverse, gain[...])
                dx1[sl, :] = total
                low = total.astype(narrow)
                da[sl, :] = low
                sums[0:1, :] += jnp.sum(grad * normal, axis=0, keepdims=True)
                sums[1:2, :] += jnp.sum(grad, axis=0, keepdims=True)
                sums[2:3, :] += jnp.sum(low.astype(single), axis=0, keepdims=True)
                sums[3:4, :] += jnp.sum(cot, axis=0, keepdims=True)


def mlp_half(first, residents, w1a, w1b, w2a, w2b):
    width, local = w1a.shape
    count = local // BLOCK

    def early(shape, dim):
        def index(i):
            at = jnp.minimum(i, count - 1)
            return (0, at) if dim == 1 else (at, 0)

        return pl.BlockSpec(shape, index)

    def late(shape, dim):
        def index(i):
            at = jnp.maximum(i - count, 0)
            return (0, at) if dim == 1 else (at, 0)

        return pl.BlockSpec(shape, index)

    slab = (SLAB, width)
    flipped = (width, SLAB)
    in_specs = [whole(a.shape) for a in residents]
    if first:
        operands = (*residents, w1a, w2a, w1a, w2a)
        in_specs += [ANY, ANY, early((width, BLOCK), 1), early((BLOCK, width), 0)]
        outs = [
            (of(slab, single), whole(slab)),
            (of(slab), whole(slab)),
            (of(flipped), whole(flipped)),
            (of(flipped), whole(flipped)),
            (of(slab, single), whole(slab)),
            (of(slab, single), whole(slab)),
        ]
        scratch = [
            pltpu.VMEM((width, local), narrow),
            pltpu.VMEM((local, width), narrow),
            pltpu.SemaphoreType.DMA((2,)),
            pltpu.SemaphoreType.DMA((2,)),
        ]
        params = pltpu.CompilerParams(
            vmem_limit_bytes=VMEM, collective_id=2, has_side_effects=True
        )
    else:
        operands = (*residents, w1a, w1b, w2a, w2b)
        in_specs += [
            early((width, BLOCK), 1),
            late((width, BLOCK), 1),
            early((BLOCK, width), 0),
            late((BLOCK, width), 0),
        ]
        outs = [
            (of(slab), whole(slab)),
            (of(slab, single), whole(slab)),
            (of(slab), whole(slab)),
            (of((8, width), single), whole((8, width))),
        ]
        scratch = [pltpu.VMEM(slab, single), pltpu.VMEM(slab, single)]
        params = pltpu.CompilerParams(vmem_limit_bytes=VMEM)
    outs += [
        (of((width, local)), early((width, BLOCK), 1)),
        (of((width, local)), late((width, BLOCK), 1)),
        (of((width, local)), early((width, BLOCK), 1)),
        (of((width, local)), late((width, BLOCK), 1)),
        (of((2, 8, local), single), whole((2, 8, local))),
    ]
    scratch += [
        pltpu.VMEM((width, BLOCK), narrow),
        pltpu.VMEM((BLOCK, width), narrow),
        pltpu.VMEM((1, BLOCK), single),
        pltpu.VMEM((SLAB, BLOCK), narrow),
        pltpu.VMEM((SLAB, BLOCK), narrow),
    ]
    return pl.pallas_call(
        functools.partial(mlp_kernel, first),
        out_shape=[o[0] for o in outs],
        grid=(2 * count,),
        in_specs=in_specs,
        out_specs=[o[1] for o in outs],
        scratch_shapes=scratch,
        compiler_params=params,
        cost_estimate=pl.CostEstimate(
            flops=18_000_000_000, bytes_accessed=40_000_000, transcendentals=4_000_000
        ),
        name="mlp",
    )(*operands)


def backward_kernel(first, rows_held, *refs):
    (da, n1, qkv, mixed, weights, wrel, bits, lanes, sides, keys) = refs[:10]
    if first:
        (dn1, keep, give, bias, grel, acc, dqkv) = refs[10:]
    else:
        (prior, xs, dx1, gain) = refs[10:14]
        (back, sums, keep, give, bias, grel, acc, dqkv) = refs[14:]
    _, col0, high, wide, offset, live = slot_fields(rows_held)
    half, width = weights.shape[1:]

    @pl.when(pl.program_id(0) == 0)
    def _():
        acc[...] = jnp.zeros_like(acc)
        bias[...] = jnp.zeros_like(bias)
        grel[...] = jnp.zeros_like(grel)
        if not first:
            back[...] = jnp.zeros_like(back)
            sums[...] = jnp.zeros_like(sums)

    @pl.when(live)
    def _():
        _, valid = positions(0, col0, high, wide)
        place = pl.ds(pl.multiple_of(offset, 16), ROWS)
        da_win = jnp.where(valid, da[place, :].astype(single), 0.0).astype(narrow)
        acc[3] += dot_tn(mixed[0], da_win)
        dmix = dot_nt(da_win, weights[3]).astype(narrow)
        low_lane = lax.broadcasted_iota(jnp.int32, (ROWS, LANES), 1) < 64
        for pair in range(half // LANES):
            cut = slice(pair * LANES, (pair + 1) * LANES)
            q, k8, v, rel = (qkv[0, j, :, cut] for j in range(4))
            do = dmix[:, cut]
            dqs, dks, dvs = [], [], []
            for head in range(2):
                mine, other = sides[head : head + 1], sides[1 - head : 2 - head]
                full_key = k8 * mine + keys[...] * other
                scores = dot_nt(full_key, q * mine + rel * other)
                top = jnp.max(scores, axis=0, keepdims=True)
                probs = jnp.exp(scores - top)
                probs = probs * (1.0 / jnp.sum(probs, axis=0, keepdims=True))
                dprobs = dot_nt(v, do * mine)
                mean = jnp.sum(probs * dprobs, axis=0, keepdims=True)
                dscores = (probs * (dprobs - mean)).astype(narrow)
                dvs.append(dot(probs.astype(narrow), do))
                dks.append(dot(dscores, q))
                dqs.append(dot_tn(dscores, full_key))
            dv = jnp.where(low_lane, dvs[0], dvs[1])
            dk = jnp.where(low_lane, dks[0], dks[1]) * 0.125
            dq = jnp.where(low_lane, dqs[0], dqs[1])
            drel = jnp.where(low_lane, dqs[1], dqs[0]) * lanes[0:1]
            drel = shift_right(drel, bits).astype(narrow)
            dq = dq + dot_nt(drel, wrel[...])
            grel[...] += dot_tn(drel, q)
            dqkv[0, :, cut] = dq.astype(narrow)
            dqkv[1, :, cut] = dk.astype(narrow)
            dqkv[2, :, cut] = dv.astype(narrow)
        total = None
        for j in range(3):
            piece = dqkv[j]
            acc[j] += dot_tn(piece, n1[0])
            bias[j : j + 1, :] += jnp.sum(piece.astype(single), axis=0, keepdims=True)
            back_part = dot(piece, weights[j])
            total = back_part if total is None else total + back_part
        if first:
            dn1[0] = total
        else:
            grad = jnp.where(valid, total + prior[0], 0.0)
            normal, inverse = norm_parts(xs[place, :].astype(single))
            sums[0:1, :] += jnp.sum(grad * normal, axis=0, keepdims=True)
            sums[1:2, :] += jnp.sum(grad, axis=0, keepdims=True)
            result = dx1[place, :] + norm_back(grad, normal, inverse, gain[...])
            back[place, :] = jnp.where(valid, result, 0.0).astype(narrow)

    @pl.when(pl.program_id(0) == SLOTS - 1)
    def _():
        part = half // 2
        for j in range(4):
            keep[j * part : (j + 1) * part, :] = acc[j, :part, :].astype(narrow)
            give[j * part : (j + 1) * part, :] = acc[j, part:, :].astype(narrow)


def backward_half(rows_held, da, n1, qkv, mixed, weights, wrel, tables, final):
    first = final is None
    half, width = weights.shape[1:]
    operands = [da, n1, qkv, mixed, weights, wrel, *tables]
    in_specs = [whole(a.shape) for a in operands]
    for at in (1, 2, 3):
        in_specs[at] = by_slot(operands[at].shape[1:])
    if first:
        outs = [(of((SLOTS, ROWS, width), single), by_slot((ROWS, width)))]
    else:
        prior, xs, dx1, gain = final
        operands += [prior, xs, dx1, gain]
        in_specs += [by_slot((ROWS, width)), whole(xs.shape), whole(dx1.shape), whole(gain.shape)]
        outs = [
            (of((SLAB, width)), whole((SLAB, width))),
            (of((8, width), single), whole((8, width))),
        ]
    outs += [
        (of((2 * half, width)), whole((2 * half, width))),
        (of((2 * half, width)), whole((2 * half, width))),
        (of((8, half), single), whole((8, half))),
        (of((LANES, LANES), single), whole((LANES, LANES))),
    ]
    return pl.pallas_call(
        functools.partial(backward_kernel, first, rows_held),
        out_shape=[o[0] for o in outs],
        grid=(SLOTS,),
        in_specs=in_specs,
        out_specs=[o[1] for o in outs],
        scratch_shapes=[
            pltpu.VMEM((4, half, width), single),
            pltpu.VMEM((3, ROWS, half), narrow),
        ],
        compiler_params=pltpu.CompilerParams(vmem_limit_bytes=VMEM),
        cost_estimate=pl.CostEstimate(
            flops=26_000_000_000, bytes_accessed=40_000_000, transcendentals=4_000_000
        ),
        name="attention_backward",
    )(*operands)


def place_kernel(rows_held, slab, ext):
    row0, col0, high, wide, offset, live = slot_fields(rows_held)

    @pl.when(pl.program_id(0) == 0)
    def _():
        ext[...] = jnp.zeros_like(ext)

    @pl.when(live)
    def _():
        target, _ = positions(1, col0, high, wide)
        token = lax.broadcasted_iota(jnp.int32, (WIN * GRID, ROWS), 0)
        choose = jnp.where(token == target, 1.0, 0.0).astype(narrow)
        window = slab[pl.ds(pl.multiple_of(offset, 16), ROWS), :]
        where_to = pl.ds(pl.multiple_of(row0 * GRID, GRID), WIN * GRID)
        ext[where_to, :] += dot(choose, window).astype(narrow)


def place_windows(rows_held, slab):
    width = slab.shape[1]
    tokens = (rows_held + LEFT + RIGHT) * GRID
    return pl.pallas_call(
        functools.partial(place_kernel, rows_held),
        out_shape=of((tokens, width)),
        grid=(SLOTS,),
        in_specs=[whole(slab.shape)],
        out_specs=whole((tokens, width)),
        compiler_params=pltpu.CompilerParams(vmem_limit_bytes=VMEM),
        cost_estimate=pl.CostEstimate(
            flops=2_000_000_000, bytes_accessed=6_000_000, transcendentals=0
        ),
        name="place_windows",
    )(slab)


CORE_SWAP = ((0, 1), (1, 0), (2, 3), (3, 2))
CHIP_SWAP = ((0, 2), (2, 0), (1, 3), (3, 1))
UP = ((0, 1), (1, 2), (2, 3))
DOWN = ((1, 0), (2, 1), (3, 2))


def swap(value, pairs):
    return jax.tree.map(lambda a: lax.ppermute(a, "tensor", pairs), value)


def add_low(a, b):
    return jax.tree.map(lambda u, v: (u.astype(single) + v.astype(single)).astype(narrow), a, b)


def collect(ext, rows):
    width = ext.shape[-1]
    grid = ext.reshape(rows + LEFT + RIGHT, GRID, width)
    from_below = lax.ppermute(grid[:LEFT], "tensor", DOWN)
    from_above = lax.ppermute(grid[LEFT + rows :], "tensor", UP)
    mine = grid[LEFT : LEFT + rows]
    mine = mine + jnp.pad(from_below, ((rows - LEFT, 0), (0, 0), (0, 0)))
    mine = mine + jnp.pad(from_above, ((0, rows - RIGHT), (0, 0), (0, 0)))
    return mine.reshape(1, rows * GRID, width)


def shards(
    inputs,
    w_qkv,
    qv_bias,
    w_proj,
    proj_bias,
    w_fc1,
    fc1_bias,
    w_fc2,
    fc2_bias,
    norm1_gain,
    norm1_shift,
    norm2_gain,
    norm2_shift,
    rel_h,
    rel_w,
    cotangent,
):
    width = inputs.shape[2]
    rows = inputs.shape[1] // GRID
    local = w_qkv.shape[2]
    heads = local // HD
    device = lax.axis_index("tensor")
    tables = lane_tables()

    block = jnp.zeros((2, 32, HD), narrow)
    block = block.at[0, : 2 * WIN - 1].set(rel_h[::-1]).at[1, : 2 * WIN - 1].set(rel_w[::-1])
    block = block.reshape(HD, HD).T
    wrel = jnp.zeros((LANES, LANES), narrow).at[:HD, HD:].set(block).at[HD:, :HD].set(block)

    pack = jnp.concatenate([w_qkv.transpose(0, 2, 1).reshape(3 * local, width), w_proj])
    small = jnp.zeros((8, fc1_bias.shape[0]), single).at[0].set(fc1_bias)
    for j in range(2):
        small = small.at[1 + 2 * j, :local].set(qv_bias[j])
        small = small.at[2 + 2 * j, local : 2 * local].set(qv_bias[j])
    norm1 = (norm1_gain[None], norm1_shift[None])

    (
        xs, n1, near_qkv, near_mixed, near_attn, near_peak,
        near_w, across, beside1, beside2, smalls,
    ) = near_forward(inputs[0], pack, w_fc1, w_fc2, small, norm1, wrel, tables)
    gs, far_qkv, far_mixed, far_attn, far_peak, far_w, across1, across2 = far_forward(
        cotangent[0], across, w_fc1, w_fc2, smalls, n1, wrel, tables
    )

    x1, n2, n2t, gt, branch, dn2, *far_fc = mlp_half(
        True,
        (xs, near_attn, far_attn, gs, proj_bias[None], norm2_gain[None], norm2_shift[None], smalls),
        across1,
        None,
        across2,
        None,
    )
    out, dx1, da, sums2, *near_fc = mlp_half(
        False,
        (x1, n2, n2t, gs, gt, branch, dn2, fc2_bias[None], norm2_gain[None], smalls),
        w_fc1,
        beside1,
        w_fc2,
        beside2,
    )

    dn1, far_keep, far_give, far_bias, far_rel = backward_half(
        rows, da, n1, far_qkv, far_mixed, far_w, wrel, tables, None
    )
    back, sums1, near_keep, near_give, near_bias, near_rel = backward_half(
        rows, da, n1, near_qkv, near_mixed, near_w, wrel, tables, (dn1, xs, dx1, norm1_gain[None])
    )

    output = collect(place_windows(rows, out), rows)
    input_grad = collect(place_windows(rows, back), rows)

    far_total = add_low(
        (far_fc[0], far_fc[2], far_keep), swap((far_fc[1], far_fc[3], far_give), CORE_SWAP)
    )
    near_total = add_low(
        (near_fc[0], near_fc[2], near_keep), swap((near_fc[1], near_fc[3], near_give), CORE_SWAP)
    )
    totals = add_low(near_total, swap(far_total, CHIP_SWAP))
    totals = lax.psum(totals, "dp")
    gw1, gw2, gpack = jax.tree.map(lambda a: a.astype(single), totals)

    blocks = near_rel + far_rel
    blocks = blocks[HD:, :HD] + blocks[:HD, HD:]
    grad_rel = jnp.stack([blocks[: 2 * WIN - 1][::-1], blocks[32 : 32 + 2 * WIN - 1][::-1]])
    fc_bias = jnp.concatenate([near_fc[4][:, 0], far_fc[4][:, 0]])
    qv = jnp.concatenate(
        [b[jnp.array([0, 2])].reshape(2, 2, local).transpose(1, 0, 2) for b in (near_bias, far_bias)]
    )
    biases = jnp.concatenate([fc_bias, qv.reshape(SPLIT, 2 * local)], axis=1)
    biases = biases[jnp.arange(SPLIT) ^ device]
    sums, grad_rel, biases = lax.psum(
        (jnp.concatenate([sums1[:2], sums2[:4]]), grad_rel, biases), ("dp", "tensor")
    )
    biases = biases[device]

    def peaks(peak):
        top = jnp.max(peak, axis=1)[: 2 * heads]
        return jnp.maximum(top[:heads], lax.ppermute(top[heads:], "tensor", CORE_SWAP))

    head_max = jnp.maximum(
        peaks(near_peak), lax.ppermute(peaks(far_peak), "tensor", CHIP_SWAP)
    )
    head_max = lax.pmax(head_max, "dp")
    factor = jnp.sqrt(CLIP / jnp.maximum(head_max, CLIP))
    clipped_qk = (w_qkv[:2].astype(single) * jnp.repeat(factor, HD)).astype(narrow)

    return (
        output,
        input_grad,
        gpack[: 3 * local].reshape(3, local, width).transpose(0, 2, 1),
        biases[fc1_bias.shape[0] :].reshape(2, local),
        gpack[3 * local :],
        sums[4],
        gw1,
        biases[: fc1_bias.shape[0]],
        gw2.T,
        sums[5],
        sums[:4],
        grad_rel,
        clipped_qk,
        head_max,
    )


def solution(mesh):
    return jax.shard_map(
        shards,
        mesh=mesh,
        in_specs=(
            P("dp", "tensor", None),
            P(None, None, "tensor"),
            P(None, "tensor"),
            P("tensor", None),
            P(),
            P(None, "tensor"),
            P("tensor"),
            P("tensor", None),
            P(),
            P(),
            P(),
            P(),
            P(),
            P(),
            P(),
            P("dp", "tensor", None),
        ),
        out_specs=(
            P("dp", "tensor", None),
            P("dp", "tensor", None),
            P(None, None, "tensor"),
            P(None, "tensor"),
            P("tensor", None),
            P(),
            P(None, "tensor"),
            P("tensor"),
            P("tensor", None),
            P(),
            P(),
            P(),
            P(None, None, "tensor"),
            P("tensor"),
        ),
        check_vma=False,
    )
```

time: 688 us -> 533 us (0.77)
  waiting for transfers between devices: 137 us -> 60.3 us
  starting transfers between devices: 98.4 us -> 26.7 us
  Pallas kernels: 256 us -> 297 us
  local copies, waits for them, and re-layouts: 67.5 us -> 40.3 us
  other arithmetic: 45.4 us -> 26.6 us
    ppermute x30 -> x9, waiting for transfers between devices: 99.1 us -> 0.02 us  [swap(): return jax.tree.map(lambda a: lax.ppermute(a, 'tensor', pairs), value)]
    ppermute x30 -> x9, starting transfers between devices: 78.6 us -> 13.9 us  [swap(): return jax.tree.map(lambda a: lax.ppermute(a, 'tensor', pairs), value)]
    pallas_call x6, Pallas kernels: 161 us -> 197 us  [the longest x2 78 us: backward_half(): pl.pallas_call(functools.partial(backward_kernel, first, rows_held), out_...]
    psum x1, waiting for transfers between devices: 35.2 us -> 57.6 us  [shards(): totals = lax.psum(totals, 'dp')]
    slice x13 -> x6, local copies, waits for them, and re-layouts: 18 us -> 6.31 us  [the longest x1 2.6 us: shards(): gpack[:3 * local].reshape(3, local, width).transpose(0, 2, 1)]
    concatenate x6 -> x3, other arithmetic: 12.8 us -> 2.37 us  [the longest x1 2.36 us: shards(): jnp.concatenate([w_qkv.transpose(0, 2, 1).reshape(3 * local, width), w_pr...]
    ppermute x6 -> x0, local copies, waits for them, and re-layouts: 9.84 us -> none  [swap(): return jax.tree.map(lambda a: lax.ppermute(a, 'tensor', pairs), value)]
    ppermute x4 -> x0, starting transfers between devices: 8.07 us -> none  [the longest x2 5.5 us: spread(): above = lax.ppermute(grid[rows - LEFT:], 'tensor', UP)]
  transfers between devices with their start and end apart: 42 -> 17, of which waited for: 13 -> 3; matrix products, arithmetic and copies ran while one was open for 14% -> 8% of each run, Pallas kernels for 37% -> 26%
where the time goes in v2:
time: 533 us; the launch traced here: 532 us
  Pallas kernels  297 us (56%)
  blocking collectives  66 us (12%)
  waiting for transfers between devices  60.3 us (11%)
  local copies, waits for them, and re-layouts  40.3 us (8%)
  starting transfers between devices  26.7 us (5%)
  other arithmetic  26.6 us (5%)
  between operations  14.5 us (3%)
    pallas_call x2, Pallas kernels, mlp_half(): pl.pallas_call(functools.partial(mlp_kernel, first), out_shape=[o[0] for...  100 us
    pallas_call x2, Pallas kernels, backward_half(): pl.pallas_call(functools.partial(backward_kernel, first, rows_held), out_...  78 us
    pallas_call x1, Pallas kernels, near_forward(): pl.pallas_call(near_kernel, out_shape=[o[0] for o in outs], grid=(SLOTS,)...  61.7 us
    psum x1, waiting for transfers between devices, shards(): totals = lax.psum(totals, 'dp')  57.6 us
    psum x1, blocking collectives, shards(): lax.psum((jnp.concatenate([sums1[:2], sums2[:4]]), grad_rel, biases), ('d...  46.2 us
    pallas_call x1, Pallas kernels, far_forward(): pl.pallas_call(far_kernel, out_shape=[o[0] for o in outs], grid=(SLOTS,),...  43.8 us
    pmax x1, blocking collectives, shards(): head_max = lax.pmax(head_max, 'dp')  19.8 us
    ppermute x9, starting transfers between devices, swap(): return jax.tree.map(lambda a: lax.ppermute(a, 'tensor', pairs), value)  13.9 us
  transfers between devices with their start and end apart: 17, of which 3 were waited for; matrix products, arithmetic and copies ran while one was open for 8% of the time, Pallas kernels for 26%

profile of v2, /device:TPU:0, one launch (start us, length us, event | category | flops | bytes accessed | tf_op | source)
XLA Modules:
  0.0 531.8 jit_solution(10147884396445893129)
XLA Ops:
  20.0 2.4 pad_maximum_fusion.pack
  22.3 2.1 scatter.41
  25.4 61.7 %near_forward.1 = (bf16[1248,768]{1,0:T(8,128)(2,1)}, bf16[7,208,768]{2,1,0:T(8,128)(2,1)}, bf16[7,4,208,384]{3,2,1,0:T(8,128)(2,1)}, bf16[7,208,384]{2,1,0:T(8,...) custom-call(bf16[1024,768]{1,0:T(8,128)(2,1)} %bitcast.50, ...), custom_call_target="tpu_custom_call" | custom-call | flops 12999999488 | bytes 30000000 | tf_op jit(solution)/shard_map/near_forward/pallas_call | solution.py:469
  87.1 43.8 %far_forward.1 = (bf16[1248,768]{1,0:T(8,128)(2,1)}, bf16[7,4,208,384]{3,2,1,0:T(8,128)(2,1)}, bf16[7,208,384]{2,1,0:T(8,128)(2,1)}, f32[1248,768]{1,0:T(8,128)}...) custom-call(bf16[1024,768]{1,0:T(8,128)(2,1)} %bitcast.51, ...), custom_call_target="tpu_custom_call" | custom-call | flops 12999999488 | bytes 30000000 | tf_op jit(solution)/shard_map/far_forward/pallas_call | solution.py:508
  131.0 53.1 %mlp.2 = (f32[1248,768]{1,0:T(8,128)}, bf16[1248,768]{1,0:T(8,128)(2,1)}, bf16[768,1248]{1,0:T(8,128)(2,1)}, bf16[768,1248]{1,0:T(8,128)(2,1)}, f32[1248,768]{1,...) custom-call(bf16[1248,768]{1,0:T(8,128)(2,1)} %get-tuple-element.172, ...), custom_call_target="tpu_custom_call" | custom-call | flops 17999998976 | bytes 40000000 | tf_op jit(solution)/shard_map/mlp/pallas_call | solution.py:749
  184.8 47.0 %mlp.3 = (bf16[1248,768]{1,0:T(8,128)(2,1)}, f32[1248,768]{1,0:T(8,128)}, bf16[1248,768]{1,0:T(8,128)(2,1)}, f32[8,768]{1,0:T(8,128)}, bf16[768,768]{1,0:T(8,128...) custom-call(f32[1248,768]{1,0:T(8,128)} %get-tuple-element.181.refs_, ...), custom_call_target="tpu_custom_call" | custom-call | flops 17999998976 | bytes 40000000 | tf_op jit(solution)/shard_map/mlp/pallas_call | solution.py:749
  232.9 36.8 %attention_backward.2 = (f32[7,208,768]{2,1,0:T(8,128)}, bf16[768,768]{1,0:T(8,128)(2,1)}, bf16[768,768]{1,0:T(8,128)(2,1)}, f32[8,384]{1,0:T(8,128)}, f32[128,128]{1,0:T(8,128)}) custom-call(bf16[1248,768]{1,0:T(8,128)(2,1)} %get-tuple-element.190.refs_0_, bf16[7,208,768]{2,1,0:T(8,128)(2,1)} %get-tuple-element.176.n1_in.refs_1_, ...), custom_call_target="tpu_custom_call" | custom-call | flops 25999998976 | bytes 40000000 | tf_op jit(solution)/shard_map/attention_backward/pallas_call | solution.py:867
  270.1 5.5 %collective-permute-start.9 = (bf16[768,768]{1,0:T(8,128)(2,1)S(1)}, bf16[768,768]{1,0:T(8,128)(2,1)}, u32[]{:S(2)}, u32[]{:S(2)}) collective-permute-start(bf16[768,768]{1,0:T(8,128)(2,1)S(1)} %add_convert_fusion.4), channel_id=1, source_target_pairs={{0,2},{2,0},{1,3},{3,1},{4,6},{6,4},{5,7},{7,5},{8,10},{10,8},{9,1... | collective-permute-start | bytes 3538952 | tf_op jit(solution)/shard_map/ppermute | solution.py:926
  275.6 1.6 add_convert_fusion.1
  278.1 41.2 %attention_backward.3 = (bf16[1248,768]{1,0:T(8,128)(2,1)}, f32[8,768]{1,0:T(8,128)}, bf16[768,768]{1,0:T(8,128)(2,1)}, bf16[768,768]{1,0:T(8,128)(2,1)}, f32[8,384]{1,0:T(8,128)}, /*index=5*/f32[128,128]{1,0:T(8,128)}) custom-call(bf16[1248,768]{1,0:T(8,128)(2,1)} %get-tuple-element.190.refs_0_, bf16[7,208,768]{2,1,0:T(8,128)(2,1)} %get-tuple-element.176.n1_in.refs_1_, ...), custom_call_target="tpu_custom_call" | custom-call | flops 25999998976 | bytes 40000000 | tf_op jit(solution)/shard_map/attention_backward/pallas_call | solution.py:867
  319.4 1.9 add_convert_fusion.7
  321.3 6.1 %collective-permute-start.6 = (bf16[768,768]{1,0:T(8,128)(2,1)S(1)}, bf16[768,768]{1,0:T(8,128)(2,1)}, u32[]{:S(2)}, u32[]{:S(2)}) collective-permute-start(bf16[768,768]{1,0:T(8,128)(2,1)S(1)} %add_convert_fusion.7), channel_id=1, source_target_pairs={{0,2},{2,0},{1,3},{3,1},{4,6},{6,4},{5,7},{7,5},{8,10},{10,8},{9,1... | collective-permute-start | bytes 3538952 | tf_op jit(solution)/shard_map/ppermute | solution.py:926
  327.5 6.9 %place_windows.3 = bf16[2176,768]{1,0:T(8,128)(2,1)} custom-call(bf16[1248,768]{1,0:T(8,128)(2,1)} %get-tuple-element.199.slab), custom_call_target="tpu_custom_call" | custom-call | flops 2000000000 | bytes 6000000 | tf_op jit(solution)/shard_map/place_windows/pallas_call | solution.py:905
  334.3 2.4 slice.351
  336.7 1.9 slice.350
  338.6 6.9 %place_windows.2 = bf16[2176,768]{1,0:T(8,128)(2,1)} custom-call(bf16[1248,768]{1,0:T(8,128)(2,1)} %get-tuple-element.189.slab), custom_call_target="tpu_custom_call" | custom-call | flops 2000000000 | bytes 6000000 | tf_op jit(solution)/shard_map/place_windows/pallas_call | solution.py:905
  345.5 2.4 slice.348
  347.9 1.9 slice.347
  354.6 2.6 collective-permute-start.3
  357.2 3.5 add_convert_fusion.3
  362.1 4.1 collective-permute-start.1
  366.1 3.2 fusion
  371.8 3.1 add_convert_fusion.6
  378.6 46.2 %all-reduce.6 = (f32[4,1152]{1,0:T(4,128)S(1)}, f32[6,768]{1,0:T(8,128)S(1)}, f32[2,27,64]{2,1,0:T(8,128)S(1)}) all-reduce(f32[4,1152]{1,0:T(4,128)S(1)} %gather_fusion.2, f32[6,768]{1,0:T(8,128)S(1)} %pad_maximum_fusion.2, f32[2,27,64]{2,1,0:T(8,128)S(1)} %pad_maximum_fusion.1), channel_id=1, replica_groups=mesh['dp'=8,'tensor'=4] {'dp','tensor'}, use_global_device_ids=true, to_apply=%region_2.0 | all-reduce | flops 12672 | bytes 101376 | tf_op jit(solution)/shard_map/psum | solution.py:1035
  428.6 2.3 collective-permute-start.15
  433.1 19.8 %pmax.7 = f32[3]{0:T(128)S(1)} all-reduce(f32[3]{0:T(128)S(1)} %maximum_maximum_fusion), channel_id=1, replica_groups=mesh['dp'=8,'tensor'=4] {'dp'}, use_global_device_ids=true, to_apply=%region_9.10 | all-reduce | flops 3 | bytes 24 | tf_op jit(solution)/shard_map/pmax | solution.py:1047
  454.1 2.9 pad_add_fusion
  457.0 2.8 pad_add_fusion.1
  459.8 57.6 %all-reduce.10.cloned.1.call-done = (bf16[768,768]{1,0:T(8,128)(2,1)}, bf16[768,768]{0,1:T(8,128)(2,1)}, bf16[768,768]{1,0:T(8,128)(2,1)}) async-done(((bf16[768,768]{1,0:T(8,128)(2,1)}, bf16[768,768]{0,1:T(8,128)(2,1)}, bf16[768,768]{1,0:T(8,128)(2,1)}), (bf16[768,768]{1,0:T(8,128)(2,1)}, bf16[768,768]{0,1:T(8,128)(2,1)}, bf16[768,768]{1,0:T(8,128)(2,1)})) %all-reduce.10.cloned.1.call-update) | async-done | bytes 3538960 | tf_op jit(solution)/shard_map/psum | solution.py:1023
  517.4 2.6 slice.352
  521.5 1.6 convert_element_type.119
  523.1 1.8 copy.46
  (142 shorter events, 37.8 us)
Async XLA Ops:
  7.2 510.2 %all-reduce.10.cloned.1.call-start = ((), (), s32[]{:S(2)}) async-start(), calls=%async_computation | async-start | bytes 7077888 | tf_op jit(solution)/shard_map/psum | solution.py:1023
  19.3 3.0 copy-start.14
  131.0 53.2 %copy-start.19 = (f32[768]{0:T(1024)S(1)}, f32[768]{0:T(1024)}, u32[]{:S(2)}) copy-start(f32[768]{0:T(1024)} %param.48) | copy-start | bytes 9220
  184.1 85.7 %collective-permute-start.8 = (bf16[768,768]{1,0:T(8,128)(2,1)}, bf16[768,768]{1,0:T(8,128)(2,1)S(1)}, u32[]{:S(2)}, u32[]{:S(2)}) collective-permute-start(bf16[768,768]{1,0:T(8,128)(2,1)} %get-tuple-element.213), channel_id=1, source_target_pairs={{0,1},{1,0},{2,3},{3,2},{4,5},{5,4},{6,7},{7,6},{8,9},{9,8},{10,11... | collective-permute-start | bytes 3538952 | tf_op jit(solution)/shard_map/ppermute | solution.py:926
  231.8 89.5 %collective-permute-start.7 = (bf16[768,768]{1,0:T(8,128)(2,1)}, bf16[768,768]{1,0:T(8,128)(2,1)}, u32[]{:S(2)}, u32[]{:S(2)}) collective-permute-start(bf16[768,768]{1,0:T(8,128)(2,1)} %get-tuple-element.211), channel_id=1, source_target_pairs={{0,1},{1,0},{2,3},{3,2},{4,5},{5,4},{6,7},{7,6},{8,9},{9,8},{10,11... | collective-permute-start | bytes 3538952 | tf_op jit(solution)/shard_map/ppermute | solution.py:926
  232.3 43.2 %collective-permute-start.11 = (bf16[768,768]{1,0:T(8,128)(2,1)}, bf16[768,768]{1,0:T(8,128)(2,1)}, u32[]{:S(2)}, u32[]{:S(2)}) collective-permute-start(bf16[768,768]{1,0:T(8,128)(2,1)} %get-tuple-element.217), channel_id=1, source_target_pairs={{0,1},{1,0},{2,3},{3,2},{4,5},{5,4},{6,7},{7,6},{8,9},{9,8},{10,11... | collective-permute-start | bytes 3538952 | tf_op jit(solution)/shard_map/ppermute | solution.py:926
  232.4 128.3 %collective-permute-start.10 = (bf16[768,768]{1,0:T(8,128)(2,1)}, bf16[768,768]{1,0:T(8,128)(2,1)}, u32[]{:S(2)}, u32[]{:S(2)}) collective-permute-start(bf16[768,768]{1,0:T(8,128)(2,1)} %get-tuple-element.215), channel_id=1, source_target_pairs={{0,1},{1,0},{2,3},{3,2},{4,5},{5,4},{6,7},{7,6},{8,9},{9,8},{10,11... | collective-permute-start | bytes 3538952 | tf_op jit(solution)/shard_map/ppermute | solution.py:926
  232.9 36.9 %copy-start.5 = (bf16[768,768]{1,0:T(8,128)(2,1)S(1)}, bf16[768,768]{1,0:T(8,128)(2,1)}, u32[]{:S(2)}) copy-start(bf16[768,768]{1,0:T(8,128)(2,1)} %get-tuple-element.212) | copy-start | bytes 3538948
  269.6 49.7 %collective-permute-start.5 = (bf16[768,768]{1,0:T(8,128)(2,1)}, bf16[768,768]{1,0:T(8,128)(2,1)}, u32[]{:S(2)}, u32[]{:S(2)}) collective-permute-start(bf16[768,768]{1,0:T(8,128)(2,1)} %get-tuple-element.203), channel_id=1, source_target_pairs={{0,1},{1,0},{2,3},{3,2},{4,5},{5,4},{6,7},{7,6},{8,9},{9,8},{10,11... | collective-permute-start | bytes 3538952 | tf_op jit(solution)/shard_map/ppermute | solution.py:926
  269.8 5.8 %copy-start.4 = (bf16[768,768]{1,0:T(8,128)(2,1)S(1)}, bf16[768,768]{1,0:T(8,128)(2,1)}, u32[]{:S(2)}) copy-start(bf16[768,768]{1,0:T(8,128)(2,1)} %get-tuple-element.216) | copy-start | bytes 3538948
  270.1 84.5 %collective-permute-start.9 = (bf16[768,768]{1,0:T(8,128)(2,1)S(1)}, bf16[768,768]{1,0:T(8,128)(2,1)}, u32[]{:S(2)}, u32[]{:S(2)}) collective-permute-start(bf16[768,768]{1,0:T(8,128)(2,1)S(1)} %add_convert_fusion.4), channel_id=1, source_target_pairs={{0,2},{2,0},{1,3},{3,1},{4,6},{6,4},{5,7},{7,5},{8,10},{10,8},{9,1... | collective-permute-start | bytes 3538952 | tf_op jit(solution)/shard_map/ppermute | solution.py:926
  277.2 84.9 %collective-permute-start.12 = (bf16[768,768]{1,0:T(8,128)(2,1)S(1)}, bf16[768,768]{1,0:T(8,128)(2,1)}, u32[]{:S(2)}, u32[]{:S(2)}) collective-permute-start(bf16[768,768]{1,0:T(8,128)(2,1)S(1)} %add_convert_fusion.1), channel_id=1, source_target_pairs={{0,2},{2,0},{1,3},{3,1},{4,6},{6,4},{5,7},{7,5},{8,10},{10,8},{9,1... | collective-permute-start | bytes 3538952 | tf_op jit(solution)/shard_map/ppermute | solution.py:926
  319.3 50.0 %collective-permute-start.4 = (bf16[768,768]{1,0:T(8,128)(2,1)}, bf16[768,768]{1,0:T(8,128)(2,1)}, u32[]{:S(2)}, u32[]{:S(2)}) collective-permute-start(bf16[768,768]{1,0:T(8,128)(2,1)} %get-tuple-element.201), channel_id=1, source_target_pairs={{0,1},{1,0},{2,3},{3,2},{4,5},{5,4},{6,7},{7,6},{8,9},{9,8},{10,11... | collective-permute-start | bytes 3538952 | tf_op jit(solution)/shard_map/ppermute | solution.py:926
  321.3 49.3 %collective-permute-start.6 = (bf16[768,768]{1,0:T(8,128)(2,1)S(1)}, bf16[768,768]{1,0:T(8,128)(2,1)}, u32[]{:S(2)}, u32[]{:S(2)}) collective-permute-start(bf16[768,768]{1,0:T(8,128)(2,1)S(1)} %add_convert_fusion.7), channel_id=1, source_target_pairs={{0,2},{2,0},{1,3},{3,1},{4,6},{6,4},{5,7},{7,5},{8,10},{10,8},{9,1... | collective-permute-start | bytes 3538952 | tf_op jit(solution)/shard_map/ppermute | solution.py:926
  347.9 3.3 copy-start.18
  347.9 4.7 copy-start.10
  354.6 99.5 %collective-permute-start.3 = (bf16[12,64,768]{2,1,0:T(8,128)(2,1)}, bf16[12,64,768]{2,1,0:T(8,128)(2,1)}, u32[]{:S(2)}, u32[]{:S(2)}) collective-permute-start(bf16[12,64,768]{2,1,0:T(8,128)(2,1)} %bitcast.43), channel_id=1, source_target_pairs={{0,1},{1,2},{2,3},{4,5},{5,6},{6,7},{8,9},{9,10},{10,11},{12,13},{... | collective-permute-start | bytes 3538952 | tf_op jit(solution)/shard_map/ppermute | solution.py:937
  357.2 8.9 %copy-start.6 = (bf16[768,768]{1,0:T(8,128)(2,1)S(1)}, bf16[768,768]{1,0:T(8,128)(2,1)}, u32[]{:S(2)}) copy-start(bf16[768,768]{1,0:T(8,128)(2,1)} %get-tuple-element.214) | copy-start | bytes 3538948
  360.8 93.3 %collective-permute-start.2 = (bf16[6,64,768]{2,1,0:T(8,128)(2,1)}, bf16[6,64,768]{2,1,0:T(8,128)(2,1)}, u32[]{:S(2)}, u32[]{:S(2)}) collective-permute-start(bf16[6,64,768]{2,1,0:T(8,128)(2,1)} %bitcast.15), channel_id=1, source_target_pairs={{1,0},{2,1},{3,2},{5,4},{6,5},{7,6},{9,8},{10,9},{11,10},{13,12},{... | collective-permute-start | bytes 1769480 | tf_op jit(solution)/shard_map/ppermute | solution.py:936
  362.1 94.9 %collective-permute-start.1 = (bf16[12,64,768]{2,1,0:T(8,128)(2,1)}, bf16[12,64,768]{2,1,0:T(8,128)(2,1)}, u32[]{:S(2)}, u32[]{:S(2)}) collective-permute-start(bf16[12,64,768]{2,1,0:T(8,128)(2,1)} %bitcast.12), channel_id=1, source_target_pairs={{0,1},{1,2},{2,3},{4,5},{5,6},{6,7},{8,9},{9,10},{10,11},{12,13},{... | collective-permute-start | bytes 3538952 | tf_op jit(solution)/shard_map/ppermute | solution.py:937
  366.1 5.7 %copy-start.7 = (bf16[768,768]{1,0:T(8,128)(2,1)S(1)}, bf16[768,768]{1,0:T(8,128)(2,1)}, u32[]{:S(2)}) copy-start(bf16[768,768]{1,0:T(8,128)(2,1)} %get-tuple-element.200) | copy-start | bytes 3538948
  369.3 87.7 %collective-permute-start = (bf16[6,64,768]{2,1,0:T(8,128)(2,1)}, bf16[6,64,768]{2,1,0:T(8,128)(2,1)}, u32[]{:S(2)}, u32[]{:S(2)}) collective-permute-start(bf16[6,64,768]{2,1,0:T(8,128)(2,1)} %bitcast.11), channel_id=1, source_target_pairs={{1,0},{2,1},{3,2},{5,4},{6,5},{7,6},{9,8},{10,9},{11,10},{13,12},{... | collective-permute-start | bytes 1769480 | tf_op jit(solution)/shard_map/ppermute | solution.py:936
  370.6 56.9 %collective-permute-start.14 = (f32[3]{0:T(128)}, f32[3]{0:T(128)S(1)}, u32[]{:S(2)}, u32[]{:S(2)}) collective-permute-start(f32[3]{0:T(128)} %slice.339), channel_id=1, source_target_pairs={{0,1},{1,0},{2,3},{3,2},{4,5},{5,4},{6,7},{7,6},{8,9},{9,8},{10,11... | collective-permute-start | bytes 44 | tf_op jit(solution)/shard_map/ppermute | solution.py:1042
  374.9 2.2 copy-start.15
  377.9 48.1 %copy-start.17 = (f32[8,208]{1,0:T(8,128)S(1)}, f32[8,208]{1,0:T(8,128)}, u32[]{:S(2)}) copy-start(f32[8,208]{1,0:T(8,128)} %get-tuple-element.220) | copy-start | bytes 19972
  377.9 75.1 %copy-start.1 = (bf16[3,768,192]{1,2,0:T(8,128)(2,1)S(1)}, bf16[3,768,192]{1,2,0:T(8,128)(2,1)}, u32[]{:S(2)}) copy-start(bf16[3,768,192]{1,2,0:T(8,128)(2,1)} %param.41) | copy-start | bytes 2654212
  377.9 76.1 %slice-start.1 = ((bf16[2176,768]{1,0:T(8,128)(2,1)}), bf16[1024,768]{1,0:T(8,128)(2,1)S(1)}, s32[]{:S(2)}) async-start(bf16[2176,768]{1,0:T(8,128)(2,1)} %place_windows.3), calls=%async_computation.2 | async-start | bytes 3145728 | tf_op jit(solution)/shard_map/slice | solution.py:938
  427.5 1.1 collective-permute-start.13
  428.6 3.8 collective-permute-start.15
  452.9 4.1 copy-start.20
  454.1 2.9 slice-start
  517.4 2.6 copy-start
  (8 other events, 12.2 us)
Sparse Core Ops, SparseCore 0:
  375.1 142.2 all-reduce.9

commit v3 on v2

--- a/solution.py
+++ b/solution.py
@@ -156,6 +156,113 @@
 
     def local(self, at, source, target):
         return pltpu.make_async_copy(source, target, self.locals.at[at])
+
+
+def mate_of(image, bit):
+    unit = 1 << bit
+    return image + unit * (1 - 2 * ((image // unit) % 2))
+
+
+def rows_at(start, count):
+    return pl.ds(pl.multiple_of(start, 16), count)
+
+
+def add_rows(target, target_at, sources, count):
+    chunk = 48 if count % 48 == 0 else 16
+
+    @pl.loop(0, count // chunk)
+    def _(c):
+        total = None
+        for ref, at in sources:
+            value = ref[rows_at(at + c * chunk, chunk), :].astype(single)
+            total = value if total is None else total + value
+        target[rows_at(target_at + c * chunk, chunk), :] = total.astype(target.dtype)
+
+
+HALVINGS = 3
+
+
+class Reducer:
+    def __init__(self, send, base, image, images, rows):
+        bits = images.bit_length() - 1
+        assert images == 1 << bits and bits >= HALVINGS
+        self.send, self.base, self.image = send, base, image
+        self.extra_bits = range(HALVINGS, bits)
+        self.stages = [[] for _ in range(HALVINGS)]
+        self.final = []
+        landing = 0
+        for start, order in ((0, (0, 1, 2)), (rows // 2, (1, 0, 2))):
+            length = rows // 2
+            for stage, bit in enumerate(order):
+                length //= 2
+                mine = (image // (1 << bit)) % 2
+                keep = start + mine * length
+                give = start + (1 - mine) * length
+                self.stages[stage].append((mate_of(image, bit), keep, give, length, landing))
+                landing += length
+                start = keep
+            self.final.append((start, length))
+        self.extra_landing = []
+        for _ in self.extra_bits:
+            for _, length in self.final:
+                self.extra_landing.append(landing)
+                landing += length
+        self.landing_rows = landing
+        self.copies = 2 * HALVINGS + len(self.extra_landing)
+        self.mates = [{"dp": mate_of(image, bit)} for bit in range(bits)]
+
+    def out(self, stage, held, landing):
+        copies = []
+        for part, (mate, _, give, length, at) in enumerate(self.stages[stage]):
+            copies.append(
+                self.send.remote(
+                    self.base + 2 * stage + part,
+                    held.at[rows_at(give, length), :],
+                    landing.at[pl.ds(at, length), :],
+                    {"dp": mate},
+                )
+            )
+        return copies
+
+    def start(self, stage, held, landing):
+        for copy in self.out(stage, held, landing):
+            copy.start()
+
+    def finish(self, stage, held, landing):
+        for copy in self.out(stage, held, landing):
+            copy.wait()
+        for _, keep, _, length, at in self.stages[stage]:
+            add_rows(held, keep, [(held, keep), (landing, at)], length)
+
+    def extras(self, held, landing):
+        for k, bit in enumerate(self.extra_bits):
+            copies = []
+            for part, (start, length) in enumerate(self.final):
+                at = 2 * k + part
+                copies.append(
+                    self.send.remote(
+                        self.base + 2 * HALVINGS + at,
+                        held.at[rows_at(start, length), :],
+                        landing.at[pl.ds(self.extra_landing[at], length), :],
+                        {"dp": mate_of(self.image, bit)},
+                    )
+                )
+            for copy in copies:
+                copy.start()
+            for copy in copies:
+                copy.wait()
+            for part, (start, length) in enumerate(self.final):
+                at = self.extra_landing[2 * k + part]
+                add_rows(held, start, [(held, start), (landing, at)], length)
+
+    def back(self, base, stage, held):
+        copies = []
+        for part, (mate, keep, _, length, _) in enumerate(self.stages[stage]):
+            cut = rows_at(keep, length)
+            copies.append(
+                self.send.remote(base + 2 * stage + part, held.at[cut, :], held.at[cut, :], {"dp": mate})
+            )
+        return copies
 
 
 def attend(n1, valid, weights, qbias, vbias, wrel, bits, lanes, sides, keys, qkv, mixed, peak):
@@ -550,16 +657,26 @@
         (corner1, corner2, sends, recvs, w1, w2, b1, hs, zs) = refs[23:]
         kinds = (2, 3)
     else:
-        (x1, n2, n2t, gs, gt, branch0, dn20, fbias, gain, smalls, w1a, w1b, w2a, w2b) = refs[:14]
-        (out, dx1, da, sums, gw1a, gw1b, gw2a, gw2b, gb) = refs[14:23]
-        (branch, dn2, w1, w2, b1, hs, zs) = refs[23:]
+        (x1, n2, n2t, gs, gt, branch0, dn20, fbias, gain, smalls, keep1, keep2) = refs[:12]
+        (give1, give2, w1a, w1b, w2a, w2b) = refs[12:18]
+        (out, dx1, da, sums, far1, far2, gw1a, gw1b, gw2a, gw2b, gb) = refs[18:29]
+        (branch, dn2, got1, got2, sends, recvs, w1, w2, b1, hs, zs) = refs[29:]
         kinds = (0, 1)
     step = pl.program_id(0)
     count = pl.num_programs(0) // 2
     rows, width = gs.shape
+    beside, across, _ = partners(lax.axis_index("tensor"))
+    send = Sender(sends, recvs, None)
+    if not first:
+        swaps = [
+            send.remote(0, give1, got1, {"tensor": beside}),
+            send.remote(1, give2, got2, {"tensor": beside}),
+        ]
+        crossings = [
+            send.remote(2, got1, far1, {"tensor": across}),
+            send.remote(3, got2, far2, {"tensor": across}),
+        ]
     if first:
-        beside, _, _ = partners(lax.axis_index("tensor"))
-        send = Sender(sends, recvs, None)
         corners = [
             send.remote(0, src1, corner1, {"tensor": beside}),
             send.remote(1, src2, corner2, {"tensor": beside}),
@@ -588,6 +705,9 @@
                 n2t[cut, :] = n2[:, cut].T
                 gt[cut, :] = gs[:, cut].T
         else:
+            greet([{"tensor": beside}, {"tensor": across}])
+            for copy in swaps:
+                copy.start()
 
             @pl.loop(0, SLAB // ROWS)
             def _(c):
@@ -636,6 +756,17 @@
         branch[sl, :] += dot(h, w2[...])
         dn2[sl, :] += dot_nt(dz, w1[...])
 
+    if not first:
+
+        @pl.when(step == 0)
+        def _():
+            for copy, got, keep, crossing in zip(
+                swaps, (got1, got2), (keep1, keep2), crossings, strict=True
+            ):
+                copy.wait()
+                add_rows(got, 0, [(got, 0), (keep, 0)], got.shape[0])
+                crossing.start()
+
     def store(gw1, gw2):
         @pl.loop(0, width // 256)
         def _(r):
@@ -655,6 +786,8 @@
 
         @pl.when(step == 2 * count - 1)
         def _():
+            for copy in crossings:
+                copy.wait()
             sums[...] = jnp.zeros_like(sums)
 
             @pl.loop(0, SLAB // ROWS)
@@ -675,7 +808,7 @@
                 sums[3:4, :] += jnp.sum(cot, axis=0, keepdims=True)
 
 
-def mlp_half(first, residents, w1a, w1b, w2a, w2b):
+def mlp_half(first, residents, gives, w1a, w1b, w2a, w2b):
     width, local = w1a.shape
     count = local // BLOCK
 
@@ -717,8 +850,10 @@
             vmem_limit_bytes=VMEM, collective_id=2, has_side_effects=True
         )
     else:
-        operands = (*residents, w1a, w1b, w2a, w2b)
+        operands = (*residents, *gives, w1a, w1b, w2a, w2b)
         in_specs += [
+            ANY,
+            ANY,
             early((width, BLOCK), 1),
             late((width, BLOCK), 1),
             early((BLOCK, width), 0),
@@ -729,9 +864,20 @@
             (of(slab, single), whole(slab)),
             (of(slab), whole(slab)),
             (of((8, width), single), whole((8, width))),
+            (of((width, local)), ANY),
+            (of((width, local)), ANY),
         ]
-        scratch = [pltpu.VMEM(slab, single), pltpu.VMEM(slab, single)]
-        params = pltpu.CompilerParams(vmem_limit_bytes=VMEM)
+        scratch = [
+            pltpu.VMEM(slab, single),
+            pltpu.VMEM(slab, single),
+            pltpu.VMEM((width, local), narrow),
+            pltpu.VMEM((width, local), narrow),
+            pltpu.SemaphoreType.DMA((4,)),
+            pltpu.SemaphoreType.DMA((4,)),
+        ]
+        params = pltpu.CompilerParams(
+            vmem_limit_bytes=VMEM, collective_id=3, has_side_effects=True
+        )
     outs += [
         (of((width, local)), early((width, BLOCK), 1)),
         (of((width, local)), late((width, BLOCK), 1)),
@@ -761,13 +907,86 @@
     )(*operands)
 
 
-def backward_kernel(first, rows_held, *refs):
+def backward_kernel(first, rows_held, images, *refs):
     (da, n1, qkv, mixed, weights, wrel, bits, lanes, sides, keys) = refs[:10]
     if first:
-        (dn1, keep, give, bias, grel, acc, dqkv) = refs[10:]
+        (keep1, keep2, far1, far2, give1, give2) = refs[10:16]
+        (dn1, keep, give, bias, grel, reduced, acc, dqkv) = refs[16:24]
+        (got, total_fc, landing, sends, recvs) = refs[24:]
+        fc_rows = 2 * keep1.shape[0]
     else:
-        (prior, xs, dx1, gain) = refs[10:14]
-        (back, sums, keep, give, bias, grel, acc, dqkv) = refs[14:]
+        (prior, xs, dx1, gain, keep_far, give_far, reduced) = refs[10:17]
+        (back, sums, keep, give, bias, grel, cross, summed, acc, dqkv) = refs[17:27]
+        (got, sends, recvs, locals_) = refs[27:]
+        fc_rows = summed.shape[0]
+    step = pl.program_id(0)
+    image = lax.axis_index("dp")
+    beside, across, _ = partners(lax.axis_index("tensor"))
+    send = Sender(sends, recvs, None if first else locals_)
+    reducer = Reducer(send, 2, image, images, fc_rows)
+    if first:
+        swaps = [
+            send.remote(k, g, got.at[pl.ds(k * fc_rows // 2, fc_rows // 2), :], {"tensor": beside})
+            for k, g in enumerate((give1, give2))
+        ]
+
+        @pl.when(step == 0)
+        def _():
+            greet([{"tensor": beside}] + reducer.mates)
+            for copy in swaps:
+                copy.start()
+
+        @pl.when(step == 1)
+        def _():
+            part = fc_rows // 2
+            for k, (mine, crossed) in enumerate(((keep1, far1), (keep2, far2))):
+                swaps[k].wait()
+                add_rows(
+                    total_fc, k * part, [(mine, 0), (got, k * part), (crossed, 0)], part
+                )
+            reducer.start(0, total_fc, landing)
+
+        for stage, at in ((0, 4), (1, 5)):
+
+            @pl.when(step == at)
+            def _():
+                reducer.finish(stage, total_fc, landing)
+                reducer.start(stage + 1, total_fc, landing)
+
+    else:
+        swap_far = send.remote(0, give_far, got, {"tensor": beside})
+        crossing = send.remote(1, got, cross, {"tensor": across})
+
+        @pl.when(step == 0)
+        def _():
+            greet([{"tensor": beside}, {"tensor": across}] + reducer.mates)
+            swap_far.start()
+            seeds = [
+                send.local(k, reduced.at[k], summed.at[rows_at(start, length), :])
+                for k, (start, length) in enumerate(reducer.final)
+            ]
+            for copy in seeds:
+                copy.start()
+            for copy in seeds:
+                copy.wait()
+            for copy in reducer.back(2, 2, summed):
+                copy.start()
+
+        @pl.when(step == 1)
+        def _():
+            swap_far.wait()
+            add_rows(got, 0, [(got, 0), (keep_far, 0)], got.shape[0])
+            crossing.start()
+
+        for stage, at in ((1, 3), (0, 5)):
+
+            @pl.when(step == at)
+            def _():
+                for copy in reducer.back(2, stage + 1, summed):
+                    copy.wait()
+                for copy in reducer.back(2, stage, summed):
+                    copy.start()
+
     _, col0, high, wide, offset, live = slot_fields(rows_held)
     half, width = weights.shape[1:]
 
@@ -839,33 +1058,64 @@
         for j in range(4):
             keep[j * part : (j + 1) * part, :] = acc[j, :part, :].astype(narrow)
             give[j * part : (j + 1) * part, :] = acc[j, part:, :].astype(narrow)
-
-
-def backward_half(rows_held, da, n1, qkv, mixed, weights, wrel, tables, final):
-    first = final is None
+        if first:
+            reducer.finish(2, total_fc, landing)
+            reducer.extras(total_fc, landing)
+            for k, (start, length) in enumerate(reducer.final):
+                reduced[k] = total_fc[rows_at(start, length), :]
+        else:
+            for copy in reducer.back(2, 0, summed):
+                copy.wait()
+            crossing.wait()
+
+
+def backward_half(first, rows_held, images, da, n1, qkv, mixed, weights, wrel, tables, final):
     half, width = weights.shape[1:]
     operands = [da, n1, qkv, mixed, weights, wrel, *tables]
     in_specs = [whole(a.shape) for a in operands]
     for at in (1, 2, 3):
         in_specs[at] = by_slot(operands[at].shape[1:])
+    extra_bits = images.bit_length() - 1 - HALVINGS
+    operands += final
     if first:
+        fc_rows = 2 * final[0].shape[0]
+        last = fc_rows >> (HALVINGS + 1)
+        in_specs += [whole(a.shape) for a in final[:4]] + [ANY, ANY]
         outs = [(of((SLOTS, ROWS, width), single), by_slot((ROWS, width)))]
+        more = [(of((2, last, width)), whole((2, last, width)))]
+        landing = fc_rows - 2 * last + 2 * last * extra_bits
+        copies = 2 + 2 * HALVINGS + 2 * extra_bits
+        scratch = [
+            pltpu.VMEM((fc_rows, width), narrow),
+            pltpu.VMEM((fc_rows, width), narrow),
+            pltpu.VMEM((landing, width), narrow),
+            pltpu.SemaphoreType.DMA((copies,)),
+            pltpu.SemaphoreType.DMA((copies,)),
+        ]
     else:
-        prior, xs, dx1, gain = final
-        operands += [prior, xs, dx1, gain]
+        prior, xs, dx1, gain, keep_far, give_far, reduced = final
+        fc_rows = reduced.shape[1] << (HALVINGS + 1)
         in_specs += [by_slot((ROWS, width)), whole(xs.shape), whole(dx1.shape), whole(gain.shape)]
+        in_specs += [whole(keep_far.shape), ANY, ANY]
         outs = [
             (of((SLAB, width)), whole((SLAB, width))),
             (of((8, width), single), whole((8, width))),
+        ]
+        more = [(of(keep_far.shape), ANY), (of((fc_rows, width)), ANY)]
+        scratch = [
+            pltpu.VMEM(keep_far.shape, narrow),
+            pltpu.SemaphoreType.DMA((2 + 2 * HALVINGS,)),
+            pltpu.SemaphoreType.DMA((2 + 2 * HALVINGS,)),
+            pltpu.SemaphoreType.DMA((2,)),
         ]
     outs += [
         (of((2 * half, width)), whole((2 * half, width))),
         (of((2 * half, width)), whole((2 * half, width))),
         (of((8, half), single), whole((8, half))),
         (of((LANES, LANES), single), whole((LANES, LANES))),
-    ]
+    ] + more
     return pl.pallas_call(
-        functools.partial(backward_kernel, first, rows_held),
+        functools.partial(backward_kernel, first, rows_held, images),
         out_shape=[o[0] for o in outs],
         grid=(SLOTS,),
         in_specs=in_specs,
@@ -873,8 +1123,11 @@
         scratch_shapes=[
             pltpu.VMEM((4, half, width), single),
             pltpu.VMEM((3, ROWS, half), narrow),
+            *scratch,
         ],
-        compiler_params=pltpu.CompilerParams(vmem_limit_bytes=VMEM),
+        compiler_params=pltpu.CompilerParams(
+            vmem_limit_bytes=VMEM, collective_id=4 if first else 5, has_side_effects=True
+        ),
         cost_estimate=pl.CostEstimate(
             flops=26_000_000_000, bytes_accessed=40_000_000, transcendentals=4_000_000
         ),
@@ -882,63 +1135,208 @@
     )(*operands)
 
 
-def place_kernel(rows_held, slab, ext):
-    row0, col0, high, wide, offset, live = slot_fields(rows_held)
-
-    @pl.when(pl.program_id(0) == 0)
-    def _():
-        ext[...] = jnp.zeros_like(ext)
-
-    @pl.when(live)
-    def _():
-        target, _ = positions(1, col0, high, wide)
-        token = lax.broadcasted_iota(jnp.int32, (WIN * GRID, ROWS), 0)
-        choose = jnp.where(token == target, 1.0, 0.0).astype(narrow)
-        window = slab[pl.ds(pl.multiple_of(offset, 16), ROWS), :]
-        where_to = pl.ds(pl.multiple_of(row0 * GRID, GRID), WIN * GRID)
-        ext[where_to, :] += dot(choose, window).astype(narrow)
-
-
-def place_windows(rows_held, slab):
-    width = slab.shape[1]
-    tokens = (rows_held + LEFT + RIGHT) * GRID
+def place_windows(rows_held, device, slab, ext):
+    @pl.loop(0, ext.shape[0] // GRID)
+    def _(r):
+        ext[rows_at(r * GRID, GRID), :] = jnp.zeros((GRID, ext.shape[1]), narrow)
+
+    @pl.loop(0, SLOTS)
+    def _(slot):
+        row0, col0, high, wide, offset, live = window_fields(rows_held, device, slot)
+
+        @pl.when(live)
+        def _():
+            target, _ = positions(1, col0, high, wide)
+            token = lax.broadcasted_iota(jnp.int32, (WIN * GRID, ROWS), 0)
+            choose = jnp.where(token == target, 1.0, 0.0).astype(narrow)
+            window = slab[rows_at(offset, ROWS), :]
+            where_to = pl.ds(pl.multiple_of(row0 * GRID, GRID), WIN * GRID)
+            ext[where_to, :] += dot(choose, window).astype(narrow)
+
+
+def tail_kernel(
+    rows_held, images,
+    out, back, keep, crossed, sums1, sums2, bias0, bias1, rel0, rel1, fb0, fb1, peak0, peak1, give,
+    output, input_grad, packed, totals, tops,
+    ext0, ext1, below0, below1, above0, above1, got, landing, held, sum_land, top_land, sends, recvs,
+):
+    device, image = lax.axis_index("tensor"), lax.axis_index("dp")
+    width = out.shape[1]
+    beside, across, corner = partners(device)
+    send = Sender(sends, recvs, None)
+    reducer = Reducer(send, 1, image, images, held.shape[0])
+    back_base = 1 + reducer.copies
+    halo_base = back_base + 2 * HALVINGS
+    small_base = halo_base + 4
+    tokens = rows_held * GRID
+    top, bottom = LEFT * GRID, RIGHT * GRID
+    held_by = (device, beside, across, corner)
+    ring = [{"tensor": beside}, {"tensor": across}] + reducer.mates
+
+    greet([{"tensor": place} for place in (beside, across, corner)] + reducer.mates)
+    swap = send.remote(0, give, got, {"tensor": beside})
+    swap.start()
+
+    totals[...] = jnp.zeros_like(totals)
+    tops[...] = jnp.zeros_like(tops)
+    totals[0:2, :] = sums1[0:2, :]
+    totals[2:6, :] = sums2[0:4, :]
+    rel = rel0[...] + rel1[...]
+    rel = rel[HD:] + pltpu.roll(rel[:HD], HD, 1)
+    for g in range(HD // 8):
+        at = 8 * (1 + g // 6)
+        totals[at : at + 8, (g % 6) * LANES : (g % 6 + 1) * LANES] = rel[8 * g : 8 * g + 8]
+    half = bias0.shape[1]
+    for k, (fb, bias, peak) in enumerate(
+        ((fb0, bias0, peak0), (fb0, bias0, peak0), (fb1, bias1, peak1), (fb1, bias1, peak1))
+    ):
+        odd = k % 2
+        totals[pl.ds(24 + held_by[k], 1), :] = fb[odd, 0:1, :]
+        for j, row in enumerate((0, 2)):
+            value = bias[row : row + 1, :]
+            if odd:
+                value = pltpu.roll(value, half // 2, 1)
+            totals[pl.ds(28 + held_by[k], 1), j * half : (j + 1) * half] = value
+        best = jnp.broadcast_to(jnp.max(peak[...], axis=1, keepdims=True), (8, LANES))
+        if odd:
+            best = pltpu.roll(best, 8 - half // LANES, 0)
+        tops[pl.ds(pl.multiple_of(held_by[k] * 8, 8), 8), :] = best
+
+    def small_copies(k):
+        return [
+            send.remote(small_base + 2 * k, totals, sum_land.at[k], ring[k]),
+            send.remote(small_base + 2 * k + 1, tops, top_land.at[k], ring[k]),
+        ]
+
+    def small_start(k):
+        for copy in small_copies(k):
+            copy.start()
+
+    def small_finish(k):
+        for copy in small_copies(k):
+            copy.wait()
+        totals[...] += sum_land[k]
+        tops[...] = jnp.maximum(tops[...], top_land[k])
+
+    def halo(base, ext, below, above):
+        up = send.remote(
+            base, ext.at[pl.ds(0, top), :], below, {"tensor": (device + SPLIT - 1) % SPLIT}
+        )
+        down = send.remote(
+            base + 1, ext.at[pl.ds(top + tokens, bottom), :], above, {"tensor": (device + 1) % SPLIT}
+        )
+        return up, down
+
+    def halo_start(copies):
+        up, down = copies
+        pl.when(device > 0)(up.start)
+        pl.when(device < SPLIT - 1)(down.start)
+
+    def halo_finish(copies, ext, below, above, result):
+        up, down = copies
+        pl.when(device > 0)(up.wait_send)
+        pl.when(device < SPLIT - 1)(down.wait_send)
+        add_rows(result, 0, [(ext, top)], tokens)
+
+        @pl.when(device < SPLIT - 1)
+        def _():
+            up.wait_recv()
+            at = tokens - top
+            add_rows(result, at, [(result, at), (below, 0)], top)
+
+        @pl.when(device > 0)
+        def _():
+            down.wait_recv()
+            add_rows(result, 0, [(result, 0), (above, 0)], bottom)
+
+    small_start(0)
+    place_windows(rows_held, device, back, ext1)
+    halos1 = halo(halo_base, ext1, below1, above1)
+    halo_start(halos1)
+    swap.wait()
+    add_rows(held, 0, [(keep, 0), (got, 0), (crossed, 0)], held.shape[0])
+    reducer.start(0, held, landing)
+    small_finish(0)
+    small_start(1)
+    place_windows(rows_held, device, out, ext0)
+    halos0 = halo(halo_base + 2, ext0, below0, above0)
+    halo_start(halos0)
+    small_finish(1)
+    small_start(2)
+    reducer.finish(0, held, landing)
+    reducer.start(1, held, landing)
+    small_finish(2)
+    small_start(3)
+    reducer.finish(1, held, landing)
+    reducer.start(2, held, landing)
+    small_finish(3)
+    small_start(4)
+    reducer.finish(2, held, landing)
+    reducer.extras(held, landing)
+    for start, length in reducer.final:
+        packed[rows_at(start, length), :] = held[rows_at(start, length), :]
+    stages = [reducer.back(back_base, stage, packed) for stage in range(HALVINGS)]
+    for copy in stages[2]:
+        copy.start()
+    for k in range(4, len(ring)):
+        small_finish(k)
+        if k + 1 < len(ring):
+            small_start(k + 1)
+    for copy in stages[2]:
+        copy.wait()
+    for copy in stages[1]:
+        copy.start()
+    halo_finish(halos1, ext1, below1, above1, input_grad)
+    for copy in stages[1]:
+        copy.wait()
+    for copy in stages[0]:
+        copy.start()
+    halo_finish(halos0, ext0, below0, above0, output)
+    for copy in stages[0]:
+        copy.wait()
+
+
+def tail(rows_held, images, *operands):
+    width = operands[0].shape[1]
+    packed = operands[2].shape
+    tokens = rows_held * GRID
+    bits = images.bit_length() - 1
+    extra = bits - HALVINGS
+    last = packed[0] >> (HALVINGS + 1)
+    copies = 1 + 4 * HALVINGS + 2 * extra + 4 + 2 * (2 + bits)
+    ext = ((rows_held + LEFT + RIGHT) * GRID, width)
+    outs = [
+        of((tokens, width)), of((tokens, width)), of(packed),
+        of((32, width), single), of((32, LANES), single),
+    ]
     return pl.pallas_call(
-        functools.partial(place_kernel, rows_held),
-        out_shape=of((tokens, width)),
-        grid=(SLOTS,),
-        in_specs=[whole(slab.shape)],
-        out_specs=whole((tokens, width)),
-        compiler_params=pltpu.CompilerParams(vmem_limit_bytes=VMEM),
+        functools.partial(tail_kernel, rows_held, images),
+        out_shape=outs,
+        in_specs=[pl.BlockSpec(memory_space=pltpu.VMEM)] * (len(operands) - 1) + [ANY],
+        out_specs=[pl.BlockSpec(memory_space=pltpu.VMEM)] * len(outs),
+        scratch_shapes=[
+            pltpu.VMEM(ext, narrow),
+            pltpu.VMEM(ext, narrow),
+            pltpu.VMEM((LEFT * GRID, width), narrow),
+            pltpu.VMEM((LEFT * GRID, width), narrow),
+            pltpu.VMEM((RIGHT * GRID, width), narrow),
+            pltpu.VMEM((RIGHT * GRID, width), narrow),
+            pltpu.VMEM(packed, narrow),
+            pltpu.VMEM((packed[0] - 2 * last + 2 * last * extra, width), narrow),
+            pltpu.VMEM(packed, narrow),
+            pltpu.VMEM((2 + bits, 32, width), single),
+            pltpu.VMEM((2 + bits, 32, LANES), single),
+            pltpu.SemaphoreType.DMA((copies,)),
+            pltpu.SemaphoreType.DMA((copies,)),
+        ],
+        compiler_params=pltpu.CompilerParams(
+            vmem_limit_bytes=VMEM, collective_id=6, has_side_effects=True
+        ),
         cost_estimate=pl.CostEstimate(
-            flops=2_000_000_000, bytes_accessed=6_000_000, transcendentals=0
+            flops=4_000_000_000, bytes_accessed=20_000_000, transcendentals=0
         ),
-        name="place_windows",
-    )(slab)
-
-
-CORE_SWAP = ((0, 1), (1, 0), (2, 3), (3, 2))
-CHIP_SWAP = ((0, 2), (2, 0), (1, 3), (3, 1))
-UP = ((0, 1), (1, 2), (2, 3))
-DOWN = ((1, 0), (2, 1), (3, 2))
-
-
-def swap(value, pairs):
-    return jax.tree.map(lambda a: lax.ppermute(a, "tensor", pairs), value)
-
-
-def add_low(a, b):
-    return jax.tree.map(lambda u, v: (u.astype(single) + v.astype(single)).astype(narrow), a, b)
-
-
-def collect(ext, rows):
-    width = ext.shape[-1]
-    grid = ext.reshape(rows + LEFT + RIGHT, GRID, width)
-    from_below = lax.ppermute(grid[:LEFT], "tensor", DOWN)
-    from_above = lax.ppermute(grid[LEFT + rows :], "tensor", UP)
-    mine = grid[LEFT : LEFT + rows]
-    mine = mine + jnp.pad(from_below, ((rows - LEFT, 0), (0, 0), (0, 0)))
-    mine = mine + jnp.pad(from_above, ((0, rows - RIGHT), (0, 0), (0, 0)))
-    return mine.reshape(1, rows * GRID, width)
+        name="tail",
+    )(*operands)
 
 
 def shards(
@@ -989,77 +1387,61 @@
     x1, n2, n2t, gt, branch, dn2, *far_fc = mlp_half(
         True,
         (xs, near_attn, far_attn, gs, proj_bias[None], norm2_gain[None], norm2_shift[None], smalls),
+        None,
         across1,
         None,
         across2,
         None,
     )
-    out, dx1, da, sums2, *near_fc = mlp_half(
+    out, dx1, da, sums2, far1, far2, *near_fc = mlp_half(
         False,
-        (x1, n2, n2t, gs, gt, branch, dn2, fc2_bias[None], norm2_gain[None], smalls),
+        (
+            x1, n2, n2t, gs, gt, branch, dn2, fc2_bias[None], norm2_gain[None], smalls,
+            far_fc[0], far_fc[2],
+        ),
+        (far_fc[1], far_fc[3]),
         w_fc1,
         beside1,
         w_fc2,
         beside2,
     )
 
-    dn1, far_keep, far_give, far_bias, far_rel = backward_half(
-        rows, da, n1, far_qkv, far_mixed, far_w, wrel, tables, None
+    images = lax.axis_size("dp")
+    dn1, far_keep, far_give, far_bias, far_rel, reduced = backward_half(
+        True, rows, images, da, n1, far_qkv, far_mixed, far_w, wrel, tables,
+        [near_fc[0], near_fc[2], far1, far2, near_fc[1], near_fc[3]],
     )
-    back, sums1, near_keep, near_give, near_bias, near_rel = backward_half(
-        rows, da, n1, near_qkv, near_mixed, near_w, wrel, tables, (dn1, xs, dx1, norm1_gain[None])
+    back, sums1, near_keep, near_give, near_bias, near_rel, crossed, summed = backward_half(
+        False, rows, images, da, n1, near_qkv, near_mixed, near_w, wrel, tables,
+        [dn1, xs, dx1, norm1_gain[None], far_keep, far_give, reduced],
     )
-
-    output = collect(place_windows(rows, out), rows)
-    input_grad = collect(place_windows(rows, back), rows)
-
-    far_total = add_low(
-        (far_fc[0], far_fc[2], far_keep), swap((far_fc[1], far_fc[3], far_give), CORE_SWAP)
+    output, input_grad, gpack, totals, tops = tail(
+        rows, images, out, back, near_keep, crossed, sums1, sums2, near_bias, far_bias,
+        near_rel, far_rel, near_fc[4], far_fc[4], near_peak, far_peak, near_give,
     )
-    near_total = add_low(
-        (near_fc[0], near_fc[2], near_keep), swap((near_fc[1], near_fc[3], near_give), CORE_SWAP)
-    )
-    totals = add_low(near_total, swap(far_total, CHIP_SWAP))
-    totals = lax.psum(totals, "dp")
-    gw1, gw2, gpack = jax.tree.map(lambda a: a.astype(single), totals)
-
-    blocks = near_rel + far_rel
-    blocks = blocks[HD:, :HD] + blocks[:HD, HD:]
+
+    hidden = fc1_bias.shape[0]
+    summed = summed.astype(single)
+    gpack = gpack.astype(single)
+    blocks = totals[8:24].reshape(2, 8, 6, LANES).transpose(0, 2, 1, 3).reshape(-1, LANES)[:HD, :HD]
     grad_rel = jnp.stack([blocks[: 2 * WIN - 1][::-1], blocks[32 : 32 + 2 * WIN - 1][::-1]])
-    fc_bias = jnp.concatenate([near_fc[4][:, 0], far_fc[4][:, 0]])
-    qv = jnp.concatenate(
-        [b[jnp.array([0, 2])].reshape(2, 2, local).transpose(1, 0, 2) for b in (near_bias, far_bias)]
-    )
-    biases = jnp.concatenate([fc_bias, qv.reshape(SPLIT, 2 * local)], axis=1)
-    biases = biases[jnp.arange(SPLIT) ^ device]
-    sums, grad_rel, biases = lax.psum(
-        (jnp.concatenate([sums1[:2], sums2[:4]]), grad_rel, biases), ("dp", "tensor")
-    )
-    biases = biases[device]
-
-    def peaks(peak):
-        top = jnp.max(peak, axis=1)[: 2 * heads]
-        return jnp.maximum(top[:heads], lax.ppermute(top[heads:], "tensor", CORE_SWAP))
-
-    head_max = jnp.maximum(
-        peaks(near_peak), lax.ppermute(peaks(far_peak), "tensor", CHIP_SWAP)
-    )
-    head_max = lax.pmax(head_max, "dp")
+    qv = lax.dynamic_slice_in_dim(totals, 28 + device, 1)[0].reshape(2, 2 * local)[:, :local]
+    head_max = lax.dynamic_slice(tops, (8 * device, 0), (heads, 1))[:, 0]
     factor = jnp.sqrt(CLIP / jnp.maximum(head_max, CLIP))
     clipped_qk = (w_qkv[:2].astype(single) * jnp.repeat(factor, HD)).astype(narrow)
 
     return (
-        output,
-        input_grad,
+        output[None],
+        input_grad[None],
         gpack[: 3 * local].reshape(3, local, width).transpose(0, 2, 1),
-        biases[fc1_bias.shape[0] :].reshape(2, local),
+        qv,
         gpack[3 * local :],
-        sums[4],
-        gw1,
-        biases[: fc1_bias.shape[0]],
-        gw2.T,
-        sums[5],
-        sums[:4],
+        totals[4],
+        summed[:hidden],
+        lax.dynamic_slice_in_dim(totals, 24 + device, 1)[0],
+        summed[hidden:].T,
+        totals[5],
+        totals[:4],
         grad_rel,
         clipped_qk,
         head_max,

time: 533 us -> 446 us (0.84)
  Pallas kernels: 297 us -> 409 us
  blocking collectives: 66 us -> 0 us
  waiting for transfers between devices: 60.3 us -> 0 us
  starting transfers between devices: 26.7 us -> 0 us
  other arithmetic: 26.6 us -> 6.08 us
  between operations: 14.5 us -> 0.89 us
  local copies, waits for them, and re-layouts: 40.3 us -> 29.7 us
    pallas_call x4 -> x3, Pallas kernels: 91.7 us -> 177 us  [the longest x2 117 us: backward_half(): pl.pallas_call(functools.partial(backward_kernel, first, rows_held, image...]
    psum x1 -> x0, waiting for transfers between devices: 57.6 us -> none  [shards(): totals = lax.psum(totals, 'dp')]
    psum x1 -> x0, blocking collectives: 46.2 us -> none  [shards(): lax.psum((jnp.concatenate([sums1[:2], sums2[:4]]), grad_rel, biases), ('d...]
    ppermute x16 -> x0, starting transfers between devices: 26.7 us -> none  [the longest x9 13.9 us: swap(): return jax.tree.map(lambda a: lax.ppermute(a, 'tensor', pairs), value)]
    pallas_call x2, Pallas kernels: 100 us -> 126 us  [mlp_half(): pl.pallas_call(functools.partial(mlp_kernel, first), out_shape=[o[0] for...]
    pmax x1 -> x0, blocking collectives: 19.8 us -> none  [shards(): head_max = lax.pmax(head_max, 'dp')]
    convert_element_type x6 -> x1, other arithmetic: 12 us -> 0.36 us  [shards(): summed = summed.astype(single)]
    slice x17 -> x5, local copies, waits for them, and re-layouts: 13.9 us -> 5.75 us  [the longest x1 1.58 us: shards(): summed[:hidden]]
  transfers between devices with their start and end apart: 17 -> 0, of which waited for: 3 -> 0; matrix products, arithmetic and copies ran while one was open for 8% -> 0% of each run, Pallas kernels for 26% -> 0%
where the time goes in v3:
time: 446 us; the launch traced here: 445 us
  Pallas kernels  409 us (92%)
  local copies, waits for them, and re-layouts  29.7 us (7%)
  other arithmetic  6.08 us (1%)
    pallas_call x2, Pallas kernels, mlp_half(): pl.pallas_call(functools.partial(mlp_kernel, first), out_shape=[o[0] for...  126 us
    pallas_call x2, Pallas kernels, backward_half(): pl.pallas_call(functools.partial(backward_kernel, first, rows_held, image...  117 us
    pallas_call x1, Pallas kernels, near_forward(): pl.pallas_call(near_kernel, out_shape=[o[0] for o in outs], grid=(SLOTS,)...  61.9 us
    pallas_call x1, Pallas kernels, tail(): pl.pallas_call(functools.partial(tail_kernel, rows_held, images), out_sha...  59.5 us
    pallas_call x1, Pallas kernels, far_forward(): pl.pallas_call(far_kernel, out_shape=[o[0] for o in outs], grid=(SLOTS,),...  43.8 us

profile of v3, /device:TPU:0, one launch (start us, length us, event | category | flops | bytes accessed | tf_op | source)
XLA Modules:
  0.0 445.3 jit_solution(14786632316536534344)
XLA Ops:
  0.7 0.8 fusion.1
  1.4 0.7 reshape.305
  3.5 0.7 rev.12
  4.2 0.7 rev.13
  5.2 0.7 and_reduce_fusion
  5.8 0.7 broadcast_select_fusion
  6.5 0.6 fusion.2
  7.1 2.1 scatter.41
  9.6 1.3 broadcast_in_dim.34.gain.refs_13_
  10.9 2.4 pad_maximum_fusion.pack
  13.8 61.9 %near_forward.1 = (bf16[1248,768]{1,0:T(8,128)(2,1)}, bf16[7,208,768]{2,1,0:T(8,128)(2,1)}, bf16[7,4,208,384]{3,2,1,0:T(8,128)(2,1)}, bf16[7,208,384]{2,1,0:T(8,...) custom-call(bf16[1024,768]{1,0:T(8,128)(2,1)} %bitcast.37, ...), custom_call_target="tpu_custom_call" | custom-call | flops 12999999488 | bytes 30000000 | tf_op jit(solution)/shard_map/near_forward/pallas_call | solution.py:576
  75.7 43.8 %far_forward.1 = (bf16[1248,768]{1,0:T(8,128)(2,1)}, bf16[7,4,208,384]{3,2,1,0:T(8,128)(2,1)}, bf16[7,208,384]{2,1,0:T(8,128)(2,1)}, f32[1248,768]{1,0:T(8,128)}...) custom-call(bf16[1024,768]{1,0:T(8,128)(2,1)} %bitcast.38, ...), custom_call_target="tpu_custom_call" | custom-call | flops 12999999488 | bytes 30000000 | tf_op jit(solution)/shard_map/far_forward/pallas_call | solution.py:615
  121.3 53.1 %mlp.2 = (f32[1248,768]{1,0:T(8,128)}, bf16[1248,768]{1,0:T(8,128)(2,1)}, bf16[768,1248]{1,0:T(8,128)(2,1)}, bf16[768,1248]{1,0:T(8,128)(2,1)}, f32[1248,768]{1,...) custom-call(bf16[1248,768]{1,0:T(8,128)(2,1)} %get-tuple-element.182, ...), custom_call_target="tpu_custom_call" | custom-call | flops 17999998976 | bytes 40000000 | tf_op jit(solution)/shard_map/mlp/pallas_call | solution.py:895
  174.5 0.6 broadcast_in_dim.40.refs_7_
  175.0 73.1 %mlp.3 = (bf16[1248,768]{1,0:T(8,128)(2,1)}, f32[1248,768]{1,0:T(8,128)}, bf16[1248,768]{1,0:T(8,128)(2,1)}, f32[8,768]{1,0:T(8,128)}, bf16[768,768]{1,0:T(8,128...) custom-call(f32[1248,768]{1,0:T(8,128)} %get-tuple-element.191.refs_, ...), custom_call_target="tpu_custom_call" | custom-call | flops 17999998976 | bytes 40000000 | tf_op jit(solution)/shard_map/mlp/pallas_call | solution.py:895
  248.1 53.6 %attention_backward.2 = (f32[7,208,768]{2,1,0:T(8,128)}, bf16[768,768]{1,0:T(8,128)(2,1)}, bf16[768,768]{1,0:T(8,128)(2,1)}, f32[8,384]{1,0:T(8,128)}, f32[128,128]{1,0:T(8,128)}, /*index=5*/bf16[2,96,768]{2,1,0:T(8,128)(2,1)}) custom-call(bf16[1248,768]{1,0:T(8,128)(2,1)} %get-tuple-element.204.refs_0_, ...), custom_call_target="tpu_custom_call" | custom-call | flops 25999998976 | bytes 40000000 | tf_op jit(solution)/shard_map/attention_backward/pallas_call | solution.py:1117
  301.7 63.8 %attention_backward.3 = (bf16[1248,768]{1,0:T(8,128)(2,1)}, f32[8,768]{1,0:T(8,128)}, bf16[768,768]{1,0:T(8,128)(2,1)}, bf16[768,768]{1,0:T(8,128)(2,1)}, f32[8,...) custom-call(bf16[1248,768]{1,0:T(8,128)(2,1)} %get-tuple-element.204.refs_0_, ...), custom_call_target="tpu_custom_call" | custom-call | flops 25999998976 | bytes 40000000 | tf_op jit(solution)/shard_map/attention_backward/pallas_call | solution.py:1117
  365.5 59.5 %tail.1 = (bf16[1024,768]{1,0:T(8,128)(2,1)}, bf16[1024,768]{1,0:T(8,128)(2,1)}, bf16[768,768]{1,0:T(8,128)(2,1)}, f32[32,768]{1,0:T(8,128)}, f32[32,128]{1,0:T(8,128)}) custom-call(bf16[1248,768]{1,0:T(8,128)(2,1)} %get-tuple-element.203.out, bf16[1248,768]{1,0:T(8,128)(2,1)} %get-tuple-element.222.back, bf16[768,768]{1,0:T(8,128)(2,1)} %get-tuple-element.223.keep, ...), custom_call_target="tpu_custom_call" | custom-call | flops 4000000000 | bytes 20000000 | tf_op jit(solution)/shard_map/tail/pallas_call | solution.py:1312
  425.0 0.8 slice.248
  425.8 0.6 copy.39
  426.8 1.6 slice_bitcast_fusion
  428.4 3.1 copy.38
  431.5 1.3 slice.252
  432.8 0.8 dynamic-slice_reduce_fusion.2
  433.8 2.0 multiply_convert_fusion
  435.9 0.9 slice.254
  436.7 1.4 slice_reduce_fusion
  438.8 1.3 slice.247
  440.1 1.6 slice.255
  442.2 1.1 copy.49
  443.4 0.8 copy-done.2
  444.2 1.1 copy.50
  (48 shorter events, 6.1 us)
Async XLA Ops:
  0.6 12.6 %copy-start.6 = (f32[768]{0:T(1024)S(1)}, f32[768]{0:T(1024)}, u32[]{:S(2)}) copy-start(f32[768]{0:T(1024)} %param.48) | copy-start | bytes 9220
  3.5 10.4 %copy-start.5 = (f32[8,768]{1,0:T(8,128)}, f32[8,768]{1,0:T(8,128)S(1)}, u32[]{:S(2)}) copy-start(f32[8,768]{1,0:T(8,128)S(1)} %scatter.36.small) | copy-start | bytes 73732
  9.6 4.2 copy-start.4
  75.7 43.9 %copy-start.7 = (f32[768]{0:T(1024)S(1)}, f32[768]{0:T(1024)}, u32[]{:S(2)}) copy-start(f32[768]{0:T(1024)} %param.49) | copy-start | bytes 9220
  75.7 44.5 %copy-start.8 = (f32[768]{0:T(1024)S(1)}, f32[768]{0:T(1024)}, u32[]{:S(2)}) copy-start(f32[768]{0:T(1024)} %param.42) | copy-start | bytes 9220
  75.7 45.0 %copy-start.9 = (f32[768]{0:T(1024)S(1)}, f32[768]{0:T(1024)}, u32[]{:S(2)}) copy-start(f32[768]{0:T(1024)} %param.50) | copy-start | bytes 9220
  121.3 53.1 %copy-start.10 = (f32[768]{0:T(1024)S(1)}, f32[768]{0:T(1024)}, u32[]{:S(2)}) copy-start(f32[768]{0:T(1024)} %param.46) | copy-start | bytes 9220
  365.5 61.0 %copy-start = (bf16[1536,768]{1,0:T(8,128)(2,1)S(1)}, bf16[1536,768]{1,0:T(8,128)(2,1)}, u32[]{:S(2)}) copy-start(bf16[1536,768]{1,0:T(8,128)(2,1)} %get-tuple-element.240) | copy-start | bytes 7077892
  428.4 3.1 copy-start.1
  433.6 8.0 %copy-start.11 = (f32[3]{0:T(128)}, f32[3]{0:T(128)S(1)}, u32[]{:S(2)}) copy-start(f32[3]{0:T(128)S(1)} %dynamic-slice_reduce_fusion.2) | copy-start | bytes 40
  440.1 2.1 copy-start.3
  442.2 2.0 copy-start.2

commit v4 on v0

v4 whole, which is shorter than its diff:
```python
import functools

import jax
import jax.numpy as jnp
import numpy as np
from jax import lax
from jax.experimental import pallas as pl
from jax.experimental.pallas import tpu as pltpu
from jax.sharding import PartitionSpec as P

HD = 64
GRID = 64
WIN = 14
TILES = 5
SPAN = WIN * WIN
ROWS = 208
SLOTS = 7
SLAB = 6 * ROWS
SPLIT = 4
SHORT = 112
LEFT = 6
RIGHT = 12
LANES = 128
EPS = 1e-6
CLIP = 3.0
VMEM = 60 * 1024 * 1024

single = jnp.float32
narrow = jnp.bfloat16

def lane_tables():
    row = np.arange(ROWS)
    x, y = row // WIN, row % WIN
    lane = np.arange(LANES) % 64
    part = lane // 32
    at = lane % 32
    amount = np.where(part[None, :] == 0, 13 - x[:, None], 13 - y[:, None])
    amount = np.where((row < SPAN)[:, None], amount, 0)
    bits = np.stack([(amount >> b) & 1 for b in range(4)]).astype(np.float32)
    lanes = np.zeros((8, LANES), np.float32)
    lanes[0] = at < WIN
    lanes[1] = (at >= 16) & (at < 16 + WIN)
    lanes[2] = lane == 31
    sides = np.zeros((16, LANES), np.float32)
    sides[0] = np.arange(LANES) < 64
    sides[1] = np.arange(LANES) >= 64
    place = np.where(part[None, :] == 0, x[:, None], y[:, None])
    hot = ((at % 16)[None, :] == place) & ((at % 16) < WIN)[None, :] & (row < SPAN)[:, None]
    keys = hot.astype(np.float32)
    keys[SPAN:, lane == 31] = -1e30
    return (
        jnp.asarray(bits),
        jnp.asarray(lanes),
        jnp.asarray(sides, narrow),
        jnp.asarray(keys, narrow),
    )


def dot(a, b):
    return jnp.dot(a, b, preferred_element_type=single)


def dot_nt(a, b):
    return lax.dot_general(a, b, (((1,), (1,)), ((), ())), preferred_element_type=single)


def dot_tn(a, b):
    return lax.dot_general(a, b, (((0,), (0,)), ((), ())), preferred_element_type=single)


def norm_parts(values):
    centre = values - jnp.mean(values, axis=-1, keepdims=True)
    inverse = lax.rsqrt(jnp.mean(centre * centre, axis=-1, keepdims=True) + EPS)
    return centre * inverse, inverse


def norm_back(grad, normal, inverse, gain):
    scaled = grad * gain
    first = jnp.mean(scaled, axis=-1, keepdims=True)
    second = jnp.mean(scaled * normal, axis=-1, keepdims=True)
    return inverse * (scaled - first - normal * second)


def slot_fields(rows_held):
    return window_fields(rows_held, lax.axis_index("tensor"), pl.program_id(0) % SLOTS)


def window_fields(rows_held, device, slot):
    window = device * (SLOTS - 1) + slot
    i, j = window // TILES, window % TILES
    last = device // (SPLIT - 1)
    live = slot < SLOTS - 1 + last
    row0 = i * WIN - device * rows_held + LEFT
    high = jnp.minimum(WIN, GRID - i * WIN)
    wide = jnp.minimum(WIN, GRID - j * WIN)
    tall = jnp.where(last == 1, SLOTS - TILES, SLOTS)
    offset = ROWS * jnp.minimum(slot, tall) + SHORT * jnp.maximum(slot - tall, 0)
    return row0, j * WIN, high, wide, offset, live


def positions(axis, first_col, high, wide):
    shape = (ROWS, 1) if axis == 0 else (1, ROWS)
    row = lax.broadcasted_iota(jnp.int32, shape, axis)
    x = lax.shift_right_logical(row * 4682, 16)
    y = row - x * WIN
    valid = (x < high) & (y < wide)
    return jnp.where(valid, x * GRID + first_col + y, -1), valid


def gather_window(source, target):
    token = lax.broadcasted_iota(jnp.int32, (ROWS, WIN * GRID), 1)
    choose = jnp.where(token == target, 1.0, 0.0).astype(narrow)
    return dot(choose, source)


def shift_left(values, bits):
    for b in range(4):
        values = jnp.where(bits[b] > 0.5, pltpu.roll(values, LANES - (1 << b), 1), values)
    return values


def shift_right(values, bits):
    for b in range(4):
        values = jnp.where(bits[b] > 0.5, pltpu.roll(values, 1 << b, 1), values)
    return values


def partners(device):
    beside = device + 1 - 2 * (device % 2)
    across = (device + 2) % SPLIT
    corner = (beside + 2) % SPLIT
    return beside, across, corner


def greet(places):
    barrier = pltpu.get_barrier_semaphore()
    for place in places:
        pl.semaphore_signal(barrier, inc=1, device_id=place, device_id_type=pl.DeviceIdType.MESH)
    pl.semaphore_wait(barrier, len(places))


class Sender:
    def __init__(self, sends, recvs, locals_):
        self.sends, self.recvs, self.locals = sends, recvs, locals_

    def remote(self, at, source, target, place):
        return pltpu.make_async_remote_copy(
            src_ref=source,
            dst_ref=target,
            send_sem=self.sends.at[at],
            recv_sem=self.recvs.at[at],
            device_id=place,
            device_id_type=pl.DeviceIdType.MESH,
        )

    def local(self, at, source, target):
        return pltpu.make_async_copy(source, target, self.locals.at[at])


def mate_of(image, bit):
    unit = 1 << bit
    return image + unit * (1 - 2 * ((image // unit) % 2))


def rows_at(start, count):
    return pl.ds(pl.multiple_of(start, 16), count)


def add_rows(target, target_at, sources, count):
    chunk = 48 if count % 48 == 0 else 16

    @pl.loop(0, count // chunk)
    def _(c):
        total = None
        for ref, at in sources:
            value = ref[rows_at(at + c * chunk, chunk), :].astype(single)
            total = value if total is None else total + value
        target[rows_at(target_at + c * chunk, chunk), :] = total.astype(target.dtype)


HALVINGS = 3


class Halver:
    def __init__(self, send, base, image, images, start, rows, order):
        bits = images.bit_length() - 1
        assert images == 1 << bits and bits >= HALVINGS
        self.send, self.base, self.image = send, base, image
        self.extra_bits = range(HALVINGS, bits)
        self.stages = []
        landing, length = 0, rows
        for bit in order:
            length //= 2
            mine = (image // (1 << bit)) % 2
            keep, give = start + mine * length, start + (1 - mine) * length
            self.stages.append((mate_of(image, bit), keep, give, length, landing))
            landing += length
            start = keep
        self.final = (start, length)
        self.landing = landing

    @staticmethod
    def copies(images):
        return 2 * HALVINGS + images.bit_length() - 1 - HALVINGS

    @staticmethod
    def landing_rows(images, rows):
        last = rows >> HALVINGS
        return rows - last + last * (images.bit_length() - 1 - HALVINGS)

    def out(self, stage, held, landing):
        mate, _, give, length, at = self.stages[stage]
        return self.send.remote(
            self.base + stage,
            held.at[rows_at(give, length), :],
            landing.at[pl.ds(at, length), :],
            {"dp": mate},
        )

    def start(self, stage, held, landing):
        self.out(stage, held, landing).start()

    def finish(self, stage, held, landing):
        self.out(stage, held, landing).wait()
        _, keep, _, length, at = self.stages[stage]
        add_rows(held, keep, [(held, keep), (landing, at)], length)

    def extras(self, held, landing):
        start, length = self.final
        for k, bit in enumerate(self.extra_bits):
            at = self.landing + k * length
            copy = self.send.remote(
                self.base + HALVINGS + k,
                held.at[rows_at(start, length), :],
                landing.at[pl.ds(at, length), :],
                {"dp": mate_of(self.image, bit)},
            )
            copy.start()
            copy.wait()
            add_rows(held, start, [(held, start), (landing, at)], length)

    def back(self, stage, held):
        mate, keep, _, length, _ = self.stages[stage]
        cut = rows_at(keep, length)
        at = self.base + HALVINGS + len(self.extra_bits) + stage
        return self.send.remote(at, held.at[cut, :], held.at[cut, :], {"dp": mate})


def dp_mates(image, images):
    return [{"dp": mate_of(image, bit)} for bit in range(images.bit_length() - 1)]


def attend(n1, valid, weights, qbias, vbias, wrel, bits, lanes, sides, keys, qkv, mixed, peak):
    half = weights.shape[1]
    query = jnp.where(valid, dot_nt(n1, weights[0]) + qbias, 0.0).astype(narrow)
    key8 = dot_nt(n1, weights[1]).astype(narrow) * jnp.asarray(0.125, narrow)
    value = (dot_nt(n1, weights[2]) + vbias).astype(narrow)
    qkv[0, 0] = query
    qkv[0, 1] = key8
    qkv[0, 2] = value
    low_lane = lax.broadcasted_iota(jnp.int32, (ROWS, LANES), 1) < 64
    for pair in range(half // LANES):
        cut = slice(pair * LANES, (pair + 1) * LANES)
        q, k8, v = query[:, cut], key8[:, cut], value[:, cut]
        rel = shift_left(dot(q, wrel[...]), bits)
        rest = rel - rel.astype(narrow).astype(single)
        rel = rel * lanes[0:1] + pltpu.roll(rest, 16, 1) * lanes[1:2] + lanes[2:3]
        rel = rel.astype(narrow)
        qkv[0, 3, :, cut] = rel
        pieces = []
        for head in range(2):
            mine, other = sides[head : head + 1], sides[1 - head : 2 - head]
            only = q * mine
            logits = dot_nt(only, k8)
            at = 2 * pair + head
            peak[at : at + 1, :] = jnp.maximum(
                peak[at : at + 1, :], jnp.max(logits, axis=0, keepdims=True)
            )
            scores = dot_nt(only + rel * other, k8 * mine + keys[...] * other)
            top = jnp.max(scores, axis=1, keepdims=True)
            probs = jnp.exp(scores - top)
            total = jnp.sum(probs, axis=1, keepdims=True)
            pieces.append(dot(probs.astype(narrow), v) * (1.0 / total))
        mixed[0, :, cut] = jnp.where(low_lane, pieces[0], pieces[1]).astype(narrow)
    return dot(mixed[0], weights[3])


def halo_copies(send, base, grid, ext, device, rows):
    top, bottom = LEFT * GRID, RIGHT * GRID
    held_rows = rows * GRID
    down = send.remote(
        base,
        grid.at[pl.ds(held_rows - top, top), :],
        ext.at[pl.ds(0, top), :],
        {"tensor": (device + 1) % SPLIT},
    )
    up = send.remote(
        base + 1,
        grid.at[pl.ds(0, bottom), :],
        ext.at[pl.ds(top + held_rows, bottom), :],
        {"tensor": (device + SPLIT - 1) % SPLIT},
    )
    return down, up


def when_all(*conditions):
    def run(action):
        flag = conditions[0]
        for more in conditions[1:]:
            flag = jnp.logical_and(flag, more)
        pl.when(flag)(action)

    return run


def forward_kernel(
    x, g, pack, fc1, fc2, small, gain, shift, wrel, bits, lanes, sides, keys,
    xs, gs, n1_all, qkv, mixed, attn, peak, weights_out, across1, across2, beside1, beside2, small_out,
    xext, gext, weights, smalls, sends, recvs, locals_,
):
    step = pl.program_id(0)
    far, slot = step // SLOTS, step % SLOTS
    device, image = lax.axis_index("tensor"), lax.axis_index("dp")
    tokens, width = x.shape
    rows = tokens // GRID
    part = pack.shape[1]
    half = 2 * part
    beside, across, corner = partners(device)
    side = image % 2
    mate = {"dp": mate_of(image, 0)}
    send = Sender(sends, recvs, locals_)
    first, last = device > 0, device < SPLIT - 1

    def cut(array, halves, index):
        size = array.shape[0] // halves
        return array.at[rows_at(index * size, size), :]

    x_down, x_up = halo_copies(send, 0, x, xext, device, rows)
    g_down, g_up = halo_copies(send, 2, g, gext, device, rows)
    own_pack = send.remote(4, pack, weights.at[0, :, pl.ds(part, part), :], {"tensor": beside})
    notes = [
        send.remote(5 + k, small, smalls.at[k + 1], {"tensor": place})
        for k, place in enumerate((beside, across, corner))
    ]
    taken = pl.ds(pl.multiple_of(side * (part // 2), 16), part // 2)
    awaited = pl.ds(pl.multiple_of((1 - side) * (part // 2), 16), part // 2)
    pack_x = send.remote(8, pack.at[:, taken, :], weights.at[1, :, taken, :], {"tensor": across})
    pack_y = send.remote(9, weights.at[1, :, taken, :], weights.at[1, :, taken, :], mate)

    def beside_rows(which):
        half_rows = part // 2
        start = jnp.where(which == 0, side, 1 - side) * half_rows + part
        return pl.ds(pl.multiple_of(start, 16), half_rows)

    corner_x = send.remote(
        10, weights.at[1, :, taken, :], weights.at[1, :, beside_rows(0), :], {"tensor": beside}
    )
    corner_y = send.remote(
        11, weights.at[1, :, awaited, :], weights.at[1, :, beside_rows(1), :], {"tensor": beside}
    )
    fc_beside = [
        send.remote(12, fc1, beside1, {"tensor": beside}),
        send.remote(13, fc2, beside2, {"tensor": beside}),
    ]
    fc_x = [
        send.remote(14 + k, cut(source, 2, side), cut(target, 2, side), {"tensor": across})
        for k, (source, target) in enumerate(((fc1, across1), (fc2, across2)))
    ]
    fc_y = [
        send.remote(16 + k, cut(target, 2, side), cut(target, 2, side), mate)
        for k, target in enumerate((across1, across2))
    ]
    own = [
        send.local(0, pack, weights.at[0, :, pl.ds(0, part), :]),
        send.local(1, x, xext.at[pl.ds(LEFT * GRID, tokens), :]),
        send.local(2, small, smalls.at[0]),
    ]
    g_own = send.local(3, g, gext.at[pl.ds(LEFT * GRID, tokens), :])
    kept = [send.local(4, weights, weights_out), send.local(5, smalls, small_out)]

    @pl.when(step == 0)
    def _():
        for ref in (xs, gs, attn, peak):
            ref[...] = jnp.zeros_like(ref)
        for ref in (xext, gext):
            ref[pl.ds(0, LEFT * GRID), :] = jnp.zeros((LEFT * GRID, width), narrow)
            ref[pl.ds(LEFT * GRID + tokens, RIGHT * GRID), :] = jnp.zeros(
                (RIGHT * GRID, width), narrow
            )
        greet([{"tensor": place} for place in (beside, across, corner)] + [mate])
        own_pack.start()
        for copy in notes + own:
            copy.start()
        pl.when(last)(x_down.start)
        pl.when(first)(x_up.start)
        pack_x.start()
        for copy in own + notes + [own_pack]:
            copy.wait()
        pl.when(first)(x_down.wait_recv)

    @pl.when(step == 1)
    def _():
        for copy in fc_beside + [g_own]:
            copy.start()

    when_all(step == 3, last)(x_up.wait_recv)

    @pl.when(step == 4)
    def _():
        pack_x.wait_recv()
        pack_y.start()
        corner_x.start()
        fc_x[0].start()
        pl.when(last)(g_down.start)
        pl.when(first)(g_up.start)

    @pl.when(step == SLOTS)
    def _():
        pack_y.wait_recv()
        corner_y.start()
        fc_x[1].start()
        corner_x.wait_recv()
        corner_y.wait_recv()
        for copy in kept:
            copy.start()

    for k, at in ((0, 9), (1, 11)):

        @pl.when(step == at)
        def _():
            fc_x[k].wait_recv()
            fc_y[k].start()

    row0, col0, high, wide, offset, live = slot_fields(rows)

    @pl.when(live & (far == 0))
    def _():
        target, valid = positions(0, col0, high, wide)
        source = xext[pl.ds(pl.multiple_of(row0 * GRID, GRID), WIN * GRID), :]
        window = gather_window(source, target)
        xs[rows_at(offset, ROWS), :] = window.astype(narrow)
        normal, _ = norm_parts(window)
        n1_all[slot] = jnp.where(valid, normal * gain[...] + shift[...], 0.0).astype(narrow)

    @pl.when(live)
    def _():
        _, valid = positions(0, col0, high, wide)
        place = rows_at(offset, ROWS)
        qbias = smalls[2 * far, 1:2, :half] + smalls[2 * far + 1, 2:3, :half]
        vbias = smalls[2 * far, 3:4, :half] + smalls[2 * far + 1, 4:5, :half]
        terms = attend(
            n1_all[slot], valid, weights.at[far], qbias, vbias, wrel, bits, lanes, sides, keys,
            qkv, mixed, peak.at[far],
        )
        attn[place, :] += jnp.where(valid, terms, 0.0)

    @pl.when(step == 2 * SLOTS - 1)
    def _():
        g_own.wait()
        for down, up in ((x_down, x_up), (g_down, g_up)):
            pl.when(last)(down.wait_send)
            pl.when(first)(up.wait_send)
        pl.when(first)(g_down.wait_recv)
        pl.when(last)(g_up.wait_recv)

        @pl.loop(0, SLOTS)
        def _(slot):
            row0, col0, high, wide, offset, live = window_fields(rows, device, slot)

            @pl.when(live)
            def _():
                target, _ = positions(0, col0, high, wide)
                source = gext[pl.ds(pl.multiple_of(row0 * GRID, GRID), WIN * GRID), :]
                gs[rows_at(offset, ROWS), :] = gather_window(source, target).astype(narrow)

        for copy in (pack_x, pack_y, corner_x, corner_y, *fc_x):
            copy.wait_send()
        for copy in kept + fc_beside + fc_y:
            copy.wait()


def whole(shape):
    zeros = (0,) * len(shape)
    return pl.BlockSpec(shape, lambda *_: zeros, pipeline_mode=pl.Buffered(1))


def by_slot(shape):
    rest = (0,) * len(shape)
    return pl.BlockSpec((1,) + tuple(shape), lambda s, *_: (s,) + rest)


ANY = pl.BlockSpec(memory_space=pl.ANY)


def of(shape, dtype=narrow):
    return jax.ShapeDtypeStruct(shape, dtype)


def forward(x, g, pack, fc1, fc2, small, norm, wrel, tables):
    tokens, width = x.shape
    half = 2 * pack.shape[1]
    slab = (SLAB, width)
    outs = [
        (of(slab), whole(slab)),
        (of(slab), whole(slab)),
        (of((SLOTS, ROWS, width)), whole((SLOTS, ROWS, width))),
        (of((2 * SLOTS, 4, ROWS, half)), by_slot((4, ROWS, half))),
        (of((2 * SLOTS, ROWS, half)), by_slot((ROWS, half))),
        (of(slab, single), whole(slab)),
        (of((2, 8, ROWS), single), whole((2, 8, ROWS))),
        (of((2, 4, half, width)), ANY),
        (of(fc1.shape), ANY),
        (of(fc2.shape), ANY),
        (of(fc1.shape), ANY),
        (of(fc2.shape), ANY),
        (of((SPLIT,) + small.shape, single), ANY),
    ]
    operands = (x, g, pack, fc1, fc2, small, *norm, wrel, *tables)
    ext = (tokens + (LEFT + RIGHT) * GRID, width)
    return pl.pallas_call(
        forward_kernel,
        out_shape=[o[0] for o in outs],
        grid=(2 * SLOTS,),
        in_specs=[ANY] * 6 + [whole(a.shape) for a in operands[6:]],
        out_specs=[o[1] for o in outs],
        scratch_shapes=[
            pltpu.VMEM(ext, narrow),
            pltpu.VMEM(ext, narrow),
            pltpu.VMEM((2, 4, half, width), narrow),
            pltpu.VMEM((SPLIT,) + small.shape, single),
            pltpu.SemaphoreType.DMA((18,)),
            pltpu.SemaphoreType.DMA((18,)),
            pltpu.SemaphoreType.DMA((6,)),
        ],
        compiler_params=pltpu.CompilerParams(
            vmem_limit_bytes=VMEM, collective_id=0, has_side_effects=True
        ),
        cost_estimate=pl.CostEstimate(
            flops=26_000_000_000, bytes_accessed=60_000_000, transcendentals=8_000_000
        ),
        name="attention_forward",
    )(*operands)


BLOCK = 256
CHUNK = 416


def gelu_parts(z):
    size = jnp.abs(z)
    bell = jnp.exp(-0.5 * z * z)
    t = 1.0 / (1.0 + 0.2316418882663604 * size)
    poly = 0.5 * 1.061405429 * t + (0.5 * -1.453152027)
    poly = poly * t + 0.5 * 1.421413741
    poly = poly * t + 0.5 * -0.284496736
    poly = poly * t + 0.5 * 0.254829592
    tail = poly * t * bell
    phi_total = jnp.where(z >= 0, 1.0 - tail, tail)
    return z * phi_total, phi_total + z * bell * 0.3989422804014327


def mlp_kernel(
    xs, attn, gs, pbias, gain, shift, fbias, smalls, src1, src2,
    w1_across, w1_beside, w1_own, w2_across, w2_beside, w2_own,
    out, dx1, da, sums, near1, near2, far1, far2, rest, gb,
    n2, n2t, gt, branch, dn2, corner1, corner2, keep1, keep2, give1, give2, got1, got2, near_got1,
    near_got2, w1, w2, b1, hs, zs, sends, recvs,
):
    step = pl.program_id(0)
    count = pl.num_programs(0) // SPLIT
    group, index = step // count, step % count
    width = gs.shape[1]
    cut = pl.ds(pl.multiple_of(index * BLOCK, BLOCK), BLOCK)
    holder = jnp.where(group == 0, 2, jnp.where(group == 1, 3, jnp.where(group == 2, 1, 0)))
    beside, across, _ = partners(lax.axis_index("tensor"))
    send = Sender(sends, recvs, None)
    corners = [
        send.remote(0, src1, corner1, {"tensor": beside}),
        send.remote(1, src2, corner2, {"tensor": beside}),
    ]
    swaps = [
        send.remote(2, give1, got1, {"tensor": beside}),
        send.remote(3, give2, got2, {"tensor": beside}),
    ]
    upper = got2.shape[0] // 2
    crossings = [
        send.remote(4, got1, far1, {"tensor": across}),
        send.remote(5, got2.at[pl.ds(0, upper), :], far2, {"tensor": across}),
    ]
    near_swaps = [
        send.remote(6, corner1, near_got1, {"tensor": beside}),
        send.remote(7, corner2, near_got2, {"tensor": beside}),
    ]

    @pl.when(step == 0)
    def _():
        gb[...] = jnp.zeros_like(gb)
        greet([{"tensor": beside}, {"tensor": across}])
        for copy in corners:
            copy.start()

        @pl.loop(0, SLAB // ROWS)
        def _(c):
            sl = rows_at(c * ROWS, ROWS)
            middle = xs[sl, :].astype(single) + (attn[sl, :] + pbias[...])
            dx1[sl, :] = middle
            normal, _ = norm_parts(middle)
            n2[sl, :] = (normal * gain[...] + shift[...]).astype(narrow)
            branch[sl, :] = jnp.zeros((ROWS, width), single)
            dn2[sl, :] = jnp.zeros((ROWS, width), single)

        for j in range(width // LANES):
            lanes = slice(j * LANES, (j + 1) * LANES)
            n2t[lanes, :] = n2[:, lanes].T
            gt[lanes, :] = gs[:, lanes].T

    @pl.when(step == count)
    def _():
        for copy in corners:
            copy.wait()

    @pl.when(step == 2 * count)
    def _():
        for copy in swaps:
            copy.start()

    for k, (first, second) in enumerate(
        ((w1_across, w2_across), (None, None), (w1_beside, w2_beside), (w1_own, w2_own))
    ):

        @pl.when(group == k)
        def _():
            if first is None:
                w1[...] = corner1[:, cut]
                w2[...] = corner2[cut, :]
            else:
                w1[...] = first[...]
                w2[...] = second[...]

    b1[...] = smalls[holder, 0:1, cut]

    @pl.loop(0, SLAB // CHUNK)
    def _(c):
        sl = rows_at(c * CHUNK, CHUNK)
        z = dot(n2[sl, :], w1[...]) + b1[0:1]
        dh = dot_nt(gs[sl, :], w2[...])
        act, slope = gelu_parts(z)
        h = act.astype(narrow)
        dz = (dh * slope).astype(narrow)
        hs[sl, :] = h
        zs[sl, :] = dz
        gb[holder, 0:1, cut] += jnp.sum(dz.astype(single), axis=0, keepdims=True)
        branch[sl, :] += dot(h, w2[...])
        dn2[sl, :] += dot_nt(dz, w1[...])

    @pl.when(step == 2 * count)
    def _():
        for copy, got, keep, crossing in zip(
            swaps, (got1, got2), (keep1, keep2), crossings, strict=True
        ):
            copy.wait()
            add_rows(got, 0, [(got, 0), (keep, 0)], got.shape[0])
            crossing.start()
        rest[...] = got2[pl.ds(upper, upper), :]

    for k, (first, second) in enumerate(
        ((keep1, keep2), (give1, give2), (corner1, corner2), (near1, near2))
    ):

        @pl.when(group == k)
        def _():
            @pl.loop(0, width // 256)
            def _(r):
                sl = rows_at(r * 256, 256)
                first[sl, cut] = dot(n2t[sl, :], zs[...]).astype(narrow)
                second[sl, cut] = dot(gt[sl, :], hs[...]).astype(narrow)

    @pl.when(step == 3 * count - 1)
    def _():
        for copy in near_swaps:
            copy.start()

    @pl.when(step == 4 * count - 1)
    def _():
        for copy, near, got in zip(
            near_swaps, (near1, near2), (near_got1, near_got2), strict=True
        ):
            copy.wait()
            add_rows(near, 0, [(near, 0), (got, 0)], near.shape[0])
        sums[...] = jnp.zeros_like(sums)

        @pl.loop(0, SLAB // ROWS)
        def _(c):
            sl = rows_at(c * ROWS, ROWS)
            middle = dx1[sl, :]
            normal, inverse = norm_parts(middle)
            out[sl, :] = (middle + (branch[sl, :] + fbias[...])).astype(narrow)
            grad = dn2[sl, :]
            cot = gs[sl, :].astype(single)
            total = cot + norm_back(grad, normal, inverse, gain[...])
            dx1[sl, :] = total
            low = total.astype(narrow)
            da[sl, :] = low
            sums[0:1, :] += jnp.sum(grad * normal, axis=0, keepdims=True)
            sums[1:2, :] += jnp.sum(grad, axis=0, keepdims=True)
            sums[2:3, :] += jnp.sum(low.astype(single), axis=0, keepdims=True)
            sums[3:4, :] += jnp.sum(cot, axis=0, keepdims=True)

        for copy in crossings:
            copy.wait()


def mlp(residents, across, beside, own):
    width, local = own[0].shape
    count = local // BLOCK

    def block(shape, group, dim):
        def index(i):
            at = jnp.clip(i - group * count, 0, count - 1)
            return (0, at) if dim == 1 else (at, 0)

        return pl.BlockSpec(shape, index)

    slab = (SLAB, width)
    square = (width, local)
    in_specs = [whole(a.shape) for a in residents] + [ANY, ANY]
    in_specs += [block((width, BLOCK), group, 1) for group in (0, 2, 3)]
    in_specs += [block((BLOCK, width), group, 0) for group in (0, 2, 3)]
    outs = [
        (of(slab), whole(slab)),
        (of(slab, single), whole(slab)),
        (of(slab), whole(slab)),
        (of((8, width), single), whole((8, width))),
        (of(square), whole(square)),
        (of(square), whole(square)),
        (of(square), ANY),
        (of((width // 2, local)), ANY),
        (of((width // 2, local)), whole((width // 2, local))),
        (of((SPLIT, 8, local), single), whole((SPLIT, 8, local))),
    ]
    flipped = pltpu.VMEM((width, SLAB), narrow)
    return pl.pallas_call(
        mlp_kernel,
        out_shape=[o[0] for o in outs],
        grid=(SPLIT * count,),
        in_specs=in_specs,
        out_specs=[o[1] for o in outs],
        scratch_shapes=[
            pltpu.VMEM(slab, narrow),
            flipped,
            flipped,
            pltpu.VMEM(slab, single),
            pltpu.VMEM(slab, single),
            *[pltpu.VMEM(square, narrow)] * 10,
            pltpu.VMEM((width, BLOCK), narrow),
            pltpu.VMEM((BLOCK, width), narrow),
            pltpu.VMEM((1, BLOCK), single),
            pltpu.VMEM((SLAB, BLOCK), narrow),
            pltpu.VMEM((SLAB, BLOCK), narrow),
            pltpu.SemaphoreType.DMA((8,)),
            pltpu.SemaphoreType.DMA((8,)),
        ],
        compiler_params=pltpu.CompilerParams(
            vmem_limit_bytes=VMEM, collective_id=1, has_side_effects=True
        ),
        cost_estimate=pl.CostEstimate(
            flops=36_000_000_000, bytes_accessed=60_000_000, transcendentals=8_000_000
        ),
        name="mlp",
    )(*residents, *across, across[0], beside[0], own[0], across[1], beside[1], own[1])


def backward_kernel(
    rows_held, images,
    da, n1, qkv, mixed, weights, wrel, bits, lanes, sides, keys, xs, dx1, gain, near1, near2, far1, far2, rest,
    back, sums, keep, give, bias, grel, crossed, summed1, summed2,
    acc, dqkv, dmix, dn1, keep_far, give_far, got_far, held1, held2, land1, land2, rest_got,
    sends, recvs, locals_,
):
    step = pl.program_id(0)
    slot, far = step % SLOTS, 1 - step // SLOTS
    image = lax.axis_index("dp")
    beside, across, _ = partners(lax.axis_index("tensor"))
    send = Sender(sends, recvs, locals_)
    half, width = weights.shape[2:]
    per = Halver.copies(images)
    sum1 = Halver(send, 3, image, images, 0, held1.shape[0], (0, 1, 2))
    sum2 = Halver(send, 3 + per, image, images, 0, held2.shape[0], (0, 1, 2))
    rest_cross = send.remote(0, rest, rest_got, {"tensor": across})
    far_swap = send.remote(1, give_far, got_far, {"tensor": beside})
    far_cross = send.remote(2, got_far, crossed, {"tensor": across})
    upper = held2.shape[0] - rest_got.shape[0]

    def seed(k, halver, held, summed):
        start, length = halver.final
        copy = send.local(k, held.at[rows_at(start, length), :], summed.at[rows_at(start, length), :])
        copy.start()
        copy.wait()

    def begin():
        greet([{"tensor": beside}, {"tensor": across}] + dp_mates(image, images))
        rest_cross.start()
        add_rows(held1, 0, [(near1, 0), (far1, 0)], held1.shape[0])
        sum1.start(0, held1, land1)

    def second():
        add_rows(held2, 0, [(near2, 0), (far2, 0)], upper)
        rest_cross.wait()
        add_rows(held2, upper, [(near2, upper), (rest_got, 0)], rest_got.shape[0])

    def third():
        sum1.finish(0, held1, land1)
        sum1.start(1, held1, land1)
        sum2.start(0, held2, land2)

    def fourth():
        sum1.finish(1, held1, land1)
        sum1.start(2, held1, land1)

    def fifth():
        sum2.finish(0, held2, land2)
        sum2.start(1, held2, land2)
        sum1.finish(2, held1, land1)
        sum1.extras(held1, land1)
        seed(0, sum1, held1, summed1)
        sum1.back(2, summed1).start()

    def sixth():
        far_swap.start()
        sum2.finish(1, held2, land2)
        sum2.start(2, held2, land2)
        sum1.back(2, summed1).wait()
        sum1.back(1, summed1).start()

    def seventh():
        far_swap.wait()
        add_rows(got_far, 0, [(got_far, 0), (keep_far, 0)], got_far.shape[0])
        far_cross.start()

    def eighth():
        sum2.finish(2, held2, land2)
        sum2.extras(held2, land2)
        seed(1, sum2, held2, summed2)
        sum2.back(2, summed2).start()
        sum1.back(1, summed1).wait()
        sum1.back(0, summed1).start()

    def ninth():
        sum2.back(2, summed2).wait()
        sum2.back(1, summed2).start()

    def tenth():
        sum2.back(1, summed2).wait()
        sum1.back(0, summed1).wait()
        sum2.back(0, summed2).start()

    events = {
        (0, 0): begin,
        (2, 2): second,
        (3, 1): third,
        (4, 2): fourth,
        (5, 3): fifth,
        (7, 0): sixth,
        (8, 0): seventh,
        (8, 2): eighth,
        (10, 0): ninth,
        (11, 1): tenth,
    }

    def fire(section):
        for (at, place), event in events.items():
            if place == section:
                pl.when(step == at)(event)

    _, col0, high, wide, offset, live = slot_fields(rows_held)
    place = rows_at(offset, ROWS)

    @pl.when(slot == 0)
    def _():
        acc[...] = jnp.zeros_like(acc)

    @pl.when(step == 0)
    def _():
        for ref in (bias, grel, back, sums):
            ref[...] = jnp.zeros_like(ref)

    fire(0)

    @pl.when(live)
    def _():
        _, valid = positions(0, col0, high, wide)
        da_win = jnp.where(valid, da[place, :].astype(single), 0.0).astype(narrow)
        acc[3] += dot_tn(mixed[0], da_win)
        dmix[...] = dot_nt(da_win, weights[far, 3]).astype(narrow)

    def one_pair(pair):
        low_lane = lax.broadcasted_iota(jnp.int32, (ROWS, LANES), 1) < 64
        cut = slice(pair * LANES, (pair + 1) * LANES)
        q, k8, v, rel = (qkv[0, j, :, cut] for j in range(4))
        do = dmix[:, cut]
        dqs, dks, dvs = [], [], []
        for head in range(2):
            mine, other = sides[head : head + 1], sides[1 - head : 2 - head]
            full_key = k8 * mine + keys[...] * other
            scores = dot_nt(full_key, q * mine + rel * other)
            top = jnp.max(scores, axis=0, keepdims=True)
            probs = jnp.exp(scores - top)
            probs = probs * (1.0 / jnp.sum(probs, axis=0, keepdims=True))
            dprobs = dot_nt(v, do * mine)
            mean = jnp.sum(probs * dprobs, axis=0, keepdims=True)
            dscores = (probs * (dprobs - mean)).astype(narrow)
            dvs.append(dot(probs.astype(narrow), do))
            dks.append(dot(dscores, q))
            dqs.append(dot_tn(dscores, full_key))
        dv = jnp.where(low_lane, dvs[0], dvs[1])
        dk = jnp.where(low_lane, dks[0], dks[1]) * 0.125
        dq = jnp.where(low_lane, dqs[0], dqs[1])
        drel = jnp.where(low_lane, dqs[1], dqs[0]) * lanes[0:1]
        drel = shift_right(drel, bits).astype(narrow)
        dq = dq + dot_nt(drel, wrel[...])
        grel[...] += dot_tn(drel, q)
        dqkv[0, :, cut] = dq.astype(narrow)
        dqkv[1, :, cut] = dk.astype(narrow)
        dqkv[2, :, cut] = dv.astype(narrow)

    for pair in range(half // LANES):
        fire(pair + 1)
        pl.when(live)(functools.partial(one_pair, pair))

    @pl.when(live)
    def _():
        total = None
        for j in range(3):
            piece = dqkv[j]
            acc[j] += dot_tn(piece, n1[0])
            bias[far, j : j + 1, :] += jnp.sum(piece.astype(single), axis=0, keepdims=True)
            back_part = dot(piece, weights[far, j])
            total = back_part if total is None else total + back_part

        @pl.when(far == 1)
        def _():
            dn1[slot] = total

        @pl.when(far == 0)
        def _():
            _, valid = positions(0, col0, high, wide)
            grad = jnp.where(valid, total + dn1[slot], 0.0)
            normal, inverse = norm_parts(xs[place, :].astype(single))
            sums[0:1, :] += jnp.sum(grad * normal, axis=0, keepdims=True)
            sums[1:2, :] += jnp.sum(grad, axis=0, keepdims=True)
            result = dx1[place, :] + norm_back(grad, normal, inverse, gain[...])
            back[place, :] = jnp.where(valid, result, 0.0).astype(narrow)

    def flush(keep, give):
        part = half // 2
        for j in range(4):
            keep[j * part : (j + 1) * part, :] = acc[j, :part, :].astype(narrow)
            give[j * part : (j + 1) * part, :] = acc[j, part:, :].astype(narrow)

    @pl.when(step == SLOTS - 1)
    def _():
        flush(keep_far, give_far)

    @pl.when(step == 2 * SLOTS - 1)
    def _():
        flush(keep, give)
        sum2.back(0, summed2).wait()
        far_cross.wait()


def backward(rows_held, images, da, n1, qkv, mixed, weights, wrel, tables, residents, rest):
    half, width = weights.shape[2:]
    operands = [da, n1, qkv, mixed, weights, wrel, *tables, *residents, rest]
    in_specs = [whole(a.shape) for a in operands]
    in_specs[1] = pl.BlockSpec((1, ROWS, width), lambda i: (i % SLOTS, 0, 0))

    def halved(i):
        return (1 - i // SLOTS) * SLOTS + i % SLOTS

    in_specs[2] = pl.BlockSpec((1, 4, ROWS, half), lambda i: (halved(i), 0, 0, 0))
    in_specs[3] = pl.BlockSpec((1, ROWS, half), lambda i: (halved(i), 0, 0))
    in_specs[-1] = ANY
    packed = (2 * half, width)
    square = residents[3].shape
    outs = [
        (of((SLAB, width)), whole((SLAB, width))),
        (of((8, width), single), whole((8, width))),
        (of(packed), whole(packed)),
        (of(packed), whole(packed)),
        (of((2, 8, half), single), whole((2, 8, half))),
        (of((LANES, LANES), single), whole((LANES, LANES))),
        (of(packed), ANY),
        (of(square), ANY),
        (of(square), ANY),
    ]
    landing = (Halver.landing_rows(images, square[0]), width)
    copies = 3 + 2 * Halver.copies(images)
    return pl.pallas_call(
        functools.partial(backward_kernel, rows_held, images),
        out_shape=[o[0] for o in outs],
        grid=(2 * SLOTS,),
        in_specs=in_specs,
        out_specs=[o[1] for o in outs],
        scratch_shapes=[
            pltpu.VMEM((4, half, width), single),
            pltpu.VMEM((3, ROWS, half), narrow),
            pltpu.VMEM((ROWS, half), narrow),
            pltpu.VMEM((SLOTS, ROWS, width), single),
            *[pltpu.VMEM(packed, narrow)] * 3,
            *[pltpu.VMEM(square, narrow)] * 2,
            *[pltpu.VMEM(landing, narrow)] * 2,
            pltpu.VMEM(rest.shape, narrow),
            pltpu.SemaphoreType.DMA((copies,)),
            pltpu.SemaphoreType.DMA((copies,)),
            pltpu.SemaphoreType.DMA((2,)),
        ],
        compiler_params=pltpu.CompilerParams(
            vmem_limit_bytes=VMEM, collective_id=2, has_side_effects=True
        ),
        cost_estimate=pl.CostEstimate(
            flops=52_000_000_000, bytes_accessed=80_000_000, transcendentals=8_000_000
        ),
        name="attention_backward",
    )(*operands)


def clear_rows(ext):
    @pl.loop(0, ext.shape[0] // GRID)
    def _(r):
        ext[rows_at(r * GRID, GRID), :] = jnp.zeros((GRID, ext.shape[1]), narrow)


def place_windows(rows_held, device, slab, ext, first, last):
    @pl.loop(first, last)
    def _(slot):
        row0, col0, high, wide, offset, live = window_fields(rows_held, device, slot)

        @pl.when(live)
        def _():
            target, _ = positions(1, col0, high, wide)
            token = lax.broadcasted_iota(jnp.int32, (WIN * GRID, ROWS), 0)
            choose = jnp.where(token == target, 1.0, 0.0).astype(narrow)
            window = slab[rows_at(offset, ROWS), :]
            where_to = pl.ds(pl.multiple_of(row0 * GRID, GRID), WIN * GRID)
            ext[where_to, :] += dot(choose, window).astype(narrow)


def tail_kernel(
    rows_held, images,
    out, back, keep, crossed, sums1, sums2, bias, rel_sum, fc_bias, peak, give,
    output, input_grad, packed, totals, tops,
    ext0, ext1, below0, below1, above0, above1, got, landing, held, sum_land, top_land, sends, recvs,
):
    device, image = lax.axis_index("tensor"), lax.axis_index("dp")
    beside, across, corner = partners(device)
    send = Sender(sends, recvs, None)
    per = Halver.copies(images)
    middle = held.shape[0] // 2
    landing_rows = Halver.landing_rows(images, middle)
    landings = [landing.at[pl.ds(k * landing_rows, landing_rows), :] for k in range(2)]
    halvers = [
        Halver(send, 1 + k * per, image, images, k * middle, middle, order)
        for k, order in enumerate(((0, 1, 2), (1, 0, 2)))
    ]
    halo_base = 1 + 2 * per
    small_base = halo_base + 4
    tokens = rows_held * GRID
    top, bottom = LEFT * GRID, RIGHT * GRID
    held_by = (device, beside, across, corner)
    mates = dp_mates(image, images)
    ring = [{"tensor": beside}, {"tensor": across}] + mates

    def reduce_start(stage):
        for halver, land in zip(halvers, landings, strict=True):
            halver.start(stage, held, land)

    def reduce_finish(stage):
        for halver, land in zip(halvers, landings, strict=True):
            halver.finish(stage, held, land)

    def hand_start(stage):
        for halver in halvers:
            halver.back(stage, packed).start()

    def hand_finish(stage):
        for halver in halvers:
            halver.back(stage, packed).wait()

    greet([{"tensor": place} for place in (beside, across, corner)] + mates)
    swap = send.remote(0, give, got, {"tensor": beside})
    swap.start()

    totals[...] = jnp.zeros_like(totals)
    tops[...] = jnp.zeros_like(tops)
    totals[0:2, :] = sums1[0:2, :]
    totals[2:6, :] = sums2[0:4, :]
    rel = rel_sum[...]
    rel = rel[HD:] + pltpu.roll(rel[:HD], HD, 1)
    for g in range(HD // 8):
        at = 8 * (1 + g // 6)
        totals[at : at + 8, (g % 6) * LANES : (g % 6 + 1) * LANES] = rel[8 * g : 8 * g + 8]
    half = bias.shape[2]
    for k in range(SPLIT):
        far, odd = k // 2, k % 2
        totals[pl.ds(24 + held_by[k], 1), :] = fc_bias[k, 0:1, :]
        for j, row in enumerate((0, 2)):
            value = bias[far, row : row + 1, :]
            if odd:
                value = pltpu.roll(value, half // 2, 1)
            totals[pl.ds(28 + held_by[k], 1), j * half : (j + 1) * half] = value
        best = jnp.broadcast_to(jnp.max(peak[far], axis=1, keepdims=True), (8, LANES))
        if odd:
            best = pltpu.roll(best, 8 - half // LANES, 0)
        tops[pl.ds(pl.multiple_of(held_by[k] * 8, 8), 8), :] = best

    def small_copies(k):
        return [
            send.remote(small_base + 2 * k, totals, sum_land.at[k], ring[k]),
            send.remote(small_base + 2 * k + 1, tops, top_land.at[k], ring[k]),
        ]

    def small_start(k):
        for copy in small_copies(k):
            copy.start()

    def small_finish(k):
        for copy in small_copies(k):
            copy.wait()
        totals[...] += sum_land[k]
        tops[...] = jnp.maximum(tops[...], top_land[k])

    def halo(base, ext, below, above):
        up = send.remote(
            base, ext.at[pl.ds(0, top), :], below, {"tensor": (device + SPLIT - 1) % SPLIT}
        )
        down = send.remote(
            base + 1, ext.at[pl.ds(top + tokens, bottom), :], above, {"tensor": (device + 1) % SPLIT}
        )
        return up, down

    def halo_start(copies):
        up, down = copies
        pl.when(device > 0)(up.start)
        pl.when(device < SPLIT - 1)(down.start)

    def halo_finish(copies, ext, below, above, result):
        up, down = copies
        pl.when(device > 0)(up.wait_send)
        pl.when(device < SPLIT - 1)(down.wait_send)
        add_rows(result, 0, [(ext, top)], tokens)

        @pl.when(device < SPLIT - 1)
        def _():
            up.wait_recv()
            at = tokens - top
            add_rows(result, at, [(result, at), (below, 0)], top)

        @pl.when(device > 0)
        def _():
            down.wait_recv()
            add_rows(result, 0, [(result, 0), (above, 0)], bottom)

    small_start(0)
    clear_rows(ext0)
    clear_rows(ext1)
    swap.wait()
    add_rows(held, 0, [(keep, 0), (got, 0), (crossed, 0)], held.shape[0])
    reduce_start(0)
    small_finish(0)
    small_start(1)
    place_windows(rows_held, device, back, ext1, 0, SLOTS)
    halos1 = halo(halo_base, ext1, below1, above1)
    halo_start(halos1)
    small_finish(1)
    small_start(2)
    reduce_finish(0)
    reduce_start(1)
    place_windows(rows_held, device, out, ext0, 0, 3)
    small_finish(2)
    small_start(3)
    reduce_finish(1)
    reduce_start(2)
    place_windows(rows_held, device, out, ext0, 3, SLOTS)
    halos0 = halo(halo_base + 2, ext0, below0, above0)
    halo_start(halos0)
    small_finish(3)
    small_start(4)
    reduce_finish(2)
    for halver, land in zip(halvers, landings, strict=True):
        halver.extras(held, land)
        start, length = halver.final
        packed[rows_at(start, length), :] = held[rows_at(start, length), :]
    hand_start(2)
    for k in range(4, len(ring)):
        small_finish(k)
        if k + 1 < len(ring):
            small_start(k + 1)
    halo_finish(halos1, ext1, below1, above1, input_grad)
    hand_finish(2)
    hand_start(1)
    hand_finish(1)
    hand_start(0)
    halo_finish(halos0, ext0, below0, above0, output)
    hand_finish(0)


def tail(rows_held, images, *operands):
    width = operands[0].shape[1]
    packed = operands[2].shape
    tokens = rows_held * GRID
    bits = images.bit_length() - 1
    landing = 2 * Halver.landing_rows(images, packed[0] // 2)
    copies = 1 + 2 * Halver.copies(images) + 4 + 2 * (2 + bits)
    ext = ((rows_held + LEFT + RIGHT) * GRID, width)
    outs = [
        of((tokens, width)), of((tokens, width)), of(packed),
        of((32, width), single), of((32, LANES), single),
    ]
    return pl.pallas_call(
        functools.partial(tail_kernel, rows_held, images),
        out_shape=outs,
        in_specs=[pl.BlockSpec(memory_space=pltpu.VMEM)] * (len(operands) - 1) + [ANY],
        out_specs=[pl.BlockSpec(memory_space=pltpu.VMEM)] * len(outs),
        scratch_shapes=[
            pltpu.VMEM(ext, narrow),
            pltpu.VMEM(ext, narrow),
            pltpu.VMEM((LEFT * GRID, width), narrow),
            pltpu.VMEM((LEFT * GRID, width), narrow),
            pltpu.VMEM((RIGHT * GRID, width), narrow),
            pltpu.VMEM((RIGHT * GRID, width), narrow),
            pltpu.VMEM(packed, narrow),
            pltpu.VMEM((landing, width), narrow),
            pltpu.VMEM(packed, narrow),
            pltpu.VMEM((2 + bits, 32, width), single),
            pltpu.VMEM((2 + bits, 32, LANES), single),
            pltpu.SemaphoreType.DMA((copies,)),
            pltpu.SemaphoreType.DMA((copies,)),
        ],
        compiler_params=pltpu.CompilerParams(
            vmem_limit_bytes=VMEM, collective_id=3, has_side_effects=True
        ),
        cost_estimate=pl.CostEstimate(
            flops=4_000_000_000, bytes_accessed=20_000_000, transcendentals=0
        ),
        name="tail",
    )(*operands)


def shards(
    inputs,
    w_qkv,
    qv_bias,
    w_proj,
    proj_bias,
    w_fc1,
    fc1_bias,
    w_fc2,
    fc2_bias,
    norm1_gain,
    norm1_shift,
    norm2_gain,
    norm2_shift,
    rel_h,
    rel_w,
    cotangent,
):
    width = inputs.shape[2]
    rows = inputs.shape[1] // GRID
    local = w_qkv.shape[2]
    heads = local // HD
    device = lax.axis_index("tensor")
    tables = lane_tables()

    block = jnp.zeros((2, 32, HD), narrow)
    block = block.at[0, : 2 * WIN - 1].set(rel_h[::-1]).at[1, : 2 * WIN - 1].set(rel_w[::-1])
    block = block.reshape(HD, HD).T
    wrel = jnp.zeros((LANES, LANES), narrow).at[:HD, HD:].set(block).at[HD:, :HD].set(block)

    pack = jnp.concatenate([w_qkv.transpose(0, 2, 1), w_proj[None]])
    small = jnp.zeros((8, fc1_bias.shape[0]), single).at[0].set(fc1_bias)
    for j in range(2):
        small = small.at[1 + 2 * j, :local].set(qv_bias[j])
        small = small.at[2 + 2 * j, local : 2 * local].set(qv_bias[j])
    norm1 = (norm1_gain[None], norm1_shift[None])

    (
        xs, gs, n1, qkv, mixed, attn, peak,
        weights, across1, across2, beside1, beside2, smalls,
    ) = forward(inputs[0], cotangent[0], pack, w_fc1, w_fc2, small, norm1, wrel, tables)
    out, dx1, da, sums2, near1, near2, far1, far2, rest, fc_bias = mlp(
        (
            xs, attn, gs, proj_bias[None], norm2_gain[None], norm2_shift[None], fc2_bias[None],
            smalls,
        ),
        (across1, across2),
        (beside1, beside2),
        (w_fc1, w_fc2),
    )
    images = lax.axis_size("dp")
    back, sums1, keep, give, bias, rel_sum, crossed, summed1, summed2 = backward(
        rows, images, da, n1, qkv, mixed, weights, wrel, tables,
        [xs, dx1, norm1_gain[None], near1, near2, far1, far2], rest,
    )
    output, input_grad, gpack, totals, tops = tail(
        rows, images, out, back, keep, crossed, sums1, sums2, bias, rel_sum, fc_bias, peak, give
    )

    gpack = gpack.astype(single)
    blocks = totals[8:24].reshape(2, 8, 6, LANES).transpose(0, 2, 1, 3).reshape(-1, LANES)[:HD, :HD]
    grad_rel = jnp.stack([blocks[: 2 * WIN - 1][::-1], blocks[32 : 32 + 2 * WIN - 1][::-1]])
    qv = lax.dynamic_slice_in_dim(totals, 28 + device, 1)[0].reshape(2, 2 * local)[:, :local]
    head_max = lax.dynamic_slice(tops, (8 * device, 0), (heads, 1))[:, 0]
    factor = jnp.sqrt(CLIP / jnp.maximum(head_max, CLIP))
    clipped_qk = (w_qkv[:2].astype(single) * jnp.repeat(factor, HD)).astype(narrow)

    return (
        output[None],
        input_grad[None],
        gpack[: 3 * local].reshape(3, local, width).transpose(0, 2, 1),
        qv,
        gpack[3 * local :],
        totals[4],
        summed1.astype(single),
        lax.dynamic_slice_in_dim(totals, 24 + device, 1)[0],
        summed2.T.astype(single),
        totals[5],
        totals[:4],
        grad_rel,
        clipped_qk,
        head_max,
    )


def solution(mesh):
    return jax.shard_map(
        shards,
        mesh=mesh,
        in_specs=(
            P("dp", "tensor", None),
            P(None, None, "tensor"),
            P(None, "tensor"),
            P("tensor", None),
            P(),
            P(None, "tensor"),
            P("tensor"),
            P("tensor", None),
            P(),
            P(),
            P(),
            P(),
            P(),
            P(),
            P(),
            P("dp", "tensor", None),
        ),
        out_specs=(
            P("dp", "tensor", None),
            P("dp", "tensor", None),
            P(None, None, "tensor"),
            P(None, "tensor"),
            P("tensor", None),
            P(),
            P(None, "tensor"),
            P("tensor"),
            P("tensor", None),
            P(),
            P(),
            P(),
            P(None, None, "tensor"),
            P("tensor"),
        ),
        check_vma=False,
    )
```

time: 1600 us -> 374 us (0.23); the launches traced: 1580 us -> 374 us
  local copies, waits for them, and re-layouts: 590 us -> 26.7 us
  waiting for transfers between devices: 486 us -> 0 us
  Pallas kernels: 0 us -> 340 us
  matrix products: 241 us -> 0 us
  other arithmetic: 163 us -> 6.44 us
  blocking collectives: 83.5 us -> 0 us
    pallas_call x0 -> x4, Pallas kernels: none -> 340 us  [the longest x1 103 us: backward(): pl.pallas_call(functools.partial(backward_kernel, rows_held, images), out...]
    add x9 -> x0, local copies, waits for them, and re-layouts: 274 us -> none  [the longest x6 266 us: scores_of(): logits.reshape(count, groups, WIN, WIN, WIN, WIN) + rel_rows[..., :, None]]
    dot_general x28 -> x0, matrix products: 241 us -> none  [the longest x1 36.9 us: shards(): jnp.einsum('btd,fd->btf', out_full, w_fc2, preferred_element_type=single)]
    all_gather x4 -> x0, waiting for transfers between devices: 177 us -> none  [the longest x1 46.6 us: shards(): lax.all_gather(first.astype(narrow), 'tensor', axis=1, tiled=True)]
    psum x1 -> x0, waiting for transfers between devices: 156 us -> none  [shards(): lax.psum((grad_qkv, grad_qv_bias, grad_proj, grad_fc1, grad_fc1_bias, gra...]
    reduce_scatter x4 -> x0, waiting for transfers between devices: 152 us -> none  [the longest x1 58.1 us: shards(): lax.psum_scatter(attn_terms.astype(jnp.bfloat16), 'tensor', scatter_dimen...]
    reduce_sum x9 -> x0, other arithmetic: 126 us -> none  [the longest x1 94.8 us: shards(): grad_rows = jnp.sum(grad_grid, axis=5, dtype=single)]
    reshape x10 -> x1, local copies, waits for them, and re-layouts: 105 us -> 0.09 us  [shards(): block = block.reshape(HD, HD).T]
  transfers between devices with their start and end apart: 9 -> 0, of which waited for: 8 -> 0; matrix products, arithmetic and copies ran while one was open for 6% -> 0% of each run, Pallas kernels for 0% -> 0%
where the time goes in v4:
time: 374 us
  Pallas kernels  340 us (91%)
  local copies, waits for them, and re-layouts  26.7 us (7%)
  other arithmetic  6.44 us (2%)
    pallas_call x1, Pallas kernels, backward(): pl.pallas_call(functools.partial(backward_kernel, rows_held, images), out...  103 us
    pallas_call x1, Pallas kernels, forward(): pl.pallas_call(forward_kernel, out_shape=[o[0] for o in outs], grid=(2 *...  88.8 us
    pallas_call x1, Pallas kernels, mlp(): pl.pallas_call(mlp_kernel, out_shape=[o[0] for o in outs], grid=(SPLIT *...  88.7 us
    pallas_call x1, Pallas kernels, tail(): pl.pallas_call(functools.partial(tail_kernel, rows_held, images), out_sha...  59.4 us

profile of v4, /device:TPU:0, one launch (start us, length us, event | category | flops | bytes accessed | tf_op | source)
XLA Modules:
  0.0 373.7 jit_solution(3472244402428600820)
XLA Ops:
  0.6 0.8 fusion.1
  1.4 0.7 reshape.301
  3.5 0.7 rev.12
  4.2 0.7 rev.13
  5.2 0.7 and_reduce_fusion
  5.8 0.7 broadcast_select_fusion
  6.5 0.6 fusion.2
  7.1 2.1 scatter.41
  9.6 1.3 broadcast_in_dim.37.gain
  10.9 2.4 pad_maximum_fusion.pack
  13.3 0.6 broadcast_in_dim.38.shift
  13.9 88.8 %attention_forward.1 = (bf16[1248,768]{1,0:T(8,128)(2,1)}, bf16[1248,768]{1,0:T(8,128)(2,1)}, bf16[7,208,768]{2,1,0:T(8,128)(2,1)}, bf16[14,4,208,384]{3,2,1,0:T...) custom-call(bf16[1024,768]{1,0:T(8,128)(2,1)} %bitcast.37, ...), custom_call_target="tpu_custom_call" | custom-call | flops 25999998976 | bytes 60000000 | tf_op jit(solution)/shard_map/attention_forward/pallas_call | solution.py:520
  102.7 0.6 broadcast_in_dim.40.pbias
  103.3 0.6 broadcast_in_dim.41.gain
  103.9 0.6 broadcast_in_dim.42.shift
  105.0 88.7 %mlp.1 = (bf16[1248,768]{1,0:T(8,128)(2,1)}, f32[1248,768]{1,0:T(8,128)}, bf16[1248,768]{1,0:T(8,128)(2,1)}, f32[8,768]{1,0:T(8,128)}, bf16[768,768]{1,0:T(8,128...) custom-call(bf16[1248,768]{1,0:T(8,128)(2,1)} %get-tuple-element.159, ...), custom_call_target="tpu_custom_call" | custom-call | flops 35999997952 | bytes 60000000 | tf_op jit(solution)/shard_map/mlp/pallas_call | solution.py:742
  193.8 102.8 %attention_backward.1 = (bf16[1248,768]{1,0:T(8,128)(2,1)}, f32[8,768]{1,0:T(8,128)}, bf16[768,768]{1,0:T(8,128)(2,1)}, bf16[768,768]{1,0:T(8,128)(2,1)}, f32[2,...) custom-call(bf16[1248,768]{1,0:T(8,128)(2,1)} %get-tuple-element.168, ...), custom_call_target="tpu_custom_call" | custom-call | flops 51999997952 | bytes 80000000 | tf_op jit(solution)/shard_map/attention_backward/pallas_call | solution.py:998
  296.6 59.4 %tail.1 = (bf16[1024,768]{1,0:T(8,128)(2,1)}, bf16[1024,768]{1,0:T(8,128)(2,1)}, bf16[768,768]{1,0:T(8,128)(2,1)}, f32[32,768]{1,0:T(8,128)}, f32[32,128]{1,0:T(8,128)}) custom-call(bf16[1248,768]{1,0:T(8,128)(2,1)} %get-tuple-element.167.out, bf16[1248,768]{1,0:T(8,128)(2,1)} %get-tuple-element.179.back, bf16[768,768]{1,0:T(8,128)(2,1)} %get-tuple-element.180.keep, ...), custom_call_target="tpu_custom_call" | custom-call | flops 4000000000 | bytes 20000000 | tf_op jit(solution)/shard_map/tail/pallas_call | solution.py:1219
  356.0 0.8 slice.240
  356.8 0.6 copy.39
  357.5 2.6 slice.244
  360.0 0.9 dynamic-slice_reduce_fusion.2
  361.1 1.0 multiply_convert_fusion
  362.1 0.9 slice.246
  363.2 2.0 copy.38
  365.1 1.4 slice_reduce_fusion
  366.6 0.6 slice.245
  367.1 1.3 slice.239
  368.5 1.6 convert_element_type.19
  370.6 1.1 copy.49
  371.8 0.8 copy-done.2
  372.6 1.1 copy.50
  (48 shorter events, 3.5 us)
Async XLA Ops:
  3.5 9.8 %copy-start.7 = (f32[8,768]{1,0:T(8,128)}, f32[8,768]{1,0:T(8,128)S(1)}, u32[]{:S(2)}) copy-start(f32[8,768]{1,0:T(8,128)S(1)} %scatter.36.small) | copy-start | bytes 73732
  9.6 3.7 copy-start.6
  10.9 2.4 copy-start.8
  13.8 88.9 %copy-start.9 = (f32[768]{0:T(1024)S(1)}, f32[768]{0:T(1024)}, u32[]{:S(2)}) copy-start(f32[768]{0:T(1024)} %param.42) | copy-start | bytes 9220
  13.8 89.5 %copy-start.10 = (f32[768]{0:T(1024)S(1)}, f32[768]{0:T(1024)}, u32[]{:S(2)}) copy-start(f32[768]{0:T(1024)} %param.49) | copy-start | bytes 9220
  13.9 90.0 %copy-start.11 = (f32[768]{0:T(1024)S(1)}, f32[768]{0:T(1024)}, u32[]{:S(2)}) copy-start(f32[768]{0:T(1024)} %param.50) | copy-start | bytes 9220
  13.9 90.6 %copy-start.12 = (f32[768]{0:T(1024)S(1)}, f32[768]{0:T(1024)}, u32[]{:S(2)}) copy-start(f32[768]{0:T(1024)} %param.46) | copy-start | bytes 9220
  357.5 3.7 copy-start.1
  360.0 2.1 copy-start
  360.9 2.0 copy-start.13
  361.1 1.9 copy-start.5
  363.1 5.3 %copy-start.4 = (bf16[768,768]{1,0:T(8,128)(2,1)S(1)}, bf16[768,768]{1,0:T(8,128)(2,1)}, u32[]{:S(2)}) copy-start(bf16[768,768]{1,0:T(8,128)(2,1)} %get-tuple-element.193) | copy-start | bytes 3538948
  368.5 2.1 copy-start.3
  370.6 2.0 copy-start.2

commit v5 on v4

--- a/solution.py
+++ b/solution.py
@@ -15,9 +15,11 @@
 SPAN = WIN * WIN
 ROWS = 208
 SLOTS = 7
-SLAB = 6 * ROWS
+EDGE = GRID % WIN
+SHORT = EDGE * WIN
+SLAB = (SLOTS - 2) * ROWS + SHORT
+STRIP = SLAB // 6
 SPLIT = 4
-SHORT = 112
 LEFT = 6
 RIGHT = 12
 LANES = 128
@@ -30,13 +32,28 @@
 
 def lane_tables():
     row = np.arange(ROWS)
-    x, y = row // WIN, row % WIN
+    late = np.maximum(row - SHORT, 0)
+    outer = WIN - EDGE
+    orders = (
+        (row // WIN, row % WIN),
+        (
+            np.where(row < SHORT, row // EDGE, late // outer),
+            np.where(row < SHORT, row % EDGE, EDGE + late % outer),
+        ),
+    )
     lane = np.arange(LANES) % 64
     part = lane // 32
     at = lane % 32
-    amount = np.where(part[None, :] == 0, 13 - x[:, None], 13 - y[:, None])
-    amount = np.where((row < SPAN)[:, None], amount, 0)
-    bits = np.stack([(amount >> b) & 1 for b in range(4)]).astype(np.float32)
+    bits, keys = [], []
+    for x, y in orders:
+        amount = np.where(part[None, :] == 0, x[:, None], y[:, None])
+        amount = np.where((row < SPAN)[:, None], amount, 0)
+        bits.append(np.stack([(amount >> b) & 1 for b in range(4)]).astype(np.float32))
+        place = WIN - 1 - np.where(part[None, :] == 0, x[:, None], y[:, None])
+        hot = ((at % 16)[None, :] == place) & ((at % 16) < WIN)[None, :] & (row < SPAN)[:, None]
+        hot = hot.astype(np.float32)
+        hot[SPAN:, lane == 31] = -1e30
+        keys.append(hot)
     lanes = np.zeros((8, LANES), np.float32)
     lanes[0] = at < WIN
     lanes[1] = (at >= 16) & (at < 16 + WIN)
@@ -44,15 +61,11 @@
     sides = np.zeros((16, LANES), np.float32)
     sides[0] = np.arange(LANES) < 64
     sides[1] = np.arange(LANES) >= 64
-    place = np.where(part[None, :] == 0, x[:, None], y[:, None])
-    hot = ((at % 16)[None, :] == place) & ((at % 16) < WIN)[None, :] & (row < SPAN)[:, None]
-    keys = hot.astype(np.float32)
-    keys[SPAN:, lane == 31] = -1e30
     return (
-        jnp.asarray(bits),
+        jnp.asarray(np.stack(bits)),
         jnp.asarray(lanes),
         jnp.asarray(sides, narrow),
-        jnp.asarray(keys, narrow),
+        jnp.asarray(np.stack(keys), narrow),
     )
 
 
@@ -86,42 +99,50 @@
 
 
 def window_fields(rows_held, device, slot):
-    window = device * (SLOTS - 1) + slot
+    first = device * (SLOTS - 1)
+    window = first + slot
     i, j = window // TILES, window % TILES
     last = device // (SPLIT - 1)
     live = slot < SLOTS - 1 + last
     row0 = i * WIN - device * rows_held + LEFT
     high = jnp.minimum(WIN, GRID - i * WIN)
     wide = jnp.minimum(WIN, GRID - j * WIN)
-    tall = jnp.where(last == 1, SLOTS - TILES, SLOTS)
-    offset = ROWS * jnp.minimum(slot, tall) + SHORT * jnp.maximum(slot - tall, 0)
-    return row0, j * WIN, high, wide, offset, live
-
-
-def positions(axis, first_col, high, wide):
-    shape = (ROWS, 1) if axis == 0 else (1, ROWS)
+
+    def short_before(n):
+        return jnp.minimum(n // TILES, TILES - 1) + jnp.maximum(n - TILES * (TILES - 1), 0)
+
+    offset = ROWS * slot - (ROWS - SHORT) * (short_before(window) - short_before(first))
+    return row0, j * WIN, j // (TILES - 1), high * wide, offset, live
+
+
+def positions(axis, count, first_col, kind, inside):
+    shape = (count, 1) if axis == 0 else (1, count)
     row = lax.broadcasted_iota(jnp.int32, shape, axis)
     x = lax.shift_right_logical(row * 4682, 16)
-    y = row - x * WIN
-    valid = (x < high) & (y < wide)
-    return jnp.where(valid, x * GRID + first_col + y, -1), valid
+    plain = x * GRID + (row - x * WIN)
+    x = lax.shift_right_logical(row, EDGE.bit_length() - 1)
+    edge = x * GRID + (row - x * EDGE)
+    token = jnp.where(kind == 1, edge, plain) + first_col
+    return jnp.where(row < inside, token, -1), row < inside
 
 
 def gather_window(source, target):
-    token = lax.broadcasted_iota(jnp.int32, (ROWS, WIN * GRID), 1)
+    token = lax.broadcasted_iota(jnp.int32, (target.shape[0], WIN * GRID), 1)
     choose = jnp.where(token == target, 1.0, 0.0).astype(narrow)
     return dot(choose, source)
 
 
 def shift_left(values, bits):
     for b in range(4):
-        values = jnp.where(bits[b] > 0.5, pltpu.roll(values, LANES - (1 << b), 1), values)
+        taken = bits[b, : values.shape[0]] > 0.5
+        values = jnp.where(taken, pltpu.roll(values, LANES - (1 << b), 1), values)
     return values
 
 
 def shift_right(values, bits):
     for b in range(4):
-        values = jnp.where(bits[b] > 0.5, pltpu.roll(values, 1 << b, 1), values)
+        taken = bits[b, : values.shape[0]] > 0.5
+        values = jnp.where(taken, pltpu.roll(values, 1 << b, 1), values)
     return values
 
 
@@ -167,15 +188,15 @@
 
 
 def add_rows(target, target_at, sources, count):
-    chunk = 48 if count % 48 == 0 else 16
+    chunk = next(c for c in (96, 48, 16) if count % c == 0)
 
     @pl.loop(0, count // chunk)
     def _(c):
         total = None
         for ref, at in sources:
-            value = ref[rows_at(at + c * chunk, chunk), :].astype(single)
+            value = ref[rows_at(at + c * chunk, chunk), :]
             total = value if total is None else total + value
-        target[rows_at(target_at + c * chunk, chunk), :] = total.astype(target.dtype)
+        target[rows_at(target_at + c * chunk, chunk), :] = total
 
 
 HALVINGS = 3
@@ -252,21 +273,27 @@
 
 def attend(n1, valid, weights, qbias, vbias, wrel, bits, lanes, sides, keys, qkv, mixed, peak):
     half = weights.shape[1]
+    count = n1.shape[0]
     query = jnp.where(valid, dot_nt(n1, weights[0]) + qbias, 0.0).astype(narrow)
     key8 = dot_nt(n1, weights[1]).astype(narrow) * jnp.asarray(0.125, narrow)
     value = (dot_nt(n1, weights[2]) + vbias).astype(narrow)
-    qkv[0, 0] = query
-    qkv[0, 1] = key8
-    qkv[0, 2] = value
-    low_lane = lax.broadcasted_iota(jnp.int32, (ROWS, LANES), 1) < 64
+    qkv[0, 0, :count] = query
+    qkv[0, 1, :count] = key8
+    qkv[0, 2, :count] = value
+    if count < ROWS:
+        left = ROWS - count
+        qkv[0, 1, count:] = jnp.zeros((left, half), narrow)
+        qkv[0, 2, count:] = jnp.broadcast_to(vbias, (left, half)).astype(narrow)
+    low_lane = lax.broadcasted_iota(jnp.int32, (count, LANES), 1) < 64
     for pair in range(half // LANES):
         cut = slice(pair * LANES, (pair + 1) * LANES)
-        q, k8, v = query[:, cut], key8[:, cut], value[:, cut]
-        rel = shift_left(dot(q, wrel[...]), bits)
+        q = query[:, cut]
+        k8, v = qkv[0, 1, :, cut], qkv[0, 2, :, cut]
+        rel = shift_left(dot_nt(q, wrel[...]), bits)
         rest = rel - rel.astype(narrow).astype(single)
         rel = rel * lanes[0:1] + pltpu.roll(rest, 16, 1) * lanes[1:2] + lanes[2:3]
         rel = rel.astype(narrow)
-        qkv[0, 3, :, cut] = rel
+        qkv[0, 3, :count, cut] = rel
         pieces = []
         for head in range(2):
             mine, other = sides[head : head + 1], sides[1 - head : 2 - head]
@@ -281,201 +308,275 @@
             probs = jnp.exp(scores - top)
             total = jnp.sum(probs, axis=1, keepdims=True)
             pieces.append(dot(probs.astype(narrow), v) * (1.0 / total))
-        mixed[0, :, cut] = jnp.where(low_lane, pieces[0], pieces[1]).astype(narrow)
-    return dot(mixed[0], weights[3])
-
-
-def halo_copies(send, base, grid, ext, device, rows):
-    top, bottom = LEFT * GRID, RIGHT * GRID
-    held_rows = rows * GRID
-    down = send.remote(
-        base,
-        grid.at[pl.ds(held_rows - top, top), :],
-        ext.at[pl.ds(0, top), :],
-        {"tensor": (device + 1) % SPLIT},
-    )
-    up = send.remote(
-        base + 1,
-        grid.at[pl.ds(0, bottom), :],
-        ext.at[pl.ds(top + held_rows, bottom), :],
-        {"tensor": (device + SPLIT - 1) % SPLIT},
-    )
-    return down, up
-
-
-def when_all(*conditions):
-    def run(action):
-        flag = conditions[0]
-        for more in conditions[1:]:
-            flag = jnp.logical_and(flag, more)
-        pl.when(flag)(action)
-
-    return run
+        mixed[0, :count, cut] = jnp.where(low_lane, pieces[0], pieces[1]).astype(narrow)
+    return dot(mixed[0, :count], weights[3])
+
+
+class Halo:
+    def __init__(self, send, base, grid, ext, device, rows):
+        below, above = {"tensor": (device + 1) % SPLIT}, {"tensor": (device + SPLIT - 1) % SPLIT}
+        self.has_below, self.has_above = device < SPLIT - 1, device > 0
+        self.cross_below, self.cross_above = device == 1, device == 2
+
+        def copy(at, first, count, first_col, cols, target_row, place):
+            window = (pl.ds(first, count), pl.ds(first_col, cols), slice(None))
+            return send.remote(
+                at, grid.at[window], ext.at[(pl.ds(target_row, count), *window[1:])], place
+            )
+
+        few, many = 4, 10
+        self.down = copy(base, rows - LEFT, LEFT, 0, GRID, 0, below)
+        self.down_cross = copy(base, rows - few, few, 16, GRID - 16, LEFT - few, below)
+        self.up = copy(base + 1, 0, RIGHT, 0, GRID, LEFT + rows, above)
+        self.up_cross = copy(base + 1, 0, many, 0, 32, LEFT + rows, above)
+
+    def _each(self, down_here, up_here, act):
+        for here, crossing, plain, crossed in (
+            (*down_here, self.down, self.down_cross),
+            (*up_here, self.up, self.up_cross),
+        ):
+
+            @pl.when(here & jnp.logical_not(crossing))
+            def _():
+                act(plain)
+
+            @pl.when(crossing)
+            def _():
+                act(crossed)
+
+    def _senders(self, act):
+        self._each((self.has_below, self.cross_below), (self.has_above, self.cross_above), act)
+
+    def start(self):
+        self._senders(lambda copy: copy.start())
+
+    def wait_send(self):
+        self._senders(lambda copy: copy.wait_send())
+
+    def wait_from_above(self):
+        pl.when(self.has_above & jnp.logical_not(self.cross_above))(self.down.wait_recv)
+        pl.when(self.cross_above)(self.down_cross.wait_recv)
+
+    def wait_from_below(self):
+        pl.when(self.has_below & jnp.logical_not(self.cross_below))(self.up.wait_recv)
+        pl.when(self.cross_below)(self.up_cross.wait_recv)
+
+
+class Quartet:
+    def __init__(self, send, base, image, pieces, across):
+        side, deep = image % 2, (image // 2) % 2
+        beside, behind = {"dp": mate_of(image, 0)}, {"dp": mate_of(image, 1)}
+        mine = 2 * deep + side
+        from_beside, from_behind = 2 * deep + 1 - side, 2 * (1 - deep) + side
+        self.first, self.second, self.third = [], [], []
+        for k, (source, target, view) in enumerate(pieces):
+            at = base + 5 * k
+
+            def copy(number, origin, quarter, part, place):
+                return send.remote(at + number, view(origin, quarter, part), view(target, quarter, part), place)
+
+            self.first.append(copy(0, source, mine, None, across))
+            self.second.append(copy(1, target, mine, None, beside))
+            self.second.append(copy(2, target, mine, None, behind))
+            if view(target, from_behind, 0) is not None:
+                self.third.append(copy(3, target, from_behind, 0, beside))
+            self.third.append(copy(4, target, from_beside, 1, behind))
+
+
+def quarter_rows(array, quarter, part):
+    size = array.shape[0] // 4
+    start = quarter * size
+    if part is not None:
+        size //= 2
+        start += part * size
+    return array.at[rows_at(start, size), :]
+
+
+def start_all(copies):
+    for copy in copies:
+        copy.start()
+
+
+def receive_all(copies):
+    for copy in copies:
+        copy.wait_recv()
 
 
 def forward_kernel(
-    x, g, pack, fc1, fc2, small, gain, shift, wrel, bits, lanes, sides, keys,
+    x, g, wqkv, wproj, fc1, fc2, notes_in, params, wrel, bits, lanes, sides, keys,
     xs, gs, n1_all, qkv, mixed, attn, peak, weights_out, across1, across2, beside1, beside2, small_out,
     xext, gext, weights, smalls, sends, recvs, locals_,
 ):
     step = pl.program_id(0)
     far, slot = step // SLOTS, step % SLOTS
     device, image = lax.axis_index("tensor"), lax.axis_index("dp")
-    tokens, width = x.shape
-    rows = tokens // GRID
-    part = pack.shape[1]
+    rows, _, width = x.shape
+    part = wproj.shape[0]
     half = 2 * part
     beside, across, corner = partners(device)
-    side = image % 2
-    mate = {"dp": mate_of(image, 0)}
     send = Sender(sends, recvs, locals_)
-    first, last = device > 0, device < SPLIT - 1
-
-    def cut(array, halves, index):
-        size = array.shape[0] // halves
-        return array.at[rows_at(index * size, size), :]
-
-    x_down, x_up = halo_copies(send, 0, x, xext, device, rows)
-    g_down, g_up = halo_copies(send, 2, g, gext, device, rows)
-    own_pack = send.remote(4, pack, weights.at[0, :, pl.ds(part, part), :], {"tensor": beside})
+    x_halo = Halo(send, 0, x, xext, device, rows)
+    g_halo = Halo(send, 2, g, gext, device, rows)
+    small = notes_in.at[pl.ds(0, 8), :]
+
+    own_pack = [
+        send.remote(4, wqkv, weights.at[0, 0:3, pl.ds(part, part), :], {"tensor": beside}),
+        send.remote(5, wproj, weights.at[0, 3, pl.ds(part, part), :], {"tensor": beside}),
+    ]
     notes = [
-        send.remote(5 + k, small, smalls.at[k + 1], {"tensor": place})
+        send.remote(6 + k, small, smalls.at[k + 1], {"tensor": place})
         for k, place in enumerate((beside, across, corner))
     ]
-    taken = pl.ds(pl.multiple_of(side * (part // 2), 16), part // 2)
-    awaited = pl.ds(pl.multiple_of((1 - side) * (part // 2), 16), part // 2)
-    pack_x = send.remote(8, pack.at[:, taken, :], weights.at[1, :, taken, :], {"tensor": across})
-    pack_y = send.remote(9, weights.at[1, :, taken, :], weights.at[1, :, taken, :], mate)
-
-    def beside_rows(which):
-        half_rows = part // 2
-        start = jnp.where(which == 0, side, 1 - side) * half_rows + part
-        return pl.ds(pl.multiple_of(start, 16), half_rows)
-
-    corner_x = send.remote(
-        10, weights.at[1, :, taken, :], weights.at[1, :, beside_rows(0), :], {"tensor": beside}
+    fc_beside = [
+        send.remote(9, fc1, beside1, {"tensor": beside}),
+        send.remote(10, fc2, beside2, {"tensor": beside}),
+    ]
+    corner_pack = send.remote(
+        11, weights.at[1, :, pl.ds(0, part), :], weights.at[1, :, pl.ds(part, part), :], {"tensor": beside}
     )
-    corner_y = send.remote(
-        11, weights.at[1, :, awaited, :], weights.at[1, :, beside_rows(1), :], {"tensor": beside}
+
+    def of_qkv(array, quarter, half_of):
+        size = part // 4
+        cut = rows_at(quarter * size, size)
+        if array is wqkv:
+            return array.at[:, cut, :]
+        if half_of is None:
+            return array.at[1, 0:3, cut, :]
+        return array.at[1, 0:2, cut, :] if half_of == 0 else array.at[1, 2:3, cut, :]
+
+    def of_proj(array, quarter, half_of):
+        size = part // 4
+        cut = rows_at(quarter * size, size)
+        if array is wproj:
+            return array.at[cut, :]
+        return None if half_of == 0 else array.at[1, 3, cut, :]
+
+    pack_far = Quartet(
+        send, 12, image, ((wqkv, weights, of_qkv), (wproj, weights, of_proj)), {"tensor": across}
     )
-    fc_beside = [
-        send.remote(12, fc1, beside1, {"tensor": beside}),
-        send.remote(13, fc2, beside2, {"tensor": beside}),
+    fc_far = Quartet(
+        send, 22, image, ((fc1, across1, quarter_rows), (fc2, across2, quarter_rows)), {"tensor": across}
+    )
+    own = [
+        send.local(0, wqkv, weights.at[0, 0:3, pl.ds(0, part), :]),
+        send.local(1, wproj, weights.at[0, 3, pl.ds(0, part), :]),
+        send.local(2, x, xext.at[pl.ds(LEFT, rows)]),
+        send.local(3, small, smalls.at[0]),
     ]
-    fc_x = [
-        send.remote(14 + k, cut(source, 2, side), cut(target, 2, side), {"tensor": across})
-        for k, (source, target) in enumerate(((fc1, across1), (fc2, across2)))
-    ]
-    fc_y = [
-        send.remote(16 + k, cut(target, 2, side), cut(target, 2, side), mate)
-        for k, target in enumerate((across1, across2))
-    ]
-    own = [
-        send.local(0, pack, weights.at[0, :, pl.ds(0, part), :]),
-        send.local(1, x, xext.at[pl.ds(LEFT * GRID, tokens), :]),
-        send.local(2, small, smalls.at[0]),
-    ]
-    g_own = send.local(3, g, gext.at[pl.ds(LEFT * GRID, tokens), :])
-    kept = [send.local(4, weights, weights_out), send.local(5, smalls, small_out)]
+    g_own = send.local(4, g, gext.at[pl.ds(LEFT, rows)])
+    kept = [send.local(5, weights, weights_out), send.local(6, smalls, small_out)]
 
     @pl.when(step == 0)
     def _():
+        for ref in (xext, gext):
+            ref[pl.ds(0, LEFT)] = jnp.zeros((LEFT, GRID, width), narrow)
+            ref[pl.ds(LEFT + rows, RIGHT)] = jnp.zeros((RIGHT, GRID, width), narrow)
+        greet(
+            [{"tensor": place} for place in (beside, across, corner)]
+            + [{"dp": mate_of(image, bit)} for bit in range(2)]
+        )
+        start_all(own_pack + notes + own)
+        x_halo.start()
+        start_all(pack_far.first)
         for ref in (xs, gs, attn, peak):
             ref[...] = jnp.zeros_like(ref)
-        for ref in (xext, gext):
-            ref[pl.ds(0, LEFT * GRID), :] = jnp.zeros((LEFT * GRID, width), narrow)
-            ref[pl.ds(LEFT * GRID + tokens, RIGHT * GRID), :] = jnp.zeros(
-                (RIGHT * GRID, width), narrow
-            )
-        greet([{"tensor": place} for place in (beside, across, corner)] + [mate])
-        own_pack.start()
-        for copy in notes + own:
-            copy.start()
-        pl.when(last)(x_down.start)
-        pl.when(first)(x_up.start)
-        pack_x.start()
-        for copy in own + notes + [own_pack]:
+        for copy in own + notes + own_pack:
             copy.wait()
-        pl.when(first)(x_down.wait_recv)
+        x_halo.wait_from_above()
 
     @pl.when(step == 1)
     def _():
-        for copy in fc_beside + [g_own]:
-            copy.start()
-
-    when_all(step == 3, last)(x_up.wait_recv)
+        start_all(fc_beside + [g_own])
+
+    @pl.when(step == 2)
+    def _():
+        receive_all(pack_far.first)
+        start_all(pack_far.second)
+        start_all(fc_far.first)
+
+    @pl.when(step == 3)
+    def _():
+        x_halo.wait_from_below()
 
     @pl.when(step == 4)
     def _():
-        pack_x.wait_recv()
-        pack_y.start()
-        corner_x.start()
-        fc_x[0].start()
-        pl.when(last)(g_down.start)
-        pl.when(first)(g_up.start)
+        receive_all(pack_far.second)
+        start_all(pack_far.third)
+
+    @pl.when(step == 5)
+    def _():
+        receive_all(fc_far.first)
+        start_all(fc_far.second)
+        g_halo.start()
+
+    @pl.when(step == 6)
+    def _():
+        receive_all(pack_far.third)
+        corner_pack.start()
 
     @pl.when(step == SLOTS)
     def _():
-        pack_y.wait_recv()
-        corner_y.start()
-        fc_x[1].start()
-        corner_x.wait_recv()
-        corner_y.wait_recv()
-        for copy in kept:
-            copy.start()
-
-    for k, at in ((0, 9), (1, 11)):
-
-        @pl.when(step == at)
+        corner_pack.wait_recv()
+        start_all(kept)
+
+    @pl.when(step == SLOTS + 2)
+    def _():
+        receive_all(fc_far.second)
+        start_all(fc_far.third)
+
+    row0, col0, kind, inside, offset, live = slot_fields(rows)
+    whole_window = inside == SPAN
+    tables = (wrel, bits.at[kind], lanes, sides, keys.at[kind])
+
+    def work(count):
+        place = rows_at(offset, count)
+
+        @pl.when(far == 0)
         def _():
-            fc_x[k].wait_recv()
-            fc_y[k].start()
-
-    row0, col0, high, wide, offset, live = slot_fields(rows)
-
-    @pl.when(live & (far == 0))
-    def _():
-        target, valid = positions(0, col0, high, wide)
-        source = xext[pl.ds(pl.multiple_of(row0 * GRID, GRID), WIN * GRID), :]
-        window = gather_window(source, target)
-        xs[rows_at(offset, ROWS), :] = window.astype(narrow)
-        normal, _ = norm_parts(window)
-        n1_all[slot] = jnp.where(valid, normal * gain[...] + shift[...], 0.0).astype(narrow)
-
-    @pl.when(live)
-    def _():
-        _, valid = positions(0, col0, high, wide)
-        place = rows_at(offset, ROWS)
+            target, valid = positions(0, count, col0, kind, inside)
+            source = xext[pl.ds(row0, WIN)].reshape(WIN * GRID, width)
+            window = gather_window(source, target)
+            xs[place, :] = window.astype(narrow)
+            normal, _ = norm_parts(window)
+            n1 = jnp.where(valid, normal * params[8:9] + params[9:10], 0.0).astype(narrow)
+            n1_all[slot, :count] = n1
+
+        _, valid = positions(0, count, col0, kind, inside)
         qbias = smalls[2 * far, 1:2, :half] + smalls[2 * far + 1, 2:3, :half]
         vbias = smalls[2 * far, 3:4, :half] + smalls[2 * far + 1, 4:5, :half]
         terms = attend(
-            n1_all[slot], valid, weights.at[far], qbias, vbias, wrel, bits, lanes, sides, keys,
+            n1_all[slot, :count], valid, weights.at[far], qbias, vbias, *tables,
             qkv, mixed, peak.at[far],
         )
         attn[place, :] += jnp.where(valid, terms, 0.0)
 
+    pl.when(live & whole_window)(functools.partial(work, ROWS))
+    pl.when(live & jnp.logical_not(whole_window))(functools.partial(work, SHORT))
+
     @pl.when(step == 2 * SLOTS - 1)
     def _():
         g_own.wait()
-        for down, up in ((x_down, x_up), (g_down, g_up)):
-            pl.when(last)(down.wait_send)
-            pl.when(first)(up.wait_send)
-        pl.when(first)(g_down.wait_recv)
-        pl.when(last)(g_up.wait_recv)
+        g_halo.wait_from_above()
+        g_halo.wait_from_below()
 
         @pl.loop(0, SLOTS)
         def _(slot):
-            row0, col0, high, wide, offset, live = window_fields(rows, device, slot)
+            row0, col0, kind, inside, offset, live = window_fields(rows, device, slot)
 
             @pl.when(live)
             def _():
-                target, _ = positions(0, col0, high, wide)
-                source = gext[pl.ds(pl.multiple_of(row0 * GRID, GRID), WIN * GRID), :]
+                target, _ = positions(0, ROWS, col0, kind, inside)
+                source = gext[pl.ds(row0, WIN)].reshape(WIN * GRID, width)
                 gs[rows_at(offset, ROWS), :] = gather_window(source, target).astype(narrow)
 
-        for copy in (pack_x, pack_y, corner_x, corner_y, *fc_x):
+        for halo in (x_halo, g_halo):
+            halo.wait_send()
+        for group in (pack_far, fc_far):
+            for copy in group.first + group.second:
+                copy.wait_send()
+        for copy in pack_far.third + [corner_pack]:
             copy.wait_send()
-        for copy in kept + fc_beside + fc_y:
+        for copy in kept + fc_beside + fc_far.third:
             copy.wait()
 
 
@@ -496,9 +597,9 @@
     return jax.ShapeDtypeStruct(shape, dtype)
 
 
-def forward(x, g, pack, fc1, fc2, small, norm, wrel, tables):
-    tokens, width = x.shape
-    half = 2 * pack.shape[1]
+def forward(x, g, wqkv, wproj, fc1, fc2, params, wrel, tables):
+    rows, _, width = x.shape
+    half = 2 * wproj.shape[0]
     slab = (SLAB, width)
     outs = [
         (of(slab), whole(slab)),
@@ -513,24 +614,24 @@
         (of(fc2.shape), ANY),
         (of(fc1.shape), ANY),
         (of(fc2.shape), ANY),
-        (of((SPLIT,) + small.shape, single), ANY),
+        (of((SPLIT, 8, width), single), ANY),
     ]
-    operands = (x, g, pack, fc1, fc2, small, *norm, wrel, *tables)
-    ext = (tokens + (LEFT + RIGHT) * GRID, width)
+    operands = (x, g, wqkv, wproj, fc1, fc2, params, params, wrel, *tables)
+    ext = (rows + LEFT + RIGHT, GRID, width)
     return pl.pallas_call(
         forward_kernel,
         out_shape=[o[0] for o in outs],
         grid=(2 * SLOTS,),
-        in_specs=[ANY] * 6 + [whole(a.shape) for a in operands[6:]],
+        in_specs=[ANY] * 7 + [whole(a.shape) for a in operands[7:]],
         out_specs=[o[1] for o in outs],
         scratch_shapes=[
             pltpu.VMEM(ext, narrow),
             pltpu.VMEM(ext, narrow),
             pltpu.VMEM((2, 4, half, width), narrow),
-            pltpu.VMEM((SPLIT,) + small.shape, single),
-            pltpu.SemaphoreType.DMA((18,)),
-            pltpu.SemaphoreType.DMA((18,)),
-            pltpu.SemaphoreType.DMA((6,)),
+            pltpu.VMEM((SPLIT, 8, width), single),
+            pltpu.SemaphoreType.DMA((32,)),
+            pltpu.SemaphoreType.DMA((32,)),
+            pltpu.SemaphoreType.DMA((7,)),
         ],
         compiler_params=pltpu.CompilerParams(
             vmem_limit_bytes=VMEM, collective_id=0, has_side_effects=True
@@ -543,7 +644,7 @@
 
 
 BLOCK = 256
-CHUNK = 416
+CHUNK = SLAB // 3
 
 
 def gelu_parts(z):
@@ -560,11 +661,11 @@
 
 
 def mlp_kernel(
-    xs, attn, gs, pbias, gain, shift, fbias, smalls, src1, src2,
+    xs, attn, gs, params, smalls, src1, src2,
     w1_across, w1_beside, w1_own, w2_across, w2_beside, w2_own,
-    out, dx1, da, sums, near1, near2, far1, far2, rest, gb,
+    out, dx1, da, sums, near1, near2, far1, rest, gb,
     n2, n2t, gt, branch, dn2, corner1, corner2, keep1, keep2, give1, give2, got1, got2, near_got1,
-    near_got2, w1, w2, b1, hs, zs, sends, recvs,
+    near_got2, landing, w1, w2, b1, hs, zs, sends, recvs,
 ):
     step = pl.program_id(0)
     count = pl.num_programs(0) // SPLIT
@@ -582,32 +683,33 @@
         send.remote(2, give1, got1, {"tensor": beside}),
         send.remote(3, give2, got2, {"tensor": beside}),
     ]
+    crossing = send.remote(4, got1, far1, {"tensor": across})
+    image = lax.axis_index("dp")
+    mate = {"dp": mate_of(image, 0)}
     upper = got2.shape[0] // 2
-    crossings = [
-        send.remote(4, got1, far1, {"tensor": across}),
-        send.remote(5, got2.at[pl.ds(0, upper), :], far2, {"tensor": across}),
+    mine = (image % 2) * upper
+    halving = send.remote(7, got2.at[rows_at(upper - mine, upper), :], landing, mate)
+    near_swaps = [
+        send.remote(5, corner1, near_got1, {"tensor": beside}),
+        send.remote(6, corner2, near_got2, {"tensor": beside}),
     ]
-    near_swaps = [
-        send.remote(6, corner1, near_got1, {"tensor": beside}),
-        send.remote(7, corner2, near_got2, {"tensor": beside}),
-    ]
 
     @pl.when(step == 0)
     def _():
         gb[...] = jnp.zeros_like(gb)
-        greet([{"tensor": beside}, {"tensor": across}])
+        greet([{"tensor": beside}, {"tensor": across}, mate])
         for copy in corners:
             copy.start()
 
-        @pl.loop(0, SLAB // ROWS)
+        @pl.loop(0, SLAB // STRIP)
         def _(c):
-            sl = rows_at(c * ROWS, ROWS)
-            middle = xs[sl, :].astype(single) + (attn[sl, :] + pbias[...])
+            sl = rows_at(c * STRIP, STRIP)
+            middle = xs[sl, :].astype(single) + (attn[sl, :] + params[10:11])
             dx1[sl, :] = middle
             normal, _ = norm_parts(middle)
-            n2[sl, :] = (normal * gain[...] + shift[...]).astype(narrow)
-            branch[sl, :] = jnp.zeros((ROWS, width), single)
-            dn2[sl, :] = jnp.zeros((ROWS, width), single)
+            n2[sl, :] = (normal * params[11:12] + params[12:13]).astype(narrow)
+            branch[sl, :] = jnp.zeros((STRIP, width), single)
+            dn2[sl, :] = jnp.zeros((STRIP, width), single)
 
         for j in range(width // LANES):
             lanes = slice(j * LANES, (j + 1) * LANES)
@@ -655,13 +757,12 @@
 
     @pl.when(step == 2 * count)
     def _():
-        for copy, got, keep, crossing in zip(
-            swaps, (got1, got2), (keep1, keep2), crossings, strict=True
-        ):
-            copy.wait()
-            add_rows(got, 0, [(got, 0), (keep, 0)], got.shape[0])
-            crossing.start()
-        rest[...] = got2[pl.ds(upper, upper), :]
+        swaps[0].wait()
+        add_rows(got1, 0, [(got1, 0), (keep1, 0)], got1.shape[0])
+        crossing.start()
+        swaps[1].wait()
+        add_rows(got2, 0, [(got2, 0), (keep2, 0)], got2.shape[0])
+        halving.start()
 
     for k, (first, second) in enumerate(
         ((keep1, keep2), (give1, give2), (corner1, corner2), (near1, near2))
@@ -680,6 +781,11 @@
         for copy in near_swaps:
             copy.start()
 
+    @pl.when(step == 3 * count)
+    def _():
+        halving.wait()
+        add_rows(rest, 0, [(got2, mine), (landing, 0)], upper)
+
     @pl.when(step == 4 * count - 1)
     def _():
         for copy, near, got in zip(
@@ -689,15 +795,15 @@
             add_rows(near, 0, [(near, 0), (got, 0)], near.shape[0])
         sums[...] = jnp.zeros_like(sums)
 
-        @pl.loop(0, SLAB // ROWS)
+        @pl.loop(0, SLAB // STRIP)
         def _(c):
-            sl = rows_at(c * ROWS, ROWS)
+            sl = rows_at(c * STRIP, STRIP)
             middle = dx1[sl, :]
             normal, inverse = norm_parts(middle)
-            out[sl, :] = (middle + (branch[sl, :] + fbias[...])).astype(narrow)
+            out[sl, :] = (middle + (branch[sl, :] + params[13:14])).astype(narrow)
             grad = dn2[sl, :]
             cot = gs[sl, :].astype(single)
-            total = cot + norm_back(grad, normal, inverse, gain[...])
+            total = cot + norm_back(grad, normal, inverse, params[11:12])
             dx1[sl, :] = total
             low = total.astype(narrow)
             da[sl, :] = low
@@ -706,8 +812,7 @@
             sums[2:3, :] += jnp.sum(low.astype(single), axis=0, keepdims=True)
             sums[3:4, :] += jnp.sum(cot, axis=0, keepdims=True)
 
-        for copy in crossings:
-            copy.wait()
+        crossing.wait()
 
 
 def mlp(residents, across, beside, own):
@@ -734,8 +839,7 @@
         (of(square), whole(square)),
         (of(square), whole(square)),
         (of(square), ANY),
-        (of((width // 2, local)), ANY),
-        (of((width // 2, local)), whole((width // 2, local))),
+        (of((local // 2, width)), whole((local // 2, width))),
         (of((SPLIT, 8, local), single), whole((SPLIT, 8, local))),
     ]
     flipped = pltpu.VMEM((width, SLAB), narrow)
@@ -752,6 +856,7 @@
             pltpu.VMEM(slab, single),
             pltpu.VMEM(slab, single),
             *[pltpu.VMEM(square, narrow)] * 10,
+            pltpu.VMEM((width // 2, local), narrow),
             pltpu.VMEM((width, BLOCK), narrow),
             pltpu.VMEM((BLOCK, width), narrow),
             pltpu.VMEM((1, BLOCK), single),
@@ -772,7 +877,7 @@
 
 def backward_kernel(
     rows_held, images,
-    da, n1, qkv, mixed, weights, wrel, bits, lanes, sides, keys, xs, dx1, gain, near1, near2, far1, far2, rest,
+    da, n1, qkv, mixed, weights, wrel, bits, lanes, sides, keys, xs, dx1, params, near1, near2, far1, rest,
     back, sums, keep, give, bias, grel, crossed, summed1, summed2,
     acc, dqkv, dmix, dn1, keep_far, give_far, got_far, held1, held2, land1, land2, rest_got,
     sends, recvs, locals_,
@@ -784,12 +889,14 @@
     send = Sender(sends, recvs, locals_)
     half, width = weights.shape[2:]
     per = Halver.copies(images)
-    sum1 = Halver(send, 3, image, images, 0, held1.shape[0], (0, 1, 2))
+    sum1 = Halver(send, 3, image, images, 0, held1.shape[0], (1, 0, 2))
     sum2 = Halver(send, 3 + per, image, images, 0, held2.shape[0], (0, 1, 2))
     rest_cross = send.remote(0, rest, rest_got, {"tensor": across})
     far_swap = send.remote(1, give_far, got_far, {"tensor": beside})
     far_cross = send.remote(2, got_far, crossed, {"tensor": across})
-    upper = held2.shape[0] - rest_got.shape[0]
+
+    halvers = ((sum1, held1, land1), (sum2, held2, land2))
+    summed = (summed1, summed2)
 
     def seed(k, halver, held, summed):
         start, length = halver.final
@@ -800,71 +907,53 @@
     def begin():
         greet([{"tensor": beside}, {"tensor": across}] + dp_mates(image, images))
         rest_cross.start()
+        sum2.start(0, near2, land2)
         add_rows(held1, 0, [(near1, 0), (far1, 0)], held1.shape[0])
         sum1.start(0, held1, land1)
 
     def second():
-        add_rows(held2, 0, [(near2, 0), (far2, 0)], upper)
-        rest_cross.wait()
-        add_rows(held2, upper, [(near2, upper), (rest_got, 0)], rest_got.shape[0])
-
-    def third():
         sum1.finish(0, held1, land1)
         sum1.start(1, held1, land1)
-        sum2.start(0, held2, land2)
+        sum2.out(0, near2, land2).wait()
+        rest_cross.wait()
+        _, kept, _, length, at = sum2.stages[0]
+        add_rows(held2, kept, [(near2, kept), (land2, at), (rest_got, 0)], length)
+        sum2.start(1, held2, land2)
+
+    def third():
+        for halver, held, land in halvers:
+            halver.finish(1, held, land)
+            halver.start(2, held, land)
 
     def fourth():
-        sum1.finish(1, held1, land1)
-        sum1.start(2, held1, land1)
-
-    def fifth():
-        sum2.finish(0, held2, land2)
-        sum2.start(1, held2, land2)
-        sum1.finish(2, held1, land1)
-        sum1.extras(held1, land1)
-        seed(0, sum1, held1, summed1)
-        sum1.back(2, summed1).start()
-
-    def sixth():
+        for n, (halver, held, land) in enumerate(halvers):
+            halver.finish(2, held, land)
+            halver.extras(held, land)
+            seed(n, halver, held, summed[n])
+            halver.back(2, summed[n]).start()
+
+    def hand(stage):
+        for (halver, _, _), total in zip(halvers, summed, strict=True):
+            halver.back(stage + 1, total).wait()
+            halver.back(stage, total).start()
+
+    def swap_far():
         far_swap.start()
-        sum2.finish(1, held2, land2)
-        sum2.start(2, held2, land2)
-        sum1.back(2, summed1).wait()
-        sum1.back(1, summed1).start()
-
-    def seventh():
+
+    def cross_far():
         far_swap.wait()
         add_rows(got_far, 0, [(got_far, 0), (keep_far, 0)], got_far.shape[0])
         far_cross.start()
 
-    def eighth():
-        sum2.finish(2, held2, land2)
-        sum2.extras(held2, land2)
-        seed(1, sum2, held2, summed2)
-        sum2.back(2, summed2).start()
-        sum1.back(1, summed1).wait()
-        sum1.back(0, summed1).start()
-
-    def ninth():
-        sum2.back(2, summed2).wait()
-        sum2.back(1, summed2).start()
-
-    def tenth():
-        sum2.back(1, summed2).wait()
-        sum1.back(0, summed1).wait()
-        sum2.back(0, summed2).start()
-
     events = {
         (0, 0): begin,
-        (2, 2): second,
-        (3, 1): third,
-        (4, 2): fourth,
-        (5, 3): fifth,
-        (7, 0): sixth,
-        (8, 0): seventh,
-        (8, 2): eighth,
-        (10, 0): ninth,
-        (11, 1): tenth,
+        (3, 0): second,
+        (4, 2): third,
+        (7, 0): swap_far,
+        (7, 1): fourth,
+        (8, 0): cross_far,
+        (9, 2): functools.partial(hand, 1),
+        (11, 0): functools.partial(hand, 0),
     }
 
     def fire(section):
@@ -872,8 +961,12 @@
             if place == section:
                 pl.when(step == at)(event)
 
-    _, col0, high, wide, offset, live = slot_fields(rows_held)
-    place = rows_at(offset, ROWS)
+    _, col0, kind, inside, offset, live = slot_fields(rows_held)
+    whole_window = inside == SPAN
+
+    def on_window(action):
+        for count, holds in ((ROWS, whole_window), (SHORT, jnp.logical_not(whole_window))):
+            pl.when(live & holds)(functools.partial(action, count))
 
     @pl.when(slot == 0)
     def _():
@@ -886,22 +979,21 @@
 
     fire(0)
 
-    @pl.when(live)
-    def _():
-        _, valid = positions(0, col0, high, wide)
-        da_win = jnp.where(valid, da[place, :].astype(single), 0.0).astype(narrow)
-        acc[3] += dot_tn(mixed[0], da_win)
-        dmix[...] = dot_nt(da_win, weights[far, 3]).astype(narrow)
-
-    def one_pair(pair):
-        low_lane = lax.broadcasted_iota(jnp.int32, (ROWS, LANES), 1) < 64
+    def before_pairs(count):
+        da_win = da[rows_at(offset, count), :]
+        acc[3] += dot_tn(mixed[0, :count], da_win)
+        dmix[:count] = dot_nt(da_win, weights[far, 3]).astype(narrow)
+
+    on_window(before_pairs)
+
+    def one_pair(pair, count):
         cut = slice(pair * LANES, (pair + 1) * LANES)
-        q, k8, v, rel = (qkv[0, j, :, cut] for j in range(4))
-        do = dmix[:, cut]
+        q, k8, v, rel = (qkv[0, j, :n, cut] for j, n in enumerate((count, ROWS, ROWS, count)))
+        do = dmix[:count, cut]
         dqs, dks, dvs = [], [], []
         for head in range(2):
             mine, other = sides[head : head + 1], sides[1 - head : 2 - head]
-            full_key = k8 * mine + keys[...] * other
+            full_key = k8 * mine + keys[kind] * other
             scores = dot_nt(full_key, q * mine + rel * other)
             top = jnp.max(scores, axis=0, keepdims=True)
             probs = jnp.exp(scores - top)
@@ -912,44 +1004,49 @@
             dvs.append(dot(probs.astype(narrow), do))
             dks.append(dot(dscores, q))
             dqs.append(dot_tn(dscores, full_key))
+        low_lane = lax.broadcasted_iota(jnp.int32, (ROWS, LANES), 1) < 64
         dv = jnp.where(low_lane, dvs[0], dvs[1])
         dk = jnp.where(low_lane, dks[0], dks[1]) * 0.125
+        low_lane = lax.broadcasted_iota(jnp.int32, (count, LANES), 1) < 64
         dq = jnp.where(low_lane, dqs[0], dqs[1])
         drel = jnp.where(low_lane, dqs[1], dqs[0]) * lanes[0:1]
-        drel = shift_right(drel, bits).astype(narrow)
-        dq = dq + dot_nt(drel, wrel[...])
+        drel = shift_right(drel, bits.at[kind]).astype(narrow)
+        dq = dq + dot(drel, wrel[...])
         grel[...] += dot_tn(drel, q)
-        dqkv[0, :, cut] = dq.astype(narrow)
+        dqkv[0, :count, cut] = dq.astype(narrow)
         dqkv[1, :, cut] = dk.astype(narrow)
         dqkv[2, :, cut] = dv.astype(narrow)
 
     for pair in range(half // LANES):
         fire(pair + 1)
-        pl.when(live)(functools.partial(one_pair, pair))
-
-    @pl.when(live)
-    def _():
+        on_window(functools.partial(one_pair, pair))
+
+    def after_pairs(count):
         total = None
         for j in range(3):
-            piece = dqkv[j]
-            acc[j] += dot_tn(piece, n1[0])
-            bias[far, j : j + 1, :] += jnp.sum(piece.astype(single), axis=0, keepdims=True)
+            piece = dqkv[j, :count]
+            acc[j] += dot_tn(piece, n1[0, :count])
+            every = piece if j == 0 else dqkv[j]
+            bias[far, j : j + 1, :] += jnp.sum(every.astype(single), axis=0, keepdims=True)
             back_part = dot(piece, weights[far, j])
             total = back_part if total is None else total + back_part
 
         @pl.when(far == 1)
         def _():
-            dn1[slot] = total
+            dn1[slot, :count] = total
 
         @pl.when(far == 0)
         def _():
-            _, valid = positions(0, col0, high, wide)
-            grad = jnp.where(valid, total + dn1[slot], 0.0)
+            _, valid = positions(0, count, col0, kind, inside)
+            place = rows_at(offset, count)
+            grad = jnp.where(valid, total + dn1[slot, :count], 0.0)
             normal, inverse = norm_parts(xs[place, :].astype(single))
             sums[0:1, :] += jnp.sum(grad * normal, axis=0, keepdims=True)
             sums[1:2, :] += jnp.sum(grad, axis=0, keepdims=True)
-            result = dx1[place, :] + norm_back(grad, normal, inverse, gain[...])
+            result = dx1[place, :] + norm_back(grad, normal, inverse, params[8:9])
             back[place, :] = jnp.where(valid, result, 0.0).astype(narrow)
+
+    on_window(after_pairs)
 
     def flush(keep, give):
         part = half // 2
@@ -964,7 +1061,8 @@
     @pl.when(step == 2 * SLOTS - 1)
     def _():
         flush(keep, give)
-        sum2.back(0, summed2).wait()
+        for (halver, _, _), total in zip(halvers, summed, strict=True):
+            halver.back(0, total).wait()
         far_cross.wait()
 
 
@@ -1033,11 +1131,11 @@
 def place_windows(rows_held, device, slab, ext, first, last):
     @pl.loop(first, last)
     def _(slot):
-        row0, col0, high, wide, offset, live = window_fields(rows_held, device, slot)
+        row0, col0, kind, inside, offset, live = window_fields(rows_held, device, slot)
 
         @pl.when(live)
         def _():
-            target, _ = positions(1, col0, high, wide)
+            target, _ = positions(1, ROWS, col0, kind, inside)
             token = lax.broadcasted_iota(jnp.int32, (WIN * GRID, ROWS), 0)
             choose = jnp.where(token == target, 1.0, 0.0).astype(narrow)
             window = slab[rows_at(offset, ROWS), :]
@@ -1271,26 +1369,36 @@
     device = lax.axis_index("tensor")
     tables = lane_tables()
 
-    block = jnp.zeros((2, 32, HD), narrow)
-    block = block.at[0, : 2 * WIN - 1].set(rel_h[::-1]).at[1, : 2 * WIN - 1].set(rel_w[::-1])
-    block = block.reshape(HD, HD).T
-    wrel = jnp.zeros((LANES, LANES), narrow).at[:HD, HD:].set(block).at[HD:, :HD].set(block)
-
-    pack = jnp.concatenate([w_qkv.transpose(0, 2, 1), w_proj[None]])
-    small = jnp.zeros((8, fc1_bias.shape[0]), single).at[0].set(fc1_bias)
-    for j in range(2):
-        small = small.at[1 + 2 * j, :local].set(qv_bias[j])
-        small = small.at[2 + 2 * j, local : 2 * local].set(qv_bias[j])
-    norm1 = (norm1_gain[None], norm1_shift[None])
+    span = 2 * WIN - 1
+    wrel = sum(
+        jnp.pad(table, ((at, LANES - span - at), (side, HD - side)))
+        for table, at, side in (
+            (rel_h, HD, 0), (rel_w, HD + 32, 0), (rel_h, 0, HD), (rel_w, 32, HD),
+        )
+    )
+
+    entries = (
+        (fc1_bias, 0, 0), (qv_bias[0], 1, 0), (qv_bias[0], 2, local), (qv_bias[1], 3, 0),
+        (qv_bias[1], 4, local), (norm1_gain, 8, 0), (norm1_shift, 9, 0), (proj_bias, 10, 0),
+        (norm2_gain, 11, 0), (norm2_shift, 12, 0), (fc2_bias, 13, 0),
+    )
+    params = 0.0
+    for values, row, at in entries:
+        before = row * width + at
+        params = params + jnp.pad(values, (before, 16 * width - before - values.shape[0]))
+    params = params.reshape(16, width)
+    wqkv = w_qkv.transpose(0, 2, 1)
 
     (
         xs, gs, n1, qkv, mixed, attn, peak,
         weights, across1, across2, beside1, beside2, smalls,
-    ) = forward(inputs[0], cotangent[0], pack, w_fc1, w_fc2, small, norm1, wrel, tables)
-    out, dx1, da, sums2, near1, near2, far1, far2, rest, fc_bias = mlp(
+    ) = forward(
+        *(a.reshape(rows, GRID, width) for a in (inputs, cotangent)), wqkv, w_proj, w_fc1, w_fc2, params,
+        wrel, tables
+    )
+    out, dx1, da, sums2, near1, near2, far1, rest, fc_bias = mlp(
         (
-            xs, attn, gs, proj_bias[None], norm2_gain[None], norm2_shift[None], fc2_bias[None],
-            smalls,
+            xs, attn, gs, params, smalls,
         ),
         (across1, across2),
         (beside1, beside2),
@@ -1299,7 +1407,7 @@
     images = lax.axis_size("dp")
     back, sums1, keep, give, bias, rel_sum, crossed, summed1, summed2 = backward(
         rows, images, da, n1, qkv, mixed, weights, wrel, tables,
-        [xs, dx1, norm1_gain[None], near1, near2, far1, far2], rest,
+        [xs, dx1, params, near1, near2, far1], rest,
     )
     output, input_grad, gpack, totals, tops = tail(
         rows, images, out, back, keep, crossed, sums1, sums2, bias, rel_sum, fc_bias, peak, give
@@ -1307,7 +1415,7 @@
 
     gpack = gpack.astype(single)
     blocks = totals[8:24].reshape(2, 8, 6, LANES).transpose(0, 2, 1, 3).reshape(-1, LANES)[:HD, :HD]
-    grad_rel = jnp.stack([blocks[: 2 * WIN - 1][::-1], blocks[32 : 32 + 2 * WIN - 1][::-1]])
+    grad_rel = jnp.stack([blocks[: 2 * WIN - 1], blocks[32 : 32 + 2 * WIN - 1]])
     qv = lax.dynamic_slice_in_dim(totals, 28 + device, 1)[0].reshape(2, 2 * local)[:, :local]
     head_max = lax.dynamic_slice(tops, (8 * device, 0), (heads, 1))[:, 0]
     factor = jnp.sqrt(CLIP / jnp.maximum(head_max, CLIP))

time: 374 us -> 330 us (0.88)
  Pallas kernels: 340 us -> 308 us
  local copies, waits for them, and re-layouts: 26.7 us -> 16.4 us
    pallas_call x1, Pallas kernels: 88.8 us -> 70.2 us  [forward(): pl.pallas_call(forward_kernel, out_shape=[o[0] for o in outs], grid=(2 *...]
    pallas_call x1, Pallas kernels: 103 us -> 95.8 us  [backward(): pl.pallas_call(functools.partial(backward_kernel, rows_held, images), out...]
    broadcast_in_dim x7 -> x0, local copies, waits for them, and re-layouts: 4.19 us -> none  [the longest x2 1.86 us: shards(): norm1 = (norm1_gain[None], norm1_shift[None])]
    scatter x9 -> x0, local copies, waits for them, and re-layouts: 3.95 us -> none  [the longest x2 2.46 us: shards(): jnp.zeros((LANES, LANES), narrow).at[:HD, HD:].set(block).at[HD:, :HD]]
where the time goes in v5:
time: 330 us
  Pallas kernels  308 us (93%)
  local copies, waits for them, and re-layouts  16.4 us (5%)
  other arithmetic  5.08 us (2%)
    pallas_call x1, Pallas kernels, backward(): pl.pallas_call(functools.partial(backward_kernel, rows_held, images), out...  95.8 us
    pallas_call x1, Pallas kernels, mlp(): pl.pallas_call(mlp_kernel, out_shape=[o[0] for o in outs], grid=(SPLIT *...  85.3 us
    pallas_call x1, Pallas kernels, forward(): pl.pallas_call(forward_kernel, out_shape=[o[0] for o in outs], grid=(2 *...  70.2 us
    pallas_call x1, Pallas kernels, tail(): pl.pallas_call(functools.partial(tail_kernel, rows_held, images), out_sha...  56.4 us

profile of v5, /device:TPU:0, one launch (start us, length us, event | category | flops | bytes accessed | tf_op | source)
XLA Modules:
  0.0 329.9 jit_solution(7861449789145727065)
XLA Ops:
  0.6 0.8 fusion
  1.4 0.9 pad_add_fusion
  2.3 0.6 reshape.49.notes_in.params
  2.9 1.5 pad_add_fusion.1.wrel
  4.4 70.2 %attention_forward.1 = (bf16[1152,768]{1,0:T(8,128)(2,1)}, bf16[1152,768]{1,0:T(8,128)(2,1)}, bf16[7,208,768]{2,1,0:T(8,128)(2,1)}, bf16[14,4,208,384]{3,2,1,0:T...) custom-call(bf16[16,64,768]{2,1,0:T(8,128)(2,1)} %bitcast.28, ...), custom_call_target="tpu_custom_call" | custom-call | flops 25999998976 | bytes 60000000 | tf_op jit(solution)/shard_map/attention_forward/pallas_call | solution.py:621
  74.6 85.3 %mlp.1 = (bf16[1152,768]{1,0:T(8,128)(2,1)}, f32[1152,768]{1,0:T(8,128)}, bf16[1152,768]{1,0:T(8,128)(2,1)}, f32[8,768]{1,0:T(8,128)}, bf16[768,768]{1,0:T(8,128...) custom-call(bf16[1152,768]{1,0:T(8,128)(2,1)} %get-tuple-element.50., ...), custom_call_target="tpu_custom_call" | custom-call | flops 35999997952 | bytes 60000000 | tf_op jit(solution)/shard_map/mlp/pallas_call | solution.py:846
  159.9 95.8 %attention_backward.1 = (bf16[1152,768]{1,0:T(8,128)(2,1)}, f32[8,768]{1,0:T(8,128)}, bf16[768,768]{1,0:T(8,128)(2,1)}, bf16[768,768]{1,0:T(8,128)(2,1)}, f32[2,...) custom-call(bf16[1152,768]{1,0:T(8,128)(2,1)} %get-tuple-element.59., ...), custom_call_target="tpu_custom_call" | custom-call | flops 51999997952 | bytes 80000000 | tf_op jit(solution)/shard_map/attention_backward/pallas_call | solution.py:1096
  255.7 56.4 %tail.1 = (bf16[1024,768]{1,0:T(8,128)(2,1)}, bf16[1024,768]{1,0:T(8,128)(2,1)}, bf16[768,768]{1,0:T(8,128)(2,1)}, f32[32,768]{1,0:T(8,128)}, f32[32,128]{1,0:T(8,128)}) custom-call(bf16[1152,768]{1,0:T(8,128)(2,1)} %get-tuple-element.58.out, bf16[1152,768]{1,0:T(8,128)(2,1)} %get-tuple-element.69.back, bf16[768,768]{1,0:T(8,128)(2,1)} %get-tuple-element.70.keep, ...), custom_call_target="tpu_custom_call" | custom-call | flops 4000000000 | bytes 20000000 | tf_op jit(solution)/shard_map/tail/pallas_call | solution.py:1317
  312.1 0.8 slice.49
  312.9 0.6 copy.37
  313.5 2.6 slice.53
  316.2 0.9 dynamic-slice_reduce_fusion.2
  317.1 0.1 broadcast_in_dim.11
  317.2 0.1 mul.10
  317.3 0.0 copy-done.5
  317.3 1.0 multiply_convert_fusion
  318.2 0.0 copy-done
  318.2 0.9 slice.55
  319.1 0.0 copy-done.4
  319.1 0.2 convert_bitcast_fusion
  319.3 0.0 copy-done.6
  319.3 0.0 copy-start.3
  319.3 2.0 copy.36
  321.3 1.5 slice_reduce_fusion
  322.7 0.6 slice.54
  323.3 1.3 slice.48
  324.6 0.0 copy-done.3
  324.6 1.6 convert_element_type.49
  326.2 0.5 copy-done.2
  326.8 1.1 copy.40
  327.9 0.8 copy-done.1
  328.7 1.1 copy.41
  (10 shorter events, 0.0 us)
Async XLA Ops:
  313.5 3.7 %copy-start.5 = (bf16[3,768,192]{1,2,0:T(8,128)(2,1)S(1)}, bf16[3,768,192]{1,2,0:T(8,128)(2,1)}, u32[]{:S(2)}) copy-start(bf16[3,768,192]{1,2,0:T(8,128)(2,1)} %param.21) | copy-start | bytes 2654212
  313.5 4.7 %copy-start = (bf16[768,768]{1,0:T(8,128)(2,1)S(1)}, bf16[768,768]{1,0:T(8,128)(2,1)}, u32[]{:S(2)}) copy-start(bf16[768,768]{1,0:T(8,128)(2,1)} %get-tuple-element.81) | copy-start | bytes 3538948
  316.2 2.9 copy-start.4
  317.1 2.2 copy-start.6
  319.3 5.3 %copy-start.3 = (bf16[768,768]{1,0:T(8,128)(2,1)S(1)}, bf16[768,768]{1,0:T(8,128)(2,1)}, u32[]{:S(2)}) copy-start(bf16[768,768]{1,0:T(8,128)(2,1)} %get-tuple-element.83) | copy-start | bytes 3538948
  324.6 2.1 copy-start.2
  326.8 2.0 copy-start.1

commit v6 on v5

--- a/solution.py
+++ b/solution.py
@@ -643,7 +643,6 @@
     )(*operands)
 
 
-BLOCK = 256
 CHUNK = SLAB // 3
 
 
@@ -661,45 +660,48 @@
 
 
 def mlp_kernel(
-    xs, attn, gs, params, smalls, src1, src2,
-    w1_across, w1_beside, w1_own, w2_across, w2_beside, w2_own,
+    xs, attn, gs, params, smalls, across1, across2, beside1, beside2, own1, own2,
     out, dx1, da, sums, near1, near2, far1, rest, gb,
-    n2, n2t, gt, branch, dn2, corner1, corner2, keep1, keep2, give1, give2, got1, got2, near_got1,
-    near_got2, landing, w1, w2, b1, hs, zs, sends, recvs,
+    n2, n2t, gt, branch, dn2, w1, w2, grad1, grad2, got1, got2, near_got1, near_got2, landing,
+    hs, zs, sends, recvs, locals_,
 ):
     step = pl.program_id(0)
-    count = pl.num_programs(0) // SPLIT
-    group, index = step // count, step % count
+    room = step % 2
     width = gs.shape[1]
-    cut = pl.ds(pl.multiple_of(index * BLOCK, BLOCK), BLOCK)
-    holder = jnp.where(group == 0, 2, jnp.where(group == 1, 3, jnp.where(group == 2, 1, 0)))
+    holder = jnp.where(step == 0, 2, jnp.where(step == 1, 3, jnp.where(step == 2, 1, 0)))
     beside, across, _ = partners(lax.axis_index("tensor"))
-    send = Sender(sends, recvs, None)
+    send = Sender(sends, recvs, locals_)
     corners = [
-        send.remote(0, src1, corner1, {"tensor": beside}),
-        send.remote(1, src2, corner2, {"tensor": beside}),
+        send.remote(0, across1, w1.at[1], {"tensor": beside}),
+        send.remote(1, across2, w2.at[1], {"tensor": beside}),
+    ]
+    loads = [
+        [send.local(2 * k, first, w1.at[at]), send.local(2 * k + 1, second, w2.at[at])]
+        for k, (first, second, at) in enumerate(
+            ((across1, across2, 0), (beside1, beside2, 0), (own1, own2, 1))
+        )
     ]
     swaps = [
-        send.remote(2, give1, got1, {"tensor": beside}),
-        send.remote(3, give2, got2, {"tensor": beside}),
+        send.remote(2, grad1.at[1], got1, {"tensor": beside}),
+        send.remote(3, grad2.at[1], got2, {"tensor": beside}),
     ]
     crossing = send.remote(4, got1, far1, {"tensor": across})
     image = lax.axis_index("dp")
     mate = {"dp": mate_of(image, 0)}
     upper = got2.shape[0] // 2
     mine = (image % 2) * upper
-    halving = send.remote(7, got2.at[rows_at(upper - mine, upper), :], landing, mate)
+    halving = send.remote(5, got2.at[rows_at(upper - mine, upper), :], landing, mate)
     near_swaps = [
-        send.remote(5, corner1, near_got1, {"tensor": beside}),
-        send.remote(6, corner2, near_got2, {"tensor": beside}),
+        send.remote(6, grad1.at[2], near_got1, {"tensor": beside}),
+        send.remote(7, grad2.at[2], near_got2, {"tensor": beside}),
     ]
 
     @pl.when(step == 0)
     def _():
         gb[...] = jnp.zeros_like(gb)
+        start_all(loads[0])
         greet([{"tensor": beside}, {"tensor": across}, mate])
-        for copy in corners:
-            copy.start()
+        start_all(corners)
 
         @pl.loop(0, SLAB // STRIP)
         def _(c):
@@ -715,84 +717,66 @@
             lanes = slice(j * LANES, (j + 1) * LANES)
             n2t[lanes, :] = n2[:, lanes].T
             gt[lanes, :] = gs[:, lanes].T
-
-    @pl.when(step == count)
-    def _():
+        for copy in loads[0]:
+            copy.wait()
+
+    @pl.when(step == 1)
+    def _():
+        start_all(loads[1])
         for copy in corners:
             copy.wait()
 
-    @pl.when(step == 2 * count)
-    def _():
-        for copy in swaps:
-            copy.start()
-
-    for k, (first, second) in enumerate(
-        ((w1_across, w2_across), (None, None), (w1_beside, w2_beside), (w1_own, w2_own))
-    ):
-
-        @pl.when(group == k)
-        def _():
-            if first is None:
-                w1[...] = corner1[:, cut]
-                w2[...] = corner2[cut, :]
-            else:
-                w1[...] = first[...]
-                w2[...] = second[...]
-
-    b1[...] = smalls[holder, 0:1, cut]
+    @pl.when(step == 2)
+    def _():
+        start_all(swaps)
+        start_all(loads[2])
+        for copy in loads[1]:
+            copy.wait()
+
+    @pl.when(step == 3)
+    def _():
+        start_all(near_swaps)
+        for copy in loads[2]:
+            copy.wait()
 
     @pl.loop(0, SLAB // CHUNK)
     def _(c):
+        @pl.when((step == 2) & (c == 1))
+        def _():
+            swaps[0].wait()
+            add_rows(got1, 0, [(got1, 0), (grad1.at[0], 0)], got1.shape[0])
+            crossing.start()
+            swaps[1].wait()
+            add_rows(got2, 0, [(got2, 0), (grad2.at[0], 0)], got2.shape[0])
+            halving.start()
+
         sl = rows_at(c * CHUNK, CHUNK)
-        z = dot(n2[sl, :], w1[...]) + b1[0:1]
-        dh = dot_nt(gs[sl, :], w2[...])
+        z = dot(n2[sl, :], w1[room]) + smalls[holder, 0:1, :]
+        dh = dot_nt(gs[sl, :], w2[room])
         act, slope = gelu_parts(z)
         h = act.astype(narrow)
         dz = (dh * slope).astype(narrow)
         hs[sl, :] = h
         zs[sl, :] = dz
-        gb[holder, 0:1, cut] += jnp.sum(dz.astype(single), axis=0, keepdims=True)
-        branch[sl, :] += dot(h, w2[...])
-        dn2[sl, :] += dot_nt(dz, w1[...])
-
-    @pl.when(step == 2 * count)
-    def _():
-        swaps[0].wait()
-        add_rows(got1, 0, [(got1, 0), (keep1, 0)], got1.shape[0])
-        crossing.start()
-        swaps[1].wait()
-        add_rows(got2, 0, [(got2, 0), (keep2, 0)], got2.shape[0])
-        halving.start()
-
-    for k, (first, second) in enumerate(
-        ((keep1, keep2), (give1, give2), (corner1, corner2), (near1, near2))
-    ):
-
-        @pl.when(group == k)
-        def _():
-            @pl.loop(0, width // 256)
-            def _(r):
-                sl = rows_at(r * 256, 256)
-                first[sl, cut] = dot(n2t[sl, :], zs[...]).astype(narrow)
-                second[sl, cut] = dot(gt[sl, :], hs[...]).astype(narrow)
-
-    @pl.when(step == 3 * count - 1)
-    def _():
-        for copy in near_swaps:
-            copy.start()
-
-    @pl.when(step == 3 * count)
+        gb[holder, 0:1, :] += jnp.sum(dz.astype(single), axis=0, keepdims=True)
+        branch[sl, :] += dot(h, w2[room])
+        dn2[sl, :] += dot_nt(dz, w1[room])
+
+    @pl.loop(0, 2)
+    def _(r):
+        sl = rows_at(r * (width // 2), width // 2)
+        grad1[step, sl, :] = dot(n2t[sl, :], zs[...]).astype(narrow)
+        grad2[step, sl, :] = dot(gt[sl, :], hs[...]).astype(narrow)
+
+    @pl.when(step == 3)
     def _():
         halving.wait()
         add_rows(rest, 0, [(got2, mine), (landing, 0)], upper)
-
-    @pl.when(step == 4 * count - 1)
-    def _():
-        for copy, near, got in zip(
-            near_swaps, (near1, near2), (near_got1, near_got2), strict=True
+        for copy, near, grad, got in zip(
+            near_swaps, (near1, near2), (grad1, grad2), (near_got1, near_got2), strict=True
         ):
             copy.wait()
-            add_rows(near, 0, [(near, 0), (got, 0)], near.shape[0])
+            add_rows(near, 0, [(grad.at[3], 0), (got, 0)], near.shape[0])
         sums[...] = jnp.zeros_like(sums)
 
         @pl.loop(0, SLAB // STRIP)
@@ -817,20 +801,8 @@
 
 def mlp(residents, across, beside, own):
     width, local = own[0].shape
-    count = local // BLOCK
-
-    def block(shape, group, dim):
-        def index(i):
-            at = jnp.clip(i - group * count, 0, count - 1)
-            return (0, at) if dim == 1 else (at, 0)
-
-        return pl.BlockSpec(shape, index)
-
     slab = (SLAB, width)
     square = (width, local)
-    in_specs = [whole(a.shape) for a in residents] + [ANY, ANY]
-    in_specs += [block((width, BLOCK), group, 1) for group in (0, 2, 3)]
-    in_specs += [block((BLOCK, width), group, 0) for group in (0, 2, 3)]
     outs = [
         (of(slab), whole(slab)),
         (of(slab, single), whole(slab)),
@@ -842,28 +814,24 @@
         (of((local // 2, width)), whole((local // 2, width))),
         (of((SPLIT, 8, local), single), whole((SPLIT, 8, local))),
     ]
-    flipped = pltpu.VMEM((width, SLAB), narrow)
     return pl.pallas_call(
         mlp_kernel,
         out_shape=[o[0] for o in outs],
-        grid=(SPLIT * count,),
-        in_specs=in_specs,
+        grid=(SPLIT,),
+        in_specs=[whole(a.shape) for a in residents] + [ANY] * 6,
         out_specs=[o[1] for o in outs],
         scratch_shapes=[
             pltpu.VMEM(slab, narrow),
-            flipped,
-            flipped,
-            pltpu.VMEM(slab, single),
-            pltpu.VMEM(slab, single),
-            *[pltpu.VMEM(square, narrow)] * 10,
+            *[pltpu.VMEM((width, SLAB), narrow)] * 2,
+            *[pltpu.VMEM(slab, single)] * 2,
+            *[pltpu.VMEM((2, *square), narrow)] * 2,
+            *[pltpu.VMEM((SPLIT, *square), narrow)] * 2,
+            *[pltpu.VMEM(square, narrow)] * 4,
             pltpu.VMEM((width // 2, local), narrow),
-            pltpu.VMEM((width, BLOCK), narrow),
-            pltpu.VMEM((BLOCK, width), narrow),
-            pltpu.VMEM((1, BLOCK), single),
-            pltpu.VMEM((SLAB, BLOCK), narrow),
-            pltpu.VMEM((SLAB, BLOCK), narrow),
+            *[pltpu.VMEM((SLAB, local), narrow)] * 2,
             pltpu.SemaphoreType.DMA((8,)),
             pltpu.SemaphoreType.DMA((8,)),
+            pltpu.SemaphoreType.DMA((6,)),
         ],
         compiler_params=pltpu.CompilerParams(
             vmem_limit_bytes=VMEM, collective_id=1, has_side_effects=True
@@ -872,7 +840,7 @@
             flops=36_000_000_000, bytes_accessed=60_000_000, transcendentals=8_000_000
         ),
         name="mlp",
-    )(*residents, *across, across[0], beside[0], own[0], across[1], beside[1], own[1])
+    )(*residents, *across, *beside, *own)
 
 
 def backward_kernel(

time: 330 us -> 314 us (0.952)
  Pallas kernels: 308 us -> 291 us
    pallas_call x1, Pallas kernels: 85.3 us -> 69.4 us  [mlp(): pl.pallas_call(mlp_kernel, out_shape=[o[0] for o in outs], grid=(SPLIT,),...]
where the time goes in v6:
time: 314 us; the launch traced here: 313 us
  Pallas kernels  291 us (93%)
  local copies, waits for them, and re-layouts  16.4 us (5%)
  other arithmetic  5.08 us (2%)
    pallas_call x1, Pallas kernels, backward(): pl.pallas_call(functools.partial(backward_kernel, rows_held, images), out...  94.1 us
    pallas_call x1, Pallas kernels, forward(): pl.pallas_call(forward_kernel, out_shape=[o[0] for o in outs], grid=(2 *...  70.2 us
    pallas_call x1, Pallas kernels, mlp(): pl.pallas_call(mlp_kernel, out_shape=[o[0] for o in outs], grid=(SPLIT,),...  69.4 us
    pallas_call x1, Pallas kernels, tail(): pl.pallas_call(functools.partial(tail_kernel, rows_held, images), out_sha...  57.5 us

profile of v6, /device:TPU:0, one launch (start us, length us, event | category | flops | bytes accessed | tf_op | source)
XLA Modules:
  0.0 313.4 jit_solution(8992711886317582906)
XLA Ops:
  0.6 0.8 fusion
  1.4 0.9 pad_add_fusion
  2.3 0.6 reshape.49.notes_in.params
  2.9 1.5 pad_add_fusion.1.wrel
  4.4 70.2 %attention_forward.1 = (bf16[1152,768]{1,0:T(8,128)(2,1)}, bf16[1152,768]{1,0:T(8,128)(2,1)}, bf16[7,208,768]{2,1,0:T(8,128)(2,1)}, bf16[14,4,208,384]{3,2,1,0:T...) custom-call(bf16[16,64,768]{2,1,0:T(8,128)(2,1)} %bitcast.28, ...), custom_call_target="tpu_custom_call" | custom-call | flops 25999998976 | bytes 60000000 | tf_op jit(solution)/shard_map/attention_forward/pallas_call | solution.py:621
  74.6 69.4 %mlp.1 = (bf16[1152,768]{1,0:T(8,128)(2,1)}, f32[1152,768]{1,0:T(8,128)}, bf16[1152,768]{1,0:T(8,128)(2,1)}, f32[8,768]{1,0:T(8,128)}, bf16[768,768]{1,0:T(8,128...) custom-call(bf16[1152,768]{1,0:T(8,128)(2,1)} %get-tuple-element.50., ...), custom_call_target="tpu_custom_call" | custom-call | flops 35999997952 | bytes 60000000 | tf_op jit(solution)/shard_map/mlp/pallas_call | solution.py:817
  144.0 94.1 %attention_backward.1 = (bf16[1152,768]{1,0:T(8,128)(2,1)}, f32[8,768]{1,0:T(8,128)}, bf16[768,768]{1,0:T(8,128)(2,1)}, bf16[768,768]{1,0:T(8,128)(2,1)}, f32[2,...) custom-call(bf16[1152,768]{1,0:T(8,128)(2,1)} %get-tuple-element.59., ...), custom_call_target="tpu_custom_call" | custom-call | flops 51999997952 | bytes 80000000 | tf_op jit(solution)/shard_map/attention_backward/pallas_call | solution.py:1064
  238.1 57.5 %tail.1 = (bf16[1024,768]{1,0:T(8,128)(2,1)}, bf16[1024,768]{1,0:T(8,128)(2,1)}, bf16[768,768]{1,0:T(8,128)(2,1)}, f32[32,768]{1,0:T(8,128)}, f32[32,128]{1,0:T(8,128)}) custom-call(bf16[1152,768]{1,0:T(8,128)(2,1)} %get-tuple-element.58.out, bf16[1152,768]{1,0:T(8,128)(2,1)} %get-tuple-element.69.back, bf16[768,768]{1,0:T(8,128)(2,1)} %get-tuple-element.70.keep, ...), custom_call_target="tpu_custom_call" | custom-call | flops 4000000000 | bytes 20000000 | tf_op jit(solution)/shard_map/tail/pallas_call | solution.py:1285
  295.6 0.8 slice.49
  296.5 0.6 copy.37
  297.1 2.6 slice.53
  299.8 0.9 dynamic-slice_reduce_fusion.2
  300.7 0.1 broadcast_in_dim.11
  300.7 0.1 mul.10
  300.8 0.0 copy-done.5
  300.8 1.0 multiply_convert_fusion
  301.8 0.0 copy-done
  301.8 0.9 slice.55
  302.7 0.0 copy-done.4
  302.7 0.2 convert_bitcast_fusion
  302.8 0.0 copy-done.6
  302.8 0.0 copy-start.3
  302.9 2.0 copy.36
  304.8 1.5 slice_reduce_fusion
  306.3 0.6 slice.54
  306.9 1.3 slice.48
  308.2 0.0 copy-done.3
  308.2 1.6 convert_element_type.49
  309.8 0.5 copy-done.2
  310.3 1.1 copy.40
  311.5 0.8 copy-done.1
  312.3 1.1 copy.41
  (10 shorter events, 0.0 us)
Async XLA Ops:
  297.1 3.7 %copy-start.5 = (bf16[3,768,192]{1,2,0:T(8,128)(2,1)S(1)}, bf16[3,768,192]{1,2,0:T(8,128)(2,1)}, u32[]{:S(2)}) copy-start(bf16[3,768,192]{1,2,0:T(8,128)(2,1)} %param.21) | copy-start | bytes 2654212
  297.1 4.7 %copy-start = (bf16[768,768]{1,0:T(8,128)(2,1)S(1)}, bf16[768,768]{1,0:T(8,128)(2,1)}, u32[]{:S(2)}) copy-start(bf16[768,768]{1,0:T(8,128)(2,1)} %get-tuple-element.81) | copy-start | bytes 3538948
  299.7 2.9 copy-start.4
  300.6 2.2 copy-start.6
  302.8 5.3 %copy-start.3 = (bf16[768,768]{1,0:T(8,128)(2,1)S(1)}, bf16[768,768]{1,0:T(8,128)(2,1)}, u32[]{:S(2)}) copy-start(bf16[768,768]{1,0:T(8,128)(2,1)} %get-tuple-element.83) | copy-start | bytes 3538948
  308.2 2.1 copy-start.2
  310.3 2.0 copy-start.1

commit v7 on v6

--- a/solution.py
+++ b/solution.py
@@ -271,15 +271,17 @@
     return [{"dp": mate_of(image, bit)} for bit in range(images.bit_length() - 1)]
 
 
-def attend(n1, valid, weights, qbias, vbias, wrel, bits, lanes, sides, keys, qkv, mixed, peak):
-    half = weights.shape[1]
-    count = n1.shape[0]
-    query = jnp.where(valid, dot_nt(n1, weights[0]) + qbias, 0.0).astype(narrow)
-    key8 = dot_nt(n1, weights[1]).astype(narrow) * jnp.asarray(0.125, narrow)
-    value = (dot_nt(n1, weights[2]) + vbias).astype(narrow)
-    qkv[0, 0, :count] = query
-    qkv[0, 1, :count] = key8
-    qkv[0, 2, :count] = value
+def project(n1, weights, qbias, vbias, projected, place):
+    projected[0, place, :] = (dot_nt(n1, weights[0]) + qbias).astype(narrow)
+    projected[1, place, :] = dot_nt(n1, weights[1]).astype(narrow) * jnp.asarray(0.125, narrow)
+    projected[2, place, :] = (dot_nt(n1, weights[2]) + vbias).astype(narrow)
+
+
+def attend(count, place, valid, projected, vbias, wrel, bits, lanes, sides, keys, qkv, mixed, peak):
+    half = projected.shape[2]
+    qkv[0, 0, :count] = jnp.where(valid, projected[0, place, :].astype(single), 0.0).astype(narrow)
+    qkv[0, 1, :count] = projected[1, place, :]
+    qkv[0, 2, :count] = projected[2, place, :]
     if count < ROWS:
         left = ROWS - count
         qkv[0, 1, count:] = jnp.zeros((left, half), narrow)
@@ -287,8 +289,7 @@
     low_lane = lax.broadcasted_iota(jnp.int32, (count, LANES), 1) < 64
     for pair in range(half // LANES):
         cut = slice(pair * LANES, (pair + 1) * LANES)
-        q = query[:, cut]
-        k8, v = qkv[0, 1, :, cut], qkv[0, 2, :, cut]
+        q, k8, v = qkv[0, 0, :count, cut], qkv[0, 1, :, cut], qkv[0, 2, :, cut]
         rel = shift_left(dot_nt(q, wrel[...]), bits)
         rest = rel - rel.astype(narrow).astype(single)
         rel = rel * lanes[0:1] + pltpu.roll(rest, 16, 1) * lanes[1:2] + lanes[2:3]
@@ -308,8 +309,7 @@
             probs = jnp.exp(scores - top)
             total = jnp.sum(probs, axis=1, keepdims=True)
             pieces.append(dot(probs.astype(narrow), v) * (1.0 / total))
-        mixed[0, :count, cut] = jnp.where(low_lane, pieces[0], pieces[1]).astype(narrow)
-    return dot(mixed[0, :count], weights[3])
+        mixed[place, cut] = jnp.where(low_lane, pieces[0], pieces[1]).astype(narrow)
 
 
 class Halo:
@@ -405,7 +405,7 @@
 def forward_kernel(
     x, g, wqkv, wproj, fc1, fc2, notes_in, params, wrel, bits, lanes, sides, keys,
     xs, gs, n1_all, qkv, mixed, attn, peak, weights_out, across1, across2, beside1, beside2, small_out,
-    xext, gext, weights, smalls, sends, recvs, locals_,
+    xext, gext, weights, smalls, projected, sends, recvs, locals_,
 ):
     step = pl.program_id(0)
     far, slot = step // SLOTS, step % SLOTS
@@ -478,7 +478,7 @@
         start_all(own_pack + notes + own)
         x_halo.start()
         start_all(pack_far.first)
-        for ref in (xs, gs, attn, peak):
+        for ref in (xs, gs, n1_all, mixed, peak):
             ref[...] = jnp.zeros_like(ref)
         for copy in own + notes + own_pack:
             copy.wait()
@@ -527,6 +527,16 @@
     row0, col0, kind, inside, offset, live = slot_fields(rows)
     whole_window = inside == SPAN
     tables = (wrel, bits.at[kind], lanes, sides, keys.at[kind])
+
+    def biases(which):
+        return (
+            smalls[2 * which, 1:2, :half] + smalls[2 * which + 1, 2:3, :half],
+            smalls[2 * which, 3:4, :half] + smalls[2 * which + 1, 4:5, :half],
+        )
+
+    @pl.when(step == SLOTS)
+    def _():
+        project(n1_all[...], weights.at[1], *biases(1), projected, slice(None))
 
     def work(count):
         place = rows_at(offset, count)
@@ -539,22 +549,20 @@
             xs[place, :] = window.astype(narrow)
             normal, _ = norm_parts(window)
             n1 = jnp.where(valid, normal * params[8:9] + params[9:10], 0.0).astype(narrow)
-            n1_all[slot, :count] = n1
+            n1_all[place, :] = n1
+            project(n1, weights.at[0], *biases(0), projected, place)
 
         _, valid = positions(0, count, col0, kind, inside)
-        qbias = smalls[2 * far, 1:2, :half] + smalls[2 * far + 1, 2:3, :half]
-        vbias = smalls[2 * far, 3:4, :half] + smalls[2 * far + 1, 4:5, :half]
-        terms = attend(
-            n1_all[slot, :count], valid, weights.at[far], qbias, vbias, *tables,
-            qkv, mixed, peak.at[far],
+        attend(
+            count, place, valid, projected, biases(far)[1], *tables, qkv, mixed.at[far], peak.at[far]
         )
-        attn[place, :] += jnp.where(valid, terms, 0.0)
 
     pl.when(live & whole_window)(functools.partial(work, ROWS))
     pl.when(live & jnp.logical_not(whole_window))(functools.partial(work, SHORT))
 
     @pl.when(step == 2 * SLOTS - 1)
     def _():
+        attn[...] = dot(mixed[0], weights[0, 3]) + dot(mixed[1], weights[1, 3])
         g_own.wait()
         g_halo.wait_from_above()
         g_halo.wait_from_below()
@@ -604,9 +612,9 @@
     outs = [
         (of(slab), whole(slab)),
         (of(slab), whole(slab)),
-        (of((SLOTS, ROWS, width)), whole((SLOTS, ROWS, width))),
+        (of(slab), whole(slab)),
         (of((2 * SLOTS, 4, ROWS, half)), by_slot((4, ROWS, half))),
-        (of((2 * SLOTS, ROWS, half)), by_slot((ROWS, half))),
+        (of((2, SLAB, half)), whole((2, SLAB, half))),
         (of(slab, single), whole(slab)),
         (of((2, 8, ROWS), single), whole((2, 8, ROWS))),
         (of((2, 4, half, width)), ANY),
@@ -629,6 +637,7 @@
             pltpu.VMEM(ext, narrow),
             pltpu.VMEM((2, 4, half, width), narrow),
             pltpu.VMEM((SPLIT, 8, width), single),
+            pltpu.VMEM((3, SLAB, half), narrow),
             pltpu.SemaphoreType.DMA((32,)),
             pltpu.SemaphoreType.DMA((32,)),
             pltpu.SemaphoreType.DMA((7,)),
@@ -845,9 +854,9 @@
 
 def backward_kernel(
     rows_held, images,
-    da, n1, qkv, mixed, weights, wrel, bits, lanes, sides, keys, xs, dx1, params, near1, near2, far1, rest,
-    back, sums, keep, give, bias, grel, crossed, summed1, summed2,
-    acc, dqkv, dmix, dn1, keep_far, give_far, got_far, held1, held2, land1, land2, rest_got,
+    da, n1, qkv, mixed, wproj, wrel, bits, lanes, sides, keys, near1, near2, far1, rest,
+    dqkv, keep, give, bias, grel, crossed, summed1, summed2,
+    dmix, got_far, held1, held2, land1, land2, rest_got,
     sends, recvs, locals_,
 ):
     step = pl.program_id(0)
@@ -855,12 +864,12 @@
     image = lax.axis_index("dp")
     beside, across, _ = partners(lax.axis_index("tensor"))
     send = Sender(sends, recvs, locals_)
-    half, width = weights.shape[2:]
+    half = wproj.shape[2]
     per = Halver.copies(images)
     sum1 = Halver(send, 3, image, images, 0, held1.shape[0], (1, 0, 2))
     sum2 = Halver(send, 3 + per, image, images, 0, held2.shape[0], (0, 1, 2))
     rest_cross = send.remote(0, rest, rest_got, {"tensor": across})
-    far_swap = send.remote(1, give_far, got_far, {"tensor": beside})
+    far_swap = send.remote(1, give.at[0], got_far, {"tensor": beside})
     far_cross = send.remote(2, got_far, crossed, {"tensor": across})
 
     halvers = ((sum1, held1, land1), (sum2, held2, land2))
@@ -910,7 +919,7 @@
 
     def cross_far():
         far_swap.wait()
-        add_rows(got_far, 0, [(got_far, 0), (keep_far, 0)], got_far.shape[0])
+        add_rows(got_far, 0, [(got_far, 0), (keep.at[0], 0)], got_far.shape[0])
         far_cross.start()
 
     events = {
@@ -936,28 +945,22 @@
         for count, holds in ((ROWS, whole_window), (SHORT, jnp.logical_not(whole_window))):
             pl.when(live & holds)(functools.partial(action, count))
 
+    @pl.when(step == 0)
+    def _():
+        for ref in (bias, grel, dqkv):
+            ref[...] = jnp.zeros_like(ref)
+
+    fire(0)
+
     @pl.when(slot == 0)
     def _():
-        acc[...] = jnp.zeros_like(acc)
-
-    @pl.when(step == 0)
-    def _():
-        for ref in (bias, grel, back, sums):
-            ref[...] = jnp.zeros_like(ref)
-
-    fire(0)
-
-    def before_pairs(count):
-        da_win = da[rows_at(offset, count), :]
-        acc[3] += dot_tn(mixed[0, :count], da_win)
-        dmix[:count] = dot_nt(da_win, weights[far, 3]).astype(narrow)
-
-    on_window(before_pairs)
+        dmix[...] = dot_nt(da[...], wproj[far, 0]).astype(narrow)
 
     def one_pair(pair, count):
         cut = slice(pair * LANES, (pair + 1) * LANES)
         q, k8, v, rel = (qkv[0, j, :n, cut] for j, n in enumerate((count, ROWS, ROWS, count)))
-        do = dmix[:count, cut]
+        place = rows_at(offset, count)
+        do = dmix[place, cut]
         dqs, dks, dvs = [], [], []
         for head in range(2):
             mine, other = sides[head : head + 1], sides[1 - head : 2 - head]
@@ -981,54 +984,34 @@
         drel = shift_right(drel, bits.at[kind]).astype(narrow)
         dq = dq + dot(drel, wrel[...])
         grel[...] += dot_tn(drel, q)
-        dqkv[0, :count, cut] = dq.astype(narrow)
-        dqkv[1, :, cut] = dk.astype(narrow)
-        dqkv[2, :, cut] = dv.astype(narrow)
+        for j, value in enumerate((dq, dk, dv)):
+            value = value.astype(narrow).astype(single)
+            if j != 1:
+                bias[far, j : j + 1, cut] += jnp.sum(value, axis=0, keepdims=True)
+            value = value[:count]
+            if count < ROWS:
+                _, valid = positions(0, count, 0, kind, inside)
+                value = jnp.where(valid, value, 0.0)
+            dqkv[far, j, place, cut] = value.astype(narrow)
 
     for pair in range(half // LANES):
         fire(pair + 1)
         on_window(functools.partial(one_pair, pair))
 
-    def after_pairs(count):
-        total = None
-        for j in range(3):
-            piece = dqkv[j, :count]
-            acc[j] += dot_tn(piece, n1[0, :count])
-            every = piece if j == 0 else dqkv[j]
-            bias[far, j : j + 1, :] += jnp.sum(every.astype(single), axis=0, keepdims=True)
-            back_part = dot(piece, weights[far, j])
-            total = back_part if total is None else total + back_part
-
-        @pl.when(far == 1)
-        def _():
-            dn1[slot, :count] = total
-
-        @pl.when(far == 0)
-        def _():
-            _, valid = positions(0, count, col0, kind, inside)
-            place = rows_at(offset, count)
-            grad = jnp.where(valid, total + dn1[slot, :count], 0.0)
-            normal, inverse = norm_parts(xs[place, :].astype(single))
-            sums[0:1, :] += jnp.sum(grad * normal, axis=0, keepdims=True)
-            sums[1:2, :] += jnp.sum(grad, axis=0, keepdims=True)
-            result = dx1[place, :] + norm_back(grad, normal, inverse, params[8:9])
-            back[place, :] = jnp.where(valid, result, 0.0).astype(narrow)
-
-    on_window(after_pairs)
-
-    def flush(keep, give):
+    @pl.when(slot == SLOTS - 1)
+    def _():
         part = half // 2
+        at = step // SLOTS
         for j in range(4):
-            keep[j * part : (j + 1) * part, :] = acc[j, :part, :].astype(narrow)
-            give[j * part : (j + 1) * part, :] = acc[j, part:, :].astype(narrow)
-
-    @pl.when(step == SLOTS - 1)
-    def _():
-        flush(keep_far, give_far)
+            if j < 3:
+                total = dot_tn(dqkv[far, j], n1[...])
+            else:
+                total = dot_tn(mixed[far], da[...])
+            keep[at, j * part : (j + 1) * part, :] = total[:part].astype(narrow)
+            give[at, j * part : (j + 1) * part, :] = total[part:].astype(narrow)
 
     @pl.when(step == 2 * SLOTS - 1)
     def _():
-        flush(keep, give)
         for (halver, _, _), total in zip(halvers, summed, strict=True):
             halver.back(0, total).wait()
         far_cross.wait()
@@ -1038,21 +1021,21 @@
     half, width = weights.shape[2:]
     operands = [da, n1, qkv, mixed, weights, wrel, *tables, *residents, rest]
     in_specs = [whole(a.shape) for a in operands]
-    in_specs[1] = pl.BlockSpec((1, ROWS, width), lambda i: (i % SLOTS, 0, 0))
 
     def halved(i):
         return (1 - i // SLOTS) * SLOTS + i % SLOTS
 
     in_specs[2] = pl.BlockSpec((1, 4, ROWS, half), lambda i: (halved(i), 0, 0, 0))
-    in_specs[3] = pl.BlockSpec((1, ROWS, half), lambda i: (halved(i), 0, 0))
+    in_specs[4] = pl.BlockSpec(
+        (2, 1, half, width), lambda i: (0, 3, 0, 0), pipeline_mode=pl.Buffered(1)
+    )
     in_specs[-1] = ANY
     packed = (2 * half, width)
-    square = residents[3].shape
+    square = residents[0].shape
     outs = [
-        (of((SLAB, width)), whole((SLAB, width))),
-        (of((8, width), single), whole((8, width))),
-        (of(packed), whole(packed)),
-        (of(packed), whole(packed)),
+        (of((2, 3, SLAB, half)), whole((2, 3, SLAB, half))),
+        (of((2, *packed)), whole((2, *packed))),
+        (of((2, *packed)), whole((2, *packed))),
         (of((2, 8, half), single), whole((2, 8, half))),
         (of((LANES, LANES), single), whole((LANES, LANES))),
         (of(packed), ANY),
@@ -1068,11 +1051,8 @@
         in_specs=in_specs,
         out_specs=[o[1] for o in outs],
         scratch_shapes=[
-            pltpu.VMEM((4, half, width), single),
-            pltpu.VMEM((3, ROWS, half), narrow),
-            pltpu.VMEM((ROWS, half), narrow),
-            pltpu.VMEM((SLOTS, ROWS, width), single),
-            *[pltpu.VMEM(packed, narrow)] * 3,
+            pltpu.VMEM((SLAB, half), narrow),
+            pltpu.VMEM(packed, narrow),
             *[pltpu.VMEM(square, narrow)] * 2,
             *[pltpu.VMEM(landing, narrow)] * 2,
             pltpu.VMEM(rest.shape, narrow),
@@ -1113,13 +1093,24 @@
 
 def tail_kernel(
     rows_held, images,
-    out, back, keep, crossed, sums1, sums2, bias, rel_sum, fc_bias, peak, give,
+    sums2, bias, rel_sum, fc_bias, peak, params,
+    out_in, keep_in, crossed_in, xs_in, dx1_in, give, dqkv, weights,
     output, input_grad, packed, totals, tops,
-    ext0, ext1, below0, below1, above0, above1, got, landing, held, sum_land, top_land, sends, recvs,
+    ext0, ext1, below0, below1, above0, above1, got, landing, held, sum_land, top_land, back, grads,
+    packs, out, keep, crossed, xs, dx1, sends, recvs, locals_,
 ):
     device, image = lax.axis_index("tensor"), lax.axis_index("dp")
     beside, across, corner = partners(device)
-    send = Sender(sends, recvs, None)
+    send = Sender(sends, recvs, locals_)
+    early = [send.local(0, keep_in.at[1], keep), send.local(1, crossed_in, crossed)]
+    loads = [
+        send.local(2, dqkv, grads),
+        send.local(3, weights.at[:, 0:3], packs),
+        send.local(4, xs_in, xs),
+        send.local(5, dx1_in, dx1),
+    ]
+    late = send.local(6, out_in, out)
+    start_all(early + loads + [late])
     per = Halver.copies(images)
     middle = held.shape[0] // 2
     landing_rows = Halver.landing_rows(images, middle)
@@ -1153,12 +1144,10 @@
             halver.back(stage, packed).wait()
 
     greet([{"tensor": place} for place in (beside, across, corner)] + mates)
-    swap = send.remote(0, give, got, {"tensor": beside})
+    swap = send.remote(0, give.at[1], got, {"tensor": beside})
     swap.start()
-
     totals[...] = jnp.zeros_like(totals)
     tops[...] = jnp.zeros_like(tops)
-    totals[0:2, :] = sums1[0:2, :]
     totals[2:6, :] = sums2[0:4, :]
     rel = rel_sum[...]
     rel = rel[HD:] + pltpu.roll(rel[:HD], HD, 1)
@@ -1226,53 +1215,75 @@
             down.wait_recv()
             add_rows(result, 0, [(result, 0), (above, 0)], bottom)
 
-    small_start(0)
+    def norm1_back():
+        @pl.loop(0, SLAB // CHUNK)
+        def _(c):
+            sl = rows_at(c * CHUNK, CHUNK)
+            grad = None
+            for far in range(2):
+                for j in range(3):
+                    term = dot(grads[far, j, sl, :], packs[far, j])
+                    grad = term if grad is None else grad + term
+            normal, inverse = norm_parts(xs[sl, :].astype(single))
+            totals[0:1, :] += jnp.sum(grad * normal, axis=0, keepdims=True)
+            totals[1:2, :] += jnp.sum(grad, axis=0, keepdims=True)
+            result = dx1[sl, :] + norm_back(grad, normal, inverse, params[8:9])
+            back[sl, :] = result.astype(narrow)
+
     clear_rows(ext0)
     clear_rows(ext1)
+    for copy in early:
+        copy.wait()
     swap.wait()
     add_rows(held, 0, [(keep, 0), (got, 0), (crossed, 0)], held.shape[0])
     reduce_start(0)
-    small_finish(0)
-    small_start(1)
+    for copy in loads:
+        copy.wait()
+    norm1_back()
+    small_start(0)
+    reduce_finish(0)
+    reduce_start(1)
     place_windows(rows_held, device, back, ext1, 0, SLOTS)
     halos1 = halo(halo_base, ext1, below1, above1)
     halo_start(halos1)
+    small_finish(0)
+    small_start(1)
+    reduce_finish(1)
+    reduce_start(2)
+    late.wait()
+    place_windows(rows_held, device, out, ext0, 0, 4)
     small_finish(1)
     small_start(2)
-    reduce_finish(0)
-    reduce_start(1)
-    place_windows(rows_held, device, out, ext0, 0, 3)
-    small_finish(2)
-    small_start(3)
-    reduce_finish(1)
-    reduce_start(2)
-    place_windows(rows_held, device, out, ext0, 3, SLOTS)
-    halos0 = halo(halo_base + 2, ext0, below0, above0)
-    halo_start(halos0)
-    small_finish(3)
-    small_start(4)
     reduce_finish(2)
     for halver, land in zip(halvers, landings, strict=True):
         halver.extras(held, land)
         start, length = halver.final
         packed[rows_at(start, length), :] = held[rows_at(start, length), :]
     hand_start(2)
+    place_windows(rows_held, device, out, ext0, 4, SLOTS)
+    halos0 = halo(halo_base + 2, ext0, below0, above0)
+    halo_start(halos0)
+    small_finish(2)
+    small_start(3)
+    halo_finish(halos1, ext1, below1, above1, input_grad)
+    hand_finish(2)
+    hand_start(1)
+    small_finish(3)
+    small_start(4)
+    hand_finish(1)
+    hand_start(0)
     for k in range(4, len(ring)):
         small_finish(k)
         if k + 1 < len(ring):
             small_start(k + 1)
-    halo_finish(halos1, ext1, below1, above1, input_grad)
-    hand_finish(2)
-    hand_start(1)
-    hand_finish(1)
-    hand_start(0)
     halo_finish(halos0, ext0, below0, above0, output)
     hand_finish(0)
 
 
 def tail(rows_held, images, *operands):
-    width = operands[0].shape[1]
-    packed = operands[2].shape
+    width = operands[-1].shape[3]
+    half = operands[-1].shape[2]
+    packed = (2 * half, width)
     tokens = rows_held * GRID
     bits = images.bit_length() - 1
     landing = 2 * Halver.landing_rows(images, packed[0] // 2)
@@ -1285,7 +1296,7 @@
     return pl.pallas_call(
         functools.partial(tail_kernel, rows_held, images),
         out_shape=outs,
-        in_specs=[pl.BlockSpec(memory_space=pltpu.VMEM)] * (len(operands) - 1) + [ANY],
+        in_specs=[pl.BlockSpec(memory_space=pltpu.VMEM)] * (len(operands) - 8) + [ANY] * 8,
         out_specs=[pl.BlockSpec(memory_space=pltpu.VMEM)] * len(outs),
         scratch_shapes=[
             pltpu.VMEM(ext, narrow),
@@ -1299,8 +1310,16 @@
             pltpu.VMEM(packed, narrow),
             pltpu.VMEM((2 + bits, 32, width), single),
             pltpu.VMEM((2 + bits, 32, LANES), single),
+            pltpu.VMEM((SLAB, width), narrow),
+            pltpu.VMEM((2, 3, SLAB, half), narrow),
+            pltpu.VMEM((2, 3, half, width), narrow),
+            pltpu.VMEM((SLAB, width), narrow),
+            *[pltpu.VMEM(packed, narrow)] * 2,
+            pltpu.VMEM((SLAB, width), narrow),
+            pltpu.VMEM((SLAB, width), single),
             pltpu.SemaphoreType.DMA((copies,)),
             pltpu.SemaphoreType.DMA((copies,)),
+            pltpu.SemaphoreType.DMA((7,)),
         ],
         compiler_params=pltpu.CompilerParams(
             vmem_limit_bytes=VMEM, collective_id=3, has_side_effects=True
@@ -1310,6 +1329,85 @@
         ),
         name="tail",
     )(*operands)
+
+
+def finish_kernel(
+    fc1, fc2, gq, gp, totals, tops, wqkv,
+    grad_fc1, grad_fc2, grad_qkv, grad_proj, clipped, qv, fc1_bias, norms, proj_bias, fc2_bias, rel,
+):
+    device = lax.axis_index("tensor")
+    grad_fc1[...] = fc1[...].astype(single)
+    grad_fc2[...] = fc2[...].astype(single).T
+    grad_qkv[...] = gq[...].astype(single)
+    grad_proj[...] = gp[...].astype(single)
+
+    @pl.when(pl.program_id(0) == 0)
+    def _():
+        local = wqkv.shape[1]
+        limit = jnp.maximum(tops[pl.ds(pl.multiple_of(8 * device, 8), 8), :], CLIP)
+        factor = jnp.sqrt(CLIP / limit)
+        factor = jnp.concatenate([factor] * (wqkv.shape[2] // LANES), axis=1)
+        for j in range(2):
+            for head in range(local // HD):
+                cut = slice(head * HD, (head + 1) * HD)
+                scaled = wqkv[j, cut, :].astype(single) * factor[head : head + 1]
+                clipped[j, cut, :] = scaled.astype(narrow)
+            qv[j : j + 1, :] = totals[pl.ds(28 + device, 1), 2 * j * local : (2 * j + 1) * local]
+        fc1_bias[...] = totals[24 + device, :]
+        norms[...] = totals[0:4, :]
+        proj_bias[...] = totals[4, :]
+        fc2_bias[...] = totals[5, :]
+        span = 2 * WIN - 1
+        for j in range(2):
+            for first in range(0, span, 8):
+                group = (32 * j + first) // 8
+                count = min(8, span - first)
+                at, lane = 8 * (1 + group // 6), (group % 6) * LANES
+                rel[first : first + count, j, :] = totals[at : at + count, lane : lane + HD]
+
+
+def finish(summed1, summed2, gpack, totals, tops, wqkv):
+    _, local, width = wqkv.shape
+    hidden = summed1.shape[1]
+    parts = 3
+    rows, cols, lines = width // parts, hidden // parts, 3 * local // parts
+    few = local // parts
+
+    def by_rows(count, columns, first=0):
+        return pl.BlockSpec((count, columns), lambda i: (first + i, 0))
+
+    span = 2 * WIN - 1
+    outs = [
+        (of((width, hidden), single), by_rows(rows, hidden)),
+        (of((hidden, width), single), by_rows(cols, width)),
+        (of((3 * local, width), single), by_rows(lines, width)),
+        (of((local, width), single), by_rows(few, width)),
+        (of((2, local, width)), whole((2, local, width))),
+        (of((2, local), single), whole((2, local))),
+        (of((hidden,), single), whole((hidden,))),
+        (of((4, width), single), whole((4, width))),
+        (of((width,), single), whole((width,))),
+        (of((width,), single), whole((width,))),
+        (of((span, 2, HD), single), whole((span, 2, HD))),
+    ]
+    return pl.pallas_call(
+        finish_kernel,
+        out_shape=[o[0] for o in outs],
+        grid=(parts,),
+        in_specs=[
+            by_rows(rows, hidden),
+            pl.BlockSpec((width, cols), lambda i: (0, i)),
+            by_rows(lines, width),
+            by_rows(few, width, 3 * local // few),
+            whole(totals.shape),
+            whole(tops.shape),
+            whole(wqkv.shape),
+        ],
+        out_specs=[o[1] for o in outs],
+        compiler_params=pltpu.CompilerParams(vmem_limit_bytes=VMEM),
+        cost_estimate=pl.CostEstimate(flops=0, bytes_accessed=14_000_000, transcendentals=0),
+        name="finish",
+    )(summed1, summed2, gpack, gpack, totals, tops, wqkv)
 
 
 def shards(
@@ -1373,36 +1471,33 @@
         (w_fc1, w_fc2),
     )
     images = lax.axis_size("dp")
-    back, sums1, keep, give, bias, rel_sum, crossed, summed1, summed2 = backward(
-        rows, images, da, n1, qkv, mixed, weights, wrel, tables,
-        [xs, dx1, params, near1, near2, far1], rest,
+    dqkv, keep, give, bias, rel_sum, crossed, summed1, summed2 = backward(
+        rows, images, da, n1, qkv, mixed, weights, wrel, tables, [near1, near2, far1], rest
     )
     output, input_grad, gpack, totals, tops = tail(
-        rows, images, out, back, keep, crossed, sums1, sums2, bias, rel_sum, fc_bias, peak, give
+        rows, images, sums2, bias, rel_sum, fc_bias, peak, params, out, keep, crossed, xs, dx1,
+        give, dqkv, weights,
     )
-
-    gpack = gpack.astype(single)
-    blocks = totals[8:24].reshape(2, 8, 6, LANES).transpose(0, 2, 1, 3).reshape(-1, LANES)[:HD, :HD]
-    grad_rel = jnp.stack([blocks[: 2 * WIN - 1], blocks[32 : 32 + 2 * WIN - 1]])
-    qv = lax.dynamic_slice_in_dim(totals, 28 + device, 1)[0].reshape(2, 2 * local)[:, :local]
+    (
+        grad_fc1, grad_fc2, grad_qkv, grad_proj, clipped, grad_qv, grad_fc1_bias,
+        grad_norms, grad_proj_bias, grad_fc2_bias, grad_rel,
+    ) = finish(summed1, summed2, gpack, totals, tops, wqkv)
     head_max = lax.dynamic_slice(tops, (8 * device, 0), (heads, 1))[:, 0]
-    factor = jnp.sqrt(CLIP / jnp.maximum(head_max, CLIP))
-    clipped_qk = (w_qkv[:2].astype(single) * jnp.repeat(factor, HD)).astype(narrow)
 
     return (
         output[None],
         input_grad[None],
-        gpack[: 3 * local].reshape(3, local, width).transpose(0, 2, 1),
-        qv,
-        gpack[3 * local :],
-        totals[4],
-        summed1.astype(single),
-        lax.dynamic_slice_in_dim(totals, 24 + device, 1)[0],
-        summed2.T.astype(single),
-        totals[5],
-        totals[:4],
-        grad_rel,
-        clipped_qk,
+        grad_qkv.reshape(3, local, width).transpose(0, 2, 1),
+        grad_qv,
+        grad_proj,
+        grad_proj_bias,
+        grad_fc1,
+        grad_fc1_bias,
+        grad_fc2,
+        grad_fc2_bias,
+        grad_norms,
+        grad_rel.transpose(1, 0, 2),
+        clipped.transpose(0, 2, 1),
         head_max,
     )
 

time: 314 us -> 295 us (0.939)
  local copies, waits for them, and re-layouts: 16.4 us -> 5.82 us
  Pallas kernels: 291 us -> 286 us
    pallas_call x1, Pallas kernels: 94.1 us -> 81.5 us  [backward(): pl.pallas_call(functools.partial(backward_kernel, rows_held, images), out...]
    slice x6 -> x0, local copies, waits for them, and re-layouts: 7.67 us -> none  [the longest x1 2.65 us: shards(): gpack[:3 * local].reshape(3, local, width).transpose(0, 2, 1)]
    pallas_call x0 -> x1, Pallas kernels: none -> 6.23 us  [finish(): pl.pallas_call(finish_kernel, out_shape=[o[0] for o in outs], grid=(parts...]
where the time goes in v7:
time: 295 us; the launch traced here: 294 us
  Pallas kernels  286 us (97%)
  local copies, waits for them, and re-layouts  5.82 us (2%)
    pallas_call x1, Pallas kernels, backward(): pl.pallas_call(functools.partial(backward_kernel, rows_held, images), out...  81.5 us
    pallas_call x1, Pallas kernels, forward(): pl.pallas_call(forward_kernel, out_shape=[o[0] for o in outs], grid=(2 *...  70.7 us
    pallas_call x1, Pallas kernels, mlp(): pl.pallas_call(mlp_kernel, out_shape=[o[0] for o in outs], grid=(SPLIT,),...  69.8 us
    pallas_call x1, Pallas kernels, tail(): pl.pallas_call(functools.partial(tail_kernel, rows_held, images), out_sha...  57.2 us
    pallas_call x1, Pallas kernels, finish(): pl.pallas_call(finish_kernel, out_shape=[o[0] for o in outs], grid=(parts...  6.23 us

profile of v7, /device:TPU:0, one launch (start us, length us, event | category | flops | bytes accessed | tf_op | source)
XLA Modules:
  0.0 294.4 jit_solution(823195808438084579)
XLA Ops:
  0.6 0.8 fusion
  1.4 0.9 pad_add_fusion
  2.3 0.6 reshape.42.notes_in.params
  2.9 1.5 pad_add_fusion.1.wrel
  4.4 70.7 %attention_forward.1 = (bf16[1152,768]{1,0:T(8,128)(2,1)}, bf16[1152,768]{1,0:T(8,128)(2,1)}, bf16[1152,768]{1,0:T(8,128)(2,1)}, bf16[14,4,208,384]{3,2,1,0:T(8,...) custom-call(bf16[16,64,768]{2,1,0:T(8,128)(2,1)} %bitcast.19, ...), custom_call_target="tpu_custom_call" | custom-call | flops 25999998976 | bytes 60000000 | tf_op jit(solution)/shard_map/attention_forward/pallas_call | solution.py:629
  75.1 69.8 %mlp.1 = (bf16[1152,768]{1,0:T(8,128)(2,1)}, f32[1152,768]{1,0:T(8,128)}, bf16[1152,768]{1,0:T(8,128)(2,1)}, f32[8,768]{1,0:T(8,128)}, bf16[768,768]{1,0:T(8,128...) custom-call(bf16[1152,768]{1,0:T(8,128)(2,1)} %get-tuple-element.60., ...), custom_call_target="tpu_custom_call" | custom-call | flops 35999997952 | bytes 60000000 | tf_op jit(solution)/shard_map/mlp/pallas_call | solution.py:826
  145.0 81.5 %attention_backward.1 = (bf16[2,3,1152,384]{3,2,1,0:T(8,128)(2,1)}, bf16[2,768,768]{2,1,0:T(8,128)(2,1)}, bf16[2,768,768]{2,1,0:T(8,128)(2,1)}, f32[2,8,384]{2,1...) custom-call(bf16[1152,768]{1,0:T(8,128)(2,1)} %get-tuple-element.69., ...), custom_call_target="tpu_custom_call" | custom-call | flops 51999997952 | bytes 80000000 | tf_op jit(solution)/shard_map/attention_backward/pallas_call | solution.py:1047
  226.5 57.2 %tail.1 = (bf16[1024,768]{1,0:T(8,128)(2,1)}, bf16[1024,768]{1,0:T(8,128)(2,1)}, bf16[768,768]{1,0:T(8,128)(2,1)}, f32[32,768]{1,0:T(8,128)}, f32[32,128]{1,0:T(8,128)}) custom-call(f32[8,768]{1,0:T(8,128)} %get-tuple-element.68.sums2, f32[2,8,384]{2,1,0:T(8,128)} %get-tuple-element.78.bias, f32[128,128]{1,0:T(8,128)} %get-tuple-element.79.rel_sum, ...), custom_call_target="tpu_custom_call" | custom-call | flops 4000000000 | bytes 20000000 | tf_op jit(solution)/shard_map/tail/pallas_call | solution.py:1296
  283.7 0.0 copy-start.1
  283.7 6.2 %finish.1 = (f32[768,768]{1,0:T(8,128)}, f32[768,768]{1,0:T(8,128)}, f32[576,768]{1,0:T(8,128)}, f32[192,768]{1,0:T(8,128)}, bf16[2,192,768]{2,1,0:T(8,128)(2,1)...) custom-call(bf16[768,768]{1,0:T(8,128)(2,1)} %get-tuple-element.90.f, ...), custom_call_target="tpu_custom_call" | custom-call | bytes 14000000 | tf_op jit(solution)/shard_map/finish/pallas_call | solution.py:1393
  289.9 1.3 dynamic-slice_reduce_fusion
  291.2 0.0 copy-done.1
  291.2 0.0 copy-start
  291.2 1.1 copy.36
  292.4 0.8 copy-done
  293.2 1.1 copy.37
Async XLA Ops:
  283.7 7.6 %copy-start.1 = (bf16[1024,768]{1,0:T(8,128)(2,1)S(1)}, bf16[1024,768]{1,0:T(8,128)(2,1)}, u32[]{:S(2)}) copy-start(bf16[1024,768]{1,0:T(8,128)(2,1)} %get-tuple-element.88) | copy-start | bytes 4718596
  291.2 2.0 copy-start

commit v8 on v7

--- a/solution.py
+++ b/solution.py
@@ -403,8 +403,9 @@
 
 
 def forward_kernel(
-    x, g, wqkv, wproj, fc1, fc2, notes_in, params, wrel, bits, lanes, sides, keys,
-    xs, gs, n1_all, qkv, mixed, attn, peak, weights_out, across1, across2, beside1, beside2, small_out,
+    x, g, wqkv, wproj, fc1, fc2, vectors, qv_bias, rel_tables, bits, lanes, sides, keys,
+    xs, gs, n1_all, qkv, mixed, attn, peak, params, wrel, weights_out, across1, across2, beside1,
+    beside2, small_out,
     xext, gext, weights, smalls, projected, sends, recvs, locals_,
 ):
     step = pl.program_id(0)
@@ -417,7 +418,7 @@
     send = Sender(sends, recvs, locals_)
     x_halo = Halo(send, 0, x, xext, device, rows)
     g_halo = Halo(send, 2, g, gext, device, rows)
-    small = notes_in.at[pl.ds(0, 8), :]
+    small = params.at[pl.ds(0, 8), :]
 
     own_pack = [
         send.remote(4, wqkv, weights.at[0, 0:3, pl.ds(part, part), :], {"tensor": beside}),
@@ -468,6 +469,17 @@
 
     @pl.when(step == 0)
     def _():
+        params[...] = jnp.zeros_like(params)
+        for ref, row in zip(vectors, (0, 8, 9, 10, 11, 12, 13), strict=True):
+            params[row, :] = ref[...]
+        for j in range(2):
+            params[1 + 2 * j, 0:part] = qv_bias[j, :]
+            params[2 + 2 * j, part:half] = qv_bias[j, :]
+        wrel[...] = jnp.zeros_like(wrel)
+        span = 2 * WIN - 1
+        for ref, at in zip(rel_tables, (0, 32), strict=True):
+            wrel[HD + at : HD + at + span, :HD] = ref[...]
+            wrel[at : at + span, HD:] = ref[...]
         for ref in (xext, gext):
             ref[pl.ds(0, LEFT)] = jnp.zeros((LEFT, GRID, width), narrow)
             ref[pl.ds(LEFT + rows, RIGHT)] = jnp.zeros((RIGHT, GRID, width), narrow)
@@ -605,7 +617,7 @@
     return jax.ShapeDtypeStruct(shape, dtype)
 
 
-def forward(x, g, wqkv, wproj, fc1, fc2, params, wrel, tables):
+def forward(x, g, wqkv, wproj, fc1, fc2, vectors, qv_bias, rel_tables, tables):
     rows, _, width = x.shape
     half = 2 * wproj.shape[0]
     slab = (SLAB, width)
@@ -617,6 +629,8 @@
         (of((2, SLAB, half)), whole((2, SLAB, half))),
         (of(slab, single), whole(slab)),
         (of((2, 8, ROWS), single), whole((2, 8, ROWS))),
+        (of((16, width), single), whole((16, width))),
+        (of((LANES, LANES)), whole((LANES, LANES))),
         (of((2, 4, half, width)), ANY),
         (of(fc1.shape), ANY),
         (of(fc2.shape), ANY),
@@ -624,13 +638,14 @@
         (of(fc2.shape), ANY),
         (of((SPLIT, 8, width), single), ANY),
     ]
-    operands = (x, g, wqkv, wproj, fc1, fc2, params, params, wrel, *tables)
+    operands = (x, g, wqkv, wproj, fc1, fc2)
+    known = (tuple(vectors), qv_bias, tuple(rel_tables), *tables)
     ext = (rows + LEFT + RIGHT, GRID, width)
     return pl.pallas_call(
         forward_kernel,
         out_shape=[o[0] for o in outs],
         grid=(2 * SLOTS,),
-        in_specs=[ANY] * 7 + [whole(a.shape) for a in operands[7:]],
+        in_specs=[ANY] * 6 + list(jax.tree.map(lambda a: whole(a.shape), known)),
         out_specs=[o[1] for o in outs],
         scratch_shapes=[
             pltpu.VMEM(ext, narrow),
@@ -649,7 +664,7 @@
             flops=26_000_000_000, bytes_accessed=60_000_000, transcendentals=8_000_000
         ),
         name="attention_forward",
-    )(*operands)
+    )(*operands, *known)
 
 
 CHUNK = SLAB // 3
@@ -670,9 +685,9 @@
 
 def mlp_kernel(
     xs, attn, gs, params, smalls, across1, across2, beside1, beside2, own1, own2,
-    out, dx1, da, sums, near1, near2, far1, rest, gb,
+    out_away, dx1_away, da_away, sums, near1, near2, far1, rest, gb,
     n2, n2t, gt, branch, dn2, w1, w2, grad1, grad2, got1, got2, near_got1, near_got2, landing,
-    hs, zs, sends, recvs, locals_,
+    hs, zs, out, dx1, da, sends, recvs, locals_,
 ):
     step = pl.program_id(0)
     room = step % 2
@@ -700,6 +715,14 @@
     upper = got2.shape[0] // 2
     mine = (image % 2) * upper
     halving = send.remote(5, got2.at[rows_at(upper - mine, upper), :], landing, mate)
+
+    def leaving(c):
+        sl = rows_at(c * STRIP, STRIP)
+        return [
+            send.local(6 + 3 * c + k, here.at[sl, :], away.at[sl, :])
+            for k, (here, away) in enumerate(((out, out_away), (dx1, dx1_away), (da, da_away)))
+        ]
+
     near_swaps = [
         send.remote(6, grad1.at[2], near_got1, {"tensor": beside}),
         send.remote(7, grad2.at[2], near_got2, {"tensor": beside}),
@@ -800,12 +823,17 @@
             dx1[sl, :] = total
             low = total.astype(narrow)
             da[sl, :] = low
+            for copy in leaving(c):
+                copy.start()
             sums[0:1, :] += jnp.sum(grad * normal, axis=0, keepdims=True)
             sums[1:2, :] += jnp.sum(grad, axis=0, keepdims=True)
             sums[2:3, :] += jnp.sum(low.astype(single), axis=0, keepdims=True)
             sums[3:4, :] += jnp.sum(cot, axis=0, keepdims=True)
 
         crossing.wait()
+        for c in range(SLAB // STRIP):
+            for copy in leaving(c):
+                copy.wait()
 
 
 def mlp(residents, across, beside, own):
@@ -813,9 +841,9 @@
     slab = (SLAB, width)
     square = (width, local)
     outs = [
-        (of(slab), whole(slab)),
-        (of(slab, single), whole(slab)),
-        (of(slab), whole(slab)),
+        (of(slab), ANY),
+        (of(slab, single), ANY),
+        (of(slab), ANY),
         (of((8, width), single), whole((8, width))),
         (of(square), whole(square)),
         (of(square), whole(square)),
@@ -838,9 +866,12 @@
             *[pltpu.VMEM(square, narrow)] * 4,
             pltpu.VMEM((width // 2, local), narrow),
             *[pltpu.VMEM((SLAB, local), narrow)] * 2,
+            pltpu.VMEM(slab, narrow),
+            pltpu.VMEM(slab, single),
+            pltpu.VMEM(slab, narrow),
             pltpu.SemaphoreType.DMA((8,)),
             pltpu.SemaphoreType.DMA((8,)),
-            pltpu.SemaphoreType.DMA((6,)),
+            pltpu.SemaphoreType.DMA((6 + 3 * (SLAB // STRIP),)),
         ],
         compiler_params=pltpu.CompilerParams(
             vmem_limit_bytes=VMEM, collective_id=1, has_side_effects=True
@@ -929,8 +960,7 @@
         (7, 0): swap_far,
         (7, 1): fourth,
         (8, 0): cross_far,
-        (9, 2): functools.partial(hand, 1),
-        (11, 0): functools.partial(hand, 0),
+        (10, 2): functools.partial(hand, 1),
     }
 
     def fire(section):
@@ -1013,7 +1043,7 @@
     @pl.when(step == 2 * SLOTS - 1)
     def _():
         for (halver, _, _), total in zip(halvers, summed, strict=True):
-            halver.back(0, total).wait()
+            halver.back(1, total).wait()
         far_cross.wait()
 
 
@@ -1094,14 +1124,15 @@
 def tail_kernel(
     rows_held, images,
     sums2, bias, rel_sum, fc_bias, peak, params,
-    out_in, keep_in, crossed_in, xs_in, dx1_in, give, dqkv, weights,
-    output, input_grad, packed, totals, tops,
+    out_in, keep_in, crossed_in, xs_in, dx1_in, part1, part2, give, dqkv, weights,
+    output, input_grad, packed, totals, tops, summed1, summed2,
     ext0, ext1, below0, below1, above0, above1, got, landing, held, sum_land, top_land, back, grads,
     packs, out, keep, crossed, xs, dx1, sends, recvs, locals_,
 ):
     device, image = lax.axis_index("tensor"), lax.axis_index("dp")
     beside, across, corner = partners(device)
     send = Sender(sends, recvs, locals_)
+    hand_base = 1 + 2 * Halver.copies(images) + 4 + 2 * (1 + images.bit_length())
     early = [send.local(0, keep_in.at[1], keep), send.local(1, crossed_in, crossed)]
     loads = [
         send.local(2, dqkv, grads),
@@ -1111,6 +1142,19 @@
     ]
     late = send.local(6, out_in, out)
     start_all(early + loads + [late])
+    hand_last, stay = [], []
+    for k, (part, summed, order) in enumerate(
+        ((part1, summed1, (1, 0, 2)), (part2, summed2, (0, 1, 2)))
+    ):
+        mate, kept, _, length, _ = Halver(
+            send, 0, image, images, 0, part.shape[0], order
+        ).stages[0]
+        cut = rows_at(kept, length)
+        stay.append(send.local(7 + k, part.at[cut, :], summed.at[cut, :]))
+        hand_last.append(
+            send.remote(hand_base + k, part.at[cut, :], summed.at[cut, :], {"dp": mate})
+        )
+    start_all(stay)
     per = Halver.copies(images)
     middle = held.shape[0] // 2
     landing_rows = Halver.landing_rows(images, middle)
@@ -1250,6 +1294,7 @@
     small_start(1)
     reduce_finish(1)
     reduce_start(2)
+    start_all(hand_last)
     late.wait()
     place_windows(rows_held, device, out, ext0, 0, 4)
     small_finish(1)
@@ -1278,6 +1323,8 @@
             small_start(k + 1)
     halo_finish(halos0, ext0, below0, above0, output)
     hand_finish(0)
+    for copy in stay + hand_last:
+        copy.wait()
 
 
 def tail(rows_held, images, *operands):
@@ -1287,17 +1334,18 @@
     tokens = rows_held * GRID
     bits = images.bit_length() - 1
     landing = 2 * Halver.landing_rows(images, packed[0] // 2)
-    copies = 1 + 2 * Halver.copies(images) + 4 + 2 * (2 + bits)
+    copies = 1 + 2 * Halver.copies(images) + 4 + 2 * (2 + bits) + 2
     ext = ((rows_held + LEFT + RIGHT) * GRID, width)
     outs = [
         of((tokens, width)), of((tokens, width)), of(packed),
         of((32, width), single), of((32, LANES), single),
+        of(operands[-5].shape), of(operands[-4].shape),
     ]
     return pl.pallas_call(
         functools.partial(tail_kernel, rows_held, images),
         out_shape=outs,
-        in_specs=[pl.BlockSpec(memory_space=pltpu.VMEM)] * (len(operands) - 8) + [ANY] * 8,
-        out_specs=[pl.BlockSpec(memory_space=pltpu.VMEM)] * len(outs),
+        in_specs=[pl.BlockSpec(memory_space=pltpu.VMEM)] * (len(operands) - 10) + [ANY] * 10,
+        out_specs=[pl.BlockSpec(memory_space=pltpu.VMEM)] * 5 + [ANY] * 2,
         scratch_shapes=[
             pltpu.VMEM(ext, narrow),
             pltpu.VMEM(ext, narrow),
@@ -1319,7 +1367,7 @@
             pltpu.VMEM((SLAB, width), single),
             pltpu.SemaphoreType.DMA((copies,)),
             pltpu.SemaphoreType.DMA((copies,)),
-            pltpu.SemaphoreType.DMA((7,)),
+            pltpu.SemaphoreType.DMA((9,)),
         ],
         compiler_params=pltpu.CompilerParams(
             vmem_limit_bytes=VMEM, collective_id=3, has_side_effects=True
@@ -1332,10 +1380,13 @@
 
 
 def finish_kernel(
-    fc1, fc2, gq, gp, totals, tops, wqkv,
-    grad_fc1, grad_fc2, grad_qkv, grad_proj, clipped, qv, fc1_bias, norms, proj_bias, fc2_bias, rel,
+    fc1, fc2, gq, gp, out_in, back_in, totals, tops, wqkv,
+    grad_fc1, grad_fc2, grad_qkv, grad_proj, out, back, clipped, qv, fc1_bias, norms, proj_bias,
+    fc2_bias, rel, head_max,
 ):
     device = lax.axis_index("tensor")
+    out[...] = out_in[...]
+    back[...] = back_in[...]
     grad_fc1[...] = fc1[...].astype(single)
     grad_fc2[...] = fc2[...].astype(single).T
     grad_qkv[...] = gq[...].astype(single)
@@ -1344,7 +1395,9 @@
     @pl.when(pl.program_id(0) == 0)
     def _():
         local = wqkv.shape[1]
-        limit = jnp.maximum(tops[pl.ds(pl.multiple_of(8 * device, 8), 8), :], CLIP)
+        largest = tops[pl.ds(pl.multiple_of(8 * device, 8), 8), :]
+        head_max[...] = largest.T[0, : local // HD]
+        limit = jnp.maximum(largest, CLIP)
         factor = jnp.sqrt(CLIP / limit)
         factor = jnp.concatenate([factor] * (wqkv.shape[2] // LANES), axis=1)
         for j in range(2):
@@ -1366,10 +1419,13 @@
                 rel[first : first + count, j, :] = totals[at : at + count, lane : lane + HD]
 
 
-def finish(summed1, summed2, gpack, totals, tops, wqkv):
+def finish(summed1, summed2, gpack, output, input_grad, totals, tops, wqkv):
     _, local, width = wqkv.shape
     hidden = summed1.shape[1]
     parts = 3
+    batch = output.shape[0] // 2
+    pages = pl.BlockSpec((batch, width), lambda i: (jnp.minimum(i, 1), 0))
+    heads = local // HD
     rows, cols, lines = width // parts, hidden // parts, 3 * local // parts
     few = local // parts
 
@@ -1382,6 +1438,8 @@
         (of((hidden, width), single), by_rows(cols, width)),
         (of((3 * local, width), single), by_rows(lines, width)),
         (of((local, width), single), by_rows(few, width)),
+        (of(output.shape), pages),
+        (of(output.shape), pages),
         (of((2, local, width)), whole((2, local, width))),
         (of((2, local), single), whole((2, local))),
         (of((hidden,), single), whole((hidden,))),
@@ -1389,6 +1447,7 @@
         (of((width,), single), whole((width,))),
         (of((width,), single), whole((width,))),
         (of((span, 2, HD), single), whole((span, 2, HD))),
+        (of((heads,), single), whole((heads,))),
     ]
     return pl.pallas_call(
         finish_kernel,
@@ -1399,6 +1458,8 @@
             pl.BlockSpec((width, cols), lambda i: (0, i)),
             by_rows(lines, width),
             by_rows(few, width, 3 * local // few),
+            pages,
+            pages,
             whole(totals.shape),
             whole(tops.shape),
             whole(wqkv.shape),
@@ -1407,7 +1468,7 @@
         compiler_params=pltpu.CompilerParams(vmem_limit_bytes=VMEM),
         cost_estimate=pl.CostEstimate(flops=0, bytes_accessed=14_000_000, transcendentals=0),
         name="finish",
-    )(summed1, summed2, gpack, gpack, totals, tops, wqkv)
+    )(summed1, summed2, gpack, gpack, output, input_grad, totals, tops, wqkv)
 
 
 def shards(
@@ -1431,36 +1492,19 @@
     width = inputs.shape[2]
     rows = inputs.shape[1] // GRID
     local = w_qkv.shape[2]
-    heads = local // HD
-    device = lax.axis_index("tensor")
     tables = lane_tables()
 
-    span = 2 * WIN - 1
-    wrel = sum(
-        jnp.pad(table, ((at, LANES - span - at), (side, HD - side)))
-        for table, at, side in (
-            (rel_h, HD, 0), (rel_w, HD + 32, 0), (rel_h, 0, HD), (rel_w, 32, HD),
-        )
-    )
-
-    entries = (
-        (fc1_bias, 0, 0), (qv_bias[0], 1, 0), (qv_bias[0], 2, local), (qv_bias[1], 3, 0),
-        (qv_bias[1], 4, local), (norm1_gain, 8, 0), (norm1_shift, 9, 0), (proj_bias, 10, 0),
-        (norm2_gain, 11, 0), (norm2_shift, 12, 0), (fc2_bias, 13, 0),
-    )
-    params = 0.0
-    for values, row, at in entries:
-        before = row * width + at
-        params = params + jnp.pad(values, (before, 16 * width - before - values.shape[0]))
-    params = params.reshape(16, width)
     wqkv = w_qkv.transpose(0, 2, 1)
 
     (
-        xs, gs, n1, qkv, mixed, attn, peak,
+        xs, gs, n1, qkv, mixed, attn, peak, params, wrel,
         weights, across1, across2, beside1, beside2, smalls,
     ) = forward(
-        *(a.reshape(rows, GRID, width) for a in (inputs, cotangent)), wqkv, w_proj, w_fc1, w_fc2, params,
-        wrel, tables
+        *(a.reshape(rows, GRID, width) for a in (inputs, cotangent)), wqkv, w_proj, w_fc1, w_fc2,
+        (
+            fc1_bias, norm1_gain, norm1_shift, proj_bias, norm2_gain, norm2_shift, fc2_bias,
+        ),
+        qv_bias, (rel_h, rel_w), tables
     )
     out, dx1, da, sums2, near1, near2, far1, rest, fc_bias = mlp(
         (
@@ -1471,18 +1515,17 @@
         (w_fc1, w_fc2),
     )
     images = lax.axis_size("dp")
-    dqkv, keep, give, bias, rel_sum, crossed, summed1, summed2 = backward(
+    dqkv, keep, give, bias, rel_sum, crossed, part1, part2 = backward(
         rows, images, da, n1, qkv, mixed, weights, wrel, tables, [near1, near2, far1], rest
     )
-    output, input_grad, gpack, totals, tops = tail(
+    output, input_grad, gpack, totals, tops, summed1, summed2 = tail(
         rows, images, sums2, bias, rel_sum, fc_bias, peak, params, out, keep, crossed, xs, dx1,
-        give, dqkv, weights,
+        part1, part2, give, dqkv, weights,
     )
     (
-        grad_fc1, grad_fc2, grad_qkv, grad_proj, clipped, grad_qv, grad_fc1_bias,
-        grad_norms, grad_proj_bias, grad_fc2_bias, grad_rel,
-    ) = finish(summed1, summed2, gpack, totals, tops, wqkv)
-    head_max = lax.dynamic_slice(tops, (8 * device, 0), (heads, 1))[:, 0]
+        grad_fc1, grad_fc2, grad_qkv, grad_proj, output, input_grad, clipped, grad_qv,
+        grad_fc1_bias, grad_norms, grad_proj_bias, grad_fc2_bias, grad_rel, head_max,
+    ) = finish(summed1, summed2, gpack, output, input_grad, totals, tops, wqkv)
 
     return (
         output[None],

time: 295 us -> 285 us (0.966)
  local copies, waits for them, and re-layouts: 5.82 us -> 0 us
    unnamed x6 -> x0, local copies, waits for them, and re-layouts: 3.12 us -> none
where the time goes in v8:
time: 285 us
  Pallas kernels  284 us (100%)
    pallas_call x1, Pallas kernels, backward(): pl.pallas_call(functools.partial(backward_kernel, rows_held, images), out...  79.9 us
    pallas_call x1, Pallas kernels, forward(): pl.pallas_call(forward_kernel, out_shape=[o[0] for o in outs], grid=(2 *...  71.1 us
    pallas_call x1, Pallas kernels, mlp(): pl.pallas_call(mlp_kernel, out_shape=[o[0] for o in outs], grid=(SPLIT,),...  67.7 us
    pallas_call x1, Pallas kernels, tail(): pl.pallas_call(functools.partial(tail_kernel, rows_held, images), out_sha...  57.9 us
    pallas_call x1, Pallas kernels, finish(): pl.pallas_call(finish_kernel, out_shape=[o[0] for o in outs], grid=(parts...  7.39 us

profile of v8, /device:TPU:0, one launch (start us, length us, event | category | flops | bytes accessed | tf_op | source)
XLA Modules:
  0.0 284.9 jit_solution(15503922410395934735)
XLA Ops:
  0.7 71.1 %attention_forward.1 = (bf16[1152,768]{1,0:T(8,128)(2,1)}, bf16[1152,768]{1,0:T(8,128)(2,1)}, bf16[1152,768]{1,0:T(8,128)(2,1)}, bf16[14,4,208,384]{3,2,1,0:T(8,...) custom-call(bf16[16,64,768]{2,1,0:T(8,128)(2,1)} %bitcast.13, ...), custom_call_target="tpu_custom_call" | custom-call | flops 25999998976 | bytes 60000000 | tf_op jit(solution)/shard_map/attention_forward/pallas_call | solution.py:644
  71.7 67.7 %mlp.1 = (bf16[1152,768]{1,0:T(8,128)(2,1)}, f32[1152,768]{1,0:T(8,128)}, bf16[1152,768]{1,0:T(8,128)(2,1)}, f32[8,768]{1,0:T(8,128)}, bf16[768,768]{1,0:T(8,128...) custom-call(bf16[1152,768]{1,0:T(8,128)(2,1)} %get-tuple-element.67., ...), custom_call_target="tpu_custom_call" | custom-call | flops 35999997952 | bytes 60000000 | tf_op jit(solution)/shard_map/mlp/pallas_call | solution.py:854
  139.5 79.9 %attention_backward.1 = (bf16[2,3,1152,384]{3,2,1,0:T(8,128)(2,1)}, bf16[2,768,768]{2,1,0:T(8,128)(2,1)}, bf16[2,768,768]{2,1,0:T(8,128)(2,1)}, f32[2,8,384]{2,1...) custom-call(bf16[1152,768]{1,0:T(8,128)(2,1)} %get-tuple-element.77., ...), custom_call_target="tpu_custom_call" | custom-call | flops 51999997952 | bytes 80000000 | tf_op jit(solution)/shard_map/attention_backward/pallas_call | solution.py:1077
  219.4 57.9 %tail.1 = (bf16[1024,768]{1,0:T(8,128)(2,1)}, bf16[1024,768]{1,0:T(8,128)(2,1)}, bf16[768,768]{1,0:T(8,128)(2,1)}, f32[32,768]{1,0:T(8,128)}, f32[32,128]{1,0:T(...) custom-call(f32[8,768]{1,0:T(8,128)} %get-tuple-element.76.sums2, f32[2,8,384]{2,1,0:T(8,128)} %get-tuple-element.87.bias, ...), custom_call_target="tpu_custom_call" | custom-call | flops 4000000000 | bytes 20000000 | tf_op jit(solution)/shard_map/tail/pallas_call | solution.py:1344
  277.3 7.4 %finish.1 = (f32[768,768]{1,0:T(8,128)}, f32[768,768]{1,0:T(8,128)}, f32[576,768]{1,0:T(8,128)}, f32[192,768]{1,0:T(8,128)}, bf16[1024,768]{1,0:T(8,128)(2,1)}, ...) custom-call(bf16[768,768]{1,0:T(8,128)(2,1)} %get-tuple-element.99.f, ...), custom_call_target="tpu_custom_call" | custom-call | bytes 14000000 | tf_op jit(solution)/shard_map/finish/pallas_call | solution.py:1452

commit v9 on v8

--- a/solution.py
+++ b/solution.py
@@ -404,9 +404,9 @@
 
 def forward_kernel(
     x, g, wqkv, wproj, fc1, fc2, vectors, qv_bias, rel_tables, bits, lanes, sides, keys,
-    xs, gs, n1_all, qkv, mixed, attn, peak, params, wrel, weights_out, across1, across2, beside1,
+    xs_out, gs, n1_out, qkv, mixed, attn, peak, params, wrel, weights_out, across1, across2, beside1,
     beside2, small_out,
-    xext, gext, weights, smalls, projected, sends, recvs, locals_,
+    xext, gext, weights, smalls, projected, xs, n1_all, sends, recvs, locals_,
 ):
     step = pl.program_id(0)
     far, slot = step // SLOTS, step % SLOTS
@@ -465,7 +465,12 @@
         send.local(3, small, smalls.at[0]),
     ]
     g_own = send.local(4, g, gext.at[pl.ds(LEFT, rows)])
-    kept = [send.local(5, weights, weights_out), send.local(6, smalls, small_out)]
+    kept = [
+        send.local(5, weights, weights_out),
+        send.local(6, smalls, small_out),
+        send.local(7, xs, xs_out),
+        send.local(8, n1_all, n1_out),
+    ]
 
     @pl.when(step == 0)
     def _():
@@ -622,9 +627,9 @@
     half = 2 * wproj.shape[0]
     slab = (SLAB, width)
     outs = [
+        (of(slab), ANY),
         (of(slab), whole(slab)),
-        (of(slab), whole(slab)),
-        (of(slab), whole(slab)),
+        (of(slab), ANY),
         (of((2 * SLOTS, 4, ROWS, half)), by_slot((4, ROWS, half))),
         (of((2, SLAB, half)), whole((2, SLAB, half))),
         (of(slab, single), whole(slab)),
@@ -653,9 +658,11 @@
             pltpu.VMEM((2, 4, half, width), narrow),
             pltpu.VMEM((SPLIT, 8, width), single),
             pltpu.VMEM((3, SLAB, half), narrow),
+            pltpu.VMEM(slab, narrow),
+            pltpu.VMEM(slab, narrow),
             pltpu.SemaphoreType.DMA((32,)),
             pltpu.SemaphoreType.DMA((32,)),
-            pltpu.SemaphoreType.DMA((7,)),
+            pltpu.SemaphoreType.DMA((9,)),
         ],
         compiler_params=pltpu.CompilerParams(
             vmem_limit_bytes=VMEM, collective_id=0, has_side_effects=True
@@ -1287,16 +1294,17 @@
     small_start(0)
     reduce_finish(0)
     reduce_start(1)
-    place_windows(rows_held, device, back, ext1, 0, SLOTS)
-    halos1 = halo(halo_base, ext1, below1, above1)
-    halo_start(halos1)
+    place_windows(rows_held, device, back, ext1, 0, 3)
     small_finish(0)
     small_start(1)
     reduce_finish(1)
     reduce_start(2)
     start_all(hand_last)
+    place_windows(rows_held, device, back, ext1, 3, SLOTS)
+    halos1 = halo(halo_base, ext1, below1, above1)
+    halo_start(halos1)
     late.wait()
-    place_windows(rows_held, device, out, ext0, 0, 4)
+    place_windows(rows_held, device, out, ext0, 0, 3)
     small_finish(1)
     small_start(2)
     reduce_finish(2)
@@ -1305,18 +1313,18 @@
         start, length = halver.final
         packed[rows_at(start, length), :] = held[rows_at(start, length), :]
     hand_start(2)
-    place_windows(rows_held, device, out, ext0, 4, SLOTS)
+    place_windows(rows_held, device, out, ext0, 3, SLOTS)
     halos0 = halo(halo_base + 2, ext0, below0, above0)
     halo_start(halos0)
     small_finish(2)
     small_start(3)
-    halo_finish(halos1, ext1, below1, above1, input_grad)
     hand_finish(2)
     hand_start(1)
     small_finish(3)
     small_start(4)
     hand_finish(1)
     hand_start(0)
+    halo_finish(halos1, ext1, below1, above1, input_grad)
     for k in range(4, len(ring)):
         small_finish(k)
         if k + 1 < len(ring):

time: 285 us -> 284 us (level)
  no operation moved by 1% of the time
where the time goes in v9:
time: 284 us; the launch traced here: 283 us
  Pallas kernels  282 us (99%)
    pallas_call x1, Pallas kernels, backward(): pl.pallas_call(functools.partial(backward_kernel, rows_held, images), out...  79.9 us
    pallas_call x1, Pallas kernels, forward(): pl.pallas_call(forward_kernel, out_shape=[o[0] for o in outs], grid=(2 *...  70 us
    pallas_call x1, Pallas kernels, mlp(): pl.pallas_call(mlp_kernel, out_shape=[o[0] for o in outs], grid=(SPLIT,),...  67.8 us
    pallas_call x1, Pallas kernels, tail(): pl.pallas_call(functools.partial(tail_kernel, rows_held, images), out_sha...  57.4 us
    pallas_call x1, Pallas kernels, finish(): pl.pallas_call(finish_kernel, out_shape=[o[0] for o in outs], grid=(parts...  7.39 us

profile of v9, /device:TPU:0, one launch (start us, length us, event | category | flops | bytes accessed | tf_op | source)
XLA Modules:
  0.0 283.3 jit_solution(10961425535115808815)
XLA Ops:
  0.7 70.0 %attention_forward.1 = (bf16[1152,768]{1,0:T(8,128)(2,1)}, bf16[1152,768]{1,0:T(8,128)(2,1)}, bf16[1152,768]{1,0:T(8,128)(2,1)}, bf16[14,4,208,384]{3,2,1,0:T(8,...) custom-call(bf16[16,64,768]{2,1,0:T(8,128)(2,1)} %bitcast.13, ...), custom_call_target="tpu_custom_call" | custom-call | flops 25999998976 | bytes 60000000 | tf_op jit(solution)/shard_map/attention_forward/pallas_call | solution.py:649
  70.7 67.8 %mlp.1 = (bf16[1152,768]{1,0:T(8,128)(2,1)}, f32[1152,768]{1,0:T(8,128)}, bf16[1152,768]{1,0:T(8,128)(2,1)}, f32[8,768]{1,0:T(8,128)}, bf16[768,768]{1,0:T(8,128...) custom-call(bf16[1152,768]{1,0:T(8,128)(2,1)} %get-tuple-element.67., ...), custom_call_target="tpu_custom_call" | custom-call | flops 35999997952 | bytes 60000000 | tf_op jit(solution)/shard_map/mlp/pallas_call | solution.py:861
  138.4 79.9 %attention_backward.1 = (bf16[2,3,1152,384]{3,2,1,0:T(8,128)(2,1)}, bf16[2,768,768]{2,1,0:T(8,128)(2,1)}, bf16[2,768,768]{2,1,0:T(8,128)(2,1)}, f32[2,8,384]{2,1...) custom-call(bf16[1152,768]{1,0:T(8,128)(2,1)} %get-tuple-element.77., ...), custom_call_target="tpu_custom_call" | custom-call | flops 51999997952 | bytes 80000000 | tf_op jit(solution)/shard_map/attention_backward/pallas_call | solution.py:1084
  218.3 57.4 %tail.1 = (bf16[1024,768]{1,0:T(8,128)(2,1)}, bf16[1024,768]{1,0:T(8,128)(2,1)}, bf16[768,768]{1,0:T(8,128)(2,1)}, f32[32,768]{1,0:T(8,128)}, f32[32,128]{1,0:T(...) custom-call(f32[8,768]{1,0:T(8,128)} %get-tuple-element.76.sums2, f32[2,8,384]{2,1,0:T(8,128)} %get-tuple-element.87.bias, ...), custom_call_target="tpu_custom_call" | custom-call | flops 4000000000 | bytes 20000000 | tf_op jit(solution)/shard_map/tail/pallas_call | solution.py:1352
  275.7 7.4 %finish.1 = (f32[768,768]{1,0:T(8,128)}, f32[768,768]{1,0:T(8,128)}, f32[576,768]{1,0:T(8,128)}, f32[192,768]{1,0:T(8,128)}, bf16[1024,768]{1,0:T(8,128)(2,1)}, ...) custom-call(bf16[768,768]{1,0:T(8,128)(2,1)} %get-tuple-element.99.f, ...), custom_call_target="tpu_custom_call" | custom-call | bytes 14000000 | tf_op jit(solution)/shard_map/finish/pallas_call | solution.py:1460

commit v10 on v9

--- a/solution.py
+++ b/solution.py
@@ -962,12 +962,12 @@
 
     events = {
         (0, 0): begin,
-        (3, 0): second,
-        (4, 2): third,
+        (3, 1): second,
+        (5, 0): third,
         (7, 0): swap_far,
-        (7, 1): fourth,
+        (7, 3): fourth,
         (8, 0): cross_far,
-        (10, 2): functools.partial(hand, 1),
+        (10, 3): functools.partial(hand, 1),
     }
 
     def fire(section):

time: 284 us -> 282 us (level)
  no operation moved by 1% of the time
where the time goes in v10:
time: 282 us
  Pallas kernels  281 us (100%)
    pallas_call x1, Pallas kernels, backward(): pl.pallas_call(functools.partial(backward_kernel, rows_held, images), out...  77.9 us
    pallas_call x1, Pallas kernels, forward(): pl.pallas_call(forward_kernel, out_shape=[o[0] for o in outs], grid=(2 *...  70 us
    pallas_call x1, Pallas kernels, mlp(): pl.pallas_call(mlp_kernel, out_shape=[o[0] for o in outs], grid=(SPLIT,),...  67.8 us
    pallas_call x1, Pallas kernels, tail(): pl.pallas_call(functools.partial(tail_kernel, rows_held, images), out_sha...  57.7 us
    pallas_call x1, Pallas kernels, finish(): pl.pallas_call(finish_kernel, out_shape=[o[0] for o in outs], grid=(parts...  7.39 us

profile of v10, /device:TPU:0, one launch (start us, length us, event | category | flops | bytes accessed | tf_op | source)
XLA Modules:
  0.0 281.7 jit_solution(5223369169151758339)
XLA Ops:
  0.7 70.0 %attention_forward.1 = (bf16[1152,768]{1,0:T(8,128)(2,1)}, bf16[1152,768]{1,0:T(8,128)(2,1)}, bf16[1152,768]{1,0:T(8,128)(2,1)}, bf16[14,4,208,384]{3,2,1,0:T(8,...) custom-call(bf16[16,64,768]{2,1,0:T(8,128)(2,1)} %bitcast.13, ...), custom_call_target="tpu_custom_call" | custom-call | flops 25999998976 | bytes 60000000 | tf_op jit(solution)/shard_map/attention_forward/pallas_call | solution.py:649
  70.7 67.8 %mlp.1 = (bf16[1152,768]{1,0:T(8,128)(2,1)}, f32[1152,768]{1,0:T(8,128)}, bf16[1152,768]{1,0:T(8,128)(2,1)}, f32[8,768]{1,0:T(8,128)}, bf16[768,768]{1,0:T(8,128...) custom-call(bf16[1152,768]{1,0:T(8,128)(2,1)} %get-tuple-element.67., ...), custom_call_target="tpu_custom_call" | custom-call | flops 35999997952 | bytes 60000000 | tf_op jit(solution)/shard_map/mlp/pallas_call | solution.py:861
  138.4 77.9 %attention_backward.1 = (bf16[2,3,1152,384]{3,2,1,0:T(8,128)(2,1)}, bf16[2,768,768]{2,1,0:T(8,128)(2,1)}, bf16[2,768,768]{2,1,0:T(8,128)(2,1)}, f32[2,8,384]{2,1...) custom-call(bf16[1152,768]{1,0:T(8,128)(2,1)} %get-tuple-element.77., ...), custom_call_target="tpu_custom_call" | custom-call | flops 51999997952 | bytes 80000000 | tf_op jit(solution)/shard_map/attention_backward/pallas_call | solution.py:1084
  216.4 57.7 %tail.1 = (bf16[1024,768]{1,0:T(8,128)(2,1)}, bf16[1024,768]{1,0:T(8,128)(2,1)}, bf16[768,768]{1,0:T(8,128)(2,1)}, f32[32,768]{1,0:T(8,128)}, f32[32,128]{1,0:T(...) custom-call(f32[8,768]{1,0:T(8,128)} %get-tuple-element.76.sums2, f32[2,8,384]{2,1,0:T(8,128)} %get-tuple-element.87.bias, ...), custom_call_target="tpu_custom_call" | custom-call | flops 4000000000 | bytes 20000000 | tf_op jit(solution)/shard_map/tail/pallas_call | solution.py:1352
  274.1 7.4 %finish.1 = (f32[768,768]{1,0:T(8,128)}, f32[768,768]{1,0:T(8,128)}, f32[576,768]{1,0:T(8,128)}, f32[192,768]{1,0:T(8,128)}, bf16[1024,768]{1,0:T(8,128)(2,1)}, ...) custom-call(bf16[768,768]{1,0:T(8,128)(2,1)} %get-tuple-element.99.f, ...), custom_call_target="tpu_custom_call" | custom-call | bytes 14000000 | tf_op jit(solution)/shard_map/finish/pallas_call | solution.py:1460
